TPU v7x, 32 devices: a whole 2x2x4 slice. The times are simulated.
32 devices in a mesh: row: 4 (over y, x), col: 2 (over core), vol: 4 (over z).
Axes of the slice: x: 2, y: 2, z: 4, core: 2. Of those that a mesh axis runs over, the one named last changes fastest.
Arguments:
- panel: bfloat16 [512, 131072], P('row', ('col', 'vol')), may hold values from -0.015625 to 0.015625
- density: float32 [32, 131072], P(None, ('col', 'vol')), may hold values from -6 to 6
- source: float32 [32, 32, 16, 512], P(None, 'row', 'col', 'vol'), may hold values from -6 to 6
- class_index: int32 [32, 16, 512], P('row', 'col', 'vol'), may hold values from 0 to 15
- class_values: float32 [16], replicated, may hold values from 0.2 to 5
- trace_count: int32 [4, 8], P('row'), may hold values from 1 to 64, 128 in all within a row
- trace_cell: int32 [4, 8, 64], P('row'), may hold values from 0 to 8191
Outputs:
- density_out: float32 [32, 131072], P(None, ('col', 'vol'))
- volume_out: float32 [32, 32, 16, 512], P(None, 'row', 'col', 'vol')
Inputs may be any that keep to these rules, and one draw needn't show every extreme that they name: `trace_count`: in each row r, the counts of the 8 blocks are 1 or more and sum to 128, so that every target of row tile r has exactly one live slot; the largest count of each row is 64. `trace_cell`: only the first trace_count[r, j] slots of block j are read; two slots may hit one cell.
All inputs are finite; a program needn't handle non-finite values.
Results may differ from a plain program's by a relative error of at most 0.00035.
Values may be sent and summed in bfloat16 or wider, within the bound.
No kernel may reach another device: no remote copies, remote signals or barrier semaphores. Data moves between devices by JAX's collectives and lax.ppermute only.
A program may use at most 128 MiB of HBM per device.

v0:
```python
import math

import jax
import jax.numpy as jnp
from jax import lax
from jax.sharding import PartitionSpec as P

SWEEPS = 4
OUTER = 2


MASS_TERM = 0.1
RELAXATION = 0.5
SPECTRUM_LOW = 0.1
SPECTRUM_HIGH = 2.0


def padded_2(value, sides, width):
    for axis, dim in sides:
        size, length = (lax.axis_size(axis), value.shape[dim])
        up = [(i, (i + 1) % size) for i in range(size - 1)]
        down = [(j, i) for i, j in up]
        last = lax.slice_in_dim(value, length - width, length, axis=dim)
        first = lax.slice_in_dim(value, 0, width, axis=dim)
        before = lax.ppermute(last, axis, up)
        after = lax.ppermute(first, axis, down)
        value = jnp.concatenate([before, value, after], axis=dim)
    return value


def relax_factors(count):
    middle = (SPECTRUM_HIGH + SPECTRUM_LOW) / 2.0
    spread = (SPECTRUM_HIGH - SPECTRUM_LOW) / 2.0
    return [
        1.0 / (middle + spread * math.cos(math.pi * (2 * order + 1) / (2 * count)))
        for order in range(count)
    ]


def neighbours(padded):
    center = padded[..., 1:-1, 1:-1, 1:-1]
    beside_all = padded[..., 2:, 1:-1, 1:-1] + padded[..., :-2, 1:-1, 1:-1]
    beside_all = beside_all + padded[..., 1:-1, 2:, 1:-1] + padded[..., 1:-1, :-2, 1:-1]
    beside_all = beside_all + padded[..., 1:-1, 1:-1, 2:] + padded[..., 1:-1, 1:-1, :-2]
    return (center, beside_all)


def local(panel, density, source, class_index, class_values, trace_count, trace_cell):
    factors = relax_factors(SWEEPS)
    classes = jnp.arange(class_values.shape[0], dtype=jnp.int32)
    conduct = jnp.sum(
        jnp.where(
            class_index[None] == classes[:, None, None, None],
            class_values[:, None, None, None],
            jnp.float32(0.0),
        ),
        axis=0,
    )
    diagonal = MASS_TERM + 6.0 * conduct
    counts = trace_count[0]
    block_index = lax.axis_index(("col", "vol"))
    offsets = jnp.cumsum(counts) - counts
    target_rows = panel.shape[0]
    slot_count = trace_cell.shape[2]
    slot_ids = jnp.arange(slot_count, dtype=jnp.int32)
    target_ids = jnp.arange(target_rows, dtype=jnp.int32)
    own_count = lax.dynamic_index_in_dim(counts, block_index, keepdims=False)
    first_target = lax.dynamic_index_in_dim(offsets, block_index, keepdims=False)
    cell_ids = lax.dynamic_index_in_dim(trace_cell[0], block_index, keepdims=False)
    live_slots = slot_ids < own_count
    select = (
        ((first_target + slot_ids)[:, None] == target_ids[None, :]) & live_slots[:, None]
    ).astype(jnp.float32)
    volume = jnp.zeros(source.shape, jnp.float32)
    field_shape = volume.shape
    share_width = density.shape[1] // lax.axis_size("row")
    share_state = lax.dynamic_slice_in_dim(
        density, lax.axis_index("row") * share_width, share_width, 1
    )
    rounded = density.astype(jnp.bfloat16)
    lead = field_shape[0]
    for iteration in range(OUTER):
        partial_value = lax.dot_general(
            rounded, panel, (((1,), (1,)), ((), ())), preferred_element_type=jnp.float32
        )
        potential = lax.psum(partial_value, ("col", "vol"))
        slot_values = jnp.dot(potential, select.T, precision=lax.Precision.HIGHEST)
        right_side = source.reshape(lead, -1).at[:, cell_ids].add(slot_values).reshape(field_shape)
        relax_volume = volume
        for factor in factors:
            padded = padded_2(relax_volume, (("row", 1), ("col", 2), ("vol", 3)), 1)
            center, beside_all = neighbours(padded)
            relax_volume = (
                center + factor * (right_side - diagonal * center + conduct * beside_all) / diagonal
            )
        volume = relax_volume
        mismatch = volume.reshape(lead, -1)[:, cell_ids] - slot_values
        own_fluxes = jnp.dot(mismatch, select, precision=lax.Precision.HIGHEST)
        fluxes = lax.psum(own_fluxes, ("col", "vol"))
        update = jnp.dot(fluxes.astype(jnp.bfloat16), panel, preferred_element_type=jnp.float32)
        share_state = share_state + RELAXATION * lax.psum_scatter(
            update, "row", scatter_dimension=1, tiled=True
        )
        if iteration + 1 < OUTER:
            rounded = lax.all_gather(share_state.astype(jnp.bfloat16), "row", axis=1, tiled=True)
    density = lax.all_gather(share_state, "row", axis=1, tiled=True)
    return (density, volume)


def solution(mesh):
    placed = (
        P("row", ("col", "vol")),
        P(None, ("col", "vol")),
        P(None, "row", "col", "vol"),
        P("row", "col", "vol"),
        P(),
        P("row", None),
        P("row", None, None),
    )
    return jax.shard_map(
        local,
        mesh=mesh,
        in_specs=placed,
        out_specs=(P(None, ("col", "vol")), P(None, "row", "col", "vol")),
        check_vma=False,
    )
```

profile of v0, /device:TPU:0, one launch (start us, length us, event | category | flops | bytes accessed | tf_op | source)
XLA Modules:
  0.0 585.2 jit_solution(7050335987216102525)
XLA Ops:
  8.5 5.5 collective-permute-start.1
  22.7 28.9 %psum.28 = f32[32,128]{1,0:T(8,128)S(1)} all-reduce(f32[32,128]{1,0:T(8,128)S(1)} %fusion.79), channel_id=1, replica_groups=mesh['row'=4,'col'=2,'vol'=4] {'col','vol'}, use_global_device_ids=true, to_apply=%region_0.1 | all-reduce | flops 4096 | bytes 32768 | tf_op jit(solution)/shard_map/psum | solution.py:86
  67.1 4.6 collective-permute-start.5
  79.6 5.0 scatter_fusion
  95.4 5.0 collective-permute-start.7
  117.0 4.6 collective-permute-start.11
  129.7 5.2 collective-permute-start.13
  150.7 5.0 collective-permute-start.17
  164.1 5.9 %collective-permute-start.19 = (f32[32,1,8,128]{3,0,2,1:T(8,128)S(1)}, f32[32,1,8,128]{3,0,2,1:T(8,128)S(1)}, u32[]{:S(2)}, u32[]{:S(2)}) collective-permute-start(f32[32,1,8,128]{3,0,2,1:T(8,128)S(1)} %get-tuple-element.46), channel_id=1, source_target_pairs={{0,8},{8,16},{16,24},{1,9},{9,17},{17,25},{2,10},{10,18},{18,26},{... | collective-permute-start | bytes 393224 | tf_op jit(solution)/shard_map/ppermute | solution.py:25
  187.1 4.9 collective-permute-start.23
  204.7 29.4 %psum.29 = bf16[32,128]{1,0:T(8,128)(2,1)S(1)} all-reduce(f32[32,128]{1,0:T(8,128)S(1)} %fusion.87), channel_id=1, replica_groups=mesh['row'=4,'col'=2,'vol'=4] {'col','vol'}, use_global_device_ids=true, to_apply=%region_4.5 | all-reduce | flops 4096 | bytes 24576 | tf_op jit(solution)/shard_map/psum | solution.py:99
  238.4 38.0 %reduce-scatter.3.cloned.1.call-done = f32[32,4096]{1,0:T(8,128)} async-done(((f32[32,16384]{1,0:T(8,128)}), f32[32,4096]{1,0:T(8,128)}) %reduce-scatter.3.cloned.1.call-update) | async-done | bytes 524304 | tf_op jit(solution)/shard_map/reduce_scatter | solution.py:101
  279.7 4.6 collective-permute-start.25
  315.1 27.5 %psum.30 = f32[32,128]{1,0:T(8,128)S(1)} all-reduce(f32[32,128]{1,0:T(8,128)S(1)} %fusion.120), channel_id=1, replica_groups=mesh['row'=4,'col'=2,'vol'=4] {'col','vol'}, use_global_device_ids=true, to_apply=%region_6.7 | all-reduce | flops 4096 | bytes 32768 | tf_op jit(solution)/shard_map/psum | solution.py:86
  342.9 5.0 scatter_fusion.1
  355.0 6.1 %collective-permute-start.31 = (f32[32,1,8,128]{3,0,2,1:T(8,128)S(1)}, f32[32,1,8,128]{3,0,2,1:T(8,128)S(1)}, u32[]{:S(2)}, u32[]{:S(2)}) collective-permute-start(f32[32,1,8,128]{3,0,2,1:T(8,128)S(1)} %get-tuple-element.42), channel_id=1, source_target_pairs={{0,8},{8,16},{16,24},{1,9},{9,17},{17,25},{2,10},{10,18},{18,26},{... | collective-permute-start | bytes 393224 | tf_op jit(solution)/shard_map/ppermute | solution.py:25
  378.2 4.6 collective-permute-start.35
  390.9 5.9 %collective-permute-start.37 = (f32[32,1,8,128]{3,0,2,1:T(8,128)S(1)}, f32[32,1,8,128]{3,0,2,1:T(8,128)S(1)}, u32[]{:S(2)}, u32[]{:S(2)}) collective-permute-start(f32[32,1,8,128]{3,0,2,1:T(8,128)S(1)} %get-tuple-element.40), channel_id=1, source_target_pairs={{0,8},{8,16},{16,24},{1,9},{9,17},{17,25},{2,10},{10,18},{18,26},{... | collective-permute-start | bytes 393224 | tf_op jit(solution)/shard_map/ppermute | solution.py:25
  412.5 5.0 collective-permute-start.41
  425.9 5.9 %collective-permute-start.43 = (f32[32,1,8,128]{3,0,2,1:T(8,128)S(1)}, f32[32,1,8,128]{3,0,2,1:T(8,128)S(1)}, u32[]{:S(2)}, u32[]{:S(2)}) collective-permute-start(f32[32,1,8,128]{3,0,2,1:T(8,128)S(1)} %get-tuple-element.38), channel_id=1, source_target_pairs={{0,8},{8,16},{16,24},{1,9},{9,17},{17,25},{2,10},{10,18},{18,26},{... | collective-permute-start | bytes 393224 | tf_op jit(solution)/shard_map/ppermute | solution.py:25
  448.4 4.9 collective-permute-start.47
  466.1 29.4 %psum.31 = bf16[32,128]{1,0:T(8,128)(2,1)S(1)} all-reduce(f32[32,128]{1,0:T(8,128)S(1)} %fusion.83), channel_id=1, replica_groups=mesh['row'=4,'col'=2,'vol'=4] {'col','vol'}, use_global_device_ids=true, to_apply=%region_8.9 | all-reduce | flops 4096 | bytes 24576 | tf_op jit(solution)/shard_map/psum | solution.py:99
  499.7 38.0 %reduce-scatter.5.cloned.1.call-done = f32[32,4096]{1,0:T(8,128)} async-done(((f32[32,16384]{1,0:T(8,128)}), f32[32,4096]{1,0:T(8,128)}) %reduce-scatter.5.cloned.1.call-update) | async-done | bytes 524304 | tf_op jit(solution)/shard_map/reduce_scatter | solution.py:101
  541.4 33.8 %all-gather.5.cloned.1.call-done = f32[32,16384]{1,0:T(8,128)} async-done(((f32[32,4096]{1,0:T(8,128)}), f32[32,16384]{1,0:T(8,128)}) %all-gather.5.cloned.1.call-update) | async-done | bytes 2097168 | tf_op jit(solution)/shard_map/all_gather | solution.py:106
  (247 shorter events, 257.3 us)
Async XLA Ops:
  7.2 269.2 %reduce-scatter.3.cloned.1.call-start = ((), (), s32[]{:S(2)}) async-start(), calls=%async_computation.2 | async-start | bytes 2621440 | tf_op jit(solution)/shard_map/reduce_scatter | solution.py:101
  7.2 45.0 %collective-permute-start = (f32[32,1,8,128]{3,0,2,1:T(8,128)S(1)}, f32[32,1,8,128]{3,0,2,1:T(8,128)S(1)}, u32[]{:S(2)}, u32[]{:S(2)}) collective-permute-start(f32[32,1,8,128]{3,0,2,1:T(8,128)S(1)} %broadcast.65), channel_id=1, source_target_pairs={{8,0},{16,8},{24,16},{9,1},{17,9},{25,17},{10,2},{18,10},{26,18},{... | collective-permute-start | bytes 393224 | tf_op jit(solution)/shard_map/ppermute | solution.py:26
  8.5 43.7 %collective-permute-start.1 = (f32[32,1,8,128]{3,0,2,1:T(8,128)S(1)}, f32[32,1,8,128]{3,0,2,1:T(8,128)S(1)}, u32[]{:S(2)}, u32[]{:S(2)}) collective-permute-start(f32[32,1,8,128]{3,0,2,1:T(8,128)S(1)} %broadcast.65), channel_id=1, source_target_pairs={{0,8},{8,16},{16,24},{1,9},{9,17},{17,25},{2,10},{10,18},{18,26},{... | collective-permute-start | bytes 393224 | tf_op jit(solution)/shard_map/ppermute | solution.py:25
  63.3 24.1 %collective-permute-start.4 = (f32[32,10,10,1]{0,2,3,1:T(8,128)S(1)}, f32[32,10,10,1]{0,2,3,1:T(8,128)S(1)}, u32[]{:S(2)}, u32[]{:S(2)}) collective-permute-start(f32[32,10,10,1]{0,2,3,1:T(8,128)S(1)} %copy.75), channel_id=1, source_target_pairs={{1,0},{2,1},{3,2},{5,4},{6,5},{7,6},{9,8},{10,9},{11,10},{13,12},{... | collective-permute-start | bytes 38408 | tf_op jit(solution)/shard_map/ppermute | solution.py:26
  67.1 22.3 %collective-permute-start.5 = (f32[32,10,10,1]{0,2,3,1:T(8,128)S(1)}, f32[32,10,10,1]{0,2,3,1:T(8,128)S(1)}, u32[]{:S(2)}, u32[]{:S(2)}) collective-permute-start(f32[32,10,10,1]{0,2,3,1:T(8,128)S(1)} %copy.77), channel_id=1, source_target_pairs={{0,1},{1,2},{2,3},{4,5},{5,6},{6,7},{8,9},{9,10},{10,11},{12,13},{... | collective-permute-start | bytes 38408 | tf_op jit(solution)/shard_map/ppermute | solution.py:25
  94.1 7.8 %collective-permute-start.6 = (f32[32,1,8,128]{3,0,2,1:T(8,128)S(1)}, f32[32,1,8,128]{3,0,2,1:T(8,128)S(1)}, u32[]{:S(2)}, u32[]{:S(2)}) collective-permute-start(f32[32,1,8,128]{3,0,2,1:T(8,128)S(1)} %get-tuple-element.51), channel_id=1, source_target_pairs={{8,0},{16,8},{24,16},{9,1},{17,9},{25,17},{10,2},{18,10},{26,18},{... | collective-permute-start | bytes 393224 | tf_op jit(solution)/shard_map/ppermute | solution.py:26
  95.4 7.7 %collective-permute-start.7 = (f32[32,1,8,128]{3,0,2,1:T(8,128)S(1)}, f32[32,1,8,128]{3,0,2,1:T(8,128)S(1)}, u32[]{:S(2)}, u32[]{:S(2)}) collective-permute-start(f32[32,1,8,128]{3,0,2,1:T(8,128)S(1)} %get-tuple-element.50), channel_id=1, source_target_pairs={{0,8},{8,16},{16,24},{1,9},{9,17},{17,25},{2,10},{10,18},{18,26},{... | collective-permute-start | bytes 393224 | tf_op jit(solution)/shard_map/ppermute | solution.py:25
  113.3 8.3 %collective-permute-start.10 = (f32[32,10,10,1]{0,2,3,1:T(8,128)S(1)}, f32[32,10,10,1]{0,2,3,1:T(8,128)S(1)}, u32[]{:S(2)}, u32[]{:S(2)}) collective-permute-start(f32[32,10,10,1]{0,2,3,1:T(8,128)S(1)} %copy.80), channel_id=1, source_target_pairs={{1,0},{2,1},{3,2},{5,4},{6,5},{7,6},{9,8},{10,9},{11,10},{13,12},{... | collective-permute-start | bytes 38408 | tf_op jit(solution)/shard_map/ppermute | solution.py:26
  128.4 7.9 %collective-permute-start.12 = (f32[32,1,8,128]{3,0,2,1:T(8,128)S(1)}, f32[32,1,8,128]{3,0,2,1:T(8,128)S(1)}, u32[]{:S(2)}, u32[]{:S(2)}) collective-permute-start(f32[32,1,8,128]{3,0,2,1:T(8,128)S(1)} %get-tuple-element.49), channel_id=1, source_target_pairs={{8,0},{16,8},{24,16},{9,1},{17,9},{25,17},{10,2},{18,10},{26,18},{... | collective-permute-start | bytes 393224 | tf_op jit(solution)/shard_map/ppermute | solution.py:26
  129.7 7.8 %collective-permute-start.13 = (f32[32,1,8,128]{3,0,2,1:T(8,128)S(1)}, f32[32,1,8,128]{3,0,2,1:T(8,128)S(1)}, u32[]{:S(2)}, u32[]{:S(2)}) collective-permute-start(f32[32,1,8,128]{3,0,2,1:T(8,128)S(1)} %get-tuple-element.48), channel_id=1, source_target_pairs={{0,8},{8,16},{16,24},{1,9},{9,17},{17,25},{2,10},{10,18},{18,26},{... | collective-permute-start | bytes 393224 | tf_op jit(solution)/shard_map/ppermute | solution.py:25
  162.8 8.7 %collective-permute-start.18 = (f32[32,1,8,128]{3,0,2,1:T(8,128)S(1)}, f32[32,1,8,128]{3,0,2,1:T(8,128)S(1)}, u32[]{:S(2)}, u32[]{:S(2)}) collective-permute-start(f32[32,1,8,128]{3,0,2,1:T(8,128)S(1)} %get-tuple-element.47), channel_id=1, source_target_pairs={{8,0},{16,8},{24,16},{9,1},{17,9},{25,17},{10,2},{18,10},{26,18},{... | collective-permute-start | bytes 393224 | tf_op jit(solution)/shard_map/ppermute | solution.py:26
  164.1 8.5 %collective-permute-start.19 = (f32[32,1,8,128]{3,0,2,1:T(8,128)S(1)}, f32[32,1,8,128]{3,0,2,1:T(8,128)S(1)}, u32[]{:S(2)}, u32[]{:S(2)}) collective-permute-start(f32[32,1,8,128]{3,0,2,1:T(8,128)S(1)} %get-tuple-element.46), channel_id=1, source_target_pairs={{0,8},{8,16},{16,24},{1,9},{9,17},{17,25},{2,10},{10,18},{18,26},{... | collective-permute-start | bytes 393224 | tf_op jit(solution)/shard_map/ppermute | solution.py:25
  183.3 8.6 %collective-permute-start.22 = (f32[32,10,10,1]{0,2,3,1:T(8,128)S(1)}, f32[32,10,10,1]{0,2,3,1:T(8,128)S(1)}, u32[]{:S(2)}, u32[]{:S(2)}) collective-permute-start(f32[32,10,10,1]{0,2,3,1:T(8,128)S(1)} %copy.90), channel_id=1, source_target_pairs={{1,0},{2,1},{3,2},{5,4},{6,5},{7,6},{9,8},{10,9},{11,10},{13,12},{... | collective-permute-start | bytes 38408 | tf_op jit(solution)/shard_map/ppermute | solution.py:26
  238.3 72.8 %all-gather.3.cloned.1.call-start = ((), (), s32[]{:S(2)}) async-start(), calls=%async_computation.3 | async-start | bytes 1310720 | tf_op jit(solution)/shard_map/all_gather | solution.py:105
  278.4 259.4 %reduce-scatter.5.cloned.1.call-start = ((), (), s32[]{:S(2)}) async-start(), calls=%async_computation.4 | async-start | bytes 2621440 | tf_op jit(solution)/shard_map/reduce_scatter | solution.py:101
  353.7 9.3 %collective-permute-start.30 = (f32[32,1,8,128]{3,0,2,1:T(8,128)S(1)}, f32[32,1,8,128]{3,0,2,1:T(8,128)S(1)}, u32[]{:S(2)}, u32[]{:S(2)}) collective-permute-start(f32[32,1,8,128]{3,0,2,1:T(8,128)S(1)} %get-tuple-element.43), channel_id=1, source_target_pairs={{8,0},{16,8},{24,16},{9,1},{17,9},{25,17},{10,2},{18,10},{26,18},{... | collective-permute-start | bytes 393224 | tf_op jit(solution)/shard_map/ppermute | solution.py:26
  355.0 9.2 %collective-permute-start.31 = (f32[32,1,8,128]{3,0,2,1:T(8,128)S(1)}, f32[32,1,8,128]{3,0,2,1:T(8,128)S(1)}, u32[]{:S(2)}, u32[]{:S(2)}) collective-permute-start(f32[32,1,8,128]{3,0,2,1:T(8,128)S(1)} %get-tuple-element.42), channel_id=1, source_target_pairs={{0,8},{8,16},{16,24},{1,9},{9,17},{17,25},{2,10},{10,18},{18,26},{... | collective-permute-start | bytes 393224 | tf_op jit(solution)/shard_map/ppermute | solution.py:25
  374.5 8.3 %collective-permute-start.34 = (f32[32,10,10,1]{0,2,3,1:T(8,128)S(1)}, f32[32,10,10,1]{0,2,3,1:T(8,128)S(1)}, u32[]{:S(2)}, u32[]{:S(2)}) collective-permute-start(f32[32,10,10,1]{0,2,3,1:T(8,128)S(1)} %copy.103), channel_id=1, source_target_pairs={{1,0},{2,1},{3,2},{5,4},{6,5},{7,6},{9,8},{10,9},{11,10},{13,12},{... | collective-permute-start | bytes 38408 | tf_op jit(solution)/shard_map/ppermute | solution.py:26
  389.6 8.6 %collective-permute-start.36 = (f32[32,1,8,128]{3,0,2,1:T(8,128)S(1)}, f32[32,1,8,128]{3,0,2,1:T(8,128)S(1)}, u32[]{:S(2)}, u32[]{:S(2)}) collective-permute-start(f32[32,1,8,128]{3,0,2,1:T(8,128)S(1)} %get-tuple-element.41), channel_id=1, source_target_pairs={{8,0},{16,8},{24,16},{9,1},{17,9},{25,17},{10,2},{18,10},{26,18},{... | collective-permute-start | bytes 393224 | tf_op jit(solution)/shard_map/ppermute | solution.py:26
  390.9 8.4 %collective-permute-start.37 = (f32[32,1,8,128]{3,0,2,1:T(8,128)S(1)}, f32[32,1,8,128]{3,0,2,1:T(8,128)S(1)}, u32[]{:S(2)}, u32[]{:S(2)}) collective-permute-start(f32[32,1,8,128]{3,0,2,1:T(8,128)S(1)} %get-tuple-element.40), channel_id=1, source_target_pairs={{0,8},{8,16},{16,24},{1,9},{9,17},{17,25},{2,10},{10,18},{18,26},{... | collective-permute-start | bytes 393224 | tf_op jit(solution)/shard_map/ppermute | solution.py:25
  424.6 8.7 %collective-permute-start.42 = (f32[32,1,8,128]{3,0,2,1:T(8,128)S(1)}, f32[32,1,8,128]{3,0,2,1:T(8,128)S(1)}, u32[]{:S(2)}, u32[]{:S(2)}) collective-permute-start(f32[32,1,8,128]{3,0,2,1:T(8,128)S(1)} %get-tuple-element.39), channel_id=1, source_target_pairs={{8,0},{16,8},{24,16},{9,1},{17,9},{25,17},{10,2},{18,10},{26,18},{... | collective-permute-start | bytes 393224 | tf_op jit(solution)/shard_map/ppermute | solution.py:26
  425.9 8.5 %collective-permute-start.43 = (f32[32,1,8,128]{3,0,2,1:T(8,128)S(1)}, f32[32,1,8,128]{3,0,2,1:T(8,128)S(1)}, u32[]{:S(2)}, u32[]{:S(2)}) collective-permute-start(f32[32,1,8,128]{3,0,2,1:T(8,128)S(1)} %get-tuple-element.38), channel_id=1, source_target_pairs={{0,8},{8,16},{16,24},{1,9},{9,17},{17,25},{2,10},{10,18},{18,26},{... | collective-permute-start | bytes 393224 | tf_op jit(solution)/shard_map/ppermute | solution.py:25
  444.7 8.6 %collective-permute-start.46 = (f32[32,10,10,1]{0,2,3,1:T(8,128)S(1)}, f32[32,10,10,1]{0,2,3,1:T(8,128)S(1)}, u32[]{:S(2)}, u32[]{:S(2)}) collective-permute-start(f32[32,10,10,1]{0,2,3,1:T(8,128)S(1)} %copy.113), channel_id=1, source_target_pairs={{1,0},{2,1},{3,2},{5,4},{6,5},{7,6},{9,8},{10,9},{11,10},{13,12},{... | collective-permute-start | bytes 38408 | tf_op jit(solution)/shard_map/ppermute | solution.py:26
  499.6 75.6 %all-gather.5.cloned.1.call-start = ((), (), s32[]{:S(2)}) async-start(), calls=%async_computation.5 | async-start | bytes 2621440 | tf_op jit(solution)/shard_map/all_gather | solution.py:106
  (53 other events, 293.4 us)
Sparse Core Ops, SparseCore 0:
  238.4 37.9 reduce-scatter.2
  278.8 26.9 all-gather.2
  499.8 37.9 reduce-scatter.4
  540.0 35.1 all-gather.4
where the time goes:
time: 595 us; the launch traced here: 585 us
  waiting for transfers between devices  141 us (24%)
  starting transfers between devices  137 us (23%)
  local copies, waits for them, and re-layouts  116 us (19%)
  blocking collectives  115 us (19%)
  other arithmetic  43.5 us (7%)
  matrix products  17.5 us (3%)
  between operations  15.2 us (3%)
    ppermute x24, starting transfers between devices, padded_2(): before = lax.ppermute(last, axis, up)  106 us
    reduce_scatter x2, waiting for transfers between devices, local(): lax.psum_scatter(update, 'row', scatter_dimension=1, tiled=True)  76.1 us
    psum x2, blocking collectives, local(): fluxes = lax.psum(own_fluxes, ('col', 'vol'))  58.7 us
    psum x2, blocking collectives, local(): potential = lax.psum(partial_value, ('col', 'vol'))  56.4 us
    slice x16, local copies, waits for them, and re-layouts, padded_2(): first = lax.slice_in_dim(value, 0, width, axis=dim)  37.9 us
    all_gather x1, waiting for transfers between devices, local(): density = lax.all_gather(share_state, 'row', axis=1, tiled=True)  33.8 us
    ppermute x24, starting transfers between devices, padded_2(): after = lax.ppermute(first, axis, down)  31.3 us
    add x7, other arithmetic, local(): center + factor * (right_side - diagonal * center + conduct * beside_all)...  20.6 us
  transfers between devices with their start and end apart: 52, of which 32 were waited for; matrix products, arithmetic and copies ran while one was open for 11% of the time, Pallas kernels for 0%

commit v1 on v0

--- a/solution.py
+++ b/solution.py
@@ -1,8 +1,11 @@
+import functools
 import math
 
 import jax
 import jax.numpy as jnp
 from jax import lax
+from jax.experimental import pallas as pl
+from jax.experimental.pallas import tpu as pltpu
 from jax.sharding import PartitionSpec as P
 
 SWEEPS = 4
@@ -13,6 +16,305 @@
 RELAXATION = 0.5
 SPECTRUM_LOW = 0.1
 SPECTRUM_HIGH = 2.0
+
+ALL = ("row", "col", "vol")
+HIGHEST = lax.Precision.HIGHEST
+
+
+def relax_factors(count):
+    middle = (SPECTRUM_HIGH + SPECTRUM_LOW) / 2.0
+    spread = (SPECTRUM_HIGH - SPECTRUM_LOW) / 2.0
+    return [
+        1.0 / (middle + spread * math.cos(math.pi * (2 * order + 1) / (2 * count)))
+        for order in range(count)
+    ]
+
+
+def conduct_of(class_index, class_values):
+    classes = jnp.arange(class_values.shape[0], dtype=jnp.int32)
+    return jnp.sum(
+        jnp.where(
+            class_index[None] == classes[:, None, None, None],
+            class_values[:, None, None, None],
+            jnp.float32(0.0),
+        ),
+        axis=0,
+    )
+
+
+def exchange(value, axis):
+    size = lax.axis_size(axis)
+    got = [value]
+    for k in range(1, size):
+        got.append(lax.ppermute(value, axis, [(i, i ^ k) for i in range(size)]))
+    return jnp.stack(got)
+
+
+def slab_kernel(shape, first, place, source, others, parts, start, volume, plane_out, flux,
+                old, new, ratio, scaled):
+    rows, cols, vols, bx, by, bz = shape
+    blocks = cols * vols
+    targets = parts.shape[-1]
+    factors = relax_factors(SWEEPS)
+    height = bx * blocks * by
+    r0, c0, v0 = place[0], place[1], place[2]
+    row_ids = lax.broadcasted_iota(jnp.int32, (height, targets), 0)
+    lane_ids = lax.broadcasted_iota(jnp.int32, (bz, targets), 0)
+    zero_plane = jnp.zeros((blocks, by, bz), jnp.float32)
+    for ref in (old, new):
+        ref[0] = zero_plane
+        ref[rows * bx + 1] = zero_plane
+
+    potentials, hits, lanes = [], [], []
+    for r in range(rows):
+        if first:
+            potential = jnp.sum(parts[r], axis=0, keepdims=True)
+        else:
+            potential = jnp.zeros((1, targets), jnp.float32)
+            for s in range(rows):
+                potential = potential + jnp.sum(parts[s, :, s ^ r, :], axis=0, keepdims=True)
+        spot = others[c0, r ^ r0, v0, bx * by:bx * by + 2, :].astype(jnp.int32)
+        hit = (row_ids == spot[0:1]).astype(jnp.float32)
+        lane = lane_ids == spot[1:2]
+        weighted = jnp.where(lane, potential, 0.0)
+        added = lax.dot_general(
+            hit, weighted, (((1,), (1,)), ((), ())),
+            precision=HIGHEST, preferred_element_type=jnp.float32,
+        ).reshape(bx, blocks, by, bz)
+        potentials.append(potential)
+        hits.append(hit)
+        lanes.append(lane)
+        for j in range(blocks):
+            c, v = j // vols, j % vols
+            conduct = others[c ^ c0, r ^ r0, v ^ v0, 0:bx * by, :].reshape(bx, by, bz)
+            inverse = 1.0 / (MASS_TERM + 6.0 * conduct)
+            ratio[r * bx:(r + 1) * bx, j] = conduct * inverse
+            scaled[r * bx:(r + 1) * bx, j] = (source[r, j] + added[:, j]) * inverse
+    if not first:
+        old[1:rows * bx + 1] = start[...]
+
+    sub = lax.broadcasted_iota(jnp.int32, (by, bz), 0)
+    lan = lax.broadcasted_iota(jnp.int32, (by, bz), 1)
+    zero = jnp.zeros((by, bz), jnp.float32)
+    here, there = old, new
+    for order, factor in enumerate(factors):
+        def plane(x, here=here, there=there, order=order, factor=factor):
+            if first and order == 0:
+                there[x + 1] = factor * scaled[x]
+                return
+            tile = [here[x + 1, j] for j in range(blocks)]
+            y_up = [pltpu.roll(t, 1, 0) for t in tile]
+            y_dn = [pltpu.roll(t, by - 1, 0) for t in tile]
+            z_up = [pltpu.roll(t, 1, 1) for t in tile]
+            z_dn = [pltpu.roll(t, bz - 1, 1) for t in tile]
+            for j in range(blocks):
+                c, v = j // vols, j % vols
+                around = here[x, j] + here[x + 2, j]
+                around += jnp.where(sub == 0, y_up[j - vols] if c > 0 else zero, y_up[j])
+                around += jnp.where(sub == by - 1, y_dn[j + vols] if c < cols - 1 else zero, y_dn[j])
+                around += jnp.where(lan == 0, z_up[j - 1] if v > 0 else zero, z_up[j])
+                around += jnp.where(lan == bz - 1, z_dn[j + 1] if v < vols - 1 else zero, z_dn[j])
+                there[x + 1, j] = (1.0 - factor) * tile[j] + factor * (
+                    scaled[x, j] + ratio[x, j] * around
+                )
+
+        def step(x, carry, plane=plane):
+            plane(x)
+            return carry
+
+        lax.fori_loop(0, rows * bx, step, 0)
+        here, there = there, here
+
+    for r in range(rows):
+        part = here[1 + r * bx:1 + (r + 1) * bx]
+        if first:
+            plane_out[r * bx:(r + 1) * bx] = part
+        else:
+            for x in range(bx):
+                volume[r, :, x] = here[1 + r * bx + x]
+        met = lax.dot_general(
+            part.reshape(height, bz), hits[r], (((0,), (0,)), ((), ())),
+            precision=HIGHEST, preferred_element_type=jnp.float32,
+        )
+        value = jnp.sum(jnp.where(lanes[r], met, 0.0), axis=0, keepdims=True) - potentials[r]
+        for q in range(rows):
+            flux[q, :, q ^ r, :] = jnp.broadcast_to(value, (blocks, targets))
+
+
+def slab_call(shape, first, place, source, others, parts, start):
+    rows, cols, vols, bx, by, bz = shape
+    blocks = cols * vols
+    targets = parts.shape[-1]
+    planes = (rows * bx, blocks, by, bz)
+    padded = (rows * bx + 2, blocks, by, bz)
+    vmem = pl.BlockSpec(memory_space=pltpu.VMEM)
+    operands = [place, source, others, parts]
+    out_shape = [
+        jax.ShapeDtypeStruct(planes if first else source.shape, jnp.float32),
+        jax.ShapeDtypeStruct((rows, blocks, rows, targets), jnp.float32),
+    ]
+    if not first:
+        operands.append(start)
+
+    def body(place_ref, source_ref, others_ref, parts_ref, *rest):
+        if first:
+            out_ref, flux_ref, *scratch = rest
+            slab_kernel(shape, True, place_ref, source_ref, others_ref, parts_ref, None, None,
+                        out_ref, flux_ref, *scratch)
+        else:
+            start_ref, out_ref, flux_ref, *scratch = rest
+            slab_kernel(shape, False, place_ref, source_ref, others_ref, parts_ref, start_ref,
+                        out_ref, None, flux_ref, *scratch)
+
+    return pl.pallas_call(
+        body,
+        out_shape=out_shape,
+        in_specs=[pl.BlockSpec(memory_space=pltpu.SMEM)] + [vmem] * (len(operands) - 1),
+        out_specs=[vmem, vmem],
+        scratch_shapes=[
+            pltpu.VMEM(padded, jnp.float32),
+            pltpu.VMEM(padded, jnp.float32),
+            pltpu.VMEM(planes, jnp.float32),
+            pltpu.VMEM(planes, jnp.float32),
+        ],
+        compiler_params=pltpu.CompilerParams(vmem_limit_bytes=40 * 2 ** 20),
+        name="slab_first" if first else "slab_last",
+    )(*operands)
+
+
+def update_call(flux, chunks, density, last):
+    excitations, rows, targets = flux.shape
+    width = density.shape[1]
+    tile = math.gcd(width, 1024)
+
+    def body(flux_ref, *refs):
+        panels, density_ref, out_ref = refs[:rows], refs[rows], refs[rows + 1]
+        pieces = [panels[k][...] for k in range(rows)]
+        update = jnp.zeros((excitations, tile), jnp.float32)
+        for k in range(rows):
+            update += jnp.dot(
+                flux_ref[:, k, :].astype(jnp.bfloat16), pieces[k],
+                preferred_element_type=jnp.float32,
+            )
+        if last:
+            out_ref[...] = (density_ref[...] + RELAXATION * update).astype(out_ref.dtype)
+            return
+        part_ref = refs[rows + 2]
+        total = RELAXATION * update
+        out_ref[...] = total
+        rounded = (density_ref[...] + total).astype(jnp.bfloat16)
+
+        @pl.when(pl.program_id(0) == 0)
+        def _():
+            part_ref[...] = jnp.zeros_like(part_ref)
+
+        for k in range(rows):
+            part_ref[:, k, :] += lax.dot_general(
+                rounded, pieces[k], (((1,), (1,)), ((), ())), preferred_element_type=jnp.float32
+            )
+
+    out_shape = [jax.ShapeDtypeStruct(density.shape, jnp.bfloat16 if last else jnp.float32)]
+    out_specs = [pl.BlockSpec((excitations, tile), lambda i: (0, i))]
+    if not last:
+        out_shape.append(jax.ShapeDtypeStruct(flux.shape, jnp.float32))
+        out_specs.append(pl.BlockSpec(flux.shape, lambda i: (0, 0, 0)))
+    return pl.pallas_call(
+        body,
+        grid=(width // tile,),
+        out_shape=out_shape,
+        in_specs=[pl.BlockSpec(flux.shape, lambda i: (0, 0, 0))]
+        + [pl.BlockSpec((targets, tile), lambda i: (0, i))] * rows
+        + [pl.BlockSpec((excitations, tile), lambda i: (0, i))],
+        out_specs=out_specs,
+        name="update_last" if last else "update_first",
+    )(flux, *chunks, density)
+
+
+def final_call(place, density, updates):
+    rows = len(updates)
+    excitations, width = updates[0].shape
+
+    def body(place_ref, density_ref, *refs):
+        out_ref = refs[rows]
+        for k in range(rows):
+            @pl.when(pl.program_id(0) == k)
+            def _():
+                out_ref[...] = density_ref[...] + refs[k][...].astype(jnp.float32)
+
+    moved = pl.BlockSpec((excitations, width), lambda k, place: (0, k ^ place[0]))
+    return pl.pallas_call(
+        body,
+        grid_spec=pltpu.PrefetchScalarGridSpec(
+            num_scalar_prefetch=1,
+            grid=(rows,),
+            in_specs=[moved] + [pl.BlockSpec((excitations, width), lambda k, place: (0, 0))] * rows,
+            out_specs=moved,
+        ),
+        out_shape=jax.ShapeDtypeStruct(density.shape, jnp.float32),
+        name="density_join",
+    )(place, density, *updates)
+
+
+def split_by_excitation(panel, density, source, class_index, class_values, trace_count, trace_cell):
+    rows, cols, vols = (lax.axis_size(a) for a in ALL)
+    blocks = cols * vols
+    excitations, bx, by, bz = source.shape
+    targets, nodes = panel.shape
+    width = nodes // rows
+    here = lax.axis_index("row")
+    place = jnp.stack([lax.axis_index(a) for a in ALL]).astype(jnp.int32)
+    shape = (rows, cols, vols, bx, by, bz)
+
+    slab = lax.all_to_all(source, ALL, 0, 0, tiled=True).reshape(rows, blocks, bx, by, bz)
+
+    def columns(k):
+        return lax.dynamic_slice_in_dim(panel, (here ^ k) * width, width, 1)
+
+    chunks = [columns(0)]
+    for k in range(1, rows):
+        chunks.append(lax.ppermute(columns(k), "row", [(i, i ^ k) for i in range(rows)]))
+    share = lax.dynamic_slice_in_dim(density, here * width, width, 1)
+
+    conduct = conduct_of(class_index, class_values)
+    counts = trace_count[0]
+    offsets = jnp.cumsum(counts) - counts
+    slot_ids = jnp.arange(trace_cell.shape[2], dtype=jnp.int32)
+    live = slot_ids[None, :] < counts[:, None]
+    owner = jnp.where(live, offsets[:, None] + slot_ids[None, :], -1)
+    cell = trace_cell[0]
+    block_ids = jnp.arange(blocks, dtype=jnp.int32)[:, None]
+    line = (cell // (by * bz)) * (blocks * by) + block_ids * by + (cell // bz) % by
+    match = owner[:, :, None] == jnp.arange(targets, dtype=jnp.int32)
+    spots = [
+        jnp.sum(jnp.where(match, value[:, :, None], 0), axis=(0, 1))
+        for value in (line, cell % bz)
+    ]
+    spots = jnp.stack(spots).astype(jnp.float32)
+    spots = jnp.pad(spots, ((0, 6), (0, bz - targets) if bz > targets else (0, 0)))
+    others = jnp.concatenate([conduct.reshape(bx * by, bz), spots], axis=0)
+    for axis in ("vol", "row", "col"):
+        others = exchange(others, axis)
+
+    rounded = density.astype(jnp.bfloat16)
+    parts = lax.dot_general(
+        rounded, panel, (((1,), (1,)), ((), ())), preferred_element_type=jnp.float32
+    )
+    parts = lax.all_to_all(parts, ALL, 0, 0, tiled=True).reshape(rows, blocks, targets)
+
+    volume, flux = slab_call(shape, True, place, slab, others, parts, None)
+    flux = lax.all_to_all(flux.reshape(excitations, rows, targets), ALL, 0, 0, tiled=True)
+    total, parts = update_call(flux, chunks, share, False)
+    parts = lax.all_to_all(parts, ALL, 0, 0, tiled=True).reshape(rows, blocks, rows, targets)
+    volume, flux = slab_call(shape, False, place, slab, others, parts, volume)
+    volume = lax.all_to_all(
+        volume.reshape(excitations, bx, by, bz), ALL, 0, 0, tiled=True
+    )
+    flux = lax.all_to_all(flux.reshape(excitations, rows, targets), ALL, 0, 0, tiled=True)
+    (total,) = update_call(flux, chunks, total, True)
+    totals = [total]
+    for k in range(1, rows):
+        totals.append(lax.ppermute(total, "row", [(i, i ^ k) for i in range(rows)]))
+    return (final_call(place, density, totals), volume)
 
 
 def padded_2(value, sides, width):
@@ -28,15 +330,6 @@
     return value
 
 
-def relax_factors(count):
-    middle = (SPECTRUM_HIGH + SPECTRUM_LOW) / 2.0
-    spread = (SPECTRUM_HIGH - SPECTRUM_LOW) / 2.0
-    return [
-        1.0 / (middle + spread * math.cos(math.pi * (2 * order + 1) / (2 * count)))
-        for order in range(count)
-    ]
-
-
 def neighbours(padded):
     center = padded[..., 1:-1, 1:-1, 1:-1]
     beside_all = padded[..., 2:, 1:-1, 1:-1] + padded[..., :-2, 1:-1, 1:-1]
@@ -45,17 +338,9 @@
     return (center, beside_all)
 
 
-def local(panel, density, source, class_index, class_values, trace_count, trace_cell):
+def split_by_block(panel, density, source, class_index, class_values, trace_count, trace_cell):
     factors = relax_factors(SWEEPS)
-    classes = jnp.arange(class_values.shape[0], dtype=jnp.int32)
-    conduct = jnp.sum(
-        jnp.where(
-            class_index[None] == classes[:, None, None, None],
-            class_values[:, None, None, None],
-            jnp.float32(0.0),
-        ),
-        axis=0,
-    )
+    conduct = conduct_of(class_index, class_values)
     diagonal = MASS_TERM + 6.0 * conduct
     counts = trace_count[0]
     block_index = lax.axis_index(("col", "vol"))
@@ -107,6 +392,15 @@
     return (density, volume)
 
 
+def local(*args):
+    sizes = [lax.axis_size(a) for a in ALL]
+    source, targets = args[2], args[0].shape[0]
+    whole = math.prod(sizes) == source.shape[0] and targets == source.shape[3]
+    if whole and all(size & (size - 1) == 0 for size in sizes):
+        return split_by_excitation(*args)
+    return split_by_block(*args)
+
+
 def solution(mesh):
     placed = (
         P("row", ("col", "vol")),

time: 595 us -> 194 us (0.33); the launches traced: 585 us -> 194 us
  local copies, waits for them, and re-layouts: 116 us -> 9.22 us
  starting transfers between devices: 137 us -> 31.2 us
  blocking collectives: 115 us -> 20.9 us
  waiting for transfers between devices: 141 us -> 82.9 us
  Pallas kernels: 0 us -> 42.7 us
  other arithmetic: 43.5 us -> 0.93 us
  between operations: 15.2 us -> 0.8 us
  matrix products: 17.5 us -> 4.96 us
    ppermute x48 -> x13, starting transfers between devices: 137 us -> 15.1 us  [the longest x7 8.08 us: exchange(): got.append(lax.ppermute(value, axis, [(i, i ^ k) for i in range(size)]))]
    psum x4 -> x0, blocking collectives: 115 us -> none  [the longest x2 58.7 us: local(): fluxes = lax.psum(own_fluxes, ('col', 'vol'))]
    reduce_scatter x2 -> x0, waiting for transfers between devices: 76.1 us -> none  [local(): lax.psum_scatter(update, 'row', scatter_dimension=1, tiled=True)]
    slice x31 -> x0, local copies, waits for them, and re-layouts: 54.6 us -> none  [the longest x16 37.9 us: padded_2(): first = lax.slice_in_dim(value, 0, width, axis=dim)]
    ppermute x48 -> x13, waiting for transfers between devices: 30.6 us -> 76.1 us  [the longest x7 30.1 us: exchange(): got.append(lax.ppermute(value, axis, [(i, i ^ k) for i in range(size)]))]
    pallas_call x0 -> x5, Pallas kernels: none -> 42.7 us  [the longest x2 27.7 us: slab_call(): pl.pallas_call(body, out_shape=out_shape, in_specs=[pl.BlockSpec(memory_s...]
    all_gather x2 -> x0, waiting for transfers between devices: 33.8 us -> none  [the longest x1 33.8 us: local(): density = lax.all_gather(share_state, 'row', axis=1, tiled=True)]
    ppermute x16 -> x0, local copies, waits for them, and re-layouts: 29.4 us -> none  [the longest x8 14.8 us: padded_2(): after = lax.ppermute(first, axis, down)]
  transfers between devices with their start and end apart: 52 -> 17, of which waited for: 32 -> 10; matrix products, arithmetic and copies ran while one was open for 11% -> 4% of each run, Pallas kernels for 0% -> 11%
where the time goes in v1:
time: 194 us
  waiting for transfers between devices  82.9 us (43%)
  Pallas kernels  42.7 us (22%)
  starting transfers between devices  31.2 us (16%)
  blocking collectives  20.9 us (11%)
  local copies, waits for them, and re-layouts  9.22 us (5%)
  matrix products  4.96 us (3%)
    ppermute x7, waiting for transfers between devices, exchange(): got.append(lax.ppermute(value, axis, [(i, i ^ k) for i in range(size)]))  30.1 us
    ppermute x3, waiting for transfers between devices, split_by_excitation(): lax.ppermute(columns(k), 'row', [(i, i ^ k) for i in range(rows)])  28.4 us
    pallas_call x2, Pallas kernels, slab_call(): pl.pallas_call(body, out_shape=out_shape, in_specs=[pl.BlockSpec(memory_s...  27.7 us
    ppermute x3, waiting for transfers between devices, split_by_excitation(): totals.append(lax.ppermute(total, 'row', [(i, i ^ k) for i in range(rows)]))  17.6 us
    all_to_all x1, blocking collectives, split_by_excitation(): lax.all_to_all(parts, ALL, 0, 0, tiled=True)  11 us
    pallas_call x2, Pallas kernels, update_call(): pl.pallas_call(body, grid=(width // tile,), out_shape=out_shape, in_specs...  10.2 us
    all_to_all x1, blocking collectives, split_by_excitation(): lax.all_to_all(flux.reshape(excitations, rows, targets), ALL, 0, 0, tiled...  9.86 us
    ppermute x7, starting transfers between devices, exchange(): got.append(lax.ppermute(value, axis, [(i, i ^ k) for i in range(size)]))  8.08 us
  transfers between devices with their start and end apart: 17, of which 10 were waited for; matrix products, arithmetic and copies ran while one was open for 4% of the time, Pallas kernels for 11%

profile of v1, /device:TPU:0, one launch (start us, length us, event | category | flops | bytes accessed | tf_op | source)
XLA Modules:
  0.0 193.6 jit_solution(10769744593109106923)
XLA Ops:
  0.6 5.0 %fusion = f32[32,128]{1,0:T(8,128)} fusion(bf16[128,16384]{1,0:T(8,128)(2,1)} %param.7, f32[32,16384]{1,0:T(8,128)} %density_ref.1), kind=kOutput, calls=%fused_computation.1 | convolution fusion | flops 134742016 | bytes 6307840 | tf_op jit(solution)/shard_map/dot_general | solution.py:299
  5.6 7.3 %all-to-all-start.1 = ((f32[32,1,128]{2,1,0:T(1,128)}), f32[32,1,128]{2,1,0:T(1,128)S(1)}, u32[]{:S(2)}, u32[]{:S(2)}) async-start(f32[32,1,128]{2,1,0:T(1,128)} %bitcast.22), calls=%async_computation.1 | async-start | bytes 32768 | tf_op jit(solution)/shard_map/all_to_all | solution.py:302
  13.2 6.8 %all-to-all-done.1 = f32[32,1,128]{2,1,0:T(1,128)S(1)} async-done(((f32[32,1,128]{2,1,0:T(1,128)}), f32[32,1,128]{2,1,0:T(1,128)S(1)}, u32[]{:S(2)}, u32[]{:S(2)}) %all-to-all-start.1) | async-done | bytes 16416 | tf_op jit(solution)/shard_map/all_to_all | solution.py:302
  20.1 2.6 %all-to-all-start = ((f32[32,8,8,128]{3,2,1,0:T(8,128)}), f32[32,8,8,128]{3,2,1,0:T(8,128)S(1)}, u32[]{:S(2)}, u32[]{:S(2)}) async-start(f32[32,8,8,128]{3,2,1,0:T(8,128)} %param.9), calls=%async_computation | async-start | bytes 2097152 | tf_op jit(solution)/shard_map/all_to_all | solution.py:268
  23.2 2.7 %collective-permute-start.1 = (f32[72,128]{1,0:T(8,128)S(1)}, f32[72,128]{1,0:T(8,128)S(1)}, u32[]{:S(2)}, u32[]{:S(2)}) collective-permute-start(f32[72,128]{1,0:T(8,128)S(1)} %get-tuple-element.25), channel_id=1, source_target_pairs={{0,2},{1,3},{2,0},{3,1},{4,6},{5,7},{6,4},{7,5},{8,10},{9,11},{10,... | collective-permute-start | bytes 110600 | tf_op jit(solution)/shard_map/ppermute | solution.py:49
  27.6 24.0 %collective-permute-done.1 = f32[72,128]{1,0:T(8,128)S(1)} collective-permute-done((f32[72,128]{1,0:T(8,128)S(1)}, f32[72,128]{1,0:T(8,128)S(1)}, u32[]{:S(2)}, u32[]{:S(2)}) %collective-permute-start.1) | collective-permute-done | bytes 36896 | tf_op jit(solution)/shard_map/ppermute | solution.py:49
  55.3 2.3 %collective-permute-done.4 = f32[4,72,128]{2,1,0:T(8,128)S(1)} collective-permute-done((f32[4,72,128]{2,1,0:T(8,128)S(1)}, f32[4,72,128]{2,1,0:T(8,128)S(1)}, u32[]{:S(2)}, u32[]{:S(2)}) %collective-permute-start.4) | collective-permute-done | bytes 147488 | tf_op jit(solution)/shard_map/ppermute | solution.py:49
  59.2 2.1 %collective-permute-done.5 = f32[4,72,128]{2,1,0:T(8,128)S(1)} collective-permute-done((f32[4,72,128]{2,1,0:T(8,128)S(1)}, f32[4,72,128]{2,1,0:T(8,128)S(1)}, u32[]{:S(2)}, u32[]{:S(2)}) %collective-permute-start.5) | collective-permute-done | bytes 147488 | tf_op jit(solution)/shard_map/ppermute | solution.py:49
  61.4 4.3 %constant_dynamic-slice_fusion.1 = (bf16[128,4096]{1,0:T(8,128)(2,1)}, bf16[128,4096]{1,0:T(8,128)(2,1)}, bf16[128,4096]{1,0:T(8,128)(2,1)}, bf16[128,4096]{1,0:T(8,128)(2,1)}) fusion(bf16[128,16384]{1,0:T(8,128)(2,1)} %param.7, s32[]{:T(128)S(6)} %select_n.78, s32[]{:T(128)S(6)} %select_n.76, s32[]{:T(128)S(6)} %select_n.75, s32[]{:T(128)S(6)} %select_n.77), kind=kLoop, calls=%fused_computation.36 | loop fusion | bytes 8388624 | tf_op jit(solution)/shard_map/dynamic_slice | solution.py:271
  69.4 12.3 %slab_first.1 = (f32[32,8,8,128]{3,2,1,0:T(8,128)S(1)}, f32[4,8,4,128]{3,2,1,0:T(4,128)}) custom-call(s32[3]{0:T(128)S(1)} %pad_add_fusion.place_ref, f32[4,8,8,8,128]{4,3,2,1,0:T(8,128)S(1)} %bitcast.58, f32[2,4,4,72,128]{4,3,2,1,0:T(8,128)S(1)} %pad_maximum_fusion.others_ref, f32[4,8,128]{2,1,0:T(8,128)S(1)} %bitcast.61), custom_call_target="tpu_custom_call" | custom-call | tf_op jit(solution)/shard_map/slab_first/pallas_call | solution.py:169
  81.8 3.5 %all-to-all-start.2 = ((f32[32,4,128]{2,1,0:T(4,128)}), f32[32,4,128]{2,1,0:T(4,128)S(1)}, u32[]{:S(2)}, u32[]{:S(2)}) async-start(f32[32,4,128]{2,1,0:T(4,128)} %bitcast.24), calls=%async_computation.2 | async-start | bytes 131072 | tf_op jit(solution)/shard_map/all_to_all | solution.py:305
  85.3 1.9 constant_dynamic-slice_fusion.refs_4_
  87.2 6.4 %collective-permute-done.9.refs_3_ = bf16[128,4096]{1,0:T(8,128)(2,1)} collective-permute-done((bf16[128,4096]{1,0:T(8,128)(2,1)}, bf16[128,4096]{1,0:T(8,128)(2,1)}, u32[]{:S(2)}, u32[]{:S(2)}) %collective-permute-start.9) | collective-permute-done | bytes 1048608 | tf_op jit(solution)/shard_map/ppermute | solution.py:275
  93.6 21.6 %collective-permute-done.7.refs_1_ = bf16[128,4096]{1,0:T(8,128)(2,1)} collective-permute-done((bf16[128,4096]{1,0:T(8,128)(2,1)}, bf16[128,4096]{1,0:T(8,128)(2,1)}, u32[]{:S(2)}, u32[]{:S(2)}) %collective-permute-start.7) | collective-permute-done | bytes 1048608 | tf_op jit(solution)/shard_map/ppermute | solution.py:275
  116.3 5.6 %update_first.1 = (f32[32,4096]{1,0:T(8,128)}, f32[32,4,128]{2,1,0:T(4,128)}) custom-call(f32[32,4,128]{2,1,0:T(4,128)} %copy-done.1, bf16[128,4096]{1,0:T(8,128)(2,1)} %get-tuple-element.18.refs_0_, bf16[128,4096]{1,0:T(8,128)(2,1)} %collective-permute-done.7.refs_1_, bf16[128,4096]{1,0:T(8,128)(2,1)} %collective-permute-done.8.refs_2_, ...), custom_call_target="tpu_custom_call" | custom-call | tf_op jit(solution)/shard_map/update_first/pallas_call | solution.py:221
  121.9 11.0 %all_to_all.34 = f32[32,4,128]{2,1,0:T(4,128)S(1)} all-to-all(f32[32,4,128]{2,1,0:T(4,128)} %get-tuple-element.9), channel_id=1, replica_groups=mesh['row'=4,'col'=2,'vol'=4] {'row','col','vol'}, dimensions={0} | all-to-all | bytes 131072 | tf_op jit(solution)/shard_map/all_to_all | solution.py:307
  132.9 15.4 %slab_last.1 = (f32[4,8,8,8,128]{4,3,2,1,0:T(8,128)}, f32[4,8,4,128]{3,2,1,0:T(4,128)S(1)}) custom-call(s32[3]{0:T(128)S(1)} %pad_add_fusion.place_ref, f32[4,8,8,8,128]{4,3,2,1,0:T(8,128)S(1)} %bitcast.59, f32[2,4,4,72,128]{4,3,2,1,0:T(8,128)S(1)} %pad_maximum_fusion.others_ref, f32[4,8,4,128]{3,2,1,0:T(4,128)S(1)} %bitcast.60, ...), custom_call_target="tpu_custom_call" | custom-call | tf_op jit(solution)/shard_map/slab_last/pallas_call | solution.py:169
  148.3 9.9 %all_to_all.35.flux_ref = f32[32,4,128]{2,1,0:T(4,128)} all-to-all(f32[32,4,128]{2,1,0:T(4,128)S(1)} %bitcast.62), channel_id=1, replica_groups=mesh['row'=4,'col'=2,'vol'=4] {'row','col','vol'}, dimensions={0} | all-to-all | bytes 131072 | tf_op jit(solution)/shard_map/all_to_all | solution.py:312
  158.2 2.6 %all-to-all-start.5 = ((f32[32,8,8,128]{3,2,1,0:T(8,128)}), f32[32,8,8,128]{3,2,1,0:T(8,128)S(1)}, u32[]{:S(2)}, u32[]{:S(2)}) async-start(f32[32,8,8,128]{3,2,1,0:T(8,128)} %bitcast.27), calls=%async_computation.5 | async-start | bytes 2097152 | tf_op jit(solution)/shard_map/all_to_all | solution.py:309
  160.8 4.6 %update_last.1.refs_0_ = bf16[32,4096]{1,0:T(8,128)(2,1)} custom-call(f32[32,4,128]{2,1,0:T(4,128)} %all_to_all.35.flux_ref, bf16[128,4096]{1,0:T(8,128)(2,1)} %get-tuple-element.18.refs_0_, bf16[128,4096]{1,0:T(8,128)(2,1)} %collective-permute-done.7.refs_1_, bf16[128,4096]{1,0:T(8,128)(2,1)} %collective-permute-done.8.refs_2_, ...), custom_call_target="tpu_custom_call" | custom-call | tf_op jit(solution)/shard_map/update_last/pallas_call | solution.py:221
  165.4 2.6 %collective-permute-start.12 = (bf16[32,4096]{1,0:T(8,128)(2,1)}, bf16[32,4096]{1,0:T(8,128)(2,1)S(1)}, u32[]{:S(2)}, u32[]{:S(2)}) collective-permute-start(bf16[32,4096]{1,0:T(8,128)(2,1)} %update_last.1.refs_0_), channel_id=1, source_target_pairs={{0,24},{8,16},{16,8},{24,0},{1,25},{9,17},{17,9},{25,1},{2,26},{10... | collective-permute-start | bytes 786440 | tf_op jit(solution)/shard_map/ppermute | solution.py:316
  168.9 10.7 %collective-permute-done.12.refs_3_ = bf16[32,4096]{1,0:T(8,128)(2,1)S(1)} collective-permute-done((bf16[32,4096]{1,0:T(8,128)(2,1)}, bf16[32,4096]{1,0:T(8,128)(2,1)S(1)}, u32[]{:S(2)}, u32[]{:S(2)}) %collective-permute-start.12) | collective-permute-done | bytes 262176 | tf_op jit(solution)/shard_map/ppermute | solution.py:316
  179.6 6.9 %collective-permute-done.11.refs_2_ = bf16[32,4096]{1,0:T(8,128)(2,1)S(1)} collective-permute-done((bf16[32,4096]{1,0:T(8,128)(2,1)}, bf16[32,4096]{1,0:T(8,128)(2,1)S(1)}, u32[]{:S(2)}, u32[]{:S(2)}) %collective-permute-start.11) | collective-permute-done | bytes 262176 | tf_op jit(solution)/shard_map/ppermute | solution.py:316
  187.9 4.8 %density_join.1 = f32[32,16384]{1,0:T(8,128)} custom-call(s32[3]{0:T(128)} %copy-done, f32[32,16384]{1,0:T(8,128)} %density_ref.1, bf16[32,4096]{1,0:T(8,128)(2,1)} %update_last.1.refs_0_, bf16[32,4096]{1,0:T(8,128)(2,1)} %copy-done.4, bf16[32,4096]{1,0:T(8,128)(2,1)} %copy-done.3, bf16[32,4096]{1,0:T(8,128)(2,1)} %copy-done.2), custom_call_target="tpu_custom_call" | custom-call | tf_op jit(solution)/shard_map/density_join/pallas_call | solution.py:245
  (51 shorter events, 15.8 us)
Async XLA Ops:
  0.6 12.3 %copy-start.8 = (s32[1,8]{1,0:T(1,128)S(1)}, s32[1,8]{1,0:T(1,128)}, u32[]{:S(2)}) copy-start(s32[1,8]{1,0:T(1,128)} %param.12) | copy-start | bytes 100
  0.6 12.5 %copy-start.6 = (s32[1,8,64]{2,1,0:T(8,128)S(1)}, s32[1,8,64]{2,1,0:T(8,128)}, u32[]{:S(2)}) copy-start(s32[1,8,64]{2,1,0:T(8,128)} %param.13) | copy-start | bytes 6148
  5.6 17.4 %copy-start.5 = (s32[8,8,128]{2,1,0:T(8,128)S(1)}, s32[8,8,128]{2,1,0:T(8,128)}, u32[]{:S(2)}) copy-start(s32[8,8,128]{2,1,0:T(8,128)} %param.10) | copy-start | bytes 98308
  5.6 17.4 %copy-start.7 = (f32[16]{0:T(128)S(1)}, f32[16]{0:T(128)}, u32[]{:S(2)}) copy-start(f32[16]{0:T(128)} %param.11) | copy-start | bytes 196
  5.6 14.5 %all-to-all-start.1 = ((f32[32,1,128]{2,1,0:T(1,128)}), f32[32,1,128]{2,1,0:T(1,128)S(1)}, u32[]{:S(2)}, u32[]{:S(2)}) async-start(f32[32,1,128]{2,1,0:T(1,128)} %bitcast.22), calls=%async_computation.1 | async-start | bytes 32768 | tf_op jit(solution)/shard_map/all_to_all | solution.py:302
  20.1 49.4 %all-to-all-start = ((f32[32,8,8,128]{3,2,1,0:T(8,128)}), f32[32,8,8,128]{3,2,1,0:T(8,128)S(1)}, u32[]{:S(2)}, u32[]{:S(2)}) async-start(f32[32,8,8,128]{3,2,1,0:T(8,128)} %param.9), calls=%async_computation | async-start | bytes 2097152 | tf_op jit(solution)/shard_map/all_to_all | solution.py:268
  23.2 28.5 %collective-permute-start.1 = (f32[72,128]{1,0:T(8,128)S(1)}, f32[72,128]{1,0:T(8,128)S(1)}, u32[]{:S(2)}, u32[]{:S(2)}) collective-permute-start(f32[72,128]{1,0:T(8,128)S(1)} %get-tuple-element.25), channel_id=1, source_target_pairs={{0,2},{1,3},{2,0},{3,1},{4,6},{5,7},{6,4},{7,5},{8,10},{9,11},{10,... | collective-permute-start | bytes 110600 | tf_op jit(solution)/shard_map/ppermute | solution.py:49
  25.9 25.8 %collective-permute-start = (f32[72,128]{1,0:T(8,128)S(1)}, f32[72,128]{1,0:T(8,128)S(1)}, u32[]{:S(2)}, u32[]{:S(2)}) collective-permute-start(f32[72,128]{1,0:T(8,128)S(1)} %get-tuple-element.25), channel_id=1, source_target_pairs={{0,1},{1,0},{2,3},{3,2},{4,5},{5,4},{6,7},{7,6},{8,9},{9,8},{10,11... | collective-permute-start | bytes 110600 | tf_op jit(solution)/shard_map/ppermute | solution.py:49
  27.4 24.3 %collective-permute-start.2 = (f32[72,128]{1,0:T(8,128)S(1)}, f32[72,128]{1,0:T(8,128)S(1)}, u32[]{:S(2)}, u32[]{:S(2)}) collective-permute-start(f32[72,128]{1,0:T(8,128)S(1)} %get-tuple-element.25), channel_id=1, source_target_pairs={{0,3},{1,2},{2,1},{3,0},{4,7},{5,6},{6,5},{7,4},{8,11},{9,10},{10,... | collective-permute-start | bytes 110600 | tf_op jit(solution)/shard_map/ppermute | solution.py:49
  51.7 5.8 %collective-permute-start.4 = (f32[4,72,128]{2,1,0:T(8,128)S(1)}, f32[4,72,128]{2,1,0:T(8,128)S(1)}, u32[]{:S(2)}, u32[]{:S(2)}) collective-permute-start(f32[4,72,128]{2,1,0:T(8,128)S(1)} %get-tuple-element.23), channel_id=1, source_target_pairs={{0,16},{8,24},{16,0},{24,8},{1,17},{9,25},{17,1},{25,9},{2,18},{10... | collective-permute-start | bytes 442376 | tf_op jit(solution)/shard_map/ppermute | solution.py:49
  53.3 5.9 %collective-permute-start.3 = (f32[4,72,128]{2,1,0:T(8,128)S(1)}, f32[4,72,128]{2,1,0:T(8,128)S(1)}, u32[]{:S(2)}, u32[]{:S(2)}) collective-permute-start(f32[4,72,128]{2,1,0:T(8,128)S(1)} %get-tuple-element.23), channel_id=1, source_target_pairs={{0,8},{8,0},{16,24},{24,16},{1,9},{9,1},{17,25},{25,17},{2,10},{10... | collective-permute-start | bytes 442376 | tf_op jit(solution)/shard_map/ppermute | solution.py:49
  54.8 6.5 %collective-permute-start.5 = (f32[4,72,128]{2,1,0:T(8,128)S(1)}, f32[4,72,128]{2,1,0:T(8,128)S(1)}, u32[]{:S(2)}, u32[]{:S(2)}) collective-permute-start(f32[4,72,128]{2,1,0:T(8,128)S(1)} %get-tuple-element.23), channel_id=1, source_target_pairs={{0,24},{8,16},{16,8},{24,0},{1,25},{9,17},{17,9},{25,1},{2,26},{10... | collective-permute-start | bytes 442376 | tf_op jit(solution)/shard_map/ppermute | solution.py:49
  61.4 8.0 %collective-permute-start.6 = (f32[4,4,72,128]{3,2,1,0:T(8,128)S(1)}, f32[4,4,72,128]{3,2,1,0:T(8,128)S(1)}, u32[]{:S(2)}, u32[]{:S(2)}) collective-permute-start(f32[4,4,72,128]{3,2,1,0:T(8,128)S(1)} %get-tuple-element.21), channel_id=1, source_target_pairs={{0,4},{4,0},{1,5},{5,1},{2,6},{6,2},{3,7},{7,3},{8,12},{12,8},{9,1... | collective-permute-start | bytes 1769480 | tf_op jit(solution)/shard_map/ppermute | solution.py:49
  65.8 27.8 %collective-permute-start.9 = (bf16[128,4096]{1,0:T(8,128)(2,1)}, bf16[128,4096]{1,0:T(8,128)(2,1)}, u32[]{:S(2)}, u32[]{:S(2)}) collective-permute-start(bf16[128,4096]{1,0:T(8,128)(2,1)} %get-tuple-element.16), channel_id=1, source_target_pairs={{0,24},{8,16},{16,8},{24,0},{1,25},{9,17},{17,9},{25,1},{2,26},{10... | collective-permute-start | bytes 3145736 | tf_op jit(solution)/shard_map/ppermute | solution.py:275
  67.6 47.5 %collective-permute-start.7 = (bf16[128,4096]{1,0:T(8,128)(2,1)}, bf16[128,4096]{1,0:T(8,128)(2,1)}, u32[]{:S(2)}, u32[]{:S(2)}) collective-permute-start(bf16[128,4096]{1,0:T(8,128)(2,1)} %get-tuple-element.17), channel_id=1, source_target_pairs={{0,8},{8,0},{16,24},{24,16},{1,9},{9,1},{17,25},{25,17},{2,10},{10... | collective-permute-start | bytes 3145736 | tf_op jit(solution)/shard_map/ppermute | solution.py:275
  68.2 47.4 %collective-permute-start.8 = (bf16[128,4096]{1,0:T(8,128)(2,1)}, bf16[128,4096]{1,0:T(8,128)(2,1)}, u32[]{:S(2)}, u32[]{:S(2)}) collective-permute-start(bf16[128,4096]{1,0:T(8,128)(2,1)} %get-tuple-element.19), channel_id=1, source_target_pairs={{0,16},{8,24},{16,0},{24,8},{1,17},{9,25},{17,1},{25,9},{2,18},{10... | collective-permute-start | bytes 3145736 | tf_op jit(solution)/shard_map/ppermute | solution.py:275
  69.3 63.6 %copy-start = (s32[3]{0:T(128)}, s32[3]{0:T(128)S(1)}, u32[]{:S(2)}) copy-start(s32[3]{0:T(128)S(1)} %pad_add_fusion.place_ref) | copy-start | bytes 40
  81.8 33.9 %all-to-all-start.2 = ((f32[32,4,128]{2,1,0:T(4,128)}), f32[32,4,128]{2,1,0:T(4,128)S(1)}, u32[]{:S(2)}, u32[]{:S(2)}) async-start(f32[32,4,128]{2,1,0:T(4,128)} %bitcast.24), calls=%async_computation.2 | async-start | bytes 131072 | tf_op jit(solution)/shard_map/all_to_all | solution.py:305
  158.2 34.5 %all-to-all-start.5 = ((f32[32,8,8,128]{3,2,1,0:T(8,128)}), f32[32,8,8,128]{3,2,1,0:T(8,128)S(1)}, u32[]{:S(2)}, u32[]{:S(2)}) async-start(f32[32,8,8,128]{3,2,1,0:T(8,128)} %bitcast.27), calls=%async_computation.5 | async-start | bytes 2097152 | tf_op jit(solution)/shard_map/all_to_all | solution.py:309
  165.4 14.2 %collective-permute-start.12 = (bf16[32,4096]{1,0:T(8,128)(2,1)}, bf16[32,4096]{1,0:T(8,128)(2,1)S(1)}, u32[]{:S(2)}, u32[]{:S(2)}) collective-permute-start(bf16[32,4096]{1,0:T(8,128)(2,1)} %update_last.1.refs_0_), channel_id=1, source_target_pairs={{0,24},{8,16},{16,8},{24,0},{1,25},{9,17},{17,9},{25,1},{2,26},{10... | collective-permute-start | bytes 786440 | tf_op jit(solution)/shard_map/ppermute | solution.py:316
  168.0 18.5 %collective-permute-start.11 = (bf16[32,4096]{1,0:T(8,128)(2,1)}, bf16[32,4096]{1,0:T(8,128)(2,1)S(1)}, u32[]{:S(2)}, u32[]{:S(2)}) collective-permute-start(bf16[32,4096]{1,0:T(8,128)(2,1)} %update_last.1.refs_0_), channel_id=1, source_target_pairs={{0,16},{8,24},{16,0},{24,8},{1,17},{9,25},{17,1},{25,9},{2,18},{10... | collective-permute-start | bytes 786440 | tf_op jit(solution)/shard_map/ppermute | solution.py:316
  168.5 18.0 %collective-permute-start.10 = (bf16[32,4096]{1,0:T(8,128)(2,1)}, bf16[32,4096]{1,0:T(8,128)(2,1)S(1)}, u32[]{:S(2)}, u32[]{:S(2)}) collective-permute-start(bf16[32,4096]{1,0:T(8,128)(2,1)} %update_last.1.refs_0_), channel_id=1, source_target_pairs={{0,8},{8,0},{16,24},{24,16},{1,9},{9,1},{17,25},{25,17},{2,10},{10... | collective-permute-start | bytes 786440 | tf_op jit(solution)/shard_map/ppermute | solution.py:316
  179.6 6.9 %copy-start.2 = (bf16[32,4096]{1,0:T(8,128)(2,1)}, bf16[32,4096]{1,0:T(8,128)(2,1)S(1)}, u32[]{:S(2)}) copy-start(bf16[32,4096]{1,0:T(8,128)(2,1)S(1)} %collective-permute-done.12.refs_3_) | copy-start | bytes 786436
  186.5 0.7 copy-start.3
  (2 other events, 1.3 us)

commit v2 on v0

--- a/solution.py
+++ b/solution.py
@@ -1,8 +1,11 @@
+import functools
 import math
 
 import jax
 import jax.numpy as jnp
 from jax import lax
+from jax.experimental import pallas as pl
+from jax.experimental.pallas import tpu as pltpu
 from jax.sharding import PartitionSpec as P
 
 SWEEPS = 4
@@ -13,6 +16,351 @@
 RELAXATION = 0.5
 SPECTRUM_LOW = 0.1
 SPECTRUM_HIGH = 2.0
+
+ALL = ("row", "col", "vol")
+
+
+def relax_factors(count):
+    middle = (SPECTRUM_HIGH + SPECTRUM_LOW) / 2.0
+    spread = (SPECTRUM_HIGH - SPECTRUM_LOW) / 2.0
+    return [
+        1.0 / (middle + spread * math.cos(math.pi * (2 * order + 1) / (2 * count)))
+        for order in range(count)
+    ]
+
+
+def conduct_of(class_index, class_values):
+    classes = jnp.arange(class_values.shape[0], dtype=jnp.int32)
+    return jnp.sum(
+        jnp.where(
+            class_index[None] == classes[:, None, None, None],
+            class_values[:, None, None, None],
+            jnp.float32(0.0),
+        ),
+        axis=0,
+    )
+
+
+MATES = (0, 1, 2)
+
+
+def exchange(value, axis):
+    size = lax.axis_size(axis)
+    if axis == "row":
+        value, k = value[None], 1
+        while k < size:
+            value = jnp.concatenate([value, lax.ppermute(value, axis, [(i, i ^ k) for i in range(size)])])
+            k = 2 * k
+        return value
+    moved = [lax.ppermute(value, axis, [(i, i ^ k) for i in range(size)]) for k in range(1, size)]
+    return jnp.stack([value] + moved)
+
+
+def prepare_call(shape, place, values, others, targets):
+    rows, cols, vols, bx, by, bz = shape
+    blocks = cols * vols
+    height = bx * blocks * by
+
+    def body(place_ref, values_ref, others_ref, ratio_ref, inverse_ref, hit_ref, lane_ref):
+        r0, c0, v0 = place_ref[0], place_ref[1], place_ref[2]
+        count = values_ref.shape[0]
+        row_ids = lax.broadcasted_iota(jnp.int32, (height, targets), 0)
+        lane_ids = lax.broadcasted_iota(jnp.int32, (bz, targets), 0)
+        for r in range(rows):
+            spot = others_ref[c0, r ^ r0, v0, bx * by:bx * by + 16, :].astype(jnp.float32)
+            spot = spot.astype(jnp.int32)
+            line = spot[0:1] * (blocks * by) + spot[1:2]
+            hit_ref[r] = (row_ids == line).astype(jnp.bfloat16)
+            lane_ref[r] = (lane_ids == spot[2:3]).astype(jnp.bfloat16)
+
+        def block(index, carry):
+            r, rest = index // blocks, index % blocks
+            c, v = rest // vols, rest % vols
+            kind = others_ref[c ^ c0, r ^ r0, v ^ v0, 0:bx * by, :].astype(jnp.float32)
+            conduct = jnp.zeros((bx * by, bz), jnp.float32)
+            for i in range(count):
+                conduct = jnp.where(kind == float(i), values_ref[i], conduct)
+            inverse = 1.0 / (MASS_TERM + 6.0 * conduct)
+            ratio = (conduct * inverse).reshape(bx, by, bz)
+            start = pl.multiple_of(c * by, by)
+            ratio_ref[pl.ds(r * bx, bx), v, pl.ds(start, by)] = ratio
+            inverse_ref[pl.ds(r * bx, bx), v, pl.ds(start, by)] = inverse.reshape(bx, by, bz)
+            return carry
+
+        lax.fori_loop(0, rows * blocks, block, 0)
+
+    planes = (rows * bx, vols, cols * by, bz)
+    vmem = pl.BlockSpec(memory_space=pltpu.VMEM)
+    smem = pl.BlockSpec(memory_space=pltpu.SMEM)
+    return pl.pallas_call(
+        body,
+        out_shape=[
+            jax.ShapeDtypeStruct(planes, jnp.float32),
+            jax.ShapeDtypeStruct(planes, jnp.float32),
+            jax.ShapeDtypeStruct((rows, height, targets), jnp.bfloat16),
+            jax.ShapeDtypeStruct((rows, bz, targets), jnp.bfloat16),
+        ],
+        in_specs=[smem, smem, vmem],
+        out_specs=[vmem] * 4,
+        name="prepare",
+    )(place, values, others)
+
+
+def parts_of(value, count):
+    pieces = []
+    for _ in range(count):
+        piece = value.astype(jnp.bfloat16)
+        pieces.append(piece)
+        value = value - piece.astype(jnp.float32)
+    return pieces
+
+
+def slab_call(shape, first, source, parts, ratio, inverse, hit, lane, start):
+    rows, cols, vols, bx, by, bz = shape
+    blocks = cols * vols
+    targets = parts.shape[-1]
+    height = bx * blocks * by
+    depth = rows * bx
+    planes = (depth, vols, cols * by, bz)
+    padded = (depth + 2, vols, cols * by, bz)
+    factors = relax_factors(SWEEPS)
+
+    def body(source_ref, parts_ref, ratio_ref, inverse_ref, hit_ref, lane_ref, *rest):
+        if first:
+            out_ref, flux_ref, other_ref, scaled_ref = rest
+            volume_ref = None
+        else:
+            start_ref, volume_ref, flux_ref, out_ref, other_ref, scaled_ref = rest
+        sub = lax.broadcasted_iota(jnp.int32, (by, bz), 0)
+        lan = lax.broadcasted_iota(jnp.int32, (by, bz), 1)
+        for ref in (out_ref, other_ref):
+            ref[0] = jnp.zeros(planes[1:], jnp.float32)
+            ref[depth + 1] = jnp.zeros(planes[1:], jnp.float32)
+        here = other_ref if first else start_ref
+        potentials = []
+        for r in range(rows):
+            if first:
+                potential = jnp.sum(parts_ref[r], axis=0, keepdims=True)
+            else:
+                potential = sum(
+                    jnp.sum(parts_ref[r ^ mate, :, k, :], axis=0, keepdims=True)
+                    for k, mate in enumerate(MATES)
+                )
+            potentials.append(potential)
+            weights = [
+                lane_ref[r] * piece.astype(jnp.bfloat16) for piece in parts_of(potential, 3)
+            ]
+            added = lax.dot_general(
+                hit_ref[r], jnp.concatenate(weights, axis=0), (((1,), (1,)), ((), ())),
+                preferred_element_type=jnp.float32,
+            )
+            added = added[:, :bz] + added[:, bz:2 * bz] + added[:, 2 * bz:]
+            added = added.reshape(bx, vols, cols, by, bz)
+            for j in range(blocks):
+                c, v = j // vols, j % vols
+                span = (slice(r * bx, (r + 1) * bx), v, slice(c * by, (c + 1) * by))
+                scaled = (source_ref[r, j] + added[:, v, c]) * inverse_ref[span]
+                scaled_ref[span] = scaled
+                if first:
+                    here[1 + r * bx:1 + (r + 1) * bx, v, c * by:(c + 1) * by] = factors[0] * scaled
+
+        sweeps = factors[1:] if first else factors
+        for order, factor in enumerate(sweeps):
+            last = order + 1 == len(sweeps)
+            there = out_ref if (len(sweeps) - order) % 2 == 1 else other_ref
+
+            def plane(x, here=here, there=there, last=last, factor=factor):
+                tile = [here[x + 1, j % vols, (j // vols) * by:(j // vols + 1) * by]
+                        for j in range(blocks)]
+                z_up = [pltpu.roll(t, 1, 1) for t in tile]
+                z_dn = [pltpu.roll(t, bz - 1, 1) for t in tile]
+                for j in range(blocks):
+                    c, v = j // vols, j % vols
+                    own = slice(c * by, (c + 1) * by)
+                    around = here[x, v, own] + here[x + 2, v, own]
+                    if c > 0:
+                        around += here[x + 1, v, c * by - 1:(c + 1) * by - 1]
+                    else:
+                        around += jnp.where(sub == 0, 0.0, pltpu.roll(tile[j], 1, 0))
+                    if c < cols - 1:
+                        around += here[x + 1, v, c * by + 1:(c + 1) * by + 1]
+                    else:
+                        around += jnp.where(sub == by - 1, 0.0, pltpu.roll(tile[j], by - 1, 0))
+                    around += jnp.where(lan == 0, z_up[j - 1] if v > 0 else 0.0, z_up[j])
+                    around += jnp.where(lan == bz - 1, z_dn[j + 1] if v < vols - 1 else 0.0, z_dn[j])
+                    value = (1.0 - factor) * tile[j] + factor * (
+                        scaled_ref[x, v, own] + ratio_ref[x, v, own] * around
+                    )
+                    there[x + 1, v, own] = value
+                    if last and not first:
+                        volume_ref[x // bx, j, x % bx] = value
+
+            def step(x, carry, plane=plane):
+                plane(x)
+                return carry
+
+            lax.fori_loop(0, depth, step, 0, unroll=2)
+            here = there
+
+        for r in range(rows):
+            part = here[1 + r * bx:1 + (r + 1) * bx].reshape(height, bz)
+            met = sum(
+                jnp.dot(piece, lane_ref[r], preferred_element_type=jnp.float32)
+                for piece in parts_of(part, 2)
+            )
+            value = jnp.sum(met * hit_ref[r].astype(jnp.float32), axis=0, keepdims=True)
+            value = value - potentials[r]
+            for k, mate in enumerate(MATES):
+                flux_ref[r ^ mate, :, k, :] = jnp.broadcast_to(value, (blocks, targets))
+
+    vmem = pl.BlockSpec(memory_space=pltpu.VMEM)
+    operands = [source, parts, ratio, inverse, hit, lane] + ([] if first else [start])
+    fluxes = jax.ShapeDtypeStruct((rows, blocks, len(MATES), targets), jnp.float32)
+    field = jax.ShapeDtypeStruct(padded if first else source.shape, jnp.float32)
+    scratch = [pltpu.VMEM(padded, jnp.float32)] * (1 if first else 2)
+    return pl.pallas_call(
+        body,
+        out_shape=[field, fluxes],
+        in_specs=[vmem] * len(operands),
+        out_specs=[vmem, vmem],
+        scratch_shapes=scratch + [pltpu.VMEM(planes, jnp.float32)],
+        name="slab_first" if first else "slab_last",
+    )(*operands)
+
+
+def update_call(flux, panels):
+    excitations, width = flux.shape[0], panels[0].shape[1]
+
+    def body(flux_ref, a_own, a_mate, b_own, b_mate, a_ref, b_ref):
+        fluxes = [flux_ref[:, k, :].astype(jnp.bfloat16) for k in range(len(MATES))]
+        for out, own, mate, k in ((a_ref, a_own, a_mate, 1), (b_ref, b_own, b_mate, 2)):
+            value = jnp.dot(fluxes[0], own[...], preferred_element_type=jnp.float32)
+            value += jnp.dot(fluxes[k], mate[...], preferred_element_type=jnp.float32)
+            out[...] = value.astype(jnp.bfloat16)
+
+    vmem = pl.BlockSpec(memory_space=pltpu.VMEM)
+    return pl.pallas_call(
+        body,
+        out_shape=[jax.ShapeDtypeStruct((excitations, width), jnp.bfloat16)] * 2,
+        in_specs=[vmem] * 5,
+        out_specs=[vmem] * 2,
+        name="update",
+    )(flux, *panels)
+
+
+def potential_call(densities, halves, mates, panels):
+    excitations = densities[0].shape[0]
+    targets = panels[0].shape[0]
+
+    def body(a_density, b_density, a_half, b_half, a_other, b_other,
+             a_own, a_mate, b_own, b_mate, out_ref):
+        rounded = [
+            (density[...] + RELAXATION * (half[...].astype(jnp.float32)
+                                          + other[...].astype(jnp.float32))).astype(jnp.bfloat16)
+            for density, half, other in (
+                (a_density, a_half, a_other), (b_density, b_half, b_other))
+        ]
+
+        def met(value, panel):
+            return lax.dot_general(
+                value, panel[...], (((1,), (1,)), ((), ())), preferred_element_type=jnp.float32
+            )
+
+        out_ref[:, 0, :] = met(rounded[0], a_own) + met(rounded[1], b_own)
+        out_ref[:, 1, :] = met(rounded[0], a_mate)
+        out_ref[:, 2, :] = met(rounded[1], b_mate)
+
+    vmem = pl.BlockSpec(memory_space=pltpu.VMEM)
+    return pl.pallas_call(
+        body,
+        out_shape=jax.ShapeDtypeStruct((excitations, len(MATES), targets), jnp.float32),
+        in_specs=[vmem] * 10,
+        out_specs=vmem,
+        name="potential",
+    )(*densities, *halves, *mates, *panels)
+
+
+def trace_spots(trace_count, trace_cell, targets, shape):
+    rows, cols, vols, bx, by, bz = shape
+    counts = trace_count[0]
+    offsets = jnp.cumsum(counts) - counts
+    slot_ids = jnp.arange(trace_cell.shape[2], dtype=jnp.int32)
+    live = slot_ids[None, :] < counts[:, None]
+    owner = jnp.where(live, offsets[:, None] + slot_ids[None, :], -1)
+    cell = trace_cell[0]
+    block_ids = jnp.arange(cols * vols, dtype=jnp.int32)[:, None]
+    line = (block_ids % vols) * (cols * by) + (block_ids // vols) * by + (cell // bz) % by
+    code = ((cell // (by * bz)) * (cols * vols * by) + line) * bz + cell % bz
+    match = owner[:, :, None] == jnp.arange(targets, dtype=jnp.int32)
+    code = jnp.sum(jnp.where(match, code[:, :, None], 0), axis=(0, 1))
+    line = code // bz
+    span = cols * vols * by
+    return jnp.stack([line // span, line % span, code % bz])
+
+
+def split_by_excitation(panel, density, source, class_index, class_values, trace_count, trace_cell):
+    rows, cols, vols = (lax.axis_size(a) for a in ALL)
+    blocks = cols * vols
+    excitations, bx, by, bz = source.shape
+    targets, nodes = panel.shape
+    width = nodes // rows
+    here = lax.axis_index("row")
+    low, high = here & 1, here >> 1
+    place = jnp.stack([lax.axis_index(a) for a in ALL]).astype(jnp.int32)
+    shape = (rows, cols, vols, bx, by, bz)
+
+    def along(value, mate):
+        return lax.ppermute(value, "row", [(i, i ^ mate) for i in range(rows)])
+
+    def columns(array, place):
+        return lax.dynamic_slice_in_dim(array, place * width, width, 1)
+
+    spots = trace_spots(trace_count, trace_cell, targets, shape).astype(jnp.bfloat16)
+    others = jnp.concatenate(
+        [class_index.reshape(bx * by, bz).astype(jnp.bfloat16), jnp.pad(spots, ((0, 13), (0, 0)))]
+    )
+    for axis in ("vol", "row", "col"):
+        others = exchange(others, axis)
+
+    slab = lax.all_to_all(source, ALL, 0, 0, tiled=True).reshape(rows, blocks, bx, by, bz)
+
+    rounded = density.astype(jnp.bfloat16)
+    parts = lax.dot_general(
+        rounded, panel, (((1,), (1,)), ((), ())), preferred_element_type=jnp.float32
+    )
+    parts = lax.all_to_all(parts, ALL, 0, 0, tiled=True).reshape(rows, blocks, targets)
+
+    panels = [
+        columns(panel, low), along(columns(panel, low ^ 1), 1),
+        columns(panel, 2 + high), along(columns(panel, 2 + (high ^ 1)), 2),
+    ]
+    densities = [columns(density, low), columns(density, 2 + high)]
+
+    ratio, inverse, hit, lane = prepare_call(shape, place, class_values, others, targets)
+    volume, flux = slab_call(shape, True, slab, parts, ratio, inverse, hit, lane, None)
+    flux = lax.all_to_all(flux.reshape(excitations, len(MATES), targets), ALL, 0, 0, tiled=True)
+    halves = update_call(flux, panels)
+    mates = [along(halves[0], 2), along(halves[1], 1)]
+    parts = potential_call(densities, halves, mates, panels)
+    parts = lax.all_to_all(parts, ALL, 0, 0, tiled=True)
+    parts = parts.reshape(rows, blocks, len(MATES), targets)
+    volume, flux = slab_call(shape, False, slab, parts, ratio, inverse, hit, lane, volume)
+    flux = lax.all_to_all(flux.reshape(excitations, len(MATES), targets), ALL, 0, 0, tiled=True)
+    volume = lax.all_to_all(
+        volume.reshape(excitations, bx, by, bz), ALL, 0, 0, tiled=True
+    )
+    ends = update_call(flux, panels)
+    end_mates = [along(ends[0], 2), along(ends[1], 1)]
+    totals = []
+    for group in zip(halves, mates, ends, end_mates):
+        a, b, c, d = (value.astype(jnp.float32) for value in group)
+        totals.append((RELAXATION * ((a + b) + (c + d))).astype(jnp.bfloat16))
+    moved = [along(totals[0], 1), along(totals[1], 2)]
+    change = [
+        jnp.where(low == 0, totals[0], moved[0]), jnp.where(low == 0, moved[0], totals[0]),
+        jnp.where(high == 0, totals[1], moved[1]), jnp.where(high == 0, moved[1], totals[1]),
+    ]
+    return (density + jnp.concatenate(change, axis=1).astype(jnp.float32), volume)
 
 
 def padded_2(value, sides, width):
@@ -28,15 +376,6 @@
     return value
 
 
-def relax_factors(count):
-    middle = (SPECTRUM_HIGH + SPECTRUM_LOW) / 2.0
-    spread = (SPECTRUM_HIGH - SPECTRUM_LOW) / 2.0
-    return [
-        1.0 / (middle + spread * math.cos(math.pi * (2 * order + 1) / (2 * count)))
-        for order in range(count)
-    ]
-
-
 def neighbours(padded):
     center = padded[..., 1:-1, 1:-1, 1:-1]
     beside_all = padded[..., 2:, 1:-1, 1:-1] + padded[..., :-2, 1:-1, 1:-1]
@@ -45,17 +384,9 @@
     return (center, beside_all)
 
 
-def local(panel, density, source, class_index, class_values, trace_count, trace_cell):
+def split_by_block(panel, density, source, class_index, class_values, trace_count, trace_cell):
     factors = relax_factors(SWEEPS)
-    classes = jnp.arange(class_values.shape[0], dtype=jnp.int32)
-    conduct = jnp.sum(
-        jnp.where(
-            class_index[None] == classes[:, None, None, None],
-            class_values[:, None, None, None],
-            jnp.float32(0.0),
-        ),
-        axis=0,
-    )
+    conduct = conduct_of(class_index, class_values)
     diagonal = MASS_TERM + 6.0 * conduct
     counts = trace_count[0]
     block_index = lax.axis_index(("col", "vol"))
@@ -107,6 +438,15 @@
     return (density, volume)
 
 
+def local(*args):
+    sizes = [lax.axis_size(a) for a in ALL]
+    source, targets = args[2], args[0].shape[0]
+    whole = math.prod(sizes) == source.shape[0] and targets == source.shape[3] and sizes[0] == 4
+    if whole and all(size & (size - 1) == 0 for size in sizes):
+        return split_by_excitation(*args)
+    return split_by_block(*args)
+
+
 def solution(mesh):
     placed = (
         P("row", ("col", "vol")),

time: 595 us -> 188 us (0.32); the launches traced: 585 us -> 187 us
  local copies, waits for them, and re-layouts: 116 us -> 8.64 us
  starting transfers between devices: 137 us -> 32.6 us
  blocking collectives: 115 us -> 21.4 us
  waiting for transfers between devices: 141 us -> 73.8 us
  Pallas kernels: 0 us -> 37 us
  other arithmetic: 43.5 us -> 7.97 us
  between operations: 15.2 us -> 0.82 us
  matrix products: 17.5 us -> 4.96 us
    ppermute x48 -> x14, starting transfers between devices: 137 us -> 15.9 us  [the longest x8 8.33 us: along(): return lax.ppermute(value, 'row', [(i, i ^ mate) for i in range(rows)])]
    psum x4 -> x0, blocking collectives: 115 us -> none  [the longest x2 58.7 us: local(): fluxes = lax.psum(own_fluxes, ('col', 'vol'))]
    reduce_scatter x2 -> x0, waiting for transfers between devices: 76.1 us -> none  [local(): lax.psum_scatter(update, 'row', scatter_dimension=1, tiled=True)]
    slice x31 -> x0, local copies, waits for them, and re-layouts: 54.6 us -> none  [the longest x16 37.9 us: padded_2(): first = lax.slice_in_dim(value, 0, width, axis=dim)]
    pallas_call x0 -> x6, Pallas kernels: none -> 37 us  [the longest x2 19.8 us: slab_call(): pl.pallas_call(body, out_shape=[field, fluxes], in_specs=[vmem] * len(ope...]
    all_gather x2 -> x0, waiting for transfers between devices: 33.8 us -> none  [the longest x1 33.8 us: local(): density = lax.all_gather(share_state, 'row', axis=1, tiled=True)]
    ppermute x16 -> x0, local copies, waits for them, and re-layouts: 29.4 us -> none  [the longest x8 14.8 us: padded_2(): after = lax.ppermute(first, axis, down)]
    ppermute x48 -> x14, waiting for transfers between devices: 30.6 us -> 59.8 us  [the longest x6 32.1 us: exchange(): lax.ppermute(value, axis, [(i, i ^ k) for i in range(size)])]
  transfers between devices with their start and end apart: 52 -> 18, of which waited for: 32 -> 12; matrix products, arithmetic and copies ran while one was open for 11% -> 7% of each run, Pallas kernels for 0% -> 7%
where the time goes in v2:
time: 188 us; the launch traced here: 187 us
  waiting for transfers between devices  73.8 us (39%)
  Pallas kernels  37 us (20%)
  starting transfers between devices  32.6 us (17%)
  blocking collectives  21.4 us (11%)
  local copies, waits for them, and re-layouts  8.64 us (5%)
  other arithmetic  7.97 us (4%)
  matrix products  4.96 us (3%)
    ppermute x6, waiting for transfers between devices, exchange(): lax.ppermute(value, axis, [(i, i ^ k) for i in range(size)])  32.1 us
    ppermute x8, waiting for transfers between devices, along(): return lax.ppermute(value, 'row', [(i, i ^ mate) for i in range(rows)])  27.7 us
    pallas_call x2, Pallas kernels, slab_call(): pl.pallas_call(body, out_shape=[field, fluxes], in_specs=[vmem] * len(ope...  19.8 us
    all_to_all x1, blocking collectives, split_by_excitation(): lax.all_to_all(flux.reshape(excitations, len(MATES), targets), ALL, 0, 0,...  10.7 us
    all_to_all x1, blocking collectives, split_by_excitation(): parts = lax.all_to_all(parts, ALL, 0, 0, tiled=True)  10.7 us
    ppermute x8, starting transfers between devices, along(): return lax.ppermute(value, 'row', [(i, i ^ mate) for i in range(rows)])  8.33 us
    ppermute x6, starting transfers between devices, exchange(): lax.ppermute(value, axis, [(i, i ^ k) for i in range(size)])  7.55 us
    all_to_all x1, waiting for transfers between devices, split_by_excitation(): lax.all_to_all(flux.reshape(excitations, len(MATES), targets), ALL, 0, 0,...  7.46 us
  transfers between devices with their start and end apart: 18, of which 12 were waited for; matrix products, arithmetic and copies ran while one was open for 7% of the time, Pallas kernels for 7%

profile of v2, /device:TPU:0, one launch (start us, length us, event | category | flops | bytes accessed | tf_op | source)
XLA Modules:
  0.0 187.2 jit_solution(4015515924803296415)
XLA Ops:
  0.6 5.0 %fusion = f32[32,128]{1,0:T(8,128)} fusion(bf16[128,16384]{1,0:T(8,128)(2,1)} %param.7, f32[32,16384]{1,0:T(8,128)} %param.8), kind=kOutput, calls=%fused_computation.1 | convolution fusion | flops 134742016 | bytes 6307840 | tf_op jit(solution)/shard_map/dot_general | solution.py:328
  5.6 7.3 %all-to-all-start.1 = ((f32[32,1,128]{2,1,0:T(1,128)}), f32[32,1,128]{2,1,0:T(1,128)S(1)}, u32[]{:S(2)}, u32[]{:S(2)}) async-start(f32[32,1,128]{2,1,0:T(1,128)} %bitcast.2), calls=%async_computation.1 | async-start | bytes 32768 | tf_op jit(solution)/shard_map/all_to_all | solution.py:331
  13.5 6.6 %all-to-all-done.1 = f32[32,1,128]{2,1,0:T(1,128)S(1)} async-done(((f32[32,1,128]{2,1,0:T(1,128)}), f32[32,1,128]{2,1,0:T(1,128)S(1)}, u32[]{:S(2)}, u32[]{:S(2)}) %all-to-all-start.1) | async-done | bytes 16416 | tf_op jit(solution)/shard_map/all_to_all | solution.py:331
  20.1 2.6 %all-to-all-start = ((f32[32,8,8,128]{3,2,1,0:T(8,128)}), f32[32,8,8,128]{3,2,1,0:T(8,128)S(1)}, u32[]{:S(2)}, u32[]{:S(2)}) async-start(f32[32,8,8,128]{3,2,1,0:T(8,128)} %param.9), calls=%async_computation | async-start | bytes 2097152 | tf_op jit(solution)/shard_map/all_to_all | solution.py:325
  22.8 2.7 %collective-permute-start.1 = (bf16[80,128]{1,0:T(8,128)(2,1)S(1)}, bf16[80,128]{1,0:T(8,128)(2,1)S(1)}, u32[]{:S(2)}, u32[]{:S(2)}) collective-permute-start(bf16[80,128]{1,0:T(8,128)(2,1)S(1)} %get-tuple-element.39), channel_id=1, source_target_pairs={{0,2},{1,3},{2,0},{3,1},{4,6},{5,7},{6,4},{7,5},{8,10},{9,11},{10,... | collective-permute-start | bytes 61448 | tf_op jit(solution)/shard_map/ppermute | solution.py:55
  27.2 4.3 %constant_dynamic-slice_fusion.2 = (bf16[128,4096]{1,0:T(8,128)(2,1)}, bf16[128,4096]{1,0:T(8,128)(2,1)}, bf16[128,4096]{1,0:T(8,128)(2,1)}, bf16[128,4096]{1,0:T(8,128)(2,1)}) fusion(bf16[128,16384]{1,0:T(8,128)(2,1)} %param.7, s32[]{:T(128)S(6)} %select_n.170, s32[]{:T(128)S(6)} %select_n.168, s32[]{:T(128)S(6)} %select_n.167, s32[]{:T(128)S(6)} %select_n.169), kind=kLoop, calls=%fused_computation.56 | loop fusion | bytes 8388624 | tf_op jit(solution)/shard_map/dynamic_slice | solution.py:316
  34.7 15.8 %collective-permute-done.1 = bf16[80,128]{1,0:T(8,128)(2,1)S(1)} collective-permute-done((bf16[80,128]{1,0:T(8,128)(2,1)S(1)}, bf16[80,128]{1,0:T(8,128)(2,1)S(1)}, u32[]{:S(2)}, u32[]{:S(2)}) %collective-permute-start.1) | collective-permute-done | bytes 20512 | tf_op jit(solution)/shard_map/ppermute | solution.py:55
  52.0 11.1 %collective-permute-done.3 = bf16[1,4,80,128]{3,2,1,0:T(8,128)(2,1)S(1)} collective-permute-done((bf16[1,4,80,128]{3,2,1,0:T(8,128)(2,1)S(1)}, bf16[1,4,80,128]{3,2,1,0:T(8,128)(2,1)S(1)}, u32[]{:S(2)}, u32[]{:S(2)}) %collective-permute-start.3) | collective-permute-done | bytes 81952 | tf_op jit(solution)/shard_map/ppermute | solution.py:52
  64.7 3.8 %collective-permute-done.4 = bf16[2,4,80,128]{3,2,1,0:T(8,128)(2,1)S(1)} collective-permute-done((bf16[2,4,80,128]{3,2,1,0:T(8,128)(2,1)S(1)}, bf16[2,4,80,128]{3,2,1,0:T(8,128)(2,1)S(1)}, u32[]{:S(2)}, u32[]{:S(2)}) %collective-permute-start.4) | collective-permute-done | bytes 163872 | tf_op jit(solution)/shard_map/ppermute | solution.py:52
  73.1 4.9 %prepare.1 = (f32[32,4,16,128]{3,2,1,0:T(8,128)}, f32[32,4,16,128]{3,2,1,0:T(8,128)}, bf16[4,512,128]{2,1,0:T(8,128)(2,1)}, bf16[4,128,128]{2,1,0:T(8,128)(2,1)}) custom-call(s32[3]{0:T(128)} %pad_add_fusion.place_ref, f32[16]{0:T(128)} %values_ref.1, bf16[2,4,4,80,128]{4,3,2,1,0:T(8,128)(2,1)} %pad_maximum_fusion.others_ref), custom_call_target="tpu_custom_call" | custom-call | tf_op jit(solution)/shard_map/prepare/pallas_call | solution.py:95
  79.0 8.8 %slab_first.1 = (f32[34,4,16,128]{3,2,1,0:T(8,128)}, f32[4,8,3,128]{3,2,1,0:T(4,128)}) custom-call(f32[4,8,8,8,128]{4,3,2,1,0:T(8,128)} %bitcast.71, f32[4,8,128]{2,1,0:T(8,128)} %bitcast.75, f32[32,4,16,128]{3,2,1,0:T(8,128)} %get-tuple-element.14.ratio_ref, f32[32,4,16,128]{3,2,1,0:T(8,128)} %get-tuple-element.15.inverse_ref, ...), custom_call_target="tpu_custom_call" | custom-call | tf_op jit(solution)/shard_map/slab_first/pallas_call | solution.py:221
  87.8 4.1 %all-to-all-start.2 = ((f32[32,3,128]{2,1,0:T(4,128)}), f32[32,3,128]{2,1,0:T(4,128)S(1)}, u32[]{:S(2)}, u32[]{:S(2)}) async-start(f32[32,3,128]{2,1,0:T(4,128)} %bitcast.76), calls=%async_computation.2 | async-start | bytes 131072 | tf_op jit(solution)/shard_map/all_to_all | solution.py:341
  92.0 7.5 %all-to-all-done.2.flux_ref = f32[32,3,128]{2,1,0:T(4,128)S(1)} async-done(((f32[32,3,128]{2,1,0:T(4,128)}), f32[32,3,128]{2,1,0:T(4,128)S(1)}, u32[]{:S(2)}, u32[]{:S(2)}) %all-to-all-start.2) | async-done | bytes 49184 | tf_op jit(solution)/shard_map/all_to_all | solution.py:341
  100.1 3.8 %update.2 = (bf16[32,4096]{1,0:T(8,128)(2,1)}, bf16[32,4096]{1,0:T(8,128)(2,1)}) custom-call(f32[32,3,128]{2,1,0:T(4,128)} %copy-done.7, bf16[128,4096]{1,0:T(8,128)(2,1)} %get-tuple-element.28.a_own, bf16[128,4096]{1,0:T(8,128)(2,1)} %copy-done.3, bf16[128,4096]{1,0:T(8,128)(2,1)} %get-tuple-element.29.b_own, bf16[128,4096]{1,0:T(8,128)(2,1)} %copy-done.2), custom_call_target="tpu_custom_call" | custom-call | tf_op jit(solution)/shard_map/update/pallas_call | solution.py:242
  106.1 5.8 %collective-permute-done.8.a_other = bf16[32,4096]{1,0:T(8,128)(2,1)S(1)} collective-permute-done((bf16[32,4096]{1,0:T(8,128)(2,1)}, bf16[32,4096]{1,0:T(8,128)(2,1)S(1)}, u32[]{:S(2)}, u32[]{:S(2)}) %collective-permute-start.8) | collective-permute-done | bytes 262176 | tf_op jit(solution)/shard_map/ppermute | solution.py:313
  113.3 4.9 %potential.1 = f32[32,3,128]{2,1,0:T(4,128)} custom-call(f32[32,4096]{1,0:T(8,128)} %get-tuple-element.31.a_density, f32[32,4096]{1,0:T(8,128)} %get-tuple-element.30.b_density, bf16[32,4096]{1,0:T(8,128)(2,1)} %get-tuple-element.19.a_half, bf16[32,4096]{1,0:T(8,128)(2,1)} %get-tuple-element.20.b_half, bf16[32,4096]{1,0:T(8,128)(2,1)} %copy-done.6, ...), custom_call_target="tpu_custom_call" | custom-call | tf_op jit(solution)/shard_map/potential/pallas_call | solution.py:274
  118.2 10.7 %all_to_all.34 = f32[32,3,128]{2,1,0:T(4,128)} all-to-all(f32[32,3,128]{2,1,0:T(4,128)} %potential.1), channel_id=1, replica_groups=mesh['row'=4,'col'=2,'vol'=4] {'row','col','vol'}, dimensions={0} | all-to-all | bytes 98304 | tf_op jit(solution)/shard_map/all_to_all | solution.py:345
  128.9 11.0 %slab_last.1 = (f32[4,8,8,8,128]{4,3,2,1,0:T(8,128)}, f32[4,8,3,128]{3,2,1,0:T(4,128)}) custom-call(f32[4,8,8,8,128]{4,3,2,1,0:T(8,128)} %bitcast.72, f32[4,8,3,128]{3,2,1,0:T(4,128)} %bitcast.74, f32[32,4,16,128]{3,2,1,0:T(8,128)} %get-tuple-element.14.ratio_ref, f32[32,4,16,128]{3,2,1,0:T(8,128)} %get-tuple-element.15.inverse_ref, ...), custom_call_target="tpu_custom_call" | custom-call | tf_op jit(solution)/shard_map/slab_last/pallas_call | solution.py:221
  139.9 10.7 %all_to_all.35.flux_ref = f32[32,3,128]{2,1,0:T(4,128)} all-to-all(f32[32,3,128]{2,1,0:T(4,128)} %bitcast.77), channel_id=1, replica_groups=mesh['row'=4,'col'=2,'vol'=4] {'row','col','vol'}, dimensions={0} | all-to-all | bytes 98304 | tf_op jit(solution)/shard_map/all_to_all | solution.py:348
  150.6 3.6 %update.3 = (bf16[32,4096]{1,0:T(8,128)(2,1)}, bf16[32,4096]{1,0:T(8,128)(2,1)}) custom-call(f32[32,3,128]{2,1,0:T(4,128)} %all_to_all.35.flux_ref, bf16[128,4096]{1,0:T(8,128)(2,1)} %get-tuple-element.28.a_own, bf16[128,4096]{1,0:T(8,128)(2,1)} %copy-done.3, bf16[128,4096]{1,0:T(8,128)(2,1)} %get-tuple-element.29.b_own, bf16[128,4096]{1,0:T(8,128)(2,1)} %copy-done.2), custom_call_target="tpu_custom_call" | custom-call | tf_op jit(solution)/shard_map/update/pallas_call | solution.py:242
  154.9 2.6 %all-to-all-start.5 = ((f32[32,8,8,128]{3,2,1,0:T(8,128)}), f32[32,8,8,128]{3,2,1,0:T(8,128)S(1)}, u32[]{:S(2)}, u32[]{:S(2)}) async-start(f32[32,8,8,128]{3,2,1,0:T(8,128)} %bitcast.73), calls=%async_computation.5 | async-start | bytes 2097152 | tf_op jit(solution)/shard_map/all_to_all | solution.py:349
  159.2 9.6 %collective-permute-done.10 = bf16[32,4096]{1,0:T(8,128)(2,1)} collective-permute-done((bf16[32,4096]{1,0:T(8,128)(2,1)}, bf16[32,4096]{1,0:T(8,128)(2,1)}, u32[]{:S(2)}, u32[]{:S(2)}) %collective-permute-start.10) | collective-permute-done | bytes 262176 | tf_op jit(solution)/shard_map/ppermute | solution.py:313
  170.3 4.9 %collective-permute-done.12 = bf16[32,4096]{1,0:T(8,128)(2,1)S(1)} collective-permute-done((bf16[32,4096]{1,0:T(8,128)(2,1)}, bf16[32,4096]{1,0:T(8,128)(2,1)S(1)}, u32[]{:S(2)}, u32[]{:S(2)}) %collective-permute-start.12) | collective-permute-done | bytes 262176 | tf_op jit(solution)/shard_map/ppermute | solution.py:313
  177.9 4.4 %collective-permute-done.11 = bf16[32,4096]{1,0:T(8,128)(2,1)S(1)} collective-permute-done((bf16[32,4096]{1,0:T(8,128)(2,1)S(1)}, bf16[32,4096]{1,0:T(8,128)(2,1)S(1)}, u32[]{:S(2)}, u32[]{:S(2)}) %collective-permute-start.11) | collective-permute-done | bytes 262176 | tf_op jit(solution)/shard_map/ppermute | solution.py:313
  (67 shorter events, 29.8 us)
Async XLA Ops:
  0.6 12.3 %copy-start.11 = (s32[1,8]{1,0:T(1,128)S(1)}, s32[1,8]{1,0:T(1,128)}, u32[]{:S(2)}) copy-start(s32[1,8]{1,0:T(1,128)} %param.12) | copy-start | bytes 100
  0.6 12.5 %copy-start.10 = (s32[1,8,64]{2,1,0:T(8,128)S(1)}, s32[1,8,64]{2,1,0:T(8,128)}, u32[]{:S(2)}) copy-start(s32[1,8,64]{2,1,0:T(8,128)} %param.13) | copy-start | bytes 6148
  5.6 17.1 %copy-start.9 = (s32[8,8,128]{2,1,0:T(8,128)S(1)}, s32[8,8,128]{2,1,0:T(8,128)}, u32[]{:S(2)}) copy-start(s32[8,8,128]{2,1,0:T(8,128)} %param.10) | copy-start | bytes 98308
  5.6 14.5 %all-to-all-start.1 = ((f32[32,1,128]{2,1,0:T(1,128)}), f32[32,1,128]{2,1,0:T(1,128)S(1)}, u32[]{:S(2)}, u32[]{:S(2)}) async-start(f32[32,1,128]{2,1,0:T(1,128)} %bitcast.2), calls=%async_computation.1 | async-start | bytes 32768 | tf_op jit(solution)/shard_map/all_to_all | solution.py:331
  20.1 11.5 %copy-start.8 = (f32[32,1,128]{2,1,0:T(1,128)}, f32[32,1,128]{2,1,0:T(1,128)S(1)}, u32[]{:S(2)}) copy-start(f32[32,1,128]{2,1,0:T(1,128)S(1)} %all-to-all-done.1) | copy-start | bytes 49156
  20.1 58.0 %all-to-all-start = ((f32[32,8,8,128]{3,2,1,0:T(8,128)}), f32[32,8,8,128]{3,2,1,0:T(8,128)S(1)}, u32[]{:S(2)}, u32[]{:S(2)}) async-start(f32[32,8,8,128]{3,2,1,0:T(8,128)} %param.9), calls=%async_computation | async-start | bytes 2097152 | tf_op jit(solution)/shard_map/all_to_all | solution.py:325
  22.8 27.7 %collective-permute-start.1 = (bf16[80,128]{1,0:T(8,128)(2,1)S(1)}, bf16[80,128]{1,0:T(8,128)(2,1)S(1)}, u32[]{:S(2)}, u32[]{:S(2)}) collective-permute-start(bf16[80,128]{1,0:T(8,128)(2,1)S(1)} %get-tuple-element.39), channel_id=1, source_target_pairs={{0,2},{1,3},{2,0},{3,1},{4,6},{5,7},{6,4},{7,5},{8,10},{9,11},{10,... | collective-permute-start | bytes 61448 | tf_op jit(solution)/shard_map/ppermute | solution.py:55
  25.5 25.0 %collective-permute-start = (bf16[80,128]{1,0:T(8,128)(2,1)S(1)}, bf16[80,128]{1,0:T(8,128)(2,1)S(1)}, u32[]{:S(2)}, u32[]{:S(2)}) collective-permute-start(bf16[80,128]{1,0:T(8,128)(2,1)S(1)} %get-tuple-element.39), channel_id=1, source_target_pairs={{0,1},{1,0},{2,3},{3,2},{4,5},{5,4},{6,7},{7,6},{8,9},{9,8},{10,11... | collective-permute-start | bytes 61448 | tf_op jit(solution)/shard_map/ppermute | solution.py:55
  27.0 23.4 %collective-permute-start.2 = (bf16[80,128]{1,0:T(8,128)(2,1)S(1)}, bf16[80,128]{1,0:T(8,128)(2,1)S(1)}, u32[]{:S(2)}, u32[]{:S(2)}) collective-permute-start(bf16[80,128]{1,0:T(8,128)(2,1)S(1)} %get-tuple-element.39), channel_id=1, source_target_pairs={{0,3},{1,2},{2,1},{3,0},{4,7},{5,6},{6,5},{7,4},{8,11},{9,10},{10,... | collective-permute-start | bytes 61448 | tf_op jit(solution)/shard_map/ppermute | solution.py:55
  31.5 60.5 %collective-permute-start.7 = (bf16[128,4096]{1,0:T(8,128)(2,1)}, bf16[128,4096]{1,0:T(8,128)(2,1)S(1)}, u32[]{:S(2)}, u32[]{:S(2)}) collective-permute-start(bf16[128,4096]{1,0:T(8,128)(2,1)} %get-tuple-element.26), channel_id=1, source_target_pairs={{0,16},{8,24},{16,0},{24,8},{1,17},{9,25},{17,1},{25,9},{2,18},{10... | collective-permute-start | bytes 3145736 | tf_op jit(solution)/shard_map/ppermute | solution.py:313
  33.2 58.8 %collective-permute-start.6 = (bf16[128,4096]{1,0:T(8,128)(2,1)}, bf16[128,4096]{1,0:T(8,128)(2,1)S(1)}, u32[]{:S(2)}, u32[]{:S(2)}) collective-permute-start(bf16[128,4096]{1,0:T(8,128)(2,1)} %get-tuple-element.27), channel_id=1, source_target_pairs={{0,8},{8,0},{16,24},{24,16},{1,9},{9,1},{17,25},{25,17},{2,10},{10... | collective-permute-start | bytes 3145736 | tf_op jit(solution)/shard_map/ppermute | solution.py:313
  50.5 12.6 %collective-permute-start.3 = (bf16[1,4,80,128]{3,2,1,0:T(8,128)(2,1)S(1)}, bf16[1,4,80,128]{3,2,1,0:T(8,128)(2,1)S(1)}, u32[]{:S(2)}, u32[]{:S(2)}) collective-permute-start(bf16[1,4,80,128]{3,2,1,0:T(8,128)(2,1)S(1)} %maximum_bitcast_fusion), channel_id=1, source_target_pairs={{0,8},{8,0},{16,24},{24,16},{1,9},{9,1},{17,25},{25,17},{2,10},{10... | collective-permute-start | bytes 245768 | tf_op jit(solution)/shard_map/ppermute | solution.py:52
  63.1 5.4 %collective-permute-start.4 = (bf16[2,4,80,128]{3,2,1,0:T(8,128)(2,1)S(1)}, bf16[2,4,80,128]{3,2,1,0:T(8,128)(2,1)S(1)}, u32[]{:S(2)}, u32[]{:S(2)}) collective-permute-start(bf16[2,4,80,128]{3,2,1,0:T(8,128)(2,1)S(1)} %pad_maximum_fusion.2), channel_id=1, source_target_pairs={{0,16},{8,24},{16,0},{24,8},{1,17},{9,25},{17,1},{25,9},{2,18},{10... | collective-permute-start | bytes 491528 | tf_op jit(solution)/shard_map/ppermute | solution.py:52
  69.3 2.0 %collective-permute-start.5 = (bf16[4,4,80,128]{3,2,1,0:T(8,128)(2,1)}, bf16[4,4,80,128]{3,2,1,0:T(8,128)(2,1)}, u32[]{:S(2)}, u32[]{:S(2)}) collective-permute-start(bf16[4,4,80,128]{3,2,1,0:T(8,128)(2,1)} %get-tuple-element.37), channel_id=1, source_target_pairs={{0,4},{4,0},{1,5},{5,1},{2,6},{6,2},{3,7},{7,3},{8,12},{12,8},{9,1... | collective-permute-start | bytes 983048 | tf_op jit(solution)/shard_map/ppermute | solution.py:55
  87.8 11.6 %all-to-all-start.2 = ((f32[32,3,128]{2,1,0:T(4,128)}), f32[32,3,128]{2,1,0:T(4,128)S(1)}, u32[]{:S(2)}, u32[]{:S(2)}) async-start(f32[32,3,128]{2,1,0:T(4,128)} %bitcast.76), calls=%async_computation.2 | async-start | bytes 131072 | tf_op jit(solution)/shard_map/all_to_all | solution.py:341
  92.0 7.5 %copy-start.2 = (bf16[128,4096]{1,0:T(8,128)(2,1)}, bf16[128,4096]{1,0:T(8,128)(2,1)S(1)}, u32[]{:S(2)}) copy-start(bf16[128,4096]{1,0:T(8,128)(2,1)S(1)} %collective-permute-done.7.b_mate) | copy-start | bytes 3145732
  103.9 8.0 %collective-permute-start.8 = (bf16[32,4096]{1,0:T(8,128)(2,1)}, bf16[32,4096]{1,0:T(8,128)(2,1)S(1)}, u32[]{:S(2)}, u32[]{:S(2)}) collective-permute-start(bf16[32,4096]{1,0:T(8,128)(2,1)} %get-tuple-element.19.a_half), channel_id=1, source_target_pairs={{0,16},{8,24},{16,0},{24,8},{1,17},{9,25},{17,1},{25,9},{2,18},{10... | collective-permute-start | bytes 786440 | tf_op jit(solution)/shard_map/ppermute | solution.py:313
  104.5 8.0 %collective-permute-start.9 = (bf16[32,4096]{1,0:T(8,128)(2,1)}, bf16[32,4096]{1,0:T(8,128)(2,1)S(1)}, u32[]{:S(2)}, u32[]{:S(2)}) collective-permute-start(bf16[32,4096]{1,0:T(8,128)(2,1)} %get-tuple-element.20.b_half), channel_id=1, source_target_pairs={{0,8},{8,0},{16,24},{24,16},{1,9},{9,1},{17,25},{25,17},{2,10},{10... | collective-permute-start | bytes 786440 | tf_op jit(solution)/shard_map/ppermute | solution.py:313
  154.2 21.0 %copy-start.4 = (bf16[32,4096]{1,0:T(8,128)(2,1)S(1)}, bf16[32,4096]{1,0:T(8,128)(2,1)}, u32[]{:S(2)}) copy-start(bf16[32,4096]{1,0:T(8,128)(2,1)} %get-tuple-element.20.b_half) | copy-start | bytes 786436
  154.2 14.7 %collective-permute-start.10 = (bf16[32,4096]{1,0:T(8,128)(2,1)}, bf16[32,4096]{1,0:T(8,128)(2,1)}, u32[]{:S(2)}, u32[]{:S(2)}) collective-permute-start(bf16[32,4096]{1,0:T(8,128)(2,1)} %get-tuple-element.23), channel_id=1, source_target_pairs={{0,16},{8,24},{16,0},{24,8},{1,17},{9,25},{17,1},{25,9},{2,18},{10... | collective-permute-start | bytes 786440 | tf_op jit(solution)/shard_map/ppermute | solution.py:313
  154.9 31.4 %all-to-all-start.5 = ((f32[32,8,8,128]{3,2,1,0:T(8,128)}), f32[32,8,8,128]{3,2,1,0:T(8,128)S(1)}, u32[]{:S(2)}, u32[]{:S(2)}) async-start(f32[32,8,8,128]{3,2,1,0:T(8,128)} %bitcast.73), calls=%async_computation.5 | async-start | bytes 2097152 | tf_op jit(solution)/shard_map/all_to_all | solution.py:349
  157.5 17.6 %collective-permute-start.12 = (bf16[32,4096]{1,0:T(8,128)(2,1)}, bf16[32,4096]{1,0:T(8,128)(2,1)S(1)}, u32[]{:S(2)}, u32[]{:S(2)}) collective-permute-start(bf16[32,4096]{1,0:T(8,128)(2,1)} %get-tuple-element.24), channel_id=1, source_target_pairs={{0,8},{8,0},{16,24},{24,16},{1,9},{9,1},{17,25},{25,17},{2,10},{10... | collective-permute-start | bytes 786440 | tf_op jit(solution)/shard_map/ppermute | solution.py:313
  170.2 12.2 %collective-permute-start.11 = (bf16[32,4096]{1,0:T(8,128)(2,1)S(1)}, bf16[32,4096]{1,0:T(8,128)(2,1)S(1)}, u32[]{:S(2)}, u32[]{:S(2)}) collective-permute-start(bf16[32,4096]{1,0:T(8,128)(2,1)S(1)} %multiply_convert_fusion.1), channel_id=1, source_target_pairs={{0,8},{8,0},{16,24},{24,16},{1,9},{9,1},{17,25},{25,17},{2,10},{10... | collective-permute-start | bytes 786440 | tf_op jit(solution)/shard_map/ppermute | solution.py:313
  176.4 8.3 %collective-permute-start.13 = (bf16[32,4096]{1,0:T(8,128)(2,1)S(1)}, bf16[32,4096]{1,0:T(8,128)(2,1)S(1)}, u32[]{:S(2)}, u32[]{:S(2)}) collective-permute-start(bf16[32,4096]{1,0:T(8,128)(2,1)S(1)} %multiply_convert_fusion), channel_id=1, source_target_pairs={{0,16},{8,24},{16,0},{24,8},{1,17},{9,25},{17,1},{25,9},{2,18},{10... | collective-permute-start | bytes 786440 | tf_op jit(solution)/shard_map/ppermute | solution.py:313
  (6 other events, 15.4 us)

commit v3 on v2

--- a/solution.py
+++ b/solution.py
@@ -1,4 +1,3 @@
-import functools
 import math
 
 import jax
@@ -8,6 +7,7 @@
 from jax.experimental.pallas import tpu as pltpu
 from jax.sharding import PartitionSpec as P
 
+
 SWEEPS = 4
 OUTER = 2
 
@@ -18,6 +18,10 @@
 SPECTRUM_HIGH = 2.0
 
 ALL = ("row", "col", "vol")
+GROUP = 8
+SPOT_ROWS = 16
+PART_ROWS = 8
+VMEM_BYTES = 16 * 2 ** 20
 
 
 def relax_factors(count):
@@ -44,31 +48,74 @@
 MATES = (0, 1, 2)
 
 
-def exchange(value, axis):
+def mated(value, axis, mate):
+    return lax.ppermute(value, axis, [(i, i ^ mate) for i in range(lax.axis_size(axis))])
+
+
+def stacked(value, axis):
     size = lax.axis_size(axis)
-    if axis == "row":
-        value, k = value[None], 1
-        while k < size:
-            value = jnp.concatenate([value, lax.ppermute(value, axis, [(i, i ^ k) for i in range(size)])])
-            k = 2 * k
-        return value
-    moved = [lax.ppermute(value, axis, [(i, i ^ k) for i in range(size)]) for k in range(1, size)]
-    return jnp.stack([value] + moved)
-
-
-def prepare_call(shape, place, values, others, targets):
+    return jnp.stack([value] + [mated(value, axis, k) for k in range(1, size)])
+
+
+def gather_call(density, panel, source):
+    excitations, lines, bz = source.shape
+    targets, nodes = panel.shape
+    steps = math.gcd(excitations, 8)
+    width, few = nodes // steps, excitations // steps
+
+    def body(density_ref, panel_ref, source_ref, out_ref, part_ref):
+        index = pl.program_id(0)
+        part = lax.dot_general(
+            density_ref[...].astype(jnp.bfloat16), panel_ref[...], (((1,), (1,)), ((), ())),
+            preferred_element_type=jnp.float32,
+        )
+
+        @pl.when(index == 0)
+        def _():
+            part_ref[...] = part
+
+        @pl.when(index > 0)
+        def _():
+            part_ref[...] += part
+
+        out_ref[pl.ds(index * few, few), 0:lines] = source_ref[...]
+
+        @pl.when(index == steps - 1)
+        def _():
+            for i in range(excitations):
+                out_ref[i, lines:lines + PART_ROWS] = jnp.broadcast_to(
+                    part_ref[i:i + 1], (PART_ROWS, targets)
+                )
+
+    return pl.pallas_call(
+        body,
+        grid=(steps,),
+        out_shape=jax.ShapeDtypeStruct((excitations, lines + PART_ROWS, bz), jnp.float32),
+        in_specs=[
+            pl.BlockSpec((excitations, width), lambda i: (0, i)),
+            pl.BlockSpec((targets, width), lambda i: (0, i)),
+            pl.BlockSpec((few, lines, bz), lambda i: (i, 0, 0)),
+        ],
+        out_specs=pl.BlockSpec((excitations, lines + PART_ROWS, bz), lambda i: (0, 0, 0)),
+        scratch_shapes=[pltpu.VMEM((excitations, targets), jnp.float32)],
+        compiler_params=pltpu.CompilerParams(vmem_limit_bytes=VMEM_BYTES),
+        name="gather",
+    )(density, panel, source)
+
+
+def prepare_call(shape, place, values, kinds, spots):
     rows, cols, vols, bx, by, bz = shape
     blocks = cols * vols
     height = bx * blocks * by
-
-    def body(place_ref, values_ref, others_ref, ratio_ref, inverse_ref, hit_ref, lane_ref):
+    targets = spots.shape[-1]
+
+    def body(place_ref, values_ref, kinds_ref, spots_ref, ratio_ref, inverse_ref, hit_ref, lane_ref):
         r0, c0, v0 = place_ref[0], place_ref[1], place_ref[2]
         count = values_ref.shape[0]
         row_ids = lax.broadcasted_iota(jnp.int32, (height, targets), 0)
         lane_ids = lax.broadcasted_iota(jnp.int32, (bz, targets), 0)
         for r in range(rows):
-            spot = others_ref[c0, r ^ r0, v0, bx * by:bx * by + 16, :].astype(jnp.float32)
-            spot = spot.astype(jnp.int32)
+            spot = spots_ref[r ^ r0].astype(jnp.float32).astype(jnp.int32)
             line = spot[0:1] * (blocks * by) + spot[1:2]
             hit_ref[r] = (row_ids == line).astype(jnp.bfloat16)
             lane_ref[r] = (lane_ids == spot[2:3]).astype(jnp.bfloat16)
@@ -76,7 +123,7 @@
         def block(index, carry):
             r, rest = index // blocks, index % blocks
             c, v = rest // vols, rest % vols
-            kind = others_ref[c ^ c0, r ^ r0, v ^ v0, 0:bx * by, :].astype(jnp.float32)
+            kind = kinds_ref[c ^ c0, r ^ r0, v ^ v0].astype(jnp.float32)
             conduct = jnp.zeros((bx * by, bz), jnp.float32)
             for i in range(count):
                 conduct = jnp.where(kind == float(i), values_ref[i], conduct)
@@ -100,10 +147,11 @@
             jax.ShapeDtypeStruct((rows, height, targets), jnp.bfloat16),
             jax.ShapeDtypeStruct((rows, bz, targets), jnp.bfloat16),
         ],
-        in_specs=[smem, smem, vmem],
+        in_specs=[smem, smem, vmem, vmem],
         out_specs=[vmem] * 4,
+        compiler_params=pltpu.CompilerParams(vmem_limit_bytes=VMEM_BYTES),
         name="prepare",
-    )(place, values, others)
+    )(place, values, kinds, spots)
 
 
 def parts_of(value, count):
@@ -115,22 +163,24 @@
     return pieces
 
 
-def slab_call(shape, first, source, parts, ratio, inverse, hit, lane, start):
+def slab_call(shape, first, source, ratio, inverse, hit, lane, parts=None, start=None):
     rows, cols, vols, bx, by, bz = shape
     blocks = cols * vols
-    targets = parts.shape[-1]
+    targets = lane.shape[-1]
     height = bx * blocks * by
     depth = rows * bx
     planes = (depth, vols, cols * by, bz)
     padded = (depth + 2, vols, cols * by, bz)
     factors = relax_factors(SWEEPS)
 
-    def body(source_ref, parts_ref, ratio_ref, inverse_ref, hit_ref, lane_ref, *rest):
+    lines = bx * by
+
+    def body(source_ref, ratio_ref, inverse_ref, hit_ref, lane_ref, *rest):
         if first:
             out_ref, flux_ref, other_ref, scaled_ref = rest
             volume_ref = None
         else:
-            start_ref, volume_ref, flux_ref, out_ref, other_ref, scaled_ref = rest
+            parts_ref, start_ref, volume_ref, flux_ref, out_ref, other_ref, scaled_ref = rest
         sub = lax.broadcasted_iota(jnp.int32, (by, bz), 0)
         lan = lax.broadcasted_iota(jnp.int32, (by, bz), 1)
         for ref in (out_ref, other_ref):
@@ -140,7 +190,7 @@
         potentials = []
         for r in range(rows):
             if first:
-                potential = jnp.sum(parts_ref[r], axis=0, keepdims=True)
+                potential = sum(source_ref[r, j, lines:lines + 1] for j in range(blocks))
             else:
                 potential = sum(
                     jnp.sum(parts_ref[r ^ mate, :, k, :], axis=0, keepdims=True)
@@ -159,7 +209,8 @@
             for j in range(blocks):
                 c, v = j // vols, j % vols
                 span = (slice(r * bx, (r + 1) * bx), v, slice(c * by, (c + 1) * by))
-                scaled = (source_ref[r, j] + added[:, v, c]) * inverse_ref[span]
+                scaled = source_ref[r, j, 0:lines].reshape(bx, by, bz) + added[:, v, c]
+                scaled = scaled * inverse_ref[span]
                 scaled_ref[span] = scaled
                 if first:
                     here[1 + r * bx:1 + (r + 1) * bx, v, c * by:(c + 1) * by] = factors[0] * scaled
@@ -169,37 +220,37 @@
             last = order + 1 == len(sweeps)
             there = out_ref if (len(sweeps) - order) % 2 == 1 else other_ref
 
-            def plane(x, here=here, there=there, last=last, factor=factor):
-                tile = [here[x + 1, j % vols, (j // vols) * by:(j // vols + 1) * by]
-                        for j in range(blocks)]
-                z_up = [pltpu.roll(t, 1, 1) for t in tile]
-                z_dn = [pltpu.roll(t, bz - 1, 1) for t in tile]
-                for j in range(blocks):
-                    c, v = j // vols, j % vols
-                    own = slice(c * by, (c + 1) * by)
-                    around = here[x, v, own] + here[x + 2, v, own]
-                    if c > 0:
-                        around += here[x + 1, v, c * by - 1:(c + 1) * by - 1]
-                    else:
-                        around += jnp.where(sub == 0, 0.0, pltpu.roll(tile[j], 1, 0))
-                    if c < cols - 1:
-                        around += here[x + 1, v, c * by + 1:(c + 1) * by + 1]
-                    else:
-                        around += jnp.where(sub == by - 1, 0.0, pltpu.roll(tile[j], by - 1, 0))
-                    around += jnp.where(lan == 0, z_up[j - 1] if v > 0 else 0.0, z_up[j])
-                    around += jnp.where(lan == bz - 1, z_dn[j + 1] if v < vols - 1 else 0.0, z_dn[j])
-                    value = (1.0 - factor) * tile[j] + factor * (
-                        scaled_ref[x, v, own] + ratio_ref[x, v, own] * around
-                    )
-                    there[x + 1, v, own] = value
-                    if last and not first:
-                        volume_ref[x // bx, j, x % bx] = value
-
-            def step(x, carry, plane=plane):
-                plane(x)
+            def step(index, carry, here=here, there=there, last=last, factor=factor):
+                for x in (GROUP * index + i for i in range(GROUP)):
+                    tile = [here[x + 1, j % vols, (j // vols) * by:(j // vols + 1) * by]
+                            for j in range(blocks)]
+                    up = [pltpu.roll(t, 1, 1) for t in tile]
+                    down = [pltpu.roll(t, bz - 1, 1) for t in tile]
+                    for j in range(blocks):
+                        c, v = j // vols, j % vols
+                        own = slice(c * by, (c + 1) * by)
+                        around = here[x, v, own] + here[x + 2, v, own]
+                        if c > 0:
+                            around += here[x + 1, v, c * by - 1:(c + 1) * by - 1]
+                        else:
+                            around += jnp.where(sub == 0, 0.0, pltpu.roll(tile[j], 1, 0))
+                        if c < cols - 1:
+                            around += here[x + 1, v, c * by + 1:(c + 1) * by + 1]
+                        else:
+                            around += jnp.where(sub == by - 1, 0.0, pltpu.roll(tile[j], by - 1, 0))
+                        around += jnp.where(lan == 0, up[j - 1] if v > 0 else 0.0, up[j])
+                        around += jnp.where(
+                            lan == bz - 1, down[j + 1] if v < vols - 1 else 0.0, down[j]
+                        )
+                        value = (1.0 - factor) * tile[j] + factor * (
+                            scaled_ref[x, v, own] + ratio_ref[x, v, own] * around
+                        )
+                        there[x + 1, v, own] = value
+                        if last and not first:
+                            volume_ref[x // bx, j, x % bx] = value
                 return carry
 
-            lax.fori_loop(0, depth, step, 0, unroll=2)
+            lax.fori_loop(0, depth // GROUP, step, 0)
             here = there
 
         for r in range(rows):
@@ -214,9 +265,10 @@
                 flux_ref[r ^ mate, :, k, :] = jnp.broadcast_to(value, (blocks, targets))
 
     vmem = pl.BlockSpec(memory_space=pltpu.VMEM)
-    operands = [source, parts, ratio, inverse, hit, lane] + ([] if first else [start])
+    operands = [source, ratio, inverse, hit, lane] + ([] if first else [parts, start])
     fluxes = jax.ShapeDtypeStruct((rows, blocks, len(MATES), targets), jnp.float32)
-    field = jax.ShapeDtypeStruct(padded if first else source.shape, jnp.float32)
+    field = padded if first else (rows, blocks, bx, by, bz)
+    field = jax.ShapeDtypeStruct(field, jnp.float32)
     scratch = [pltpu.VMEM(padded, jnp.float32)] * (1 if first else 2)
     return pl.pallas_call(
         body,
@@ -224,6 +276,7 @@
         in_specs=[vmem] * len(operands),
         out_specs=[vmem, vmem],
         scratch_shapes=scratch + [pltpu.VMEM(planes, jnp.float32)],
+        compiler_params=pltpu.CompilerParams(vmem_limit_bytes=VMEM_BYTES),
         name="slab_first" if first else "slab_last",
     )(*operands)
 
@@ -244,6 +297,7 @@
         out_shape=[jax.ShapeDtypeStruct((excitations, width), jnp.bfloat16)] * 2,
         in_specs=[vmem] * 5,
         out_specs=[vmem] * 2,
+        compiler_params=pltpu.CompilerParams(vmem_limit_bytes=VMEM_BYTES),
         name="update",
     )(flux, *panels)
 
@@ -276,12 +330,13 @@
         out_shape=jax.ShapeDtypeStruct((excitations, len(MATES), targets), jnp.float32),
         in_specs=[vmem] * 10,
         out_specs=vmem,
+        compiler_params=pltpu.CompilerParams(vmem_limit_bytes=VMEM_BYTES),
         name="potential",
     )(*densities, *halves, *mates, *panels)
 
 
 def trace_spots(trace_count, trace_cell, targets, shape):
-    rows, cols, vols, bx, by, bz = shape
+    _, cols, vols, _, by, bz = shape
     counts = trace_count[0]
     offsets = jnp.cumsum(counts) - counts
     slot_ids = jnp.arange(trace_cell.shape[2], dtype=jnp.int32)
@@ -309,53 +364,50 @@
     place = jnp.stack([lax.axis_index(a) for a in ALL]).astype(jnp.int32)
     shape = (rows, cols, vols, bx, by, bz)
 
-    def along(value, mate):
-        return lax.ppermute(value, "row", [(i, i ^ mate) for i in range(rows)])
-
     def columns(array, place):
         return lax.dynamic_slice_in_dim(array, place * width, width, 1)
 
+    kinds = class_index.reshape(bx * by, bz).astype(jnp.bfloat16)
+    kinds = stacked(kinds, "vol").reshape(vols * bx * by, bz)
     spots = trace_spots(trace_count, trace_cell, targets, shape).astype(jnp.bfloat16)
-    others = jnp.concatenate(
-        [class_index.reshape(bx * by, bz).astype(jnp.bfloat16), jnp.pad(spots, ((0, 13), (0, 0)))]
-    )
-    for axis in ("vol", "row", "col"):
-        others = exchange(others, axis)
-
-    slab = lax.all_to_all(source, ALL, 0, 0, tiled=True).reshape(rows, blocks, bx, by, bz)
-
-    rounded = density.astype(jnp.bfloat16)
-    parts = lax.dot_general(
-        rounded, panel, (((1,), (1,)), ((), ())), preferred_element_type=jnp.float32
-    )
-    parts = lax.all_to_all(parts, ALL, 0, 0, tiled=True).reshape(rows, blocks, targets)
-
-    panels = [
-        columns(panel, low), along(columns(panel, low ^ 1), 1),
-        columns(panel, 2 + high), along(columns(panel, 2 + (high ^ 1)), 2),
-    ]
+    spots = jnp.pad(spots, ((0, SPOT_ROWS - spots.shape[0]), (0, 0)))
+    known = jnp.concatenate([kinds, spots])[None]
+    known = jnp.concatenate([known, mated(known, "row", 1)])
+    known = jnp.concatenate([known, mated(known, "row", 2)])
+    spots = known[:, vols * bx * by:]
+    kinds = stacked(known[:, :vols * bx * by], "col")
+    kinds = kinds.reshape(cols, rows, vols, bx * by, bz)
+
+    slab = gather_call(density, panel, source.reshape(excitations, bx * by, bz))
+    slab = lax.all_to_all(slab, ALL, 0, 0, tiled=True)
+    slab = slab.reshape(rows, blocks, bx * by + PART_ROWS, bz)
+
+    panels = [columns(panel, low), None, columns(panel, 2 + high), None]
+    panels[1] = mated(columns(panel, low ^ 1), "row", 1)
+    panels[3] = mated(columns(panel, 2 + (high ^ 1)), "row", 2)
     densities = [columns(density, low), columns(density, 2 + high)]
 
-    ratio, inverse, hit, lane = prepare_call(shape, place, class_values, others, targets)
-    volume, flux = slab_call(shape, True, slab, parts, ratio, inverse, hit, lane, None)
-    flux = lax.all_to_all(flux.reshape(excitations, len(MATES), targets), ALL, 0, 0, tiled=True)
+    ratio, inverse, hit, lane = prepare_call(shape, place, class_values, kinds, spots)
+    volume, flux = slab_call(shape, True, slab, ratio, inverse, hit, lane)
+    flux = flux.reshape(excitations, len(MATES), targets)
+    flux = lax.all_to_all(flux, ALL, 0, 0, tiled=True)
     halves = update_call(flux, panels)
-    mates = [along(halves[0], 2), along(halves[1], 1)]
+    mates = [mated(halves[0], "row", 2), mated(halves[1], "row", 1)]
     parts = potential_call(densities, halves, mates, panels)
     parts = lax.all_to_all(parts, ALL, 0, 0, tiled=True)
     parts = parts.reshape(rows, blocks, len(MATES), targets)
-    volume, flux = slab_call(shape, False, slab, parts, ratio, inverse, hit, lane, volume)
-    flux = lax.all_to_all(flux.reshape(excitations, len(MATES), targets), ALL, 0, 0, tiled=True)
-    volume = lax.all_to_all(
-        volume.reshape(excitations, bx, by, bz), ALL, 0, 0, tiled=True
-    )
+    volume, flux = slab_call(shape, False, slab, ratio, inverse, hit, lane, parts, volume)
+    flux = flux.reshape(excitations, len(MATES), targets)
+    flux = lax.all_to_all(flux, ALL, 0, 0, tiled=True)
+    volume = volume.reshape(excitations, bx, by, bz)
+    volume = lax.all_to_all(volume, ALL, 0, 0, tiled=True)
     ends = update_call(flux, panels)
-    end_mates = [along(ends[0], 2), along(ends[1], 1)]
+    end_mates = [mated(ends[0], "row", 2), mated(ends[1], "row", 1)]
     totals = []
     for group in zip(halves, mates, ends, end_mates):
         a, b, c, d = (value.astype(jnp.float32) for value in group)
         totals.append((RELAXATION * ((a + b) + (c + d))).astype(jnp.bfloat16))
-    moved = [along(totals[0], 1), along(totals[1], 2)]
+    moved = [mated(totals[0], "row", 1), mated(totals[1], "row", 2)]
     change = [
         jnp.where(low == 0, totals[0], moved[0]), jnp.where(low == 0, moved[0], totals[0]),
         jnp.where(high == 0, totals[1], moved[1]), jnp.where(high == 0, moved[1], totals[1]),
@@ -440,11 +492,14 @@
 
 def local(*args):
     sizes = [lax.axis_size(a) for a in ALL]
-    source, targets = args[2], args[0].shape[0]
-    whole = math.prod(sizes) == source.shape[0] and targets == source.shape[3] and sizes[0] == 4
-    if whole and all(size & (size - 1) == 0 for size in sizes):
+    if whole_slabs(sizes, args[0].shape[0], args[2].shape):
         return split_by_excitation(*args)
     return split_by_block(*args)
+
+
+def whole_slabs(sizes, targets, block):
+    fits = math.prod(sizes) == block[0] and sizes[0] == 4 and targets == block[3]
+    return fits and all(size & (size - 1) == 0 for size in sizes)
 
 
 def solution(mesh):

time: 188 us -> 172 us (0.915)
  Pallas kernels: 37 us -> 23.6 us
  local copies, waits for them, and re-layouts: 8.64 us -> 19.5 us
  matrix products: 4.96 us -> 0 us
  blocking collectives: 21.4 us -> 18.5 us
  other arithmetic: 7.97 us -> 5.08 us
  starting transfers between devices: 32.6 us -> 29.8 us
    unnamed x25 -> x61, local copies, waits for them, and re-layouts: 3.31 us -> 14.8 us
    pallas_call x2, Pallas kernels: 19.8 us -> 9.1 us  [slab_call(): pl.pallas_call(body, out_shape=[field, fluxes], in_specs=[vmem] * len(ope...]
    all_to_all x4 -> x3, waiting for transfers between devices: 14.1 us -> 7.48 us  [the longest x1 7.48 us: split_by_excitation(): flux = lax.all_to_all(flux, ALL, 0, 0, tiled=True)]
    ppermute x14, waiting for transfers between devices: 59.8 us -> 66.2 us  [mated(): lax.ppermute(value, axis, [(i, i ^ mate) for i in range(lax.axis_size(axi...]
    dot_general x1 -> x0, matrix products: 4.96 us -> none  [split_by_excitation(): lax.dot_general(rounded, panel, (((1,), (1,)), ((), ())), preferred_eleme...]
    pallas_call x0 -> x1, Pallas kernels: none -> 3.94 us  [gather_call(): pl.pallas_call(body, grid=(steps,), out_shape=jax.ShapeDtypeStruct((excit...]
    all_to_all x4 -> x3, starting transfers between devices: 16.8 us -> 13.4 us  [the longest x1 6 us: split_by_excitation(): slab = lax.all_to_all(slab, ALL, 0, 0, tiled=True)]
    pallas_call x2, Pallas kernels: 7.34 us -> 4.57 us  [update_call(): pl.pallas_call(body, out_shape=[jax.ShapeDtypeStruct((excitations, width)...]
  transfers between devices with their start and end apart: 18 -> 17, of which waited for: 12 -> 10; matrix products, arithmetic and copies ran while one was open for 7% -> 5% of each run, Pallas kernels for 7% -> 6%
where the time goes in v3:
time: 172 us; the launch traced here: 171 us
  waiting for transfers between devices  73.7 us (43%)
  starting transfers between devices  29.8 us (17%)
  Pallas kernels  23.6 us (14%)
  local copies, waits for them, and re-layouts  19.5 us (11%)
  blocking collectives  18.5 us (11%)
  other arithmetic  5.08 us (3%)
    ppermute x14, waiting for transfers between devices, mated(): lax.ppermute(value, axis, [(i, i ^ mate) for i in range(lax.axis_size(axi...  66.2 us
    ppermute x14, starting transfers between devices, mated(): lax.ppermute(value, axis, [(i, i ^ mate) for i in range(lax.axis_size(axi...  16.4 us
    unnamed x61, local copies, waits for them, and re-layouts  14.8 us
    all_to_all x1, blocking collectives, split_by_excitation(): parts = lax.all_to_all(parts, ALL, 0, 0, tiled=True)  9.37 us
    all_to_all x1, blocking collectives, split_by_excitation(): flux = lax.all_to_all(flux, ALL, 0, 0, tiled=True)  9.17 us
    pallas_call x2, Pallas kernels, slab_call(): pl.pallas_call(body, out_shape=[field, fluxes], in_specs=[vmem] * len(ope...  9.1 us
    all_to_all x1, waiting for transfers between devices, split_by_excitation(): flux = lax.all_to_all(flux, ALL, 0, 0, tiled=True)  7.48 us
    all_to_all x1, starting transfers between devices, split_by_excitation(): slab = lax.all_to_all(slab, ALL, 0, 0, tiled=True)  6 us
  transfers between devices with their start and end apart: 17, of which 10 were waited for; matrix products, arithmetic and copies ran while one was open for 5% of the time, Pallas kernels for 6%

profile of v3, /device:TPU:0, one launch (start us, length us, event | category | flops | bytes accessed | tf_op | source)
XLA Modules:
  0.0 171.2 jit_solution(12524287981630450825)
XLA Ops:
  1.4 5.1 %collective-permute-start.2 = (bf16[64,128]{1,0:T(8,128)(2,1)S(1)}, bf16[64,128]{1,0:T(8,128)(2,1)S(1)}, u32[]{:S(2)}, u32[]{:S(2)}) collective-permute-start(bf16[64,128]{1,0:T(8,128)(2,1)S(1)} %get-tuple-element.37), channel_id=1, source_target_pairs={{0,3},{1,2},{2,1},{3,0},{4,7},{5,6},{6,5},{7,4},{8,11},{9,10},{10,... | collective-permute-start | bytes 49160 | tf_op jit(solution)/shard_map/ppermute | solution.py:52
  7.1 2.2 %copy-done = bf16[128,16384]{1,0:T(8,128)(2,1)S(1)} copy-done((bf16[128,16384]{1,0:T(8,128)(2,1)S(1)}, bf16[128,16384]{1,0:T(8,128)(2,1)}, u32[]{:S(2)}) %copy-start) | copy-done | bytes 4194328
  12.1 3.9 %gather.1 = f32[32,72,128]{2,1,0:T(8,128)} custom-call(f32[32,16384]{1,0:T(8,128)S(1)} %copy-done.1, bf16[128,16384]{1,0:T(8,128)(2,1)S(1)} %copy-done, f32[32,64,128]{2,1,0:T(8,128)S(1)} %bitcast.69), custom_call_target="tpu_custom_call" | custom-call | tf_op jit(solution)/shard_map/gather/pallas_call | solution.py:90
  16.1 6.0 %all-to-all-start = ((f32[32,72,128]{2,1,0:T(8,128)}), f32[32,72,128]{2,1,0:T(8,128)S(1)}, u32[]{:S(2)}, u32[]{:S(2)}) async-start(f32[32,72,128]{2,1,0:T(8,128)} %gather.1), calls=%async_computation | async-start | bytes 2359296 | tf_op jit(solution)/shard_map/all_to_all | solution.py:382
  22.1 3.9 %constant_dynamic-slice_fusion.2 = (bf16[128,4096]{1,0:T(8,128)(2,1)}, bf16[128,4096]{1,0:T(8,128)(2,1)}, bf16[128,4096]{1,0:T(8,128)(2,1)S(1)}, bf16[128,4096]{1,0:T(8,128)(2,1)S(1)}) fusion(bf16[128,16384]{1,0:T(8,128)(2,1)} %panel_ref.1, s32[]{:T(128)S(6)} %select_n.170, s32[]{:T(128)S(6)} %select_n.168, s32[]{:T(128)S(6)} %select_n.167, s32[]{:T(128)S(6)} %select_n.169), kind=kLoop, calls=%fused_computation.56 | loop fusion | bytes 8388624 | tf_op jit(solution)/shard_map/dynamic_slice | solution.py:368
  26.0 1.8 %collective-permute-start.7 = (bf16[128,4096]{1,0:T(8,128)(2,1)}, bf16[128,4096]{1,0:T(8,128)(2,1)}, u32[]{:S(2)}, u32[]{:S(2)}) collective-permute-start(bf16[128,4096]{1,0:T(8,128)(2,1)} %get-tuple-element.26), channel_id=1, source_target_pairs={{0,16},{8,24},{16,0},{24,8},{1,17},{9,25},{17,1},{25,9},{2,18},{10... | collective-permute-start | bytes 3145736 | tf_op jit(solution)/shard_map/ppermute | solution.py:52
  30.5 31.0 %collective-permute-done.3 = bf16[1,272,128]{2,1,0:T(8,128)(2,1)S(1)} collective-permute-done((bf16[1,272,128]{2,1,0:T(8,128)(2,1)S(1)}, bf16[1,272,128]{2,1,0:T(8,128)(2,1)S(1)}, u32[]{:S(2)}, u32[]{:S(2)}) %collective-permute-start.3) | collective-permute-done | bytes 69664 | tf_op jit(solution)/shard_map/ppermute | solution.py:52
  63.0 3.7 %collective-permute-done.4 = bf16[2,272,128]{2,1,0:T(8,128)(2,1)S(1)} collective-permute-done((bf16[2,272,128]{2,1,0:T(8,128)(2,1)S(1)}, bf16[2,272,128]{2,1,0:T(8,128)(2,1)S(1)}, u32[]{:S(2)}, u32[]{:S(2)}) %collective-permute-start.4) | collective-permute-done | bytes 139296 | tf_op jit(solution)/shard_map/ppermute | solution.py:52
  70.5 2.8 %prepare.1 = (f32[32,4,16,128]{3,2,1,0:T(8,128)S(1)}, f32[32,4,16,128]{3,2,1,0:T(8,128)S(1)}, bf16[4,512,128]{2,1,0:T(8,128)(2,1)S(1)}, bf16[4,128,128]{2,1,0:T(8,128)(2,1)S(1)}) custom-call(s32[3]{0:T(128)S(1)} %pad_add_fusion.place_ref, f32[16]{0:T(128)S(1)} %copy-done.26, bf16[2,4,4,64,128]{4,3,2,1,0:T(8,128)(2,1)S(1)} %pad_maximum_fusion.kinds_ref, ...), custom_call_target="tpu_custom_call" | custom-call | tf_op jit(solution)/shard_map/prepare/pallas_call | solution.py:142
  79.6 4.2 %slab_first.1 = (f32[34,4,16,128]{3,2,1,0:T(8,128)S(1)}, f32[4,8,3,128]{3,2,1,0:T(4,128)}) custom-call(f32[4,8,72,128]{3,2,1,0:T(8,128)S(1)} %bitcast.67, f32[32,4,16,128]{3,2,1,0:T(8,128)S(1)} %copy-done.5, f32[32,4,16,128]{3,2,1,0:T(8,128)S(1)} %copy-done.8, bf16[4,512,128]{2,1,0:T(8,128)(2,1)S(1)} %copy-done.11, ...), custom_call_target="tpu_custom_call" | custom-call | tf_op jit(solution)/shard_map/slab_first/pallas_call | solution.py:273
  84.8 4.7 %all-to-all-start.1 = ((f32[32,3,128]{2,1,0:T(4,128)}), f32[32,3,128]{2,1,0:T(4,128)S(1)}, u32[]{:S(2)}, u32[]{:S(2)}) async-start(f32[32,3,128]{2,1,0:T(4,128)} %bitcast.19), calls=%async_computation.1 | async-start | bytes 131072 | tf_op jit(solution)/shard_map/all_to_all | solution.py:393
  89.5 7.5 %all-to-all-done.1.flux_ref = f32[32,3,128]{2,1,0:T(4,128)S(1)} async-done(((f32[32,3,128]{2,1,0:T(4,128)}), f32[32,3,128]{2,1,0:T(4,128)S(1)}, u32[]{:S(2)}, u32[]{:S(2)}) %all-to-all-start.1) | async-done | bytes 49184 | tf_op jit(solution)/shard_map/all_to_all | solution.py:393
  98.5 2.4 %update.2 = (bf16[32,4096]{1,0:T(8,128)(2,1)S(1)}, bf16[32,4096]{1,0:T(8,128)(2,1)S(1)}) custom-call(f32[32,3,128]{2,1,0:T(4,128)S(1)} %copy-done.25, bf16[128,4096]{1,0:T(8,128)(2,1)S(1)} %get-tuple-element.28.a_own, bf16[128,4096]{1,0:T(8,128)(2,1)} %collective-permute-done.6.a_mate, bf16[128,4096]{1,0:T(8,128)(2,1)S(1)} %get-tuple-element.29.b_own, ...), custom_call_target="tpu_custom_call" | custom-call | tf_op jit(solution)/shard_map/update/pallas_call | solution.py:295
  102.2 6.5 %collective-permute-done.8.a_other = bf16[32,4096]{1,0:T(8,128)(2,1)S(1)} collective-permute-done((bf16[32,4096]{1,0:T(8,128)(2,1)S(1)}, bf16[32,4096]{1,0:T(8,128)(2,1)S(1)}, u32[]{:S(2)}, u32[]{:S(2)}) %collective-permute-start.8) | collective-permute-done | bytes 262176 | tf_op jit(solution)/shard_map/ppermute | solution.py:52
  109.5 3.2 %potential.1 = f32[32,3,128]{2,1,0:T(4,128)S(1)} custom-call(f32[32,4096]{1,0:T(8,128)S(1)} %get-tuple-element.31.a_density, f32[32,4096]{1,0:T(8,128)S(1)} %get-tuple-element.30.b_density, bf16[32,4096]{1,0:T(8,128)(2,1)S(1)} %get-tuple-element.19.a_half, bf16[32,4096]{1,0:T(8,128)(2,1)S(1)} %get-tuple-element.20.b_half, ...), custom_call_target="tpu_custom_call" | custom-call | tf_op jit(solution)/shard_map/potential/pallas_call | solution.py:328
  112.7 9.4 %all_to_all.25 = f32[32,3,128]{2,1,0:T(4,128)S(1)} all-to-all(f32[32,3,128]{2,1,0:T(4,128)S(1)} %potential.1), channel_id=1, replica_groups=mesh['row'=4,'col'=2,'vol'=4] {'row','col','vol'}, dimensions={0} | all-to-all | bytes 98304 | tf_op jit(solution)/shard_map/all_to_all | solution.py:397
  122.1 4.9 %slab_last.1 = (f32[4,8,8,8,128]{4,3,2,1,0:T(8,128)}, f32[4,8,3,128]{3,2,1,0:T(4,128)S(1)}) custom-call(f32[4,8,72,128]{3,2,1,0:T(8,128)S(1)} %bitcast.68, f32[32,4,16,128]{3,2,1,0:T(8,128)S(1)} %copy-done.6, f32[32,4,16,128]{3,2,1,0:T(8,128)S(1)} %copy-done.9, bf16[4,512,128]{2,1,0:T(8,128)(2,1)S(1)} %copy-done.12, bf16[4,128,128]{2,1,0:T(8,128)(2,1)S(1)} %copy-done.23, ...), custom_call_target="tpu_custom_call" | custom-call | tf_op jit(solution)/shard_map/slab_last/pallas_call | solution.py:273
  127.0 9.2 %all_to_all.26.flux_ref = f32[32,3,128]{2,1,0:T(4,128)S(1)} all-to-all(f32[32,3,128]{2,1,0:T(4,128)S(1)} %bitcast.71), channel_id=1, replica_groups=mesh['row'=4,'col'=2,'vol'=4] {'row','col','vol'}, dimensions={0} | all-to-all | bytes 98304 | tf_op jit(solution)/shard_map/all_to_all | solution.py:401
  136.2 2.2 %update.3 = (bf16[32,4096]{1,0:T(8,128)(2,1)S(1)}, bf16[32,4096]{1,0:T(8,128)(2,1)S(1)}) custom-call(f32[32,3,128]{2,1,0:T(4,128)S(1)} %all_to_all.26.flux_ref, bf16[128,4096]{1,0:T(8,128)(2,1)S(1)} %get-tuple-element.28.a_own, bf16[128,4096]{1,0:T(8,128)(2,1)} %collective-permute-done.6.a_mate, bf16[128,4096]{1,0:T(8,128)(2,1)S(1)} %get-tuple-element.29.b_own, ...), custom_call_target="tpu_custom_call" | custom-call | tf_op jit(solution)/shard_map/update/pallas_call | solution.py:295
  139.2 2.6 %all-to-all-start.4 = ((f32[32,8,8,128]{3,2,1,0:T(8,128)}), f32[32,8,8,128]{3,2,1,0:T(8,128)S(1)}, u32[]{:S(2)}, u32[]{:S(2)}) async-start(f32[32,8,8,128]{3,2,1,0:T(8,128)} %bitcast.22), calls=%async_computation.4 | async-start | bytes 2097152 | tf_op jit(solution)/shard_map/all_to_all | solution.py:403
  143.6 9.3 %collective-permute-done.10 = bf16[32,4096]{1,0:T(8,128)(2,1)S(1)} collective-permute-done((bf16[32,4096]{1,0:T(8,128)(2,1)S(1)}, bf16[32,4096]{1,0:T(8,128)(2,1)S(1)}, u32[]{:S(2)}, u32[]{:S(2)}) %collective-permute-start.10) | collective-permute-done | bytes 262176 | tf_op jit(solution)/shard_map/ppermute | solution.py:52
  153.1 6.4 %collective-permute-done.12 = bf16[32,4096]{1,0:T(8,128)(2,1)S(1)} collective-permute-done((bf16[32,4096]{1,0:T(8,128)(2,1)S(1)}, bf16[32,4096]{1,0:T(8,128)(2,1)S(1)}, u32[]{:S(2)}, u32[]{:S(2)}) %collective-permute-start.12) | collective-permute-done | bytes 262176 | tf_op jit(solution)/shard_map/ppermute | solution.py:52
  161.2 5.5 %collective-permute-done.11 = bf16[32,4096]{1,0:T(8,128)(2,1)S(1)} collective-permute-done((bf16[32,4096]{1,0:T(8,128)(2,1)S(1)}, bf16[32,4096]{1,0:T(8,128)(2,1)S(1)}, u32[]{:S(2)}, u32[]{:S(2)}) %collective-permute-start.11) | collective-permute-done | bytes 262176 | tf_op jit(solution)/shard_map/ppermute | solution.py:52
  166.7 2.0 %collective-permute-done.13 = bf16[32,4096]{1,0:T(8,128)(2,1)S(1)} collective-permute-done((bf16[32,4096]{1,0:T(8,128)(2,1)S(1)}, bf16[32,4096]{1,0:T(8,128)(2,1)S(1)}, u32[]{:S(2)}, u32[]{:S(2)}) %collective-permute-start.13) | collective-permute-done | bytes 262176 | tf_op jit(solution)/shard_map/ppermute | solution.py:52
  (103 shorter events, 29.9 us)
Async XLA Ops:
  1.4 28.4 %collective-permute-start.2 = (bf16[64,128]{1,0:T(8,128)(2,1)S(1)}, bf16[64,128]{1,0:T(8,128)(2,1)S(1)}, u32[]{:S(2)}, u32[]{:S(2)}) collective-permute-start(bf16[64,128]{1,0:T(8,128)(2,1)S(1)} %get-tuple-element.37), channel_id=1, source_target_pairs={{0,3},{1,2},{2,1},{3,0},{4,7},{5,6},{6,5},{7,4},{8,11},{9,10},{10,... | collective-permute-start | bytes 49160 | tf_op jit(solution)/shard_map/ppermute | solution.py:52
  6.5 23.3 %collective-permute-start.1 = (bf16[64,128]{1,0:T(8,128)(2,1)S(1)}, bf16[64,128]{1,0:T(8,128)(2,1)S(1)}, u32[]{:S(2)}, u32[]{:S(2)}) collective-permute-start(bf16[64,128]{1,0:T(8,128)(2,1)S(1)} %get-tuple-element.37), channel_id=1, source_target_pairs={{0,2},{1,3},{2,0},{3,1},{4,6},{5,7},{6,4},{7,5},{8,10},{9,11},{10,... | collective-permute-start | bytes 49160 | tf_op jit(solution)/shard_map/ppermute | solution.py:52
  6.5 23.3 %collective-permute-start = (bf16[64,128]{1,0:T(8,128)(2,1)S(1)}, bf16[64,128]{1,0:T(8,128)(2,1)S(1)}, u32[]{:S(2)}, u32[]{:S(2)}) collective-permute-start(bf16[64,128]{1,0:T(8,128)(2,1)S(1)} %get-tuple-element.37), channel_id=1, source_target_pairs={{0,1},{1,0},{2,3},{3,2},{4,5},{5,4},{6,7},{7,6},{8,9},{9,8},{10,11... | collective-permute-start | bytes 49160 | tf_op jit(solution)/shard_map/ppermute | solution.py:52
  16.1 60.0 %all-to-all-start = ((f32[32,72,128]{2,1,0:T(8,128)}), f32[32,72,128]{2,1,0:T(8,128)S(1)}, u32[]{:S(2)}, u32[]{:S(2)}) async-start(f32[32,72,128]{2,1,0:T(8,128)} %gather.1), calls=%async_computation | async-start | bytes 2359296 | tf_op jit(solution)/shard_map/all_to_all | solution.py:382
  26.0 44.5 %copy-start.26 = (f32[16]{0:T(128)S(1)}, f32[16]{0:T(128)}, u32[]{:S(2)}) copy-start(f32[16]{0:T(128)} %values_ref.1) | copy-start | bytes 196
  26.0 63.5 %collective-permute-start.7 = (bf16[128,4096]{1,0:T(8,128)(2,1)}, bf16[128,4096]{1,0:T(8,128)(2,1)}, u32[]{:S(2)}, u32[]{:S(2)}) collective-permute-start(bf16[128,4096]{1,0:T(8,128)(2,1)} %get-tuple-element.26), channel_id=1, source_target_pairs={{0,16},{8,24},{16,0},{24,8},{1,17},{9,25},{17,1},{25,9},{2,18},{10... | collective-permute-start | bytes 3145736 | tf_op jit(solution)/shard_map/ppermute | solution.py:52
  27.8 61.7 %collective-permute-start.6 = (bf16[128,4096]{1,0:T(8,128)(2,1)}, bf16[128,4096]{1,0:T(8,128)(2,1)}, u32[]{:S(2)}, u32[]{:S(2)}) collective-permute-start(bf16[128,4096]{1,0:T(8,128)(2,1)} %get-tuple-element.27), channel_id=1, source_target_pairs={{0,8},{8,0},{16,24},{24,16},{1,9},{9,1},{17,25},{25,17},{2,10},{10... | collective-permute-start | bytes 3145736 | tf_op jit(solution)/shard_map/ppermute | solution.py:52
  29.9 31.6 %collective-permute-start.3 = (bf16[1,272,128]{2,1,0:T(8,128)(2,1)S(1)}, bf16[1,272,128]{2,1,0:T(8,128)(2,1)S(1)}, u32[]{:S(2)}, u32[]{:S(2)}) collective-permute-start(bf16[1,272,128]{2,1,0:T(8,128)(2,1)S(1)} %maximum_bitcast_fusion), channel_id=1, source_target_pairs={{0,8},{8,0},{16,24},{24,16},{1,9},{9,1},{17,25},{25,17},{2,10},{10... | collective-permute-start | bytes 208904 | tf_op jit(solution)/shard_map/ppermute | solution.py:52
  61.5 5.3 %collective-permute-start.4 = (bf16[2,272,128]{2,1,0:T(8,128)(2,1)S(1)}, bf16[2,272,128]{2,1,0:T(8,128)(2,1)S(1)}, u32[]{:S(2)}, u32[]{:S(2)}) collective-permute-start(bf16[2,272,128]{2,1,0:T(8,128)(2,1)S(1)} %pad_maximum_fusion.2), channel_id=1, source_target_pairs={{0,16},{8,24},{16,0},{24,8},{1,17},{9,25},{17,1},{25,9},{2,18},{10... | collective-permute-start | bytes 417800 | tf_op jit(solution)/shard_map/ppermute | solution.py:52
  67.5 1.9 %collective-permute-start.5 = (bf16[4,256,128]{2,1,0:T(8,128)(2,1)}, bf16[4,256,128]{2,1,0:T(8,128)(2,1)}, u32[]{:S(2)}, u32[]{:S(2)}) collective-permute-start(bf16[4,256,128]{2,1,0:T(8,128)(2,1)} %slice.8), channel_id=1, source_target_pairs={{0,4},{4,0},{1,5},{5,1},{2,6},{6,2},{3,7},{7,3},{8,12},{12,8},{9,1... | collective-permute-start | bytes 786440 | tf_op jit(solution)/shard_map/ppermute | solution.py:52
  76.1 21.6 %copy-start.22 = (bf16[4,128,128]{2,1,0:T(8,128)(2,1)}, bf16[4,128,128]{2,1,0:T(8,128)(2,1)S(1)}, u32[]{:S(2)}) copy-start(bf16[4,128,128]{2,1,0:T(8,128)(2,1)S(1)} %get-tuple-element.17.lane_ref) | copy-start | bytes 393220
  84.8 12.3 %all-to-all-start.1 = ((f32[32,3,128]{2,1,0:T(4,128)}), f32[32,3,128]{2,1,0:T(4,128)S(1)}, u32[]{:S(2)}, u32[]{:S(2)}) async-start(f32[32,3,128]{2,1,0:T(4,128)} %bitcast.19), calls=%async_computation.1 | async-start | bytes 131072 | tf_op jit(solution)/shard_map/all_to_all | solution.py:393
  100.9 7.9 %collective-permute-start.8 = (bf16[32,4096]{1,0:T(8,128)(2,1)S(1)}, bf16[32,4096]{1,0:T(8,128)(2,1)S(1)}, u32[]{:S(2)}, u32[]{:S(2)}) collective-permute-start(bf16[32,4096]{1,0:T(8,128)(2,1)S(1)} %get-tuple-element.19.a_half), channel_id=1, source_target_pairs={{0,16},{8,24},{16,0},{24,8},{1,17},{9,25},{17,1},{25,9},{2,18},{10... | collective-permute-start | bytes 786440 | tf_op jit(solution)/shard_map/ppermute | solution.py:52
  101.6 7.8 %collective-permute-start.9 = (bf16[32,4096]{1,0:T(8,128)(2,1)S(1)}, bf16[32,4096]{1,0:T(8,128)(2,1)S(1)}, u32[]{:S(2)}, u32[]{:S(2)}) collective-permute-start(bf16[32,4096]{1,0:T(8,128)(2,1)S(1)} %get-tuple-element.20.b_half), channel_id=1, source_target_pairs={{0,8},{8,0},{16,24},{24,16},{1,9},{9,1},{17,25},{25,17},{2,10},{10... | collective-permute-start | bytes 786440 | tf_op jit(solution)/shard_map/ppermute | solution.py:52
  109.4 12.7 %copy-start.14 = (f32[34,4,16,128]{3,2,1,0:T(8,128)S(1)}, f32[34,4,16,128]{3,2,1,0:T(8,128)}, u32[]{:S(2)}) copy-start(f32[34,4,16,128]{3,2,1,0:T(8,128)} %copy-done.13) | copy-start | bytes 3342340
  138.4 14.4 %copy-start.18 = (bf16[32,4096]{1,0:T(8,128)(2,1)S(1)}, bf16[32,4096]{1,0:T(8,128)(2,1)}, u32[]{:S(2)}) copy-start(bf16[32,4096]{1,0:T(8,128)(2,1)} %copy-done.17) | copy-start | bytes 786436
  138.4 14.4 %copy-start.20 = (bf16[32,4096]{1,0:T(8,128)(2,1)S(1)}, bf16[32,4096]{1,0:T(8,128)(2,1)}, u32[]{:S(2)}) copy-start(bf16[32,4096]{1,0:T(8,128)(2,1)} %copy-done.19) | copy-start | bytes 786436
  138.4 21.0 %copy-start.16 = (bf16[32,4096]{1,0:T(8,128)(2,1)S(1)}, bf16[32,4096]{1,0:T(8,128)(2,1)}, u32[]{:S(2)}) copy-start(bf16[32,4096]{1,0:T(8,128)(2,1)} %copy-done.15) | copy-start | bytes 786436
  138.5 14.4 %collective-permute-start.10 = (bf16[32,4096]{1,0:T(8,128)(2,1)S(1)}, bf16[32,4096]{1,0:T(8,128)(2,1)S(1)}, u32[]{:S(2)}, u32[]{:S(2)}) collective-permute-start(bf16[32,4096]{1,0:T(8,128)(2,1)S(1)} %get-tuple-element.23), channel_id=1, source_target_pairs={{0,16},{8,24},{16,0},{24,8},{1,17},{9,25},{17,1},{25,9},{2,18},{10... | collective-permute-start | bytes 786440 | tf_op jit(solution)/shard_map/ppermute | solution.py:52
  139.2 31.1 %all-to-all-start.4 = ((f32[32,8,8,128]{3,2,1,0:T(8,128)}), f32[32,8,8,128]{3,2,1,0:T(8,128)S(1)}, u32[]{:S(2)}, u32[]{:S(2)}) async-start(f32[32,8,8,128]{3,2,1,0:T(8,128)} %bitcast.22), calls=%async_computation.4 | async-start | bytes 2097152 | tf_op jit(solution)/shard_map/all_to_all | solution.py:403
  141.9 26.9 %copy-start.3 = (f32[32,16384]{1,0:T(8,128)S(1)}, f32[32,16384]{1,0:T(8,128)}, u32[]{:S(2)}) copy-start(f32[32,16384]{1,0:T(8,128)} %density_ref.1) | copy-start | bytes 6291460
  141.9 17.6 %collective-permute-start.12 = (bf16[32,4096]{1,0:T(8,128)(2,1)S(1)}, bf16[32,4096]{1,0:T(8,128)(2,1)S(1)}, u32[]{:S(2)}, u32[]{:S(2)}) collective-permute-start(bf16[32,4096]{1,0:T(8,128)(2,1)S(1)} %get-tuple-element.24), channel_id=1, source_target_pairs={{0,8},{8,0},{16,24},{24,16},{1,9},{9,1},{17,25},{25,17},{2,10},{10... | collective-permute-start | bytes 786440 | tf_op jit(solution)/shard_map/ppermute | solution.py:52
  153.0 13.7 %collective-permute-start.11 = (bf16[32,4096]{1,0:T(8,128)(2,1)S(1)}, bf16[32,4096]{1,0:T(8,128)(2,1)S(1)}, u32[]{:S(2)}, u32[]{:S(2)}) collective-permute-start(bf16[32,4096]{1,0:T(8,128)(2,1)S(1)} %multiply_convert_fusion.1), channel_id=1, source_target_pairs={{0,8},{8,0},{16,24},{24,16},{1,9},{9,1},{17,25},{25,17},{2,10},{10... | collective-permute-start | bytes 786440 | tf_op jit(solution)/shard_map/ppermute | solution.py:52
  159.6 9.1 %collective-permute-start.13 = (bf16[32,4096]{1,0:T(8,128)(2,1)S(1)}, bf16[32,4096]{1,0:T(8,128)(2,1)S(1)}, u32[]{:S(2)}, u32[]{:S(2)}) collective-permute-start(bf16[32,4096]{1,0:T(8,128)(2,1)S(1)} %multiply_convert_fusion), channel_id=1, source_target_pairs={{0,16},{8,24},{16,0},{24,8},{1,17},{9,25},{17,1},{25,9},{2,18},{10... | collective-permute-start | bytes 786440 | tf_op jit(solution)/shard_map/ppermute | solution.py:52
  (23 other events, 102.4 us)

commit v4 on v3

--- a/solution.py
+++ b/solution.py
@@ -98,7 +98,6 @@
         ],
         out_specs=pl.BlockSpec((excitations, lines + PART_ROWS, bz), lambda i: (0, 0, 0)),
         scratch_shapes=[pltpu.VMEM((excitations, targets), jnp.float32)],
-        compiler_params=pltpu.CompilerParams(vmem_limit_bytes=VMEM_BYTES),
         name="gather",
     )(density, panel, source)
 
@@ -109,7 +108,7 @@
     height = bx * blocks * by
     targets = spots.shape[-1]
 
-    def body(place_ref, values_ref, kinds_ref, spots_ref, ratio_ref, inverse_ref, hit_ref, lane_ref):
+    def body(place_ref, values_ref, kinds_ref, spots_ref, inverse_ref, hit_ref, lane_ref):
         r0, c0, v0 = place_ref[0], place_ref[1], place_ref[2]
         count = values_ref.shape[0]
         row_ids = lax.broadcasted_iota(jnp.int32, (height, targets), 0)
@@ -128,9 +127,7 @@
             for i in range(count):
                 conduct = jnp.where(kind == float(i), values_ref[i], conduct)
             inverse = 1.0 / (MASS_TERM + 6.0 * conduct)
-            ratio = (conduct * inverse).reshape(bx, by, bz)
             start = pl.multiple_of(c * by, by)
-            ratio_ref[pl.ds(r * bx, bx), v, pl.ds(start, by)] = ratio
             inverse_ref[pl.ds(r * bx, bx), v, pl.ds(start, by)] = inverse.reshape(bx, by, bz)
             return carry
 
@@ -143,13 +140,11 @@
         body,
         out_shape=[
             jax.ShapeDtypeStruct(planes, jnp.float32),
-            jax.ShapeDtypeStruct(planes, jnp.float32),
             jax.ShapeDtypeStruct((rows, height, targets), jnp.bfloat16),
             jax.ShapeDtypeStruct((rows, bz, targets), jnp.bfloat16),
         ],
         in_specs=[smem, smem, vmem, vmem],
-        out_specs=[vmem] * 4,
-        compiler_params=pltpu.CompilerParams(vmem_limit_bytes=VMEM_BYTES),
+        out_specs=[vmem] * 3,
         name="prepare",
     )(place, values, kinds, spots)
 
@@ -163,7 +158,7 @@
     return pieces
 
 
-def slab_call(shape, first, source, ratio, inverse, hit, lane, parts=None, start=None):
+def slab_call(shape, first, source, inverse, hit, lane, parts=None, start=None):
     rows, cols, vols, bx, by, bz = shape
     blocks = cols * vols
     targets = lane.shape[-1]
@@ -175,12 +170,12 @@
 
     lines = bx * by
 
-    def body(source_ref, ratio_ref, inverse_ref, hit_ref, lane_ref, *rest):
+    def body(source_ref, inverse_ref, hit_ref, lane_ref, *rest):
         if first:
-            out_ref, flux_ref, other_ref, scaled_ref = rest
+            out_ref, flux_ref, other_ref, scaled_ref, ratio_ref = rest
             volume_ref = None
         else:
-            parts_ref, start_ref, volume_ref, flux_ref, out_ref, other_ref, scaled_ref = rest
+            parts_ref, start_ref, volume_ref, flux_ref, out_ref, other_ref, scaled_ref, ratio_ref = rest
         sub = lax.broadcasted_iota(jnp.int32, (by, bz), 0)
         lan = lax.broadcasted_iota(jnp.int32, (by, bz), 1)
         for ref in (out_ref, other_ref):
@@ -210,7 +205,9 @@
                 c, v = j // vols, j % vols
                 span = (slice(r * bx, (r + 1) * bx), v, slice(c * by, (c + 1) * by))
                 scaled = source_ref[r, j, 0:lines].reshape(bx, by, bz) + added[:, v, c]
-                scaled = scaled * inverse_ref[span]
+                inverse = inverse_ref[span]
+                scaled = scaled * inverse
+                ratio_ref[span] = (1.0 - MASS_TERM * inverse) * (1.0 / 6.0)
                 scaled_ref[span] = scaled
                 if first:
                     here[1 + r * bx:1 + (r + 1) * bx, v, c * by:(c + 1) * by] = factors[0] * scaled
@@ -265,7 +262,7 @@
                 flux_ref[r ^ mate, :, k, :] = jnp.broadcast_to(value, (blocks, targets))
 
     vmem = pl.BlockSpec(memory_space=pltpu.VMEM)
-    operands = [source, ratio, inverse, hit, lane] + ([] if first else [parts, start])
+    operands = [source, inverse, hit, lane] + ([] if first else [parts, start])
     fluxes = jax.ShapeDtypeStruct((rows, blocks, len(MATES), targets), jnp.float32)
     field = padded if first else (rows, blocks, bx, by, bz)
     field = jax.ShapeDtypeStruct(field, jnp.float32)
@@ -275,8 +272,7 @@
         out_shape=[field, fluxes],
         in_specs=[vmem] * len(operands),
         out_specs=[vmem, vmem],
-        scratch_shapes=scratch + [pltpu.VMEM(planes, jnp.float32)],
-        compiler_params=pltpu.CompilerParams(vmem_limit_bytes=VMEM_BYTES),
+        scratch_shapes=scratch + [pltpu.VMEM(planes, jnp.float32)] * 2,
         name="slab_first" if first else "slab_last",
     )(*operands)
 
@@ -387,8 +383,8 @@
     panels[3] = mated(columns(panel, 2 + (high ^ 1)), "row", 2)
     densities = [columns(density, low), columns(density, 2 + high)]
 
-    ratio, inverse, hit, lane = prepare_call(shape, place, class_values, kinds, spots)
-    volume, flux = slab_call(shape, True, slab, ratio, inverse, hit, lane)
+    inverse, hit, lane = prepare_call(shape, place, class_values, kinds, spots)
+    volume, flux = slab_call(shape, True, slab, inverse, hit, lane)
     flux = flux.reshape(excitations, len(MATES), targets)
     flux = lax.all_to_all(flux, ALL, 0, 0, tiled=True)
     halves = update_call(flux, panels)
@@ -396,7 +392,7 @@
     parts = potential_call(densities, halves, mates, panels)
     parts = lax.all_to_all(parts, ALL, 0, 0, tiled=True)
     parts = parts.reshape(rows, blocks, len(MATES), targets)
-    volume, flux = slab_call(shape, False, slab, ratio, inverse, hit, lane, parts, volume)
+    volume, flux = slab_call(shape, False, slab, inverse, hit, lane, parts, volume)
     flux = flux.reshape(excitations, len(MATES), targets)
     flux = lax.all_to_all(flux, ALL, 0, 0, tiled=True)
     volume = volume.reshape(excitations, bx, by, bz)

time: 172 us -> 171 us (level)
  local copies, waits for them, and re-layouts: 19.5 us -> 7.77 us
  Pallas kernels: 23.6 us -> 32 us
  other arithmetic: 5.08 us -> 8.01 us
  waiting for transfers between devices: 73.7 us -> 71.5 us
    unnamed x61 -> x27, local copies, waits for them, and re-layouts: 14.8 us -> 3.66 us
    pallas_call x2, Pallas kernels: 9.1 us -> 13.1 us  [slab_call(): pl.pallas_call(body, out_shape=[field, fluxes], in_specs=[vmem] * len(ope...]
    pallas_call x1, Pallas kernels: 3.94 us -> 7.34 us  [gather_call(): pl.pallas_call(body, grid=(steps,), out_shape=jax.ShapeDtypeStruct((excit...]
    ppermute x14, waiting for transfers between devices: 66.2 us -> 64 us  [mated(): lax.ppermute(value, axis, [(i, i ^ mate) for i in range(lax.axis_size(axi...]
  transfers between devices with their start and end apart: 17 -> 17, of which waited for: 10 -> 9; matrix products, arithmetic and copies ran while one was open for 5% -> 7% of each run, Pallas kernels for 6% -> 10%
where the time goes in v4:
time: 171 us
  waiting for transfers between devices  71.5 us (42%)
  Pallas kernels  32 us (19%)
  starting transfers between devices  30.6 us (18%)
  blocking collectives  19.9 us (12%)
  other arithmetic  8.01 us (5%)
  local copies, waits for them, and re-layouts  7.77 us (5%)
    ppermute x14, waiting for transfers between devices, mated(): lax.ppermute(value, axis, [(i, i ^ mate) for i in range(lax.axis_size(axi...  64 us
    ppermute x14, starting transfers between devices, mated(): lax.ppermute(value, axis, [(i, i ^ mate) for i in range(lax.axis_size(axi...  16.3 us
    pallas_call x2, Pallas kernels, slab_call(): pl.pallas_call(body, out_shape=[field, fluxes], in_specs=[vmem] * len(ope...  13.1 us
    all_to_all x1, blocking collectives, split_by_excitation(): flux = lax.all_to_all(flux, ALL, 0, 0, tiled=True)  10 us
    all_to_all x1, blocking collectives, split_by_excitation(): parts = lax.all_to_all(parts, ALL, 0, 0, tiled=True)  9.85 us
    all_to_all x1, waiting for transfers between devices, split_by_excitation(): flux = lax.all_to_all(flux, ALL, 0, 0, tiled=True)  7.48 us
    pallas_call x1, Pallas kernels, gather_call(): pl.pallas_call(body, grid=(steps,), out_shape=jax.ShapeDtypeStruct((excit...  7.34 us
    all_to_all x1, starting transfers between devices, split_by_excitation(): slab = lax.all_to_all(slab, ALL, 0, 0, tiled=True)  6.11 us
  transfers between devices with their start and end apart: 17, of which 9 were waited for; matrix products, arithmetic and copies ran while one was open for 7% of the time, Pallas kernels for 10%

profile of v4, /device:TPU:0, one launch (start us, length us, event | category | flops | bytes accessed | tf_op | source)
XLA Modules:
  0.0 170.6 jit_solution(1177703871477297156)
XLA Ops:
  1.4 5.1 %collective-permute-start.2 = (bf16[64,128]{1,0:T(8,128)(2,1)S(1)}, bf16[64,128]{1,0:T(8,128)(2,1)S(1)}, u32[]{:S(2)}, u32[]{:S(2)}) collective-permute-start(bf16[64,128]{1,0:T(8,128)(2,1)S(1)} %get-tuple-element.35), channel_id=1, source_target_pairs={{0,3},{1,2},{2,1},{3,0},{4,7},{5,6},{6,5},{7,4},{8,11},{9,10},{10,... | collective-permute-start | bytes 49160 | tf_op jit(solution)/shard_map/ppermute | solution.py:52
  7.1 7.3 %gather.1 = f32[32,72,128]{2,1,0:T(8,128)} custom-call(f32[32,16384]{1,0:T(8,128)} %density_ref.1, bf16[128,16384]{1,0:T(8,128)(2,1)} %panel_ref.1, f32[32,64,128]{2,1,0:T(8,128)} %bitcast.69), custom_call_target="tpu_custom_call" | custom-call | tf_op jit(solution)/shard_map/gather/pallas_call | solution.py:90
  14.5 6.1 %all-to-all-start = ((f32[32,72,128]{2,1,0:T(8,128)}), f32[32,72,128]{2,1,0:T(8,128)}, u32[]{:S(2)}, u32[]{:S(2)}) async-start(f32[32,72,128]{2,1,0:T(8,128)} %gather.1), calls=%async_computation | async-start | bytes 2359296 | tf_op jit(solution)/shard_map/all_to_all | solution.py:378
  20.6 4.0 %constant_dynamic-slice_fusion.2 = (bf16[128,4096]{1,0:T(8,128)(2,1)}, bf16[128,4096]{1,0:T(8,128)(2,1)}, bf16[128,4096]{1,0:T(8,128)(2,1)S(1)}, bf16[128,4096]{1,0:T(8,128)(2,1)S(1)}) fusion(bf16[128,16384]{1,0:T(8,128)(2,1)} %panel_ref.1, s32[]{:T(128)S(6)} %select_n.170, s32[]{:T(128)S(6)} %select_n.168, s32[]{:T(128)S(6)} %select_n.167, s32[]{:T(128)S(6)} %select_n.169), kind=kLoop, calls=%fused_computation.56 | loop fusion | bytes 8388624 | tf_op jit(solution)/shard_map/dynamic_slice | solution.py:364
  29.0 30.9 %collective-permute-done.3 = bf16[1,272,128]{2,1,0:T(8,128)(2,1)S(1)} collective-permute-done((bf16[1,272,128]{2,1,0:T(8,128)(2,1)S(1)}, bf16[1,272,128]{2,1,0:T(8,128)(2,1)S(1)}, u32[]{:S(2)}, u32[]{:S(2)}) %collective-permute-start.3) | collective-permute-done | bytes 69664 | tf_op jit(solution)/shard_map/ppermute | solution.py:52
  61.4 3.7 %collective-permute-done.4 = bf16[2,272,128]{2,1,0:T(8,128)(2,1)S(1)} collective-permute-done((bf16[2,272,128]{2,1,0:T(8,128)(2,1)S(1)}, bf16[2,272,128]{2,1,0:T(8,128)(2,1)S(1)}, u32[]{:S(2)}, u32[]{:S(2)}) %collective-permute-start.4) | collective-permute-done | bytes 139296 | tf_op jit(solution)/shard_map/ppermute | solution.py:52
  67.7 1.8 %pad_maximum_fusion.kinds_ref = bf16[2,4,4,64,128]{4,3,2,1,0:T(8,128)(2,1)} fusion(bf16[1,4,4,64,128]{4,3,2,1,0:T(8,128)(2,1)} %bitcast.18, bf16[1,4,4,64,128]{4,3,2,1,0:T(8,128)(2,1)S(1)} %bitcast.68), kind=kLoop, calls=%fused_computation.1 | loop fusion | flops 262144 | bytes 1048576 | tf_op jit(solution)/shard_map/stack | solution.py:57
  69.6 4.4 %prepare.1 = (f32[32,4,16,128]{3,2,1,0:T(8,128)}, bf16[4,512,128]{2,1,0:T(8,128)(2,1)}, bf16[4,128,128]{2,1,0:T(8,128)(2,1)}) custom-call(s32[3]{0:T(128)} %pad_add_fusion.place_ref, f32[16]{0:T(128)} %values_ref.1, bf16[2,4,4,64,128]{4,3,2,1,0:T(8,128)(2,1)} %pad_maximum_fusion.kinds_ref, bf16[4,16,128]{2,1,0:T(8,128)(2,1)} %pad_maximum_fusion.4.spots_ref), custom_call_target="tpu_custom_call" | custom-call | tf_op jit(solution)/shard_map/prepare/pallas_call | solution.py:139
  73.9 5.9 %slab_first.1 = (f32[34,4,16,128]{3,2,1,0:T(8,128)}, f32[4,8,3,128]{3,2,1,0:T(4,128)}) custom-call(f32[4,8,72,128]{3,2,1,0:T(8,128)} %bitcast.1.source_ref, f32[32,4,16,128]{3,2,1,0:T(8,128)} %get-tuple-element.13.inverse_ref, bf16[4,512,128]{2,1,0:T(8,128)(2,1)} %get-tuple-element.14.hit_ref, bf16[4,128,128]{2,1,0:T(8,128)(2,1)} %get-tuple-element.15.lane_ref), custom_call_target="tpu_custom_call" | custom-call | tf_op jit(solution)/shard_map/slab_first/pallas_call | solution.py:270
  79.9 4.9 %all-to-all-start.1 = ((f32[32,3,128]{2,1,0:T(4,128)}), f32[32,3,128]{2,1,0:T(4,128)S(1)}, u32[]{:S(2)}, u32[]{:S(2)}) async-start(f32[32,3,128]{2,1,0:T(4,128)} %bitcast.72), calls=%async_computation.1 | async-start | bytes 131072 | tf_op jit(solution)/shard_map/all_to_all | solution.py:389
  84.8 7.5 %all-to-all-done.1.flux_ref = f32[32,3,128]{2,1,0:T(4,128)S(1)} async-done(((f32[32,3,128]{2,1,0:T(4,128)}), f32[32,3,128]{2,1,0:T(4,128)S(1)}, u32[]{:S(2)}, u32[]{:S(2)}) %all-to-all-start.1) | async-done | bytes 49184 | tf_op jit(solution)/shard_map/all_to_all | solution.py:389
  92.2 2.0 %update.2 = (bf16[32,4096]{1,0:T(8,128)(2,1)S(1)}, bf16[32,4096]{1,0:T(8,128)(2,1)S(1)}) custom-call(f32[32,3,128]{2,1,0:T(4,128)S(1)} %all-to-all-done.1.flux_ref, bf16[128,4096]{1,0:T(8,128)(2,1)S(1)} %get-tuple-element.26.a_own, bf16[128,4096]{1,0:T(8,128)(2,1)} %collective-permute-done.6.a_mate, bf16[128,4096]{1,0:T(8,128)(2,1)S(1)} %get-tuple-element.27.b_own, ...), custom_call_target="tpu_custom_call" | custom-call | tf_op jit(solution)/shard_map/update/pallas_call | solution.py:291
  95.6 6.5 %collective-permute-done.8.a_other = bf16[32,4096]{1,0:T(8,128)(2,1)S(1)} collective-permute-done((bf16[32,4096]{1,0:T(8,128)(2,1)S(1)}, bf16[32,4096]{1,0:T(8,128)(2,1)S(1)}, u32[]{:S(2)}, u32[]{:S(2)}) %collective-permute-start.8) | collective-permute-done | bytes 262176 | tf_op jit(solution)/shard_map/ppermute | solution.py:52
  102.8 2.8 %potential.1 = f32[32,3,128]{2,1,0:T(4,128)S(1)} custom-call(f32[32,4096]{1,0:T(8,128)S(1)} %get-tuple-element.29.a_density, f32[32,4096]{1,0:T(8,128)S(1)} %get-tuple-element.28.b_density, bf16[32,4096]{1,0:T(8,128)(2,1)S(1)} %get-tuple-element.17.a_half, bf16[32,4096]{1,0:T(8,128)(2,1)S(1)} %get-tuple-element.18.b_half, ...), custom_call_target="tpu_custom_call" | custom-call | tf_op jit(solution)/shard_map/potential/pallas_call | solution.py:324
  105.7 9.9 %all_to_all.25 = f32[32,3,128]{2,1,0:T(4,128)} all-to-all(f32[32,3,128]{2,1,0:T(4,128)S(1)} %potential.1), channel_id=1, replica_groups=mesh['row'=4,'col'=2,'vol'=4] {'row','col','vol'}, dimensions={0} | all-to-all | bytes 98304 | tf_op jit(solution)/shard_map/all_to_all | solution.py:393
  115.6 7.2 %slab_last.1 = (f32[4,8,8,8,128]{4,3,2,1,0:T(8,128)}, f32[4,8,3,128]{3,2,1,0:T(4,128)}) custom-call(f32[4,8,72,128]{3,2,1,0:T(8,128)} %bitcast.1.source_ref, f32[32,4,16,128]{3,2,1,0:T(8,128)} %get-tuple-element.13.inverse_ref, bf16[4,512,128]{2,1,0:T(8,128)(2,1)} %get-tuple-element.14.hit_ref, bf16[4,128,128]{2,1,0:T(8,128)(2,1)} %get-tuple-element.15.lane_ref, ...), custom_call_target="tpu_custom_call" | custom-call | tf_op jit(solution)/shard_map/slab_last/pallas_call | solution.py:270
  122.7 10.0 %all_to_all.26.flux_ref = f32[32,3,128]{2,1,0:T(4,128)S(1)} all-to-all(f32[32,3,128]{2,1,0:T(4,128)} %bitcast.73), channel_id=1, replica_groups=mesh['row'=4,'col'=2,'vol'=4] {'row','col','vol'}, dimensions={0} | all-to-all | bytes 98304 | tf_op jit(solution)/shard_map/all_to_all | solution.py:397
  132.8 2.3 %update.3 = (bf16[32,4096]{1,0:T(8,128)(2,1)}, bf16[32,4096]{1,0:T(8,128)(2,1)S(1)}) custom-call(f32[32,3,128]{2,1,0:T(4,128)S(1)} %all_to_all.26.flux_ref, bf16[128,4096]{1,0:T(8,128)(2,1)S(1)} %get-tuple-element.26.a_own, bf16[128,4096]{1,0:T(8,128)(2,1)} %collective-permute-done.6.a_mate, bf16[128,4096]{1,0:T(8,128)(2,1)S(1)} %get-tuple-element.27.b_own, ...), custom_call_target="tpu_custom_call" | custom-call | tf_op jit(solution)/shard_map/update/pallas_call | solution.py:291
  136.5 3.4 %all-to-all-start.4 = ((f32[32,8,8,128]{3,2,1,0:T(8,128)}), f32[32,8,8,128]{3,2,1,0:T(8,128)}, u32[]{:S(2)}, u32[]{:S(2)}) async-start(f32[32,8,8,128]{3,2,1,0:T(8,128)} %bitcast.67), calls=%async_computation.4 | async-start | bytes 2097152 | tf_op jit(solution)/shard_map/all_to_all | solution.py:399
  141.6 7.4 %collective-permute-done.10 = bf16[32,4096]{1,0:T(8,128)(2,1)} collective-permute-done((bf16[32,4096]{1,0:T(8,128)(2,1)}, bf16[32,4096]{1,0:T(8,128)(2,1)}, u32[]{:S(2)}, u32[]{:S(2)}) %collective-permute-start.10) | collective-permute-done | bytes 262176 | tf_op jit(solution)/shard_map/ppermute | solution.py:52
  150.2 7.2 %collective-permute-done.12 = bf16[32,4096]{1,0:T(8,128)(2,1)S(1)} collective-permute-done((bf16[32,4096]{1,0:T(8,128)(2,1)S(1)}, bf16[32,4096]{1,0:T(8,128)(2,1)S(1)}, u32[]{:S(2)}, u32[]{:S(2)}) %collective-permute-start.12) | collective-permute-done | bytes 262176 | tf_op jit(solution)/shard_map/ppermute | solution.py:52
  159.2 5.5 %collective-permute-done.11 = bf16[32,4096]{1,0:T(8,128)(2,1)S(1)} collective-permute-done((bf16[32,4096]{1,0:T(8,128)(2,1)S(1)}, bf16[32,4096]{1,0:T(8,128)(2,1)S(1)}, u32[]{:S(2)}, u32[]{:S(2)}) %collective-permute-start.11) | collective-permute-done | bytes 262176 | tf_op jit(solution)/shard_map/ppermute | solution.py:52
  164.7 2.1 %collective-permute-done.13 = bf16[32,4096]{1,0:T(8,128)(2,1)S(1)} collective-permute-done((bf16[32,4096]{1,0:T(8,128)(2,1)S(1)}, bf16[32,4096]{1,0:T(8,128)(2,1)S(1)}, u32[]{:S(2)}, u32[]{:S(2)}) %collective-permute-start.13) | collective-permute-done | bytes 262176 | tf_op jit(solution)/shard_map/ppermute | solution.py:52
  168.3 2.3 %copy.10 = f32[32,8,8,128]{3,2,1,0:T(8,128)} copy(f32[32,8,8,128]{3,2,1,0:T(8,128)} %all-to-all-done.4) | data formatting | bytes 2097152
  (69 shorter events, 19.5 us)
Async XLA Ops:
  1.4 27.0 %collective-permute-start.2 = (bf16[64,128]{1,0:T(8,128)(2,1)S(1)}, bf16[64,128]{1,0:T(8,128)(2,1)S(1)}, u32[]{:S(2)}, u32[]{:S(2)}) collective-permute-start(bf16[64,128]{1,0:T(8,128)(2,1)S(1)} %get-tuple-element.35), channel_id=1, source_target_pairs={{0,3},{1,2},{2,1},{3,0},{4,7},{5,6},{6,5},{7,4},{8,11},{9,10},{10,... | collective-permute-start | bytes 49160 | tf_op jit(solution)/shard_map/ppermute | solution.py:52
  6.5 21.9 %collective-permute-start.1 = (bf16[64,128]{1,0:T(8,128)(2,1)S(1)}, bf16[64,128]{1,0:T(8,128)(2,1)S(1)}, u32[]{:S(2)}, u32[]{:S(2)}) collective-permute-start(bf16[64,128]{1,0:T(8,128)(2,1)S(1)} %get-tuple-element.35), channel_id=1, source_target_pairs={{0,2},{1,3},{2,0},{3,1},{4,6},{5,7},{6,4},{7,5},{8,10},{9,11},{10,... | collective-permute-start | bytes 49160 | tf_op jit(solution)/shard_map/ppermute | solution.py:52
  6.5 21.9 %collective-permute-start = (bf16[64,128]{1,0:T(8,128)(2,1)S(1)}, bf16[64,128]{1,0:T(8,128)(2,1)S(1)}, u32[]{:S(2)}, u32[]{:S(2)}) collective-permute-start(bf16[64,128]{1,0:T(8,128)(2,1)S(1)} %get-tuple-element.35), channel_id=1, source_target_pairs={{0,1},{1,0},{2,3},{3,2},{4,5},{5,4},{6,7},{7,6},{8,9},{9,8},{10,11... | collective-permute-start | bytes 49160 | tf_op jit(solution)/shard_map/ppermute | solution.py:52
  14.5 59.5 %all-to-all-start = ((f32[32,72,128]{2,1,0:T(8,128)}), f32[32,72,128]{2,1,0:T(8,128)}, u32[]{:S(2)}, u32[]{:S(2)}) async-start(f32[32,72,128]{2,1,0:T(8,128)} %gather.1), calls=%async_computation | async-start | bytes 2359296 | tf_op jit(solution)/shard_map/all_to_all | solution.py:378
  20.6 7.2 %copy-start.12 = (s32[1,8]{1,0:T(1,128)S(1)}, s32[1,8]{1,0:T(1,128)}, u32[]{:S(2)}) copy-start(s32[1,8]{1,0:T(1,128)} %param.12) | copy-start | bytes 100
  20.6 7.4 %copy-start.11 = (s32[1,8,64]{2,1,0:T(8,128)S(1)}, s32[1,8,64]{2,1,0:T(8,128)}, u32[]{:S(2)}) copy-start(s32[1,8,64]{2,1,0:T(8,128)} %param.13) | copy-start | bytes 6148
  24.6 60.1 %collective-permute-start.7 = (bf16[128,4096]{1,0:T(8,128)(2,1)}, bf16[128,4096]{1,0:T(8,128)(2,1)S(1)}, u32[]{:S(2)}, u32[]{:S(2)}) collective-permute-start(bf16[128,4096]{1,0:T(8,128)(2,1)} %get-tuple-element.24), channel_id=1, source_target_pairs={{0,16},{8,24},{16,0},{24,8},{1,17},{9,25},{17,1},{25,9},{2,18},{10... | collective-permute-start | bytes 3145736 | tf_op jit(solution)/shard_map/ppermute | solution.py:52
  26.3 58.4 %collective-permute-start.6 = (bf16[128,4096]{1,0:T(8,128)(2,1)}, bf16[128,4096]{1,0:T(8,128)(2,1)}, u32[]{:S(2)}, u32[]{:S(2)}) collective-permute-start(bf16[128,4096]{1,0:T(8,128)(2,1)} %get-tuple-element.25), channel_id=1, source_target_pairs={{0,8},{8,0},{16,24},{24,16},{1,9},{9,1},{17,25},{25,17},{2,10},{10... | collective-permute-start | bytes 3145736 | tf_op jit(solution)/shard_map/ppermute | solution.py:52
  28.4 31.5 %collective-permute-start.3 = (bf16[1,272,128]{2,1,0:T(8,128)(2,1)S(1)}, bf16[1,272,128]{2,1,0:T(8,128)(2,1)S(1)}, u32[]{:S(2)}, u32[]{:S(2)}) collective-permute-start(bf16[1,272,128]{2,1,0:T(8,128)(2,1)S(1)} %maximum_bitcast_fusion), channel_id=1, source_target_pairs={{0,8},{8,0},{16,24},{24,16},{1,9},{9,1},{17,25},{25,17},{2,10},{10... | collective-permute-start | bytes 208904 | tf_op jit(solution)/shard_map/ppermute | solution.py:52
  59.9 5.2 %collective-permute-start.4 = (bf16[2,272,128]{2,1,0:T(8,128)(2,1)S(1)}, bf16[2,272,128]{2,1,0:T(8,128)(2,1)S(1)}, u32[]{:S(2)}, u32[]{:S(2)}) collective-permute-start(bf16[2,272,128]{2,1,0:T(8,128)(2,1)S(1)} %pad_maximum_fusion.2), channel_id=1, source_target_pairs={{0,16},{8,24},{16,0},{24,8},{1,17},{9,25},{17,1},{25,9},{2,18},{10... | collective-permute-start | bytes 417800 | tf_op jit(solution)/shard_map/ppermute | solution.py:52
  65.8 1.9 %collective-permute-start.5 = (bf16[4,256,128]{2,1,0:T(8,128)(2,1)S(1)}, bf16[4,256,128]{2,1,0:T(8,128)(2,1)}, u32[]{:S(2)}, u32[]{:S(2)}) collective-permute-start(bf16[4,256,128]{2,1,0:T(8,128)(2,1)S(1)} %slice.8), channel_id=1, source_target_pairs={{0,4},{4,0},{1,5},{5,1},{2,6},{6,2},{3,7},{7,3},{8,12},{12,8},{9,1... | collective-permute-start | bytes 786440 | tf_op jit(solution)/shard_map/ppermute | solution.py:52
  79.9 12.4 %all-to-all-start.1 = ((f32[32,3,128]{2,1,0:T(4,128)}), f32[32,3,128]{2,1,0:T(4,128)S(1)}, u32[]{:S(2)}, u32[]{:S(2)}) async-start(f32[32,3,128]{2,1,0:T(4,128)} %bitcast.72), calls=%async_computation.1 | async-start | bytes 131072 | tf_op jit(solution)/shard_map/all_to_all | solution.py:389
  94.3 11.4 %copy-start.2 = (bf16[32,4096]{1,0:T(8,128)(2,1)}, bf16[32,4096]{1,0:T(8,128)(2,1)S(1)}, u32[]{:S(2)}) copy-start(bf16[32,4096]{1,0:T(8,128)(2,1)S(1)} %get-tuple-element.17.a_half) | copy-start | bytes 786436
  94.3 7.9 %collective-permute-start.8 = (bf16[32,4096]{1,0:T(8,128)(2,1)S(1)}, bf16[32,4096]{1,0:T(8,128)(2,1)S(1)}, u32[]{:S(2)}, u32[]{:S(2)}) collective-permute-start(bf16[32,4096]{1,0:T(8,128)(2,1)S(1)} %get-tuple-element.17.a_half), channel_id=1, source_target_pairs={{0,16},{8,24},{16,0},{24,8},{1,17},{9,25},{17,1},{25,9},{2,18},{10... | collective-permute-start | bytes 786440 | tf_op jit(solution)/shard_map/ppermute | solution.py:52
  95.0 7.8 %collective-permute-start.9 = (bf16[32,4096]{1,0:T(8,128)(2,1)S(1)}, bf16[32,4096]{1,0:T(8,128)(2,1)S(1)}, u32[]{:S(2)}, u32[]{:S(2)}) collective-permute-start(bf16[32,4096]{1,0:T(8,128)(2,1)S(1)} %get-tuple-element.18.b_half), channel_id=1, source_target_pairs={{0,8},{8,0},{16,24},{24,16},{1,9},{9,1},{17,25},{25,17},{2,10},{10... | collective-permute-start | bytes 786440 | tf_op jit(solution)/shard_map/ppermute | solution.py:52
  135.8 13.1 %copy-start.3 = (bf16[32,4096]{1,0:T(8,128)(2,1)S(1)}, bf16[32,4096]{1,0:T(8,128)(2,1)}, u32[]{:S(2)}) copy-start(bf16[32,4096]{1,0:T(8,128)(2,1)} %copy-done.2) | copy-start | bytes 786436
  135.8 13.1 %copy-start.5 = (bf16[32,4096]{1,0:T(8,128)(2,1)S(1)}, bf16[32,4096]{1,0:T(8,128)(2,1)}, u32[]{:S(2)}) copy-start(bf16[32,4096]{1,0:T(8,128)(2,1)} %copy-done.4) | copy-start | bytes 786436
  135.8 21.6 %copy-start.1 = (bf16[32,4096]{1,0:T(8,128)(2,1)S(1)}, bf16[32,4096]{1,0:T(8,128)(2,1)}, u32[]{:S(2)}) copy-start(bf16[32,4096]{1,0:T(8,128)(2,1)} %copy-done) | copy-start | bytes 786436
  135.8 13.1 %collective-permute-start.10 = (bf16[32,4096]{1,0:T(8,128)(2,1)}, bf16[32,4096]{1,0:T(8,128)(2,1)}, u32[]{:S(2)}, u32[]{:S(2)}) collective-permute-start(bf16[32,4096]{1,0:T(8,128)(2,1)} %get-tuple-element.21), channel_id=1, source_target_pairs={{0,16},{8,24},{16,0},{24,8},{1,17},{9,25},{17,1},{25,9},{2,18},{10... | collective-permute-start | bytes 786440 | tf_op jit(solution)/shard_map/ppermute | solution.py:52
  136.5 31.8 %all-to-all-start.4 = ((f32[32,8,8,128]{3,2,1,0:T(8,128)}), f32[32,8,8,128]{3,2,1,0:T(8,128)}, u32[]{:S(2)}, u32[]{:S(2)}) async-start(f32[32,8,8,128]{3,2,1,0:T(8,128)} %bitcast.67), calls=%async_computation.4 | async-start | bytes 2097152 | tf_op jit(solution)/shard_map/all_to_all | solution.py:399
  139.9 26.9 %copy-start.9 = (f32[32,16384]{1,0:T(8,128)S(1)}, f32[32,16384]{1,0:T(8,128)}, u32[]{:S(2)}) copy-start(f32[32,16384]{1,0:T(8,128)} %density_ref.1) | copy-start | bytes 6291460
  139.9 17.5 %collective-permute-start.12 = (bf16[32,4096]{1,0:T(8,128)(2,1)S(1)}, bf16[32,4096]{1,0:T(8,128)(2,1)S(1)}, u32[]{:S(2)}, u32[]{:S(2)}) collective-permute-start(bf16[32,4096]{1,0:T(8,128)(2,1)S(1)} %copy-done.7), channel_id=1, source_target_pairs={{0,8},{8,0},{16,24},{24,16},{1,9},{9,1},{17,25},{25,17},{2,10},{10... | collective-permute-start | bytes 786440 | tf_op jit(solution)/shard_map/ppermute | solution.py:52
  150.1 14.5 %collective-permute-start.11 = (bf16[32,4096]{1,0:T(8,128)(2,1)S(1)}, bf16[32,4096]{1,0:T(8,128)(2,1)S(1)}, u32[]{:S(2)}, u32[]{:S(2)}) collective-permute-start(bf16[32,4096]{1,0:T(8,128)(2,1)S(1)} %multiply_convert_fusion.1), channel_id=1, source_target_pairs={{0,8},{8,0},{16,24},{24,16},{1,9},{9,1},{17,25},{25,17},{2,10},{10... | collective-permute-start | bytes 786440 | tf_op jit(solution)/shard_map/ppermute | solution.py:52
  157.6 9.1 %collective-permute-start.13 = (bf16[32,4096]{1,0:T(8,128)(2,1)S(1)}, bf16[32,4096]{1,0:T(8,128)(2,1)S(1)}, u32[]{:S(2)}, u32[]{:S(2)}) collective-permute-start(bf16[32,4096]{1,0:T(8,128)(2,1)S(1)} %multiply_convert_fusion), channel_id=1, source_target_pairs={{0,16},{8,24},{16,0},{24,8},{1,17},{9,25},{17,1},{25,9},{2,18},{10... | collective-permute-start | bytes 786440 | tf_op jit(solution)/shard_map/ppermute | solution.py:52
  (6 other events, 15.2 us)

commit v5 on v4

--- a/solution.py
+++ b/solution.py
@@ -18,9 +18,7 @@
 SPECTRUM_HIGH = 2.0
 
 ALL = ("row", "col", "vol")
-GROUP = 8
 SPOT_ROWS = 16
-PART_ROWS = 8
 VMEM_BYTES = 16 * 2 ** 20
 
 
@@ -52,101 +50,115 @@
     return lax.ppermute(value, axis, [(i, i ^ mate) for i in range(lax.axis_size(axis))])
 
 
-def stacked(value, axis):
-    size = lax.axis_size(axis)
-    return jnp.stack([value] + [mated(value, axis, k) for k in range(1, size)])
-
-
-def gather_call(density, panel, source):
-    excitations, lines, bz = source.shape
-    targets, nodes = panel.shape
-    steps = math.gcd(excitations, 8)
-    width, few = nodes // steps, excitations // steps
-
-    def body(density_ref, panel_ref, source_ref, out_ref, part_ref):
-        index = pl.program_id(0)
-        part = lax.dot_general(
-            density_ref[...].astype(jnp.bfloat16), panel_ref[...], (((1,), (1,)), ((), ())),
-            preferred_element_type=jnp.float32,
-        )
-
-        @pl.when(index == 0)
-        def _():
-            part_ref[...] = part
-
-        @pl.when(index > 0)
-        def _():
-            part_ref[...] += part
-
-        out_ref[pl.ds(index * few, few), 0:lines] = source_ref[...]
-
-        @pl.when(index == steps - 1)
-        def _():
-            for i in range(excitations):
-                out_ref[i, lines:lines + PART_ROWS] = jnp.broadcast_to(
-                    part_ref[i:i + 1], (PART_ROWS, targets)
-                )
-
+def start_call(density, panel, shape):
+    rows, cols, vols = shape[:3]
+    excitations, nodes = density.shape
+    targets = panel.shape[0]
+    width = nodes // rows
+
+    def body(density_ref, panel_ref, part_ref, *rest):
+        quarters = rest[:rows]
+        nodes_ref, panel_buf, total_ref, sems = rest[rows:]
+        r0, c0, v0 = (lax.axis_index(a) for a in ALL)
+        low, high = r0 & 1, r0 >> 1
+        loads = []
+        for q in range(rows):
+            span = pl.ds(q * width, width)
+            loads.append((
+                pltpu.make_async_copy(panel_ref.at[:, span], panel_buf.at[q], sems.at[q]),
+                pltpu.make_async_copy(density_ref.at[:, span], nodes_ref.at[q], sems.at[rows + q]),
+            ))
+        for pair in loads:
+            for copy in pair:
+                copy.start()
+        total = jnp.zeros((targets, excitations), jnp.float32)
+        for q in range(rows):
+            for copy in loads[q]:
+                copy.wait()
+            total += lax.dot_general(
+                panel_buf[q], nodes_ref[q].astype(jnp.bfloat16), (((1,), (1,)), ((), ())),
+                preferred_element_type=jnp.float32,
+            )
+        sources = (low, low ^ 1, 2 + high, 2 + (high ^ 1))
+        stores = [
+            pltpu.make_async_copy(panel_buf.at[source], quarter, sems.at[q])
+            for q, (source, quarter) in enumerate(zip(sources, quarters))
+        ]
+        for copy in stores:
+            copy.start()
+        total_ref[...] = total.T
+        for kc in range(cols):
+            for kr in range(rows):
+                for kv in range(vols):
+                    owner = ((r0 ^ kr) * cols + (c0 ^ kc)) * vols + (v0 ^ kv)
+                    part_ref[kc, kr, kv:kv + 1] = total_ref[pl.ds(owner, 1)]
+        for copy in stores:
+            copy.wait()
+
+    hbm = pl.BlockSpec(memory_space=pltpu.HBM)
     return pl.pallas_call(
         body,
-        grid=(steps,),
-        out_shape=jax.ShapeDtypeStruct((excitations, lines + PART_ROWS, bz), jnp.float32),
-        in_specs=[
-            pl.BlockSpec((excitations, width), lambda i: (0, i)),
-            pl.BlockSpec((targets, width), lambda i: (0, i)),
-            pl.BlockSpec((few, lines, bz), lambda i: (i, 0, 0)),
+        out_shape=[jax.ShapeDtypeStruct((cols, rows, vols, targets), jnp.float32)]
+        + [jax.ShapeDtypeStruct((targets, width), panel.dtype)] * rows,
+        in_specs=[hbm, hbm],
+        out_specs=[pl.BlockSpec(memory_space=pltpu.VMEM)] + [hbm] * rows,
+        scratch_shapes=[
+            pltpu.VMEM((rows, excitations, width), jnp.float32),
+            pltpu.VMEM((rows, targets, width), panel.dtype),
+            pltpu.VMEM((excitations, targets), jnp.float32),
+            pltpu.SemaphoreType.DMA((2 * rows,)),
         ],
-        out_specs=pl.BlockSpec((excitations, lines + PART_ROWS, bz), lambda i: (0, 0, 0)),
-        scratch_shapes=[pltpu.VMEM((excitations, targets), jnp.float32)],
-        name="gather",
-    )(density, panel, source)
-
-
-def prepare_call(shape, place, values, kinds, spots):
+        name="start",
+    )(density, panel)
+
+
+def prepare_call(shape, values, known, other):
     rows, cols, vols, bx, by, bz = shape
     blocks = cols * vols
     height = bx * blocks * by
-    targets = spots.shape[-1]
-
-    def body(place_ref, values_ref, kinds_ref, spots_ref, inverse_ref, hit_ref, lane_ref):
-        r0, c0, v0 = place_ref[0], place_ref[1], place_ref[2]
+    lines = bx * by
+    targets = known[0].shape[-1]
+
+    def body(values_ref, *refs):
+        known_refs, other_refs = refs[:rows], refs[rows:2 * rows]
+        inverse_ref, hit_ref, lane_ref = refs[2 * rows:]
+        r0, c0, v0 = (lax.axis_index(a) for a in ALL)
         count = values_ref.shape[0]
         row_ids = lax.broadcasted_iota(jnp.int32, (height, targets), 0)
         lane_ids = lax.broadcasted_iota(jnp.int32, (bz, targets), 0)
-        for r in range(rows):
-            spot = spots_ref[r ^ r0].astype(jnp.float32).astype(jnp.int32)
+        for k in range(rows):
+            spot = known_refs[k][vols * lines:].astype(jnp.float32).astype(jnp.int32)
             line = spot[0:1] * (blocks * by) + spot[1:2]
-            hit_ref[r] = (row_ids == line).astype(jnp.bfloat16)
-            lane_ref[r] = (lane_ids == spot[2:3]).astype(jnp.bfloat16)
-
-        def block(index, carry):
-            r, rest = index // blocks, index % blocks
-            c, v = rest // vols, rest % vols
-            kind = kinds_ref[c ^ c0, r ^ r0, v ^ v0].astype(jnp.float32)
-            conduct = jnp.zeros((bx * by, bz), jnp.float32)
-            for i in range(count):
-                conduct = jnp.where(kind == float(i), values_ref[i], conduct)
-            inverse = 1.0 / (MASS_TERM + 6.0 * conduct)
-            start = pl.multiple_of(c * by, by)
-            inverse_ref[pl.ds(r * bx, bx), v, pl.ds(start, by)] = inverse.reshape(bx, by, bz)
-            return carry
-
-        lax.fori_loop(0, rows * blocks, block, 0)
-
-    planes = (rows * bx, vols, cols * by, bz)
+            hit_ref[k ^ r0] = (row_ids == line).astype(jnp.bfloat16)
+            lane_ref[k ^ r0] = (lane_ids == spot[2:3]).astype(jnp.bfloat16)
+        for k in range(rows):
+            for kc, refs_of in enumerate((known_refs, other_refs)):
+                start = pl.multiple_of((kc ^ c0) * by, by)
+
+                def plane(kv, carry, source=refs_of[k], start=start, k=k):
+                    kind = source[pl.ds(pl.multiple_of(kv * lines, lines), lines)].astype(jnp.float32)
+                    conduct = jnp.zeros((lines, bz), jnp.float32)
+                    for i in range(count):
+                        conduct = jnp.where(kind == float(i), values_ref[i], conduct)
+                    inverse = 1.0 / (MASS_TERM + 6.0 * conduct)
+                    place = (pl.ds((k ^ r0) * bx, bx), kv ^ v0, pl.ds(start, by))
+                    inverse_ref[place] = inverse.reshape(bx, by, bz)
+                    return carry
+
+                lax.fori_loop(0, vols, plane, 0)
+
     vmem = pl.BlockSpec(memory_space=pltpu.VMEM)
-    smem = pl.BlockSpec(memory_space=pltpu.SMEM)
     return pl.pallas_call(
         body,
         out_shape=[
-            jax.ShapeDtypeStruct(planes, jnp.float32),
+            jax.ShapeDtypeStruct((rows * bx, vols, cols * by, bz), jnp.float32),
             jax.ShapeDtypeStruct((rows, height, targets), jnp.bfloat16),
             jax.ShapeDtypeStruct((rows, bz, targets), jnp.bfloat16),
         ],
-        in_specs=[smem, smem, vmem, vmem],
+        in_specs=[pl.BlockSpec(memory_space=pltpu.SMEM)] + [vmem] * (2 * rows),
         out_specs=[vmem] * 3,
         name="prepare",
-    )(place, values, kinds, spots)
+    )(values, *known, *other)
 
 
 def parts_of(value, count):
@@ -158,7 +170,7 @@
     return pieces
 
 
-def slab_call(shape, first, source, inverse, hit, lane, parts=None, start=None):
+def slab_call(shape, first, source, inverse, hit, lane, parts, start=None):
     rows, cols, vols, bx, by, bz = shape
     blocks = cols * vols
     targets = lane.shape[-1]
@@ -168,11 +180,9 @@
     padded = (depth + 2, vols, cols * by, bz)
     factors = relax_factors(SWEEPS)
 
-    lines = bx * by
-
     def body(source_ref, inverse_ref, hit_ref, lane_ref, *rest):
         if first:
-            out_ref, flux_ref, other_ref, scaled_ref, ratio_ref = rest
+            *part_refs, out_ref, flux_ref, other_ref, scaled_ref, ratio_ref = rest
             volume_ref = None
         else:
             parts_ref, start_ref, volume_ref, flux_ref, out_ref, other_ref, scaled_ref, ratio_ref = rest
@@ -185,7 +195,8 @@
         potentials = []
         for r in range(rows):
             if first:
-                potential = sum(source_ref[r, j, lines:lines + 1] for j in range(blocks))
+                place = pl.ds(r ^ lax.axis_index("row"), 1)
+                potential = sum(part[place, :] for part in part_refs)
             else:
                 potential = sum(
                     jnp.sum(parts_ref[r ^ mate, :, k, :], axis=0, keepdims=True)
@@ -204,7 +215,7 @@
             for j in range(blocks):
                 c, v = j // vols, j % vols
                 span = (slice(r * bx, (r + 1) * bx), v, slice(c * by, (c + 1) * by))
-                scaled = source_ref[r, j, 0:lines].reshape(bx, by, bz) + added[:, v, c]
+                scaled = source_ref[r, j] + added[:, v, c]
                 inverse = inverse_ref[span]
                 scaled = scaled * inverse
                 ratio_ref[span] = (1.0 - MASS_TERM * inverse) * (1.0 / 6.0)
@@ -218,7 +229,7 @@
             there = out_ref if (len(sweeps) - order) % 2 == 1 else other_ref
 
             def step(index, carry, here=here, there=there, last=last, factor=factor):
-                for x in (GROUP * index + i for i in range(GROUP)):
+                for x in (index,):
                     tile = [here[x + 1, j % vols, (j // vols) * by:(j // vols + 1) * by]
                             for j in range(blocks)]
                     up = [pltpu.roll(t, 1, 1) for t in tile]
@@ -247,7 +258,8 @@
                             volume_ref[x // bx, j, x % bx] = value
                 return carry
 
-            lax.fori_loop(0, depth // GROUP, step, 0)
+            for index in range(depth):
+                step(index, 0)
             here = there
 
         for r in range(rows):
@@ -262,7 +274,7 @@
                 flux_ref[r ^ mate, :, k, :] = jnp.broadcast_to(value, (blocks, targets))
 
     vmem = pl.BlockSpec(memory_space=pltpu.VMEM)
-    operands = [source, inverse, hit, lane] + ([] if first else [parts, start])
+    operands = [source, inverse, hit, lane] + (list(parts) if first else [parts, start])
     fluxes = jax.ShapeDtypeStruct((rows, blocks, len(MATES), targets), jnp.float32)
     field = padded if first else (rows, blocks, bx, by, bz)
     field = jax.ShapeDtypeStruct(field, jnp.float32)
@@ -357,34 +369,36 @@
     width = nodes // rows
     here = lax.axis_index("row")
     low, high = here & 1, here >> 1
-    place = jnp.stack([lax.axis_index(a) for a in ALL]).astype(jnp.int32)
     shape = (rows, cols, vols, bx, by, bz)
 
     def columns(array, place):
         return lax.dynamic_slice_in_dim(array, place * width, width, 1)
 
+    def around_axis(pieces, axis):
+        return [pieces[0]] + [mated(piece, axis, k) for k, piece in enumerate(pieces) if k > 0]
+
+    parts, *quarters = start_call(density, panel, shape)
+
     kinds = class_index.reshape(bx * by, bz).astype(jnp.bfloat16)
-    kinds = stacked(kinds, "vol").reshape(vols * bx * by, bz)
+    kinds = around_axis([kinds] * vols, "vol")
+    parts = parts[0] + mated(parts[1], "col", 1)
+    slab = lax.all_to_all(source, ALL, 0, 0, tiled=True)
+    slab = slab.reshape(rows, blocks, bx, by, bz)
+    parts = jnp.stack(around_axis([parts[k] for k in range(rows)], "row"))
     spots = trace_spots(trace_count, trace_cell, targets, shape).astype(jnp.bfloat16)
     spots = jnp.pad(spots, ((0, SPOT_ROWS - spots.shape[0]), (0, 0)))
-    known = jnp.concatenate([kinds, spots])[None]
-    known = jnp.concatenate([known, mated(known, "row", 1)])
-    known = jnp.concatenate([known, mated(known, "row", 2)])
-    spots = known[:, vols * bx * by:]
-    kinds = stacked(known[:, :vols * bx * by], "col")
-    kinds = kinds.reshape(cols, rows, vols, bx * by, bz)
-
-    slab = gather_call(density, panel, source.reshape(excitations, bx * by, bz))
-    slab = lax.all_to_all(slab, ALL, 0, 0, tiled=True)
-    slab = slab.reshape(rows, blocks, bx * by + PART_ROWS, bz)
-
-    panels = [columns(panel, low), None, columns(panel, 2 + high), None]
-    panels[1] = mated(columns(panel, low ^ 1), "row", 1)
-    panels[3] = mated(columns(panel, 2 + (high ^ 1)), "row", 2)
+    known = jnp.concatenate(kinds + [spots])
+    known = around_axis([known] * rows, "row")
+    parts = around_axis([parts[:, k] for k in range(vols)], "vol")
+    other = [mated(piece, "col", 1) for piece in known]
+
+    panels = [quarters[0], None, quarters[2], None]
+    panels[1] = mated(quarters[1], "row", 1)
+    panels[3] = mated(quarters[3], "row", 2)
     densities = [columns(density, low), columns(density, 2 + high)]
 
-    inverse, hit, lane = prepare_call(shape, place, class_values, kinds, spots)
-    volume, flux = slab_call(shape, True, slab, inverse, hit, lane)
+    inverse, hit, lane = prepare_call(shape, class_values, known, other)
+    volume, flux = slab_call(shape, True, slab, inverse, hit, lane, parts)
     flux = flux.reshape(excitations, len(MATES), targets)
     flux = lax.all_to_all(flux, ALL, 0, 0, tiled=True)
     halves = update_call(flux, panels)
@@ -408,7 +422,8 @@
         jnp.where(low == 0, totals[0], moved[0]), jnp.where(low == 0, moved[0], totals[0]),
         jnp.where(high == 0, totals[1], moved[1]), jnp.where(high == 0, moved[1], totals[1]),
     ]
-    return (density + jnp.concatenate(change, axis=1).astype(jnp.float32), volume)
+    density = density + jnp.concatenate(change, axis=1).astype(jnp.float32)
+    return (density, volume)
 
 
 def padded_2(value, sides, width):

time: 171 us -> 166 us (0.971)
  starting transfers between devices: 30.6 us -> 37.5 us
  waiting for transfers between devices: 71.5 us -> 67.2 us
  Pallas kernels: 32 us -> 28.9 us
  other arithmetic: 8.01 us -> 4.95 us
  local copies, waits for them, and re-layouts: 7.77 us -> 5.84 us
    ppermute x14 -> x25, starting transfers between devices: 16.3 us -> 24.2 us  [mated(): lax.ppermute(value, axis, [(i, i ^ mate) for i in range(lax.axis_size(axi...]
    ppermute x14 -> x25, waiting for transfers between devices: 64 us -> 59.8 us  [mated(): lax.ppermute(value, axis, [(i, i ^ mate) for i in range(lax.axis_size(axi...]
    dynamic_slice x2 -> x1, local copies, waits for them, and re-layouts: 4.09 us -> 0.07 us  [columns(): return lax.dynamic_slice_in_dim(array, place * width, width, 1)]
    another operation x6 -> x3, other arithmetic: 2.66 us -> 0.22 us  [the longest x2 1.84 us: stacked(): return jnp.stack([value] + [mated(value, axis, k) for k in range(1, size)])]
    pallas_call x2, Pallas kernels: 13.1 us -> 11.4 us  [slab_call(): pl.pallas_call(body, out_shape=[field, fluxes], in_specs=[vmem] * len(ope...]
    unnamed x27 -> x54, local copies, waits for them, and re-layouts: 3.66 us -> 4.33 us
  transfers between devices with their start and end apart: 17 -> 28, of which waited for: 9 -> 12; matrix products, arithmetic and copies ran while one was open for 7% -> 3% of each run, Pallas kernels for 10% -> 9%
where the time goes in v5:
time: 166 us; the launch traced here: 165 us
  waiting for transfers between devices  67.2 us (40%)
  starting transfers between devices  37.5 us (23%)
  Pallas kernels  28.9 us (17%)
  blocking collectives  19.9 us (12%)
  local copies, waits for them, and re-layouts  5.84 us (4%)
  other arithmetic  4.95 us (3%)
    ppermute x25, waiting for transfers between devices, mated(): lax.ppermute(value, axis, [(i, i ^ mate) for i in range(lax.axis_size(axi...  59.8 us
    ppermute x25, starting transfers between devices, mated(): lax.ppermute(value, axis, [(i, i ^ mate) for i in range(lax.axis_size(axi...  24.2 us
    pallas_call x2, Pallas kernels, slab_call(): pl.pallas_call(body, out_shape=[field, fluxes], in_specs=[vmem] * len(ope...  11.4 us
    all_to_all x1, blocking collectives, split_by_excitation(): flux = lax.all_to_all(flux, ALL, 0, 0, tiled=True)  10.1 us
    all_to_all x1, blocking collectives, split_by_excitation(): parts = lax.all_to_all(parts, ALL, 0, 0, tiled=True)  9.87 us
    all_to_all x1, waiting for transfers between devices, split_by_excitation(): flux = lax.all_to_all(flux, ALL, 0, 0, tiled=True)  7.47 us
    pallas_call x1, Pallas kernels, start_call(): pl.pallas_call(body, out_shape=[jax.ShapeDtypeStruct((cols, rows, vols, t...  6.28 us
    all_to_all x1, starting transfers between devices, split_by_excitation(): slab = lax.all_to_all(source, ALL, 0, 0, tiled=True)  6.13 us
  transfers between devices with their start and end apart: 28, of which 12 were waited for; matrix products, arithmetic and copies ran while one was open for 3% of the time, Pallas kernels for 9%

profile of v5, /device:TPU:0, one launch (start us, length us, event | category | flops | bytes accessed | tf_op | source)
XLA Modules:
  0.0 165.4 jit_solution(15773382530888445615)
XLA Ops:
  1.4 5.1 %collective-permute-start.2 = (bf16[64,128]{1,0:T(8,128)(2,1)S(1)}, bf16[64,128]{1,0:T(8,128)(2,1)S(1)}, u32[]{:S(2)}, u32[]{:S(2)}) collective-permute-start(bf16[64,128]{1,0:T(8,128)(2,1)S(1)} %get-tuple-element.35), channel_id=1, source_target_pairs={{0,3},{1,2},{2,1},{3,0},{4,7},{5,6},{6,5},{7,4},{8,11},{9,10},{10,... | collective-permute-start | bytes 49160 | tf_op jit(solution)/shard_map/ppermute | solution.py:50
  7.1 6.1 %all-to-all-start = ((f32[32,8,8,128]{3,2,1,0:T(8,128)}), f32[32,8,8,128]{3,2,1,0:T(8,128)}, u32[]{:S(2)}, u32[]{:S(2)}) async-start(f32[32,8,8,128]{3,2,1,0:T(8,128)} %param.9), calls=%async_computation | async-start | bytes 2097152 | tf_op jit(solution)/shard_map/all_to_all | solution.py:385
  13.3 6.3 %start.1 = (f32[2,4,4,128]{3,2,1,0:T(4,128)}, bf16[128,4096]{1,0:T(8,128)(2,1)}, bf16[128,4096]{1,0:T(8,128)(2,1)}, bf16[128,4096]{1,0:T(8,128)(2,1)}, bf16[128,4096]{1,0:T(8,128)(2,1)}) custom-call(f32[32,16384]{1,0:T(8,128)} %density_ref.1, bf16[128,16384]{1,0:T(8,128)(2,1)} %panel_ref.1), custom_call_target="tpu_custom_call" | custom-call | tf_op jit(solution)/shard_map/start/pallas_call | solution.py:99
  27.3 25.3 %collective-permute-done.13 = f32[4,128]{1,0:T(4,128)S(1)} collective-permute-done((f32[4,128]{1,0:T(4,128)S(1)}, f32[4,128]{1,0:T(4,128)S(1)}, u32[]{:S(2)}, u32[]{:S(2)}) %collective-permute-start.13) | collective-permute-done | bytes 2080 | tf_op jit(solution)/shard_map/ppermute | solution.py:50
  54.4 1.7 %collective-permute-done.11 = f32[4,128]{1,0:T(4,128)S(1)} collective-permute-done((f32[4,128]{1,0:T(4,128)S(1)}, f32[4,128]{1,0:T(4,128)S(1)}, u32[]{:S(2)}, u32[]{:S(2)}) %collective-permute-start.11) | collective-permute-done | bytes 2080 | tf_op jit(solution)/shard_map/ppermute | solution.py:50
  58.8 1.7 %collective-permute-done.4.refs_2_ = bf16[272,128]{1,0:T(8,128)(2,1)S(1)} collective-permute-done((bf16[272,128]{1,0:T(8,128)(2,1)S(1)}, bf16[272,128]{1,0:T(8,128)(2,1)S(1)}, u32[]{:S(2)}, u32[]{:S(2)}) %collective-permute-start.4) | collective-permute-done | bytes 69664 | tf_op jit(solution)/shard_map/ppermute | solution.py:50
  61.6 2.4 %collective-permute-start.16 = (f32[4,128]{1,0:T(4,128)S(1)}, f32[4,128]{1,0:T(4,128)S(1)}, u32[]{:S(2)}, u32[]{:S(2)}) collective-permute-start(f32[4,128]{1,0:T(4,128)S(1)} %get-tuple-element.42), channel_id=1, source_target_pairs={{0,3},{1,2},{2,1},{3,0},{4,7},{5,6},{6,5},{7,4},{8,11},{9,10},{10,... | collective-permute-start | bytes 6152 | tf_op jit(solution)/shard_map/ppermute | solution.py:50
  66.7 4.1 %prepare.1 = (f32[32,4,16,128]{3,2,1,0:T(8,128)}, bf16[4,512,128]{2,1,0:T(8,128)(2,1)}, bf16[4,128,128]{2,1,0:T(8,128)(2,1)}) custom-call(f32[16]{0:T(128)} %values_ref.1, bf16[272,128]{1,0:T(8,128)(2,1)} %copy-done.12, bf16[272,128]{1,0:T(8,128)(2,1)} %copy-done.16, bf16[272,128]{1,0:T(8,128)(2,1)} %copy-done.15, bf16[272,128]{1,0:T(8,128)(2,1)} %copy-done.14, ...), custom_call_target="tpu_custom_call" | custom-call | tf_op jit(solution)/shard_map/prepare/pallas_call | solution.py:151
  71.4 5.3 %slab_first.1 = (f32[34,4,16,128]{3,2,1,0:T(8,128)}, f32[4,8,3,128]{3,2,1,0:T(4,128)}) custom-call(f32[4,8,8,8,128]{4,3,2,1,0:T(8,128)} %bitcast.source_ref, f32[32,4,16,128]{3,2,1,0:T(8,128)} %get-tuple-element.18.inverse_ref, bf16[4,512,128]{2,1,0:T(8,128)(2,1)} %get-tuple-element.19.hit_ref, bf16[4,128,128]{2,1,0:T(8,128)(2,1)} %get-tuple-element.20.lane_ref, ...), custom_call_target="tpu_custom_call" | custom-call | tf_op jit(solution)/shard_map/slab_first/pallas_call | solution.py:282
  76.7 3.8 %all-to-all-start.1 = ((f32[32,3,128]{2,1,0:T(4,128)}), f32[32,3,128]{2,1,0:T(4,128)S(1)}, u32[]{:S(2)}, u32[]{:S(2)}) async-start(f32[32,3,128]{2,1,0:T(4,128)} %bitcast.82), calls=%async_computation.1 | async-start | bytes 131072 | tf_op jit(solution)/shard_map/all_to_all | solution.py:403
  80.5 7.5 %all-to-all-done.1.flux_ref = f32[32,3,128]{2,1,0:T(4,128)S(1)} async-done(((f32[32,3,128]{2,1,0:T(4,128)}), f32[32,3,128]{2,1,0:T(4,128)S(1)}, u32[]{:S(2)}, u32[]{:S(2)}) %all-to-all-start.1) | async-done | bytes 49184 | tf_op jit(solution)/shard_map/all_to_all | solution.py:403
  88.0 2.0 %update.2 = (bf16[32,4096]{1,0:T(8,128)(2,1)S(1)}, bf16[32,4096]{1,0:T(8,128)(2,1)S(1)}) custom-call(f32[32,3,128]{2,1,0:T(4,128)S(1)} %all-to-all-done.1.flux_ref, bf16[128,4096]{1,0:T(8,128)(2,1)S(1)} %copy-done, bf16[128,4096]{1,0:T(8,128)(2,1)S(1)} %collective-permute-done.17.a_mate, bf16[128,4096]{1,0:T(8,128)(2,1)S(1)} %copy-done.1, ...), custom_call_target="tpu_custom_call" | custom-call | tf_op jit(solution)/shard_map/update/pallas_call | solution.py:303
  91.4 6.5 %collective-permute-done.19.a_other = bf16[32,4096]{1,0:T(8,128)(2,1)S(1)} collective-permute-done((bf16[32,4096]{1,0:T(8,128)(2,1)S(1)}, bf16[32,4096]{1,0:T(8,128)(2,1)S(1)}, u32[]{:S(2)}, u32[]{:S(2)}) %collective-permute-start.19) | collective-permute-done | bytes 262176 | tf_op jit(solution)/shard_map/ppermute | solution.py:50
  98.6 2.8 %potential.1 = f32[32,3,128]{2,1,0:T(4,128)S(1)} custom-call(f32[32,4096]{1,0:T(8,128)S(1)} %get-tuple-element.37.a_density, f32[32,4096]{1,0:T(8,128)S(1)} %get-tuple-element.36.b_density, bf16[32,4096]{1,0:T(8,128)(2,1)S(1)} %get-tuple-element.27.a_half, bf16[32,4096]{1,0:T(8,128)(2,1)S(1)} %get-tuple-element.28.b_half, ...), custom_call_target="tpu_custom_call" | custom-call | tf_op jit(solution)/shard_map/potential/pallas_call | solution.py:336
  101.5 9.9 %all_to_all.25 = f32[32,3,128]{2,1,0:T(4,128)} all-to-all(f32[32,3,128]{2,1,0:T(4,128)S(1)} %potential.1), channel_id=1, replica_groups=mesh['row'=4,'col'=2,'vol'=4] {'row','col','vol'}, dimensions={0} | all-to-all | bytes 98304 | tf_op jit(solution)/shard_map/all_to_all | solution.py:407
  111.3 6.1 %slab_last.1 = (f32[4,8,8,8,128]{4,3,2,1,0:T(8,128)}, f32[4,8,3,128]{3,2,1,0:T(4,128)}) custom-call(f32[4,8,8,8,128]{4,3,2,1,0:T(8,128)} %bitcast.source_ref, f32[32,4,16,128]{3,2,1,0:T(8,128)} %get-tuple-element.18.inverse_ref, bf16[4,512,128]{2,1,0:T(8,128)(2,1)} %get-tuple-element.19.hit_ref, bf16[4,128,128]{2,1,0:T(8,128)(2,1)} %get-tuple-element.20.lane_ref, ...), custom_call_target="tpu_custom_call" | custom-call | tf_op jit(solution)/shard_map/slab_last/pallas_call | solution.py:282
  117.4 10.1 %all_to_all.26.flux_ref = f32[32,3,128]{2,1,0:T(4,128)S(1)} all-to-all(f32[32,3,128]{2,1,0:T(4,128)} %bitcast.83), channel_id=1, replica_groups=mesh['row'=4,'col'=2,'vol'=4] {'row','col','vol'}, dimensions={0} | all-to-all | bytes 98304 | tf_op jit(solution)/shard_map/all_to_all | solution.py:411
  127.5 2.3 %update.3 = (bf16[32,4096]{1,0:T(8,128)(2,1)}, bf16[32,4096]{1,0:T(8,128)(2,1)S(1)}) custom-call(f32[32,3,128]{2,1,0:T(4,128)S(1)} %all_to_all.26.flux_ref, bf16[128,4096]{1,0:T(8,128)(2,1)S(1)} %copy-done, bf16[128,4096]{1,0:T(8,128)(2,1)S(1)} %collective-permute-done.17.a_mate, bf16[128,4096]{1,0:T(8,128)(2,1)S(1)} %copy-done.1, ...), custom_call_target="tpu_custom_call" | custom-call | tf_op jit(solution)/shard_map/update/pallas_call | solution.py:303
  131.3 3.4 %all-to-all-start.4 = ((f32[32,8,8,128]{3,2,1,0:T(8,128)}), f32[32,8,8,128]{3,2,1,0:T(8,128)}, u32[]{:S(2)}, u32[]{:S(2)}) async-start(f32[32,8,8,128]{3,2,1,0:T(8,128)} %bitcast.80), calls=%async_computation.4 | async-start | bytes 2097152 | tf_op jit(solution)/shard_map/all_to_all | solution.py:413
  136.3 7.3 %collective-permute-done.21 = bf16[32,4096]{1,0:T(8,128)(2,1)} collective-permute-done((bf16[32,4096]{1,0:T(8,128)(2,1)}, bf16[32,4096]{1,0:T(8,128)(2,1)}, u32[]{:S(2)}, u32[]{:S(2)}) %collective-permute-start.21) | collective-permute-done | bytes 262176 | tf_op jit(solution)/shard_map/ppermute | solution.py:50
  144.9 7.3 %collective-permute-done.23 = bf16[32,4096]{1,0:T(8,128)(2,1)S(1)} collective-permute-done((bf16[32,4096]{1,0:T(8,128)(2,1)S(1)}, bf16[32,4096]{1,0:T(8,128)(2,1)S(1)}, u32[]{:S(2)}, u32[]{:S(2)}) %collective-permute-start.23) | collective-permute-done | bytes 262176 | tf_op jit(solution)/shard_map/ppermute | solution.py:50
  153.9 5.5 %collective-permute-done.22 = bf16[32,4096]{1,0:T(8,128)(2,1)S(1)} collective-permute-done((bf16[32,4096]{1,0:T(8,128)(2,1)S(1)}, bf16[32,4096]{1,0:T(8,128)(2,1)S(1)}, u32[]{:S(2)}, u32[]{:S(2)}) %collective-permute-start.22) | collective-permute-done | bytes 262176 | tf_op jit(solution)/shard_map/ppermute | solution.py:50
  159.4 2.1 %collective-permute-done.24 = bf16[32,4096]{1,0:T(8,128)(2,1)S(1)} collective-permute-done((bf16[32,4096]{1,0:T(8,128)(2,1)S(1)}, bf16[32,4096]{1,0:T(8,128)(2,1)S(1)}, u32[]{:S(2)}, u32[]{:S(2)}) %collective-permute-start.24) | collective-permute-done | bytes 262176 | tf_op jit(solution)/shard_map/ppermute | solution.py:50
  163.1 2.3 %copy.20 = f32[32,8,8,128]{3,2,1,0:T(8,128)} copy(f32[32,8,8,128]{3,2,1,0:T(8,128)} %all-to-all-done.4) | data formatting | bytes 2097152
  (114 shorter events, 27.5 us)
Async XLA Ops:
  1.4 23.6 %collective-permute-start.2 = (bf16[64,128]{1,0:T(8,128)(2,1)S(1)}, bf16[64,128]{1,0:T(8,128)(2,1)S(1)}, u32[]{:S(2)}, u32[]{:S(2)}) collective-permute-start(bf16[64,128]{1,0:T(8,128)(2,1)S(1)} %get-tuple-element.35), channel_id=1, source_target_pairs={{0,3},{1,2},{2,1},{3,0},{4,7},{5,6},{6,5},{7,4},{8,11},{9,10},{10,... | collective-permute-start | bytes 49160 | tf_op jit(solution)/shard_map/ppermute | solution.py:50
  6.5 18.5 %collective-permute-start.1 = (bf16[64,128]{1,0:T(8,128)(2,1)S(1)}, bf16[64,128]{1,0:T(8,128)(2,1)S(1)}, u32[]{:S(2)}, u32[]{:S(2)}) collective-permute-start(bf16[64,128]{1,0:T(8,128)(2,1)S(1)} %get-tuple-element.35), channel_id=1, source_target_pairs={{0,2},{1,3},{2,0},{3,1},{4,6},{5,7},{6,4},{7,5},{8,10},{9,11},{10,... | collective-permute-start | bytes 49160 | tf_op jit(solution)/shard_map/ppermute | solution.py:50
  6.5 18.5 %collective-permute-start = (bf16[64,128]{1,0:T(8,128)(2,1)S(1)}, bf16[64,128]{1,0:T(8,128)(2,1)S(1)}, u32[]{:S(2)}, u32[]{:S(2)}) collective-permute-start(bf16[64,128]{1,0:T(8,128)(2,1)S(1)} %get-tuple-element.35), channel_id=1, source_target_pairs={{0,1},{1,0},{2,3},{3,2},{4,5},{5,4},{6,7},{7,6},{8,9},{9,8},{10,11... | collective-permute-start | bytes 49160 | tf_op jit(solution)/shard_map/ppermute | solution.py:50
  7.1 63.7 %all-to-all-start = ((f32[32,8,8,128]{3,2,1,0:T(8,128)}), f32[32,8,8,128]{3,2,1,0:T(8,128)}, u32[]{:S(2)}, u32[]{:S(2)}) async-start(f32[32,8,8,128]{3,2,1,0:T(8,128)} %param.9), calls=%async_computation | async-start | bytes 2097152 | tf_op jit(solution)/shard_map/all_to_all | solution.py:385
  20.6 59.9 %collective-permute-start.17 = (bf16[128,4096]{1,0:T(8,128)(2,1)}, bf16[128,4096]{1,0:T(8,128)(2,1)S(1)}, u32[]{:S(2)}, u32[]{:S(2)}) collective-permute-start(bf16[128,4096]{1,0:T(8,128)(2,1)} %get-tuple-element.24), channel_id=1, source_target_pairs={{0,8},{8,0},{16,24},{24,16},{1,9},{9,1},{17,25},{25,17},{2,10},{10... | collective-permute-start | bytes 3145736 | tf_op jit(solution)/shard_map/ppermute | solution.py:50
  22.8 57.8 %collective-permute-start.18 = (bf16[128,4096]{1,0:T(8,128)(2,1)}, bf16[128,4096]{1,0:T(8,128)(2,1)}, u32[]{:S(2)}, u32[]{:S(2)}) collective-permute-start(bf16[128,4096]{1,0:T(8,128)(2,1)} %get-tuple-element.26), channel_id=1, source_target_pairs={{0,16},{8,24},{16,0},{24,8},{1,17},{9,25},{17,1},{25,9},{2,18},{10... | collective-permute-start | bytes 3145736 | tf_op jit(solution)/shard_map/ppermute | solution.py:50
  25.1 31.5 %collective-permute-start.6 = (bf16[272,128]{1,0:T(8,128)(2,1)S(1)}, bf16[272,128]{1,0:T(8,128)(2,1)S(1)}, u32[]{:S(2)}, u32[]{:S(2)}) collective-permute-start(bf16[272,128]{1,0:T(8,128)(2,1)S(1)} %constant_dynamic-update-slice_fusion.refs_0_), channel_id=1, source_target_pairs={{0,4},{4,0},{1,5},{5,1},{2,6},{6,2},{3,7},{7,3},{8,12},{12,8},{9,1... | collective-permute-start | bytes 208904 | tf_op jit(solution)/shard_map/ppermute | solution.py:50
  25.2 27.4 %collective-permute-start.13 = (f32[4,128]{1,0:T(4,128)S(1)}, f32[4,128]{1,0:T(4,128)S(1)}, u32[]{:S(2)}, u32[]{:S(2)}) collective-permute-start(f32[4,128]{1,0:T(4,128)S(1)} %get-tuple-element.47), channel_id=1, source_target_pairs={{0,24},{8,16},{16,8},{24,0},{1,25},{9,17},{17,9},{25,1},{2,26},{10... | collective-permute-start | bytes 6152 | tf_op jit(solution)/shard_map/ppermute | solution.py:50
  25.7 27.7 %collective-permute-start.12 = (f32[4,128]{1,0:T(4,128)S(1)}, f32[4,128]{1,0:T(4,128)S(1)}, u32[]{:S(2)}, u32[]{:S(2)}) collective-permute-start(f32[4,128]{1,0:T(4,128)S(1)} %get-tuple-element.48), channel_id=1, source_target_pairs={{0,16},{8,24},{16,0},{24,8},{1,17},{9,25},{17,1},{25,9},{2,18},{10... | collective-permute-start | bytes 6152 | tf_op jit(solution)/shard_map/ppermute | solution.py:50
  53.4 5.4 %collective-permute-start.5 = (bf16[272,128]{1,0:T(8,128)(2,1)S(1)}, bf16[272,128]{1,0:T(8,128)(2,1)S(1)}, u32[]{:S(2)}, u32[]{:S(2)}) collective-permute-start(bf16[272,128]{1,0:T(8,128)(2,1)S(1)} %constant_dynamic-update-slice_fusion.refs_0_), channel_id=1, source_target_pairs={{0,24},{8,16},{16,8},{24,0},{1,25},{9,17},{17,9},{25,1},{2,26},{10... | collective-permute-start | bytes 208904 | tf_op jit(solution)/shard_map/ppermute | solution.py:50
  56.2 4.3 %collective-permute-start.4 = (bf16[272,128]{1,0:T(8,128)(2,1)S(1)}, bf16[272,128]{1,0:T(8,128)(2,1)S(1)}, u32[]{:S(2)}, u32[]{:S(2)}) collective-permute-start(bf16[272,128]{1,0:T(8,128)(2,1)S(1)} %constant_dynamic-update-slice_fusion.refs_0_), channel_id=1, source_target_pairs={{0,16},{8,24},{16,0},{24,8},{1,17},{9,25},{17,1},{25,9},{2,18},{10... | collective-permute-start | bytes 208904 | tf_op jit(solution)/shard_map/ppermute | solution.py:50
  56.6 4.3 %collective-permute-start.3 = (bf16[272,128]{1,0:T(8,128)(2,1)S(1)}, bf16[272,128]{1,0:T(8,128)(2,1)S(1)}, u32[]{:S(2)}, u32[]{:S(2)}) collective-permute-start(bf16[272,128]{1,0:T(8,128)(2,1)S(1)} %constant_dynamic-update-slice_fusion.refs_0_), channel_id=1, source_target_pairs={{0,8},{8,0},{16,24},{24,16},{1,9},{9,1},{17,25},{25,17},{2,10},{10... | collective-permute-start | bytes 208904 | tf_op jit(solution)/shard_map/ppermute | solution.py:50
  60.9 3.9 %collective-permute-start.7 = (bf16[272,128]{1,0:T(8,128)(2,1)S(1)}, bf16[272,128]{1,0:T(8,128)(2,1)S(1)}, u32[]{:S(2)}, u32[]{:S(2)}) collective-permute-start(bf16[272,128]{1,0:T(8,128)(2,1)S(1)} %collective-permute-done.3.refs_1_), channel_id=1, source_target_pairs={{0,4},{4,0},{1,5},{5,1},{2,6},{6,2},{3,7},{7,3},{8,12},{12,8},{9,1... | collective-permute-start | bytes 208904 | tf_op jit(solution)/shard_map/ppermute | solution.py:50
  61.6 9.2 %collective-permute-start.16 = (f32[4,128]{1,0:T(4,128)S(1)}, f32[4,128]{1,0:T(4,128)S(1)}, u32[]{:S(2)}, u32[]{:S(2)}) collective-permute-start(f32[4,128]{1,0:T(4,128)S(1)} %get-tuple-element.42), channel_id=1, source_target_pairs={{0,3},{1,2},{2,1},{3,0},{4,7},{5,6},{6,5},{7,4},{8,11},{9,10},{10,... | collective-permute-start | bytes 6152 | tf_op jit(solution)/shard_map/ppermute | solution.py:50
  64.0 6.8 %collective-permute-start.15 = (f32[4,128]{1,0:T(4,128)S(1)}, f32[4,128]{1,0:T(4,128)S(1)}, u32[]{:S(2)}, u32[]{:S(2)}) collective-permute-start(f32[4,128]{1,0:T(4,128)S(1)} %get-tuple-element.43), channel_id=1, source_target_pairs={{0,2},{1,3},{2,0},{3,1},{4,6},{5,7},{6,4},{7,5},{8,10},{9,11},{10,... | collective-permute-start | bytes 6152 | tf_op jit(solution)/shard_map/ppermute | solution.py:50
  65.5 5.3 %collective-permute-start.14 = (f32[4,128]{1,0:T(4,128)S(1)}, f32[4,128]{1,0:T(4,128)S(1)}, u32[]{:S(2)}, u32[]{:S(2)}) collective-permute-start(f32[4,128]{1,0:T(4,128)S(1)} %get-tuple-element.44), channel_id=1, source_target_pairs={{0,1},{1,0},{2,3},{3,2},{4,5},{5,4},{6,7},{7,6},{8,9},{9,8},{10,11... | collective-permute-start | bytes 6152 | tf_op jit(solution)/shard_map/ppermute | solution.py:50
  76.7 11.3 %all-to-all-start.1 = ((f32[32,3,128]{2,1,0:T(4,128)}), f32[32,3,128]{2,1,0:T(4,128)S(1)}, u32[]{:S(2)}, u32[]{:S(2)}) async-start(f32[32,3,128]{2,1,0:T(4,128)} %bitcast.82), calls=%async_computation.1 | async-start | bytes 131072 | tf_op jit(solution)/shard_map/all_to_all | solution.py:403
  90.1 7.9 %collective-permute-start.19 = (bf16[32,4096]{1,0:T(8,128)(2,1)S(1)}, bf16[32,4096]{1,0:T(8,128)(2,1)S(1)}, u32[]{:S(2)}, u32[]{:S(2)}) collective-permute-start(bf16[32,4096]{1,0:T(8,128)(2,1)S(1)} %get-tuple-element.27.a_half), channel_id=1, source_target_pairs={{0,16},{8,24},{16,0},{24,8},{1,17},{9,25},{17,1},{25,9},{2,18},{10... | collective-permute-start | bytes 786440 | tf_op jit(solution)/shard_map/ppermute | solution.py:50
  90.8 7.8 %collective-permute-start.20 = (bf16[32,4096]{1,0:T(8,128)(2,1)S(1)}, bf16[32,4096]{1,0:T(8,128)(2,1)S(1)}, u32[]{:S(2)}, u32[]{:S(2)}) collective-permute-start(bf16[32,4096]{1,0:T(8,128)(2,1)S(1)} %get-tuple-element.28.b_half), channel_id=1, source_target_pairs={{0,8},{8,0},{16,24},{24,16},{1,9},{9,1},{17,25},{25,17},{2,10},{10... | collective-permute-start | bytes 786440 | tf_op jit(solution)/shard_map/ppermute | solution.py:50
  130.5 13.1 %collective-permute-start.21 = (bf16[32,4096]{1,0:T(8,128)(2,1)}, bf16[32,4096]{1,0:T(8,128)(2,1)}, u32[]{:S(2)}, u32[]{:S(2)}) collective-permute-start(bf16[32,4096]{1,0:T(8,128)(2,1)} %get-tuple-element.31), channel_id=1, source_target_pairs={{0,16},{8,24},{16,0},{24,8},{1,17},{9,25},{17,1},{25,9},{2,18},{10... | collective-permute-start | bytes 786440 | tf_op jit(solution)/shard_map/ppermute | solution.py:50
  131.3 31.8 %all-to-all-start.4 = ((f32[32,8,8,128]{3,2,1,0:T(8,128)}), f32[32,8,8,128]{3,2,1,0:T(8,128)}, u32[]{:S(2)}, u32[]{:S(2)}) async-start(f32[32,8,8,128]{3,2,1,0:T(8,128)} %bitcast.80), calls=%async_computation.4 | async-start | bytes 2097152 | tf_op jit(solution)/shard_map/all_to_all | solution.py:413
  134.7 17.5 %collective-permute-start.23 = (bf16[32,4096]{1,0:T(8,128)(2,1)S(1)}, bf16[32,4096]{1,0:T(8,128)(2,1)S(1)}, u32[]{:S(2)}, u32[]{:S(2)}) collective-permute-start(bf16[32,4096]{1,0:T(8,128)(2,1)S(1)} %copy-done.9), channel_id=1, source_target_pairs={{0,8},{8,0},{16,24},{24,16},{1,9},{9,1},{17,25},{25,17},{2,10},{10... | collective-permute-start | bytes 786440 | tf_op jit(solution)/shard_map/ppermute | solution.py:50
  144.8 14.5 %collective-permute-start.22 = (bf16[32,4096]{1,0:T(8,128)(2,1)S(1)}, bf16[32,4096]{1,0:T(8,128)(2,1)S(1)}, u32[]{:S(2)}, u32[]{:S(2)}) collective-permute-start(bf16[32,4096]{1,0:T(8,128)(2,1)S(1)} %multiply_convert_fusion.1), channel_id=1, source_target_pairs={{0,8},{8,0},{16,24},{24,16},{1,9},{9,1},{17,25},{25,17},{2,10},{10... | collective-permute-start | bytes 786440 | tf_op jit(solution)/shard_map/ppermute | solution.py:50
  152.3 9.1 %collective-permute-start.24 = (bf16[32,4096]{1,0:T(8,128)(2,1)S(1)}, bf16[32,4096]{1,0:T(8,128)(2,1)S(1)}, u32[]{:S(2)}, u32[]{:S(2)}) collective-permute-start(bf16[32,4096]{1,0:T(8,128)(2,1)S(1)} %multiply_convert_fusion), channel_id=1, source_target_pairs={{0,16},{8,24},{16,0},{24,8},{1,17},{9,25},{17,1},{25,9},{2,18},{10... | collective-permute-start | bytes 786440 | tf_op jit(solution)/shard_map/ppermute | solution.py:50
  (29 other events, 345.9 us)

commit v6 on v5

--- a/solution.py
+++ b/solution.py
@@ -61,31 +61,29 @@
         nodes_ref, panel_buf, total_ref, sems = rest[rows:]
         r0, c0, v0 = (lax.axis_index(a) for a in ALL)
         low, high = r0 & 1, r0 >> 1
-        loads = []
-        for q in range(rows):
-            span = pl.ds(q * width, width)
-            loads.append((
+        sources = (low, low ^ 1, 2 + high, 2 + (high ^ 1))
+        order = (1, 3, 0, 2)
+        loads, stores = [], []
+        for q in order:
+            span = pl.ds(pl.multiple_of(sources[q] * width, width), width)
+            pair = (
                 pltpu.make_async_copy(panel_ref.at[:, span], panel_buf.at[q], sems.at[q]),
                 pltpu.make_async_copy(density_ref.at[:, span], nodes_ref.at[q], sems.at[rows + q]),
-            ))
-        for pair in loads:
+            )
             for copy in pair:
                 copy.start()
+            loads.append(pair)
         total = jnp.zeros((targets, excitations), jnp.float32)
-        for q in range(rows):
-            for copy in loads[q]:
+        for q, pair in zip(order, loads):
+            for copy in pair:
                 copy.wait()
+            store = pltpu.make_async_copy(panel_buf.at[q], quarters[q], sems.at[2 * rows + q])
+            store.start()
+            stores.append(store)
             total += lax.dot_general(
                 panel_buf[q], nodes_ref[q].astype(jnp.bfloat16), (((1,), (1,)), ((), ())),
                 preferred_element_type=jnp.float32,
             )
-        sources = (low, low ^ 1, 2 + high, 2 + (high ^ 1))
-        stores = [
-            pltpu.make_async_copy(panel_buf.at[source], quarter, sems.at[q])
-            for q, (source, quarter) in enumerate(zip(sources, quarters))
-        ]
-        for copy in stores:
-            copy.start()
         total_ref[...] = total.T
         for kc in range(cols):
             for kr in range(rows):
@@ -106,7 +104,7 @@
             pltpu.VMEM((rows, excitations, width), jnp.float32),
             pltpu.VMEM((rows, targets, width), panel.dtype),
             pltpu.VMEM((excitations, targets), jnp.float32),
-            pltpu.SemaphoreType.DMA((2 * rows,)),
+            pltpu.SemaphoreType.DMA((3 * rows,)),
         ],
         name="start",
     )(density, panel)
@@ -159,6 +157,24 @@
         out_specs=[vmem] * 3,
         name="prepare",
     )(values, *known, *other)
+
+
+def landed_call(volume):
+    excitations = volume.shape[0]
+    few = math.gcd(excitations, 8)
+    block = pl.BlockSpec((few,) + volume.shape[1:], lambda i: (i, 0, 0, 0))
+
+    def body(in_ref, out_ref):
+        out_ref[...] = in_ref[...]
+
+    return pl.pallas_call(
+        body,
+        grid=(excitations // few,),
+        out_shape=jax.ShapeDtypeStruct(volume.shape, volume.dtype),
+        in_specs=[block],
+        out_specs=block,
+        name="landed",
+    )(volume)
 
 
 def parts_of(value, count):
@@ -411,6 +427,7 @@
     flux = lax.all_to_all(flux, ALL, 0, 0, tiled=True)
     volume = volume.reshape(excitations, bx, by, bz)
     volume = lax.all_to_all(volume, ALL, 0, 0, tiled=True)
+    volume = landed_call(volume)
     ends = update_call(flux, panels)
     end_mates = [mated(ends[0], "row", 2), mated(ends[1], "row", 1)]
     totals = []

time: 166 us -> 167 us (level)
  Pallas kernels: 28.9 us -> 31.3 us
  local copies, waits for them, and re-layouts: 5.84 us -> 3.57 us
    pallas_call x0 -> x1, Pallas kernels: none -> 3.36 us  [landed_call(): pl.pallas_call(body, grid=(excitations // few,), out_shape=jax.ShapeDtype...]
    unnamed x54 -> x53, local copies, waits for them, and re-layouts: 4.33 us -> 2.02 us
where the time goes in v6:
time: 167 us; the launch traced here: 166 us
  waiting for transfers between devices  66.5 us (40%)
  starting transfers between devices  39 us (23%)
  Pallas kernels  31.3 us (19%)
  blocking collectives  19.9 us (12%)
  other arithmetic  4.95 us (3%)
  local copies, waits for them, and re-layouts  3.57 us (2%)
    ppermute x25, waiting for transfers between devices, mated(): lax.ppermute(value, axis, [(i, i ^ mate) for i in range(lax.axis_size(axi...  59.1 us
    ppermute x25, starting transfers between devices, mated(): lax.ppermute(value, axis, [(i, i ^ mate) for i in range(lax.axis_size(axi...  25 us
    pallas_call x2, Pallas kernels, slab_call(): pl.pallas_call(body, out_shape=[field, fluxes], in_specs=[vmem] * len(ope...  11.4 us
    all_to_all x1, blocking collectives, split_by_excitation(): flux = lax.all_to_all(flux, ALL, 0, 0, tiled=True)  10.1 us
    all_to_all x1, blocking collectives, split_by_excitation(): parts = lax.all_to_all(parts, ALL, 0, 0, tiled=True)  9.87 us
    all_to_all x1, waiting for transfers between devices, split_by_excitation(): flux = lax.all_to_all(flux, ALL, 0, 0, tiled=True)  7.47 us
    all_to_all x1, starting transfers between devices, split_by_excitation(): slab = lax.all_to_all(source, ALL, 0, 0, tiled=True)  6.13 us
    pallas_call x1, Pallas kernels, start_call(): pl.pallas_call(body, out_shape=[jax.ShapeDtypeStruct((cols, rows, vols, t...  5.28 us
  transfers between devices with their start and end apart: 28, of which 12 were waited for; matrix products, arithmetic and copies ran while one was open for 3% of the time, Pallas kernels for 9%

profile of v6, /device:TPU:0, one launch (start us, length us, event | category | flops | bytes accessed | tf_op | source)
XLA Modules:
  0.0 166.3 jit_solution(13143100388138742841)
XLA Ops:
  1.4 5.1 %collective-permute-start.2 = (bf16[64,128]{1,0:T(8,128)(2,1)S(1)}, bf16[64,128]{1,0:T(8,128)(2,1)S(1)}, u32[]{:S(2)}, u32[]{:S(2)}) collective-permute-start(bf16[64,128]{1,0:T(8,128)(2,1)S(1)} %get-tuple-element.35), channel_id=1, source_target_pairs={{0,3},{1,2},{2,1},{3,0},{4,7},{5,6},{6,5},{7,4},{8,11},{9,10},{10,... | collective-permute-start | bytes 49160 | tf_op jit(solution)/shard_map/ppermute | solution.py:50
  7.1 6.1 %all-to-all-start = ((f32[32,8,8,128]{3,2,1,0:T(8,128)}), f32[32,8,8,128]{3,2,1,0:T(8,128)}, u32[]{:S(2)}, u32[]{:S(2)}) async-start(f32[32,8,8,128]{3,2,1,0:T(8,128)} %param.9), calls=%async_computation | async-start | bytes 2097152 | tf_op jit(solution)/shard_map/all_to_all | solution.py:401
  13.3 5.3 %start.1 = (f32[2,4,4,128]{3,2,1,0:T(4,128)}, bf16[128,4096]{1,0:T(8,128)(2,1)}, bf16[128,4096]{1,0:T(8,128)(2,1)}, bf16[128,4096]{1,0:T(8,128)(2,1)}, bf16[128,4096]{1,0:T(8,128)(2,1)}) custom-call(f32[32,16384]{1,0:T(8,128)} %density_ref.1, bf16[128,16384]{1,0:T(8,128)(2,1)} %panel_ref.1), custom_call_target="tpu_custom_call" | custom-call | tf_op jit(solution)/shard_map/start/pallas_call | solution.py:97
  19.6 1.6 collective-permute-start.17
  26.3 25.4 %collective-permute-done.13 = f32[4,128]{1,0:T(4,128)S(1)} collective-permute-done((f32[4,128]{1,0:T(4,128)S(1)}, f32[4,128]{1,0:T(4,128)S(1)}, u32[]{:S(2)}, u32[]{:S(2)}) %collective-permute-start.13) | collective-permute-done | bytes 2080 | tf_op jit(solution)/shard_map/ppermute | solution.py:50
  60.7 2.8 %collective-permute-start.16 = (f32[4,128]{1,0:T(4,128)S(1)}, f32[4,128]{1,0:T(4,128)S(1)}, u32[]{:S(2)}, u32[]{:S(2)}) collective-permute-start(f32[4,128]{1,0:T(4,128)S(1)} %get-tuple-element.42), channel_id=1, source_target_pairs={{0,3},{1,2},{2,1},{3,0},{4,7},{5,6},{6,5},{7,4},{8,11},{9,10},{10,... | collective-permute-start | bytes 6152 | tf_op jit(solution)/shard_map/ppermute | solution.py:50
  65.8 4.1 %prepare.1 = (f32[32,4,16,128]{3,2,1,0:T(8,128)}, bf16[4,512,128]{2,1,0:T(8,128)(2,1)}, bf16[4,128,128]{2,1,0:T(8,128)(2,1)}) custom-call(f32[16]{0:T(128)} %values_ref.1, bf16[272,128]{1,0:T(8,128)(2,1)} %copy-done.12, bf16[272,128]{1,0:T(8,128)(2,1)} %copy-done.16, bf16[272,128]{1,0:T(8,128)(2,1)} %copy-done.15, bf16[272,128]{1,0:T(8,128)(2,1)} %copy-done.14, ...), custom_call_target="tpu_custom_call" | custom-call | tf_op jit(solution)/shard_map/prepare/pallas_call | solution.py:149
  70.5 5.3 %slab_first.1 = (f32[34,4,16,128]{3,2,1,0:T(8,128)}, f32[4,8,3,128]{3,2,1,0:T(4,128)}) custom-call(f32[4,8,8,8,128]{4,3,2,1,0:T(8,128)} %bitcast.source_ref, f32[32,4,16,128]{3,2,1,0:T(8,128)} %get-tuple-element.18.inverse_ref, bf16[4,512,128]{2,1,0:T(8,128)(2,1)} %get-tuple-element.19.hit_ref, bf16[4,128,128]{2,1,0:T(8,128)(2,1)} %get-tuple-element.20.lane_ref, ...), custom_call_target="tpu_custom_call" | custom-call | tf_op jit(solution)/shard_map/slab_first/pallas_call | solution.py:298
  75.8 4.6 %all-to-all-start.1 = ((f32[32,3,128]{2,1,0:T(4,128)}), f32[32,3,128]{2,1,0:T(4,128)S(1)}, u32[]{:S(2)}, u32[]{:S(2)}) async-start(f32[32,3,128]{2,1,0:T(4,128)} %bitcast.82), calls=%async_computation.1 | async-start | bytes 131072 | tf_op jit(solution)/shard_map/all_to_all | solution.py:419
  80.4 7.5 %all-to-all-done.1.flux_ref = f32[32,3,128]{2,1,0:T(4,128)S(1)} async-done(((f32[32,3,128]{2,1,0:T(4,128)}), f32[32,3,128]{2,1,0:T(4,128)S(1)}, u32[]{:S(2)}, u32[]{:S(2)}) %all-to-all-start.1) | async-done | bytes 49184 | tf_op jit(solution)/shard_map/all_to_all | solution.py:419
  87.9 2.0 %update.2 = (bf16[32,4096]{1,0:T(8,128)(2,1)S(1)}, bf16[32,4096]{1,0:T(8,128)(2,1)S(1)}) custom-call(f32[32,3,128]{2,1,0:T(4,128)S(1)} %all-to-all-done.1.flux_ref, bf16[128,4096]{1,0:T(8,128)(2,1)S(1)} %copy-done, bf16[128,4096]{1,0:T(8,128)(2,1)S(1)} %collective-permute-done.17.a_mate, bf16[128,4096]{1,0:T(8,128)(2,1)S(1)} %copy-done.1, ...), custom_call_target="tpu_custom_call" | custom-call | tf_op jit(solution)/shard_map/update/pallas_call | solution.py:319
  91.3 6.5 %collective-permute-done.19.a_other = bf16[32,4096]{1,0:T(8,128)(2,1)S(1)} collective-permute-done((bf16[32,4096]{1,0:T(8,128)(2,1)S(1)}, bf16[32,4096]{1,0:T(8,128)(2,1)S(1)}, u32[]{:S(2)}, u32[]{:S(2)}) %collective-permute-start.19) | collective-permute-done | bytes 262176 | tf_op jit(solution)/shard_map/ppermute | solution.py:50
  98.5 2.8 %potential.1 = f32[32,3,128]{2,1,0:T(4,128)S(1)} custom-call(f32[32,4096]{1,0:T(8,128)S(1)} %get-tuple-element.37.a_density, f32[32,4096]{1,0:T(8,128)S(1)} %get-tuple-element.36.b_density, bf16[32,4096]{1,0:T(8,128)(2,1)S(1)} %get-tuple-element.27.a_half, bf16[32,4096]{1,0:T(8,128)(2,1)S(1)} %get-tuple-element.28.b_half, ...), custom_call_target="tpu_custom_call" | custom-call | tf_op jit(solution)/shard_map/potential/pallas_call | solution.py:352
  101.3 9.9 %all_to_all.25 = f32[32,3,128]{2,1,0:T(4,128)} all-to-all(f32[32,3,128]{2,1,0:T(4,128)S(1)} %potential.1), channel_id=1, replica_groups=mesh['row'=4,'col'=2,'vol'=4] {'row','col','vol'}, dimensions={0} | all-to-all | bytes 98304 | tf_op jit(solution)/shard_map/all_to_all | solution.py:423
  111.2 6.1 %slab_last.1 = (f32[4,8,8,8,128]{4,3,2,1,0:T(8,128)}, f32[4,8,3,128]{3,2,1,0:T(4,128)}) custom-call(f32[4,8,8,8,128]{4,3,2,1,0:T(8,128)} %bitcast.source_ref, f32[32,4,16,128]{3,2,1,0:T(8,128)} %get-tuple-element.18.inverse_ref, bf16[4,512,128]{2,1,0:T(8,128)(2,1)} %get-tuple-element.19.hit_ref, bf16[4,128,128]{2,1,0:T(8,128)(2,1)} %get-tuple-element.20.lane_ref, ...), custom_call_target="tpu_custom_call" | custom-call | tf_op jit(solution)/shard_map/slab_last/pallas_call | solution.py:298
  117.3 10.1 %all_to_all.26.flux_ref = f32[32,3,128]{2,1,0:T(4,128)S(1)} all-to-all(f32[32,3,128]{2,1,0:T(4,128)} %bitcast.83), channel_id=1, replica_groups=mesh['row'=4,'col'=2,'vol'=4] {'row','col','vol'}, dimensions={0} | all-to-all | bytes 98304 | tf_op jit(solution)/shard_map/all_to_all | solution.py:427
  127.3 2.3 %update.3 = (bf16[32,4096]{1,0:T(8,128)(2,1)}, bf16[32,4096]{1,0:T(8,128)(2,1)S(1)}) custom-call(f32[32,3,128]{2,1,0:T(4,128)S(1)} %all_to_all.26.flux_ref, bf16[128,4096]{1,0:T(8,128)(2,1)S(1)} %copy-done, bf16[128,4096]{1,0:T(8,128)(2,1)S(1)} %collective-permute-done.17.a_mate, bf16[128,4096]{1,0:T(8,128)(2,1)S(1)} %copy-done.1, ...), custom_call_target="tpu_custom_call" | custom-call | tf_op jit(solution)/shard_map/update/pallas_call | solution.py:319
  131.1 3.4 %all-to-all-start.4 = ((f32[32,8,8,128]{3,2,1,0:T(8,128)}), f32[32,8,8,128]{3,2,1,0:T(8,128)}, u32[]{:S(2)}, u32[]{:S(2)}) async-start(f32[32,8,8,128]{3,2,1,0:T(8,128)} %bitcast.80), calls=%async_computation.4 | async-start | bytes 2097152 | tf_op jit(solution)/shard_map/all_to_all | solution.py:429
  134.6 1.6 collective-permute-start.23
  136.2 7.3 %collective-permute-done.21 = bf16[32,4096]{1,0:T(8,128)(2,1)} collective-permute-done((bf16[32,4096]{1,0:T(8,128)(2,1)}, bf16[32,4096]{1,0:T(8,128)(2,1)}, u32[]{:S(2)}, u32[]{:S(2)}) %collective-permute-start.21) | collective-permute-done | bytes 262176 | tf_op jit(solution)/shard_map/ppermute | solution.py:50
  144.8 7.3 %collective-permute-done.23 = bf16[32,4096]{1,0:T(8,128)(2,1)S(1)} collective-permute-done((bf16[32,4096]{1,0:T(8,128)(2,1)S(1)}, bf16[32,4096]{1,0:T(8,128)(2,1)S(1)}, u32[]{:S(2)}, u32[]{:S(2)}) %collective-permute-start.23) | collective-permute-done | bytes 262176 | tf_op jit(solution)/shard_map/ppermute | solution.py:50
  153.8 5.5 %collective-permute-done.22 = bf16[32,4096]{1,0:T(8,128)(2,1)S(1)} collective-permute-done((bf16[32,4096]{1,0:T(8,128)(2,1)S(1)}, bf16[32,4096]{1,0:T(8,128)(2,1)S(1)}, u32[]{:S(2)}, u32[]{:S(2)}) %collective-permute-start.22) | collective-permute-done | bytes 262176 | tf_op jit(solution)/shard_map/ppermute | solution.py:50
  159.3 2.1 %collective-permute-done.24 = bf16[32,4096]{1,0:T(8,128)(2,1)S(1)} collective-permute-done((bf16[32,4096]{1,0:T(8,128)(2,1)S(1)}, bf16[32,4096]{1,0:T(8,128)(2,1)S(1)}, u32[]{:S(2)}, u32[]{:S(2)}) %collective-permute-start.24) | collective-permute-done | bytes 262176 | tf_op jit(solution)/shard_map/ppermute | solution.py:50
  162.9 3.4 %landed.1 = f32[32,8,8,128]{3,2,1,0:T(8,128)} custom-call(f32[32,8,8,128]{3,2,1,0:T(8,128)} %all-to-all-done.4.in_ref), custom_call_target="tpu_custom_call" | custom-call | tf_op jit(solution)/shard_map/landed/pallas_call | solution.py:170
  (114 shorter events, 27.4 us)
Async XLA Ops:
  1.4 22.6 %collective-permute-start.2 = (bf16[64,128]{1,0:T(8,128)(2,1)S(1)}, bf16[64,128]{1,0:T(8,128)(2,1)S(1)}, u32[]{:S(2)}, u32[]{:S(2)}) collective-permute-start(bf16[64,128]{1,0:T(8,128)(2,1)S(1)} %get-tuple-element.35), channel_id=1, source_target_pairs={{0,3},{1,2},{2,1},{3,0},{4,7},{5,6},{6,5},{7,4},{8,11},{9,10},{10,... | collective-permute-start | bytes 49160 | tf_op jit(solution)/shard_map/ppermute | solution.py:50
  6.5 17.5 %collective-permute-start.1 = (bf16[64,128]{1,0:T(8,128)(2,1)S(1)}, bf16[64,128]{1,0:T(8,128)(2,1)S(1)}, u32[]{:S(2)}, u32[]{:S(2)}) collective-permute-start(bf16[64,128]{1,0:T(8,128)(2,1)S(1)} %get-tuple-element.35), channel_id=1, source_target_pairs={{0,2},{1,3},{2,0},{3,1},{4,6},{5,7},{6,4},{7,5},{8,10},{9,11},{10,... | collective-permute-start | bytes 49160 | tf_op jit(solution)/shard_map/ppermute | solution.py:50
  6.5 17.5 %collective-permute-start = (bf16[64,128]{1,0:T(8,128)(2,1)S(1)}, bf16[64,128]{1,0:T(8,128)(2,1)S(1)}, u32[]{:S(2)}, u32[]{:S(2)}) collective-permute-start(bf16[64,128]{1,0:T(8,128)(2,1)S(1)} %get-tuple-element.35), channel_id=1, source_target_pairs={{0,1},{1,0},{2,3},{3,2},{4,5},{5,4},{6,7},{7,6},{8,9},{9,8},{10,11... | collective-permute-start | bytes 49160 | tf_op jit(solution)/shard_map/ppermute | solution.py:50
  7.1 62.8 %all-to-all-start = ((f32[32,8,8,128]{3,2,1,0:T(8,128)}), f32[32,8,8,128]{3,2,1,0:T(8,128)}, u32[]{:S(2)}, u32[]{:S(2)}) async-start(f32[32,8,8,128]{3,2,1,0:T(8,128)} %param.9), calls=%async_computation | async-start | bytes 2097152 | tf_op jit(solution)/shard_map/all_to_all | solution.py:401
  19.6 60.8 %collective-permute-start.17 = (bf16[128,4096]{1,0:T(8,128)(2,1)}, bf16[128,4096]{1,0:T(8,128)(2,1)S(1)}, u32[]{:S(2)}, u32[]{:S(2)}) collective-permute-start(bf16[128,4096]{1,0:T(8,128)(2,1)} %get-tuple-element.24), channel_id=1, source_target_pairs={{0,8},{8,0},{16,24},{24,16},{1,9},{9,1},{17,25},{25,17},{2,10},{10... | collective-permute-start | bytes 3145736 | tf_op jit(solution)/shard_map/ppermute | solution.py:50
  21.8 58.6 %collective-permute-start.18 = (bf16[128,4096]{1,0:T(8,128)(2,1)}, bf16[128,4096]{1,0:T(8,128)(2,1)}, u32[]{:S(2)}, u32[]{:S(2)}) collective-permute-start(bf16[128,4096]{1,0:T(8,128)(2,1)} %get-tuple-element.26), channel_id=1, source_target_pairs={{0,16},{8,24},{16,0},{24,8},{1,17},{9,25},{17,1},{25,9},{2,18},{10... | collective-permute-start | bytes 3145736 | tf_op jit(solution)/shard_map/ppermute | solution.py:50
  24.1 31.7 %collective-permute-start.6 = (bf16[272,128]{1,0:T(8,128)(2,1)S(1)}, bf16[272,128]{1,0:T(8,128)(2,1)S(1)}, u32[]{:S(2)}, u32[]{:S(2)}) collective-permute-start(bf16[272,128]{1,0:T(8,128)(2,1)S(1)} %constant_dynamic-update-slice_fusion.refs_0_), channel_id=1, source_target_pairs={{0,4},{4,0},{1,5},{5,1},{2,6},{6,2},{3,7},{7,3},{8,12},{12,8},{9,1... | collective-permute-start | bytes 208904 | tf_op jit(solution)/shard_map/ppermute | solution.py:50
  24.2 27.5 %collective-permute-start.13 = (f32[4,128]{1,0:T(4,128)S(1)}, f32[4,128]{1,0:T(4,128)S(1)}, u32[]{:S(2)}, u32[]{:S(2)}) collective-permute-start(f32[4,128]{1,0:T(4,128)S(1)} %get-tuple-element.47), channel_id=1, source_target_pairs={{0,24},{8,16},{16,8},{24,0},{1,25},{9,17},{17,9},{25,1},{2,26},{10... | collective-permute-start | bytes 6152 | tf_op jit(solution)/shard_map/ppermute | solution.py:50
  24.7 28.4 %collective-permute-start.12 = (f32[4,128]{1,0:T(4,128)S(1)}, f32[4,128]{1,0:T(4,128)S(1)}, u32[]{:S(2)}, u32[]{:S(2)}) collective-permute-start(f32[4,128]{1,0:T(4,128)S(1)} %get-tuple-element.48), channel_id=1, source_target_pairs={{0,16},{8,24},{16,0},{24,8},{1,17},{9,25},{17,1},{25,9},{2,18},{10... | collective-permute-start | bytes 6152 | tf_op jit(solution)/shard_map/ppermute | solution.py:50
  53.1 5.6 %collective-permute-start.5 = (bf16[272,128]{1,0:T(8,128)(2,1)S(1)}, bf16[272,128]{1,0:T(8,128)(2,1)S(1)}, u32[]{:S(2)}, u32[]{:S(2)}) collective-permute-start(bf16[272,128]{1,0:T(8,128)(2,1)S(1)} %constant_dynamic-update-slice_fusion.refs_0_), channel_id=1, source_target_pairs={{0,24},{8,16},{16,8},{24,0},{1,25},{9,17},{17,9},{25,1},{2,26},{10... | collective-permute-start | bytes 208904 | tf_op jit(solution)/shard_map/ppermute | solution.py:50
  55.3 4.3 %collective-permute-start.4 = (bf16[272,128]{1,0:T(8,128)(2,1)S(1)}, bf16[272,128]{1,0:T(8,128)(2,1)S(1)}, u32[]{:S(2)}, u32[]{:S(2)}) collective-permute-start(bf16[272,128]{1,0:T(8,128)(2,1)S(1)} %constant_dynamic-update-slice_fusion.refs_0_), channel_id=1, source_target_pairs={{0,16},{8,24},{16,0},{24,8},{1,17},{9,25},{17,1},{25,9},{2,18},{10... | collective-permute-start | bytes 208904 | tf_op jit(solution)/shard_map/ppermute | solution.py:50
  55.8 4.3 %collective-permute-start.3 = (bf16[272,128]{1,0:T(8,128)(2,1)S(1)}, bf16[272,128]{1,0:T(8,128)(2,1)S(1)}, u32[]{:S(2)}, u32[]{:S(2)}) collective-permute-start(bf16[272,128]{1,0:T(8,128)(2,1)S(1)} %constant_dynamic-update-slice_fusion.refs_0_), channel_id=1, source_target_pairs={{0,8},{8,0},{16,24},{24,16},{1,9},{9,1},{17,25},{25,17},{2,10},{10... | collective-permute-start | bytes 208904 | tf_op jit(solution)/shard_map/ppermute | solution.py:50
  60.1 4.4 %collective-permute-start.7 = (bf16[272,128]{1,0:T(8,128)(2,1)S(1)}, bf16[272,128]{1,0:T(8,128)(2,1)S(1)}, u32[]{:S(2)}, u32[]{:S(2)}) collective-permute-start(bf16[272,128]{1,0:T(8,128)(2,1)S(1)} %collective-permute-done.3.refs_1_), channel_id=1, source_target_pairs={{0,4},{4,0},{1,5},{5,1},{2,6},{6,2},{3,7},{7,3},{8,12},{12,8},{9,1... | collective-permute-start | bytes 208904 | tf_op jit(solution)/shard_map/ppermute | solution.py:50
  60.7 9.2 %collective-permute-start.16 = (f32[4,128]{1,0:T(4,128)S(1)}, f32[4,128]{1,0:T(4,128)S(1)}, u32[]{:S(2)}, u32[]{:S(2)}) collective-permute-start(f32[4,128]{1,0:T(4,128)S(1)} %get-tuple-element.42), channel_id=1, source_target_pairs={{0,3},{1,2},{2,1},{3,0},{4,7},{5,6},{6,5},{7,4},{8,11},{9,10},{10,... | collective-permute-start | bytes 6152 | tf_op jit(solution)/shard_map/ppermute | solution.py:50
  63.5 6.4 %collective-permute-start.15 = (f32[4,128]{1,0:T(4,128)S(1)}, f32[4,128]{1,0:T(4,128)S(1)}, u32[]{:S(2)}, u32[]{:S(2)}) collective-permute-start(f32[4,128]{1,0:T(4,128)S(1)} %get-tuple-element.43), channel_id=1, source_target_pairs={{0,2},{1,3},{2,0},{3,1},{4,6},{5,7},{6,4},{7,5},{8,10},{9,11},{10,... | collective-permute-start | bytes 6152 | tf_op jit(solution)/shard_map/ppermute | solution.py:50
  65.1 4.8 %collective-permute-start.14 = (f32[4,128]{1,0:T(4,128)S(1)}, f32[4,128]{1,0:T(4,128)S(1)}, u32[]{:S(2)}, u32[]{:S(2)}) collective-permute-start(f32[4,128]{1,0:T(4,128)S(1)} %get-tuple-element.44), channel_id=1, source_target_pairs={{0,1},{1,0},{2,3},{3,2},{4,5},{5,4},{6,7},{7,6},{8,9},{9,8},{10,11... | collective-permute-start | bytes 6152 | tf_op jit(solution)/shard_map/ppermute | solution.py:50
  75.8 12.1 %all-to-all-start.1 = ((f32[32,3,128]{2,1,0:T(4,128)}), f32[32,3,128]{2,1,0:T(4,128)S(1)}, u32[]{:S(2)}, u32[]{:S(2)}) async-start(f32[32,3,128]{2,1,0:T(4,128)} %bitcast.82), calls=%async_computation.1 | async-start | bytes 131072 | tf_op jit(solution)/shard_map/all_to_all | solution.py:419
  89.9 7.9 %collective-permute-start.19 = (bf16[32,4096]{1,0:T(8,128)(2,1)S(1)}, bf16[32,4096]{1,0:T(8,128)(2,1)S(1)}, u32[]{:S(2)}, u32[]{:S(2)}) collective-permute-start(bf16[32,4096]{1,0:T(8,128)(2,1)S(1)} %get-tuple-element.27.a_half), channel_id=1, source_target_pairs={{0,16},{8,24},{16,0},{24,8},{1,17},{9,25},{17,1},{25,9},{2,18},{10... | collective-permute-start | bytes 786440 | tf_op jit(solution)/shard_map/ppermute | solution.py:50
  90.7 7.8 %collective-permute-start.20 = (bf16[32,4096]{1,0:T(8,128)(2,1)S(1)}, bf16[32,4096]{1,0:T(8,128)(2,1)S(1)}, u32[]{:S(2)}, u32[]{:S(2)}) collective-permute-start(bf16[32,4096]{1,0:T(8,128)(2,1)S(1)} %get-tuple-element.28.b_half), channel_id=1, source_target_pairs={{0,8},{8,0},{16,24},{24,16},{1,9},{9,1},{17,25},{25,17},{2,10},{10... | collective-permute-start | bytes 786440 | tf_op jit(solution)/shard_map/ppermute | solution.py:50
  130.4 13.1 %collective-permute-start.21 = (bf16[32,4096]{1,0:T(8,128)(2,1)}, bf16[32,4096]{1,0:T(8,128)(2,1)}, u32[]{:S(2)}, u32[]{:S(2)}) collective-permute-start(bf16[32,4096]{1,0:T(8,128)(2,1)} %get-tuple-element.31), channel_id=1, source_target_pairs={{0,16},{8,24},{16,0},{24,8},{1,17},{9,25},{17,1},{25,9},{2,18},{10... | collective-permute-start | bytes 786440 | tf_op jit(solution)/shard_map/ppermute | solution.py:50
  131.1 31.8 %all-to-all-start.4 = ((f32[32,8,8,128]{3,2,1,0:T(8,128)}), f32[32,8,8,128]{3,2,1,0:T(8,128)}, u32[]{:S(2)}, u32[]{:S(2)}) async-start(f32[32,8,8,128]{3,2,1,0:T(8,128)} %bitcast.80), calls=%async_computation.4 | async-start | bytes 2097152 | tf_op jit(solution)/shard_map/all_to_all | solution.py:429
  134.6 17.5 %collective-permute-start.23 = (bf16[32,4096]{1,0:T(8,128)(2,1)S(1)}, bf16[32,4096]{1,0:T(8,128)(2,1)S(1)}, u32[]{:S(2)}, u32[]{:S(2)}) collective-permute-start(bf16[32,4096]{1,0:T(8,128)(2,1)S(1)} %copy-done.9), channel_id=1, source_target_pairs={{0,8},{8,0},{16,24},{24,16},{1,9},{9,1},{17,25},{25,17},{2,10},{10... | collective-permute-start | bytes 786440 | tf_op jit(solution)/shard_map/ppermute | solution.py:50
  144.7 14.5 %collective-permute-start.22 = (bf16[32,4096]{1,0:T(8,128)(2,1)S(1)}, bf16[32,4096]{1,0:T(8,128)(2,1)S(1)}, u32[]{:S(2)}, u32[]{:S(2)}) collective-permute-start(bf16[32,4096]{1,0:T(8,128)(2,1)S(1)} %multiply_convert_fusion.1), channel_id=1, source_target_pairs={{0,8},{8,0},{16,24},{24,16},{1,9},{9,1},{17,25},{25,17},{2,10},{10... | collective-permute-start | bytes 786440 | tf_op jit(solution)/shard_map/ppermute | solution.py:50
  152.2 9.1 %collective-permute-start.24 = (bf16[32,4096]{1,0:T(8,128)(2,1)S(1)}, bf16[32,4096]{1,0:T(8,128)(2,1)S(1)}, u32[]{:S(2)}, u32[]{:S(2)}) collective-permute-start(bf16[32,4096]{1,0:T(8,128)(2,1)S(1)} %multiply_convert_fusion), channel_id=1, source_target_pairs={{0,16},{8,24},{16,0},{24,8},{1,17},{9,25},{17,1},{25,9},{2,18},{10... | collective-permute-start | bytes 786440 | tf_op jit(solution)/shard_map/ppermute | solution.py:50
  (29 other events, 345.2 us)

commit v7 on v6

--- a/solution.py
+++ b/solution.py
@@ -19,6 +19,7 @@
 
 ALL = ("row", "col", "vol")
 SPOT_ROWS = 16
+PARTS = 2
 VMEM_BYTES = 16 * 2 ** 20
 
 
@@ -56,7 +57,8 @@
     targets = panel.shape[0]
     width = nodes // rows
 
-    def body(density_ref, panel_ref, part_ref, *rest):
+    def body(density_ref, panel_ref, *rest):
+        part_refs, rest = rest[:cols], rest[cols:]
         quarters = rest[:rows]
         nodes_ref, panel_buf, total_ref, sems = rest[rows:]
         r0, c0, v0 = (lax.axis_index(a) for a in ALL)
@@ -89,17 +91,17 @@
             for kr in range(rows):
                 for kv in range(vols):
                     owner = ((r0 ^ kr) * cols + (c0 ^ kc)) * vols + (v0 ^ kv)
-                    part_ref[kc, kr, kv:kv + 1] = total_ref[pl.ds(owner, 1)]
+                    part_refs[kc][kr, kv:kv + 1] = total_ref[pl.ds(owner, 1)]
         for copy in stores:
             copy.wait()
 
     hbm = pl.BlockSpec(memory_space=pltpu.HBM)
     return pl.pallas_call(
         body,
-        out_shape=[jax.ShapeDtypeStruct((cols, rows, vols, targets), jnp.float32)]
+        out_shape=[jax.ShapeDtypeStruct((rows, vols, targets), jnp.float32)] * cols
         + [jax.ShapeDtypeStruct((targets, width), panel.dtype)] * rows,
         in_specs=[hbm, hbm],
-        out_specs=[pl.BlockSpec(memory_space=pltpu.VMEM)] + [hbm] * rows,
+        out_specs=[pl.BlockSpec(memory_space=pltpu.VMEM)] * cols + [hbm] * rows,
         scratch_shapes=[
             pltpu.VMEM((rows, excitations, width), jnp.float32),
             pltpu.VMEM((rows, targets, width), panel.dtype),
@@ -305,14 +307,15 @@
     )(*operands)
 
 
-def update_call(flux, panels):
-    excitations, width = flux.shape[0], panels[0].shape[1]
+def update_call(flux, panels, part, parts):
+    excitations, width = flux.shape[0], panels[0].shape[1] // parts
+    span = slice(part * width, (part + 1) * width)
 
     def body(flux_ref, a_own, a_mate, b_own, b_mate, a_ref, b_ref):
         fluxes = [flux_ref[:, k, :].astype(jnp.bfloat16) for k in range(len(MATES))]
         for out, own, mate, k in ((a_ref, a_own, a_mate, 1), (b_ref, b_own, b_mate, 2)):
-            value = jnp.dot(fluxes[0], own[...], preferred_element_type=jnp.float32)
-            value += jnp.dot(fluxes[k], mate[...], preferred_element_type=jnp.float32)
+            value = jnp.dot(fluxes[0], own[:, span], preferred_element_type=jnp.float32)
+            value += jnp.dot(fluxes[k], mate[:, span], preferred_element_type=jnp.float32)
             out[...] = value.astype(jnp.bfloat16)
 
     vmem = pl.BlockSpec(memory_space=pltpu.VMEM)
@@ -326,37 +329,44 @@
     )(flux, *panels)
 
 
-def potential_call(densities, halves, mates, panels):
+def potential_call(densities, halves, mates, panels, part, before):
     excitations = densities[0].shape[0]
-    targets = panels[0].shape[0]
+    targets, width = panels[0].shape[0], panels[0].shape[1] // PARTS
+    span = slice(part * width, (part + 1) * width)
 
     def body(a_density, b_density, a_half, b_half, a_other, b_other,
-             a_own, a_mate, b_own, b_mate, out_ref):
+             a_own, a_mate, b_own, b_mate, *rest):
+        out_ref = rest[-1]
         rounded = [
-            (density[...] + RELAXATION * (half[...].astype(jnp.float32)
-                                          + other[...].astype(jnp.float32))).astype(jnp.bfloat16)
+            (density[:, span] + RELAXATION * (half[...].astype(jnp.float32)
+                                              + other[...].astype(jnp.float32))).astype(jnp.bfloat16)
             for density, half, other in (
                 (a_density, a_half, a_other), (b_density, b_half, b_other))
         ]
 
         def met(value, panel):
             return lax.dot_general(
-                value, panel[...], (((1,), (1,)), ((), ())), preferred_element_type=jnp.float32
+                value, panel[:, span], (((1,), (1,)), ((), ())), preferred_element_type=jnp.float32
             )
 
-        out_ref[:, 0, :] = met(rounded[0], a_own) + met(rounded[1], b_own)
-        out_ref[:, 1, :] = met(rounded[0], a_mate)
-        out_ref[:, 2, :] = met(rounded[1], b_mate)
+        sums = (
+            met(rounded[0], a_own) + met(rounded[1], b_own),
+            met(rounded[0], a_mate),
+            met(rounded[1], b_mate),
+        )
+        for k, value in enumerate(sums):
+            out_ref[:, k, :] = value + rest[0][:, k, :] if before is not None else value
 
     vmem = pl.BlockSpec(memory_space=pltpu.VMEM)
+    operands = [*densities, *halves, *mates, *panels] + ([] if before is None else [before])
     return pl.pallas_call(
         body,
         out_shape=jax.ShapeDtypeStruct((excitations, len(MATES), targets), jnp.float32),
-        in_specs=[vmem] * 10,
+        in_specs=[vmem] * len(operands),
         out_specs=vmem,
         compiler_params=pltpu.CompilerParams(vmem_limit_bytes=VMEM_BYTES),
         name="potential",
-    )(*densities, *halves, *mates, *panels)
+    )(*operands)
 
 
 def trace_spots(trace_count, trace_cell, targets, shape):
@@ -393,7 +403,8 @@
     def around_axis(pieces, axis):
         return [pieces[0]] + [mated(piece, axis, k) for k, piece in enumerate(pieces) if k > 0]
 
-    parts, *quarters = start_call(density, panel, shape)
+    made = start_call(density, panel, shape)
+    parts, quarters = made[:cols], made[cols:]
 
     kinds = class_index.reshape(bx * by, bz).astype(jnp.bfloat16)
     kinds = around_axis([kinds] * vols, "vol")
@@ -417,9 +428,12 @@
     volume, flux = slab_call(shape, True, slab, inverse, hit, lane, parts)
     flux = flux.reshape(excitations, len(MATES), targets)
     flux = lax.all_to_all(flux, ALL, 0, 0, tiled=True)
-    halves = update_call(flux, panels)
-    mates = [mated(halves[0], "row", 2), mated(halves[1], "row", 1)]
-    parts = potential_call(densities, halves, mates, panels)
+    halves, mates, parts = [], [], None
+    for part in range(PARTS):
+        halves.append(update_call(flux, panels, part, PARTS))
+        mates.append([mated(halves[part][0], "row", 2), mated(halves[part][1], "row", 1)])
+    for part in range(PARTS):
+        parts = potential_call(densities, halves[part], mates[part], panels, part, parts)
     parts = lax.all_to_all(parts, ALL, 0, 0, tiled=True)
     parts = parts.reshape(rows, blocks, len(MATES), targets)
     volume, flux = slab_call(shape, False, slab, inverse, hit, lane, parts, volume)
@@ -428,11 +442,16 @@
     volume = volume.reshape(excitations, bx, by, bz)
     volume = lax.all_to_all(volume, ALL, 0, 0, tiled=True)
     volume = landed_call(volume)
-    ends = update_call(flux, panels)
+    ends = update_call(flux, panels, 0, 1)
     end_mates = [mated(ends[0], "row", 2), mated(ends[1], "row", 1)]
     totals = []
-    for group in zip(halves, mates, ends, end_mates):
-        a, b, c, d = (value.astype(jnp.float32) for value in group)
+    for group in range(2):
+        firsts = [
+            jnp.concatenate([pair[group] for pair in pairs], axis=1) for pairs in (halves, mates)
+        ]
+        a, b, c, d = (
+            value.astype(jnp.float32) for value in (*firsts, ends[group], end_mates[group])
+        )
         totals.append((RELAXATION * ((a + b) + (c + d))).astype(jnp.bfloat16))
     moved = [mated(totals[0], "row", 1), mated(totals[1], "row", 2)]
     change = [

time: 167 us -> 166 us (level)
  waiting for transfers between devices: 66.5 us -> 60.8 us
  starting transfers between devices: 39 us -> 42.1 us
  Pallas kernels: 31.3 us -> 33.9 us
    ppermute x25 -> x27, waiting for transfers between devices: 59.1 us -> 53.4 us  [mated(): lax.ppermute(value, axis, [(i, i ^ mate) for i in range(lax.axis_size(axi...]
    ppermute x25 -> x27, starting transfers between devices: 25 us -> 27.1 us  [mated(): lax.ppermute(value, axis, [(i, i ^ mate) for i in range(lax.axis_size(axi...]
    pallas_call x1 -> x2, Pallas kernels: 2.83 us -> 4.18 us  [potential_call(): pl.pallas_call(body, out_shape=jax.ShapeDtypeStruct((excitations, len(MAT...]
    pallas_call x2 -> x3, Pallas kernels: 4.38 us -> 5.69 us  [update_call(): pl.pallas_call(body, out_shape=[jax.ShapeDtypeStruct((excitations, width)...]
  transfers between devices with their start and end apart: 28 -> 30, of which waited for: 12 -> 14; matrix products, arithmetic and copies ran while one was open for 3% -> 3% of each run, Pallas kernels for 9% -> 11%
where the time goes in v7:
time: 166 us; the launch traced here: 165 us
  waiting for transfers between devices  60.8 us (37%)
  starting transfers between devices  42.1 us (25%)
  Pallas kernels  33.9 us (20%)
  blocking collectives  19.9 us (12%)
  other arithmetic  4.19 us (3%)
  local copies, waits for them, and re-layouts  2.7 us (2%)
    ppermute x27, waiting for transfers between devices, mated(): lax.ppermute(value, axis, [(i, i ^ mate) for i in range(lax.axis_size(axi...  53.4 us
    ppermute x27, starting transfers between devices, mated(): lax.ppermute(value, axis, [(i, i ^ mate) for i in range(lax.axis_size(axi...  27.1 us
    pallas_call x2, Pallas kernels, slab_call(): pl.pallas_call(body, out_shape=[field, fluxes], in_specs=[vmem] * len(ope...  11.4 us
    all_to_all x1, blocking collectives, split_by_excitation(): flux = lax.all_to_all(flux, ALL, 0, 0, tiled=True)  10 us
    all_to_all x1, blocking collectives, split_by_excitation(): parts = lax.all_to_all(parts, ALL, 0, 0, tiled=True)  9.88 us
    all_to_all x1, waiting for transfers between devices, split_by_excitation(): flux = lax.all_to_all(flux, ALL, 0, 0, tiled=True)  7.47 us
    all_to_all x1, starting transfers between devices, split_by_excitation(): slab = lax.all_to_all(source, ALL, 0, 0, tiled=True)  7.46 us
    pallas_call x3, Pallas kernels, update_call(): pl.pallas_call(body, out_shape=[jax.ShapeDtypeStruct((excitations, width)...  5.69 us
  transfers between devices with their start and end apart: 30, of which 14 were waited for; matrix products, arithmetic and copies ran while one was open for 3% of the time, Pallas kernels for 11%

profile of v7, /device:TPU:0, one launch (start us, length us, event | category | flops | bytes accessed | tf_op | source)
XLA Modules:
  0.0 164.7 jit_solution(7523879607060806490)
XLA Ops:
  0.6 7.5 %all-to-all-start = ((f32[32,8,8,128]{3,2,1,0:T(8,128)}), f32[32,8,8,128]{3,2,1,0:T(8,128)}, u32[]{:S(2)}, u32[]{:S(2)}) async-start(f32[32,8,8,128]{3,2,1,0:T(8,128)} %param.9), calls=%async_computation | async-start | bytes 2097152 | tf_op jit(solution)/shard_map/all_to_all | solution.py:412
  8.2 3.6 %collective-permute-start.2 = (bf16[64,128]{1,0:T(8,128)(2,1)S(1)}, bf16[64,128]{1,0:T(8,128)(2,1)S(1)}, u32[]{:S(2)}, u32[]{:S(2)}) collective-permute-start(bf16[64,128]{1,0:T(8,128)(2,1)S(1)} %get-tuple-element.41), channel_id=1, source_target_pairs={{0,3},{1,2},{2,1},{3,0},{4,7},{5,6},{6,5},{7,4},{8,11},{9,10},{10,... | collective-permute-start | bytes 49160 | tf_op jit(solution)/shard_map/ppermute | solution.py:51
  12.6 5.2 %start.1 = (f32[4,4,128]{2,1,0:T(4,128)}, f32[4,4,128]{2,1,0:T(4,128)}, bf16[128,4096]{1,0:T(8,128)(2,1)}, bf16[128,4096]{1,0:T(8,128)(2,1)}, bf16[128,4096]{1,0:T(8,128)(2,1)}, /*index=5*/bf16[128,4096]{1,0:T(8,128)(2,1)}) custom-call(f32[32,16384]{1,0:T(8,128)} %density_ref.1, bf16[128,16384]{1,0:T(8,128)(2,1)} %panel_ref.1), custom_call_target="tpu_custom_call" | custom-call | tf_op jit(solution)/shard_map/start/pallas_call | solution.py:99
  22.5 4.2 %collective-permute-done = bf16[64,128]{1,0:T(8,128)(2,1)S(1)} collective-permute-done((bf16[64,128]{1,0:T(8,128)(2,1)S(1)}, bf16[64,128]{1,0:T(8,128)(2,1)S(1)}, u32[]{:S(2)}, u32[]{:S(2)}) %collective-permute-start) | collective-permute-done | bytes 16416 | tf_op jit(solution)/shard_map/ppermute | solution.py:51
  26.7 8.9 %collective-permute-done.1 = bf16[64,128]{1,0:T(8,128)(2,1)S(1)} collective-permute-done((bf16[64,128]{1,0:T(8,128)(2,1)S(1)}, bf16[64,128]{1,0:T(8,128)(2,1)S(1)}, u32[]{:S(2)}, u32[]{:S(2)}) %collective-permute-start.1) | collective-permute-done | bytes 16416 | tf_op jit(solution)/shard_map/ppermute | solution.py:51
  35.7 2.5 %collective-permute-start.13 = (f32[4,128]{1,0:T(4,128)S(1)}, f32[4,128]{1,0:T(4,128)S(1)}, u32[]{:S(2)}, u32[]{:S(2)}) collective-permute-start(f32[4,128]{1,0:T(4,128)S(1)} %get-tuple-element.53), channel_id=1, source_target_pairs={{0,24},{8,16},{16,8},{24,0},{1,25},{9,17},{17,9},{25,1},{2,26},{10... | collective-permute-start | bytes 6152 | tf_op jit(solution)/shard_map/ppermute | solution.py:51
  38.7 10.0 %collective-permute-done.13 = f32[4,128]{1,0:T(4,128)S(1)} collective-permute-done((f32[4,128]{1,0:T(4,128)S(1)}, f32[4,128]{1,0:T(4,128)S(1)}, u32[]{:S(2)}, u32[]{:S(2)}) %collective-permute-start.13) | collective-permute-done | bytes 2080 | tf_op jit(solution)/shard_map/ppermute | solution.py:51
  57.7 2.5 %collective-permute-start.16 = (f32[4,128]{1,0:T(4,128)S(1)}, f32[4,128]{1,0:T(4,128)S(1)}, u32[]{:S(2)}, u32[]{:S(2)}) collective-permute-start(f32[4,128]{1,0:T(4,128)S(1)} %get-tuple-element.48), channel_id=1, source_target_pairs={{0,3},{1,2},{2,1},{3,0},{4,7},{5,6},{6,5},{7,4},{8,11},{9,10},{10,... | collective-permute-start | bytes 6152 | tf_op jit(solution)/shard_map/ppermute | solution.py:51
  62.8 4.1 %prepare.1 = (f32[32,4,16,128]{3,2,1,0:T(8,128)}, bf16[4,512,128]{2,1,0:T(8,128)(2,1)}, bf16[4,128,128]{2,1,0:T(8,128)(2,1)}) custom-call(f32[16]{0:T(128)} %values_ref.1, bf16[272,128]{1,0:T(8,128)(2,1)} %copy-done.18, bf16[272,128]{1,0:T(8,128)(2,1)} %copy-done.22, bf16[272,128]{1,0:T(8,128)(2,1)} %copy-done.21, bf16[272,128]{1,0:T(8,128)(2,1)} %copy-done.20, ...), custom_call_target="tpu_custom_call" | custom-call | tf_op jit(solution)/shard_map/prepare/pallas_call | solution.py:151
  67.5 5.3 %slab_first.1 = (f32[34,4,16,128]{3,2,1,0:T(8,128)}, f32[4,8,3,128]{3,2,1,0:T(4,128)}) custom-call(f32[4,8,8,8,128]{4,3,2,1,0:T(8,128)} %bitcast.source_ref, f32[32,4,16,128]{3,2,1,0:T(8,128)} %get-tuple-element.21.inverse_ref, bf16[4,512,128]{2,1,0:T(8,128)(2,1)} %get-tuple-element.22.hit_ref, bf16[4,128,128]{2,1,0:T(8,128)(2,1)} %get-tuple-element.23.lane_ref, ...), custom_call_target="tpu_custom_call" | custom-call | tf_op jit(solution)/shard_map/slab_first/pallas_call | solution.py:300
  72.8 4.1 %all-to-all-start.1 = ((f32[32,3,128]{2,1,0:T(4,128)}), f32[32,3,128]{2,1,0:T(4,128)S(1)}, u32[]{:S(2)}, u32[]{:S(2)}) async-start(f32[32,3,128]{2,1,0:T(4,128)} %bitcast.78), calls=%async_computation.1 | async-start | bytes 131072 | tf_op jit(solution)/shard_map/all_to_all | solution.py:430
  76.9 7.5 %all-to-all-done.1.flux_ref = f32[32,3,128]{2,1,0:T(4,128)S(1)} async-done(((f32[32,3,128]{2,1,0:T(4,128)}), f32[32,3,128]{2,1,0:T(4,128)S(1)}, u32[]{:S(2)}, u32[]{:S(2)}) %all-to-all-start.1) | async-done | bytes 49184 | tf_op jit(solution)/shard_map/all_to_all | solution.py:430
  91.9 2.1 %collective-permute-done.19.a_other = bf16[32,2048]{1,0:T(8,128)(2,1)S(1)} collective-permute-done((bf16[32,2048]{1,0:T(8,128)(2,1)S(1)}, bf16[32,2048]{1,0:T(8,128)(2,1)S(1)}, u32[]{:S(2)}, u32[]{:S(2)}) %collective-permute-start.19) | collective-permute-done | bytes 131104 | tf_op jit(solution)/shard_map/ppermute | solution.py:51
  95.4 2.1 %potential.2.rest_0_ = f32[32,3,128]{2,1,0:T(4,128)S(1)} custom-call(f32[32,4096]{1,0:T(8,128)S(1)} %get-tuple-element.43.a_density, f32[32,4096]{1,0:T(8,128)S(1)} %get-tuple-element.42.b_density, bf16[32,2048]{1,0:T(8,128)(2,1)S(1)} %get-tuple-element.31.a_half, bf16[32,2048]{1,0:T(8,128)(2,1)S(1)} %get-tuple-element.34.b_half, ...), custom_call_target="tpu_custom_call" | custom-call | tf_op jit(solution)/shard_map/potential/pallas_call | solution.py:362
  97.6 2.1 %potential.3 = f32[32,3,128]{2,1,0:T(4,128)S(1)} custom-call(f32[32,4096]{1,0:T(8,128)S(1)} %get-tuple-element.43.a_density, f32[32,4096]{1,0:T(8,128)S(1)} %get-tuple-element.42.b_density, bf16[32,2048]{1,0:T(8,128)(2,1)S(1)} %get-tuple-element.32.a_half, bf16[32,2048]{1,0:T(8,128)(2,1)S(1)} %get-tuple-element.33.b_half, ...), custom_call_target="tpu_custom_call" | custom-call | tf_op jit(solution)/shard_map/potential/pallas_call | solution.py:362
  99.7 9.9 %all_to_all.25 = f32[32,3,128]{2,1,0:T(4,128)} all-to-all(f32[32,3,128]{2,1,0:T(4,128)S(1)} %potential.3), channel_id=1, replica_groups=mesh['row'=4,'col'=2,'vol'=4] {'row','col','vol'}, dimensions={0} | all-to-all | bytes 98304 | tf_op jit(solution)/shard_map/all_to_all | solution.py:437
  109.6 6.1 %slab_last.1 = (f32[4,8,8,8,128]{4,3,2,1,0:T(8,128)}, f32[4,8,3,128]{3,2,1,0:T(4,128)}) custom-call(f32[4,8,8,8,128]{4,3,2,1,0:T(8,128)} %bitcast.source_ref, f32[32,4,16,128]{3,2,1,0:T(8,128)} %get-tuple-element.21.inverse_ref, bf16[4,512,128]{2,1,0:T(8,128)(2,1)} %get-tuple-element.22.hit_ref, bf16[4,128,128]{2,1,0:T(8,128)(2,1)} %get-tuple-element.23.lane_ref, ...), custom_call_target="tpu_custom_call" | custom-call | tf_op jit(solution)/shard_map/slab_last/pallas_call | solution.py:300
  115.7 10.0 %all_to_all.26.flux_ref = f32[32,3,128]{2,1,0:T(4,128)S(1)} all-to-all(f32[32,3,128]{2,1,0:T(4,128)} %bitcast.79), channel_id=1, replica_groups=mesh['row'=4,'col'=2,'vol'=4] {'row','col','vol'}, dimensions={0} | all-to-all | bytes 98304 | tf_op jit(solution)/shard_map/all_to_all | solution.py:441
  125.7 2.3 %update.5 = (bf16[32,4096]{1,0:T(8,128)(2,1)}, bf16[32,4096]{1,0:T(8,128)(2,1)S(1)}) custom-call(f32[32,3,128]{2,1,0:T(4,128)S(1)} %all_to_all.26.flux_ref, bf16[128,4096]{1,0:T(8,128)(2,1)S(1)} %copy-done, bf16[128,4096]{1,0:T(8,128)(2,1)S(1)} %collective-permute-done.17.a_mate, bf16[128,4096]{1,0:T(8,128)(2,1)S(1)} %copy-done.1, ...), custom_call_target="tpu_custom_call" | custom-call | tf_op jit(solution)/shard_map/update/pallas_call | solution.py:322
  129.6 3.4 %all-to-all-start.4 = ((f32[32,8,8,128]{3,2,1,0:T(8,128)}), f32[32,8,8,128]{3,2,1,0:T(8,128)}, u32[]{:S(2)}, u32[]{:S(2)}) async-start(f32[32,8,8,128]{3,2,1,0:T(8,128)} %bitcast.76), calls=%async_computation.4 | async-start | bytes 2097152 | tf_op jit(solution)/shard_map/all_to_all | solution.py:443
  134.6 7.3 %collective-permute-done.23 = bf16[32,4096]{1,0:T(8,128)(2,1)} collective-permute-done((bf16[32,4096]{1,0:T(8,128)(2,1)}, bf16[32,4096]{1,0:T(8,128)(2,1)}, u32[]{:S(2)}, u32[]{:S(2)}) %collective-permute-start.23) | collective-permute-done | bytes 262176 | tf_op jit(solution)/shard_map/ppermute | solution.py:51
  143.2 7.3 %collective-permute-done.25 = bf16[32,4096]{1,0:T(8,128)(2,1)S(1)} collective-permute-done((bf16[32,4096]{1,0:T(8,128)(2,1)S(1)}, bf16[32,4096]{1,0:T(8,128)(2,1)S(1)}, u32[]{:S(2)}, u32[]{:S(2)}) %collective-permute-start.25) | collective-permute-done | bytes 262176 | tf_op jit(solution)/shard_map/ppermute | solution.py:51
  152.2 5.5 %collective-permute-done.24 = bf16[32,4096]{1,0:T(8,128)(2,1)S(1)} collective-permute-done((bf16[32,4096]{1,0:T(8,128)(2,1)S(1)}, bf16[32,4096]{1,0:T(8,128)(2,1)S(1)}, u32[]{:S(2)}, u32[]{:S(2)}) %collective-permute-start.24) | collective-permute-done | bytes 262176 | tf_op jit(solution)/shard_map/ppermute | solution.py:51
  161.4 3.4 %landed.1 = f32[32,8,8,128]{3,2,1,0:T(8,128)} custom-call(f32[32,8,8,128]{3,2,1,0:T(8,128)} %all-to-all-done.4.in_ref), custom_call_target="tpu_custom_call" | custom-call | tf_op jit(solution)/shard_map/landed/pallas_call | solution.py:172
  (133 shorter events, 36.9 us)
Async XLA Ops:
  0.6 66.3 %all-to-all-start = ((f32[32,8,8,128]{3,2,1,0:T(8,128)}), f32[32,8,8,128]{3,2,1,0:T(8,128)}, u32[]{:S(2)}, u32[]{:S(2)}) async-start(f32[32,8,8,128]{3,2,1,0:T(8,128)} %param.9), calls=%async_computation | async-start | bytes 2097152 | tf_op jit(solution)/shard_map/all_to_all | solution.py:412
  8.2 27.4 %collective-permute-start.2 = (bf16[64,128]{1,0:T(8,128)(2,1)S(1)}, bf16[64,128]{1,0:T(8,128)(2,1)S(1)}, u32[]{:S(2)}, u32[]{:S(2)}) collective-permute-start(bf16[64,128]{1,0:T(8,128)(2,1)S(1)} %get-tuple-element.41), channel_id=1, source_target_pairs={{0,3},{1,2},{2,1},{3,0},{4,7},{5,6},{6,5},{7,4},{8,11},{9,10},{10,... | collective-permute-start | bytes 49160 | tf_op jit(solution)/shard_map/ppermute | solution.py:51
  11.8 23.8 %collective-permute-start.1 = (bf16[64,128]{1,0:T(8,128)(2,1)S(1)}, bf16[64,128]{1,0:T(8,128)(2,1)S(1)}, u32[]{:S(2)}, u32[]{:S(2)}) collective-permute-start(bf16[64,128]{1,0:T(8,128)(2,1)S(1)} %get-tuple-element.41), channel_id=1, source_target_pairs={{0,2},{1,3},{2,0},{3,1},{4,6},{5,7},{6,4},{7,5},{8,10},{9,11},{10,... | collective-permute-start | bytes 49160 | tf_op jit(solution)/shard_map/ppermute | solution.py:51
  11.8 14.9 %collective-permute-start = (bf16[64,128]{1,0:T(8,128)(2,1)S(1)}, bf16[64,128]{1,0:T(8,128)(2,1)S(1)}, u32[]{:S(2)}, u32[]{:S(2)}) collective-permute-start(bf16[64,128]{1,0:T(8,128)(2,1)S(1)} %get-tuple-element.41), channel_id=1, source_target_pairs={{0,1},{1,0},{2,3},{3,2},{4,5},{5,4},{6,7},{7,6},{8,9},{9,8},{10,11... | collective-permute-start | bytes 49160 | tf_op jit(solution)/shard_map/ppermute | solution.py:51
  18.0 58.9 %collective-permute-start.17 = (bf16[128,4096]{1,0:T(8,128)(2,1)}, bf16[128,4096]{1,0:T(8,128)(2,1)S(1)}, u32[]{:S(2)}, u32[]{:S(2)}) collective-permute-start(bf16[128,4096]{1,0:T(8,128)(2,1)} %get-tuple-element.28), channel_id=1, source_target_pairs={{0,8},{8,0},{16,24},{24,16},{1,9},{9,1},{17,25},{25,17},{2,10},{10... | collective-permute-start | bytes 3145736 | tf_op jit(solution)/shard_map/ppermute | solution.py:51
  20.3 56.6 %collective-permute-start.18 = (bf16[128,4096]{1,0:T(8,128)(2,1)}, bf16[128,4096]{1,0:T(8,128)(2,1)}, u32[]{:S(2)}, u32[]{:S(2)}) collective-permute-start(bf16[128,4096]{1,0:T(8,128)(2,1)} %get-tuple-element.30), channel_id=1, source_target_pairs={{0,16},{8,24},{16,0},{24,8},{1,17},{9,25},{17,1},{25,9},{2,18},{10... | collective-permute-start | bytes 3145736 | tf_op jit(solution)/shard_map/ppermute | solution.py:51
  35.6 17.1 %collective-permute-start.6 = (bf16[272,128]{1,0:T(8,128)(2,1)S(1)}, bf16[272,128]{1,0:T(8,128)(2,1)S(1)}, u32[]{:S(2)}, u32[]{:S(2)}) collective-permute-start(bf16[272,128]{1,0:T(8,128)(2,1)S(1)} %constant_dynamic-update-slice_fusion.refs_0_), channel_id=1, source_target_pairs={{0,4},{4,0},{1,5},{5,1},{2,6},{6,2},{3,7},{7,3},{8,12},{12,8},{9,1... | collective-permute-start | bytes 208904 | tf_op jit(solution)/shard_map/ppermute | solution.py:51
  35.7 13.0 %collective-permute-start.13 = (f32[4,128]{1,0:T(4,128)S(1)}, f32[4,128]{1,0:T(4,128)S(1)}, u32[]{:S(2)}, u32[]{:S(2)}) collective-permute-start(f32[4,128]{1,0:T(4,128)S(1)} %get-tuple-element.53), channel_id=1, source_target_pairs={{0,24},{8,16},{16,8},{24,0},{1,25},{9,17},{17,9},{25,1},{2,26},{10... | collective-permute-start | bytes 6152 | tf_op jit(solution)/shard_map/ppermute | solution.py:51
  38.2 11.7 %collective-permute-start.12 = (f32[4,128]{1,0:T(4,128)S(1)}, f32[4,128]{1,0:T(4,128)S(1)}, u32[]{:S(2)}, u32[]{:S(2)}) collective-permute-start(f32[4,128]{1,0:T(4,128)S(1)} %get-tuple-element.54), channel_id=1, source_target_pairs={{0,16},{8,24},{16,0},{24,8},{1,17},{9,25},{17,1},{25,9},{2,18},{10... | collective-permute-start | bytes 6152 | tf_op jit(solution)/shard_map/ppermute | solution.py:51
  49.9 5.9 %collective-permute-start.5 = (bf16[272,128]{1,0:T(8,128)(2,1)S(1)}, bf16[272,128]{1,0:T(8,128)(2,1)S(1)}, u32[]{:S(2)}, u32[]{:S(2)}) collective-permute-start(bf16[272,128]{1,0:T(8,128)(2,1)S(1)} %constant_dynamic-update-slice_fusion.refs_0_), channel_id=1, source_target_pairs={{0,24},{8,16},{16,8},{24,0},{1,25},{9,17},{17,9},{25,1},{2,26},{10... | collective-permute-start | bytes 208904 | tf_op jit(solution)/shard_map/ppermute | solution.py:51
  52.7 4.3 %collective-permute-start.3 = (bf16[272,128]{1,0:T(8,128)(2,1)S(1)}, bf16[272,128]{1,0:T(8,128)(2,1)S(1)}, u32[]{:S(2)}, u32[]{:S(2)}) collective-permute-start(bf16[272,128]{1,0:T(8,128)(2,1)S(1)} %constant_dynamic-update-slice_fusion.refs_0_), channel_id=1, source_target_pairs={{0,8},{8,0},{16,24},{24,16},{1,9},{9,1},{17,25},{25,17},{2,10},{10... | collective-permute-start | bytes 208904 | tf_op jit(solution)/shard_map/ppermute | solution.py:51
  57.7 9.2 %collective-permute-start.16 = (f32[4,128]{1,0:T(4,128)S(1)}, f32[4,128]{1,0:T(4,128)S(1)}, u32[]{:S(2)}, u32[]{:S(2)}) collective-permute-start(f32[4,128]{1,0:T(4,128)S(1)} %get-tuple-element.48), channel_id=1, source_target_pairs={{0,3},{1,2},{2,1},{3,0},{4,7},{5,6},{6,5},{7,4},{8,11},{9,10},{10,... | collective-permute-start | bytes 6152 | tf_op jit(solution)/shard_map/ppermute | solution.py:51
  60.2 6.6 %collective-permute-start.15 = (f32[4,128]{1,0:T(4,128)S(1)}, f32[4,128]{1,0:T(4,128)S(1)}, u32[]{:S(2)}, u32[]{:S(2)}) collective-permute-start(f32[4,128]{1,0:T(4,128)S(1)} %get-tuple-element.49), channel_id=1, source_target_pairs={{0,2},{1,3},{2,0},{3,1},{4,6},{5,7},{6,4},{7,5},{8,10},{9,11},{10,... | collective-permute-start | bytes 6152 | tf_op jit(solution)/shard_map/ppermute | solution.py:51
  61.7 5.2 %collective-permute-start.14 = (f32[4,128]{1,0:T(4,128)S(1)}, f32[4,128]{1,0:T(4,128)S(1)}, u32[]{:S(2)}, u32[]{:S(2)}) collective-permute-start(f32[4,128]{1,0:T(4,128)S(1)} %get-tuple-element.50), channel_id=1, source_target_pairs={{0,1},{1,0},{2,3},{3,2},{4,5},{5,4},{6,7},{7,6},{8,9},{9,8},{10,11... | collective-permute-start | bytes 6152 | tf_op jit(solution)/shard_map/ppermute | solution.py:51
  72.8 11.6 %all-to-all-start.1 = ((f32[32,3,128]{2,1,0:T(4,128)}), f32[32,3,128]{2,1,0:T(4,128)S(1)}, u32[]{:S(2)}, u32[]{:S(2)}) async-start(f32[32,3,128]{2,1,0:T(4,128)} %bitcast.78), calls=%async_computation.1 | async-start | bytes 131072 | tf_op jit(solution)/shard_map/all_to_all | solution.py:430
  86.0 11.6 %collective-permute-start.20 = (bf16[32,2048]{1,0:T(8,128)(2,1)S(1)}, bf16[32,2048]{1,0:T(8,128)(2,1)S(1)}, u32[]{:S(2)}, u32[]{:S(2)}) collective-permute-start(bf16[32,2048]{1,0:T(8,128)(2,1)S(1)} %get-tuple-element.32.a_half), channel_id=1, source_target_pairs={{0,16},{8,24},{16,0},{24,8},{1,17},{9,25},{17,1},{25,9},{2,18},{10... | collective-permute-start | bytes 393224 | tf_op jit(solution)/shard_map/ppermute | solution.py:51
  86.8 10.8 %collective-permute-start.21 = (bf16[32,2048]{1,0:T(8,128)(2,1)S(1)}, bf16[32,2048]{1,0:T(8,128)(2,1)S(1)}, u32[]{:S(2)}, u32[]{:S(2)}) collective-permute-start(bf16[32,2048]{1,0:T(8,128)(2,1)S(1)} %get-tuple-element.33.b_half), channel_id=1, source_target_pairs={{0,8},{8,0},{16,24},{24,16},{1,9},{9,1},{17,25},{25,17},{2,10},{10... | collective-permute-start | bytes 393224 | tf_op jit(solution)/shard_map/ppermute | solution.py:51
  89.0 5.0 %collective-permute-start.19 = (bf16[32,2048]{1,0:T(8,128)(2,1)S(1)}, bf16[32,2048]{1,0:T(8,128)(2,1)S(1)}, u32[]{:S(2)}, u32[]{:S(2)}) collective-permute-start(bf16[32,2048]{1,0:T(8,128)(2,1)S(1)} %get-tuple-element.31.a_half), channel_id=1, source_target_pairs={{0,16},{8,24},{16,0},{24,8},{1,17},{9,25},{17,1},{25,9},{2,18},{10... | collective-permute-start | bytes 393224 | tf_op jit(solution)/shard_map/ppermute | solution.py:51
  90.5 5.0 %collective-permute-start.22 = (bf16[32,2048]{1,0:T(8,128)(2,1)S(1)}, bf16[32,2048]{1,0:T(8,128)(2,1)S(1)}, u32[]{:S(2)}, u32[]{:S(2)}) collective-permute-start(bf16[32,2048]{1,0:T(8,128)(2,1)S(1)} %get-tuple-element.34.b_half), channel_id=1, source_target_pairs={{0,8},{8,0},{16,24},{24,16},{1,9},{9,1},{17,25},{25,17},{2,10},{10... | collective-permute-start | bytes 393224 | tf_op jit(solution)/shard_map/ppermute | solution.py:51
  128.8 13.1 %collective-permute-start.23 = (bf16[32,4096]{1,0:T(8,128)(2,1)}, bf16[32,4096]{1,0:T(8,128)(2,1)}, u32[]{:S(2)}, u32[]{:S(2)}) collective-permute-start(bf16[32,4096]{1,0:T(8,128)(2,1)} %get-tuple-element.37), channel_id=1, source_target_pairs={{0,16},{8,24},{16,0},{24,8},{1,17},{9,25},{17,1},{25,9},{2,18},{10... | collective-permute-start | bytes 786440 | tf_op jit(solution)/shard_map/ppermute | solution.py:51
  129.6 31.8 %all-to-all-start.4 = ((f32[32,8,8,128]{3,2,1,0:T(8,128)}), f32[32,8,8,128]{3,2,1,0:T(8,128)}, u32[]{:S(2)}, u32[]{:S(2)}) async-start(f32[32,8,8,128]{3,2,1,0:T(8,128)} %bitcast.76), calls=%async_computation.4 | async-start | bytes 2097152 | tf_op jit(solution)/shard_map/all_to_all | solution.py:443
  133.0 17.5 %collective-permute-start.25 = (bf16[32,4096]{1,0:T(8,128)(2,1)S(1)}, bf16[32,4096]{1,0:T(8,128)(2,1)S(1)}, u32[]{:S(2)}, u32[]{:S(2)}) collective-permute-start(bf16[32,4096]{1,0:T(8,128)(2,1)S(1)} %copy-done.15), channel_id=1, source_target_pairs={{0,8},{8,0},{16,24},{24,16},{1,9},{9,1},{17,25},{25,17},{2,10},{10... | collective-permute-start | bytes 786440 | tf_op jit(solution)/shard_map/ppermute | solution.py:51
  143.1 14.5 %collective-permute-start.24 = (bf16[32,4096]{1,0:T(8,128)(2,1)S(1)}, bf16[32,4096]{1,0:T(8,128)(2,1)S(1)}, u32[]{:S(2)}, u32[]{:S(2)}) collective-permute-start(bf16[32,4096]{1,0:T(8,128)(2,1)S(1)} %multiply_convert_fusion.1), channel_id=1, source_target_pairs={{0,8},{8,0},{16,24},{24,16},{1,9},{9,1},{17,25},{25,17},{2,10},{10... | collective-permute-start | bytes 786440 | tf_op jit(solution)/shard_map/ppermute | solution.py:51
  150.6 9.1 %collective-permute-start.26 = (bf16[32,4096]{1,0:T(8,128)(2,1)S(1)}, bf16[32,4096]{1,0:T(8,128)(2,1)S(1)}, u32[]{:S(2)}, u32[]{:S(2)}) collective-permute-start(bf16[32,4096]{1,0:T(8,128)(2,1)S(1)} %multiply_convert_fusion), channel_id=1, source_target_pairs={{0,16},{8,24},{16,0},{24,8},{1,17},{9,25},{17,1},{25,9},{2,18},{10... | collective-permute-start | bytes 786440 | tf_op jit(solution)/shard_map/ppermute | solution.py:51
  (38 other events, 415.8 us)

commit v8 on v7

--- a/solution.py
+++ b/solution.py
@@ -18,7 +18,7 @@
 SPECTRUM_HIGH = 2.0
 
 ALL = ("row", "col", "vol")
-SPOT_ROWS = 16
+SPOT_ROWS = 32
 PARTS = 2
 VMEM_BYTES = 16 * 2 ** 20
 
@@ -51,16 +51,18 @@
     return lax.ppermute(value, axis, [(i, i ^ mate) for i in range(lax.axis_size(axis))])
 
 
-def start_call(density, panel, shape):
+def start_call(density, panel, known, shape):
     rows, cols, vols = shape[:3]
     excitations, nodes = density.shape
     targets = panel.shape[0]
     width = nodes // rows
-
-    def body(density_ref, panel_ref, *rest):
-        part_refs, rest = rest[:cols], rest[cols:]
+    lines = known.shape[0]
+    owners = cols * vols
+
+    def body(density_ref, panel_ref, known_ref, *rest):
+        sent, rest = rest[:rows], rest[rows:]
         quarters = rest[:rows]
-        nodes_ref, panel_buf, total_ref, sems = rest[rows:]
+        nodes_ref, panel_buf, total_ref, picked_ref, sems = rest[rows:]
         r0, c0, v0 = (lax.axis_index(a) for a in ALL)
         low, high = r0 & 1, r0 >> 1
         sources = (low, low ^ 1, 2 + high, 2 + (high ^ 1))
@@ -75,6 +77,8 @@
             for copy in pair:
                 copy.start()
             loads.append(pair)
+        for k in range(rows):
+            sent[k][0:lines] = known_ref[...]
         total = jnp.zeros((targets, excitations), jnp.float32)
         for q, pair in zip(order, loads):
             for copy in pair:
@@ -87,29 +91,63 @@
                 preferred_element_type=jnp.float32,
             )
         total_ref[...] = total.T
-        for kc in range(cols):
-            for kr in range(rows):
+        for kr in range(rows):
+            for kc in range(cols):
                 for kv in range(vols):
                     owner = ((r0 ^ kr) * cols + (c0 ^ kc)) * vols + (v0 ^ kv)
-                    part_refs[kc][kr, kv:kv + 1] = total_ref[pl.ds(owner, 1)]
+                    place = kc * vols + kv
+                    picked_ref[kr, place:place + 1] = total_ref[pl.ds(owner, 1)]
+            pieces = [piece.astype(jnp.float32) for piece in parts_of(picked_ref[kr], 3)]
+            pieces.append(jnp.zeros((owners, targets), jnp.float32))
+            sent[kr][lines:] = jnp.concatenate(pieces).astype(jnp.bfloat16)
         for copy in stores:
             copy.wait()
 
     hbm = pl.BlockSpec(memory_space=pltpu.HBM)
+    vmem = pl.BlockSpec(memory_space=pltpu.VMEM)
     return pl.pallas_call(
         body,
-        out_shape=[jax.ShapeDtypeStruct((rows, vols, targets), jnp.float32)] * cols
+        out_shape=[jax.ShapeDtypeStruct((lines + 4 * owners, targets), known.dtype)] * rows
         + [jax.ShapeDtypeStruct((targets, width), panel.dtype)] * rows,
-        in_specs=[hbm, hbm],
-        out_specs=[pl.BlockSpec(memory_space=pltpu.VMEM)] * cols + [hbm] * rows,
+        in_specs=[hbm, hbm, vmem],
+        out_specs=[vmem] * rows + [hbm] * rows,
         scratch_shapes=[
             pltpu.VMEM((rows, excitations, width), jnp.float32),
             pltpu.VMEM((rows, targets, width), panel.dtype),
             pltpu.VMEM((excitations, targets), jnp.float32),
+            pltpu.VMEM((rows, owners, targets), jnp.float32),
             pltpu.SemaphoreType.DMA((3 * rows,)),
         ],
         name="start",
-    )(density, panel)
+    )(density, panel, known)
+
+
+def collect_call(shape, lines, known, other):
+    rows, cols, vols = shape[:3]
+    targets = known[0].shape[1]
+    owners = cols * vols
+    height = 4 * owners
+
+    def body(*refs):
+        ins, outs = refs[:2 * rows], refs[2 * rows:]
+        for k in range(rows):
+            own, mate = (ins[k + side * rows][...].astype(jnp.float32) for side in range(2))
+            total = jnp.zeros((vols, targets), jnp.float32)
+            for p in (2, 1, 0):
+                total += own[p * owners:p * owners + vols] + mate[p * owners + vols:(p + 1) * owners]
+            for v in range(vols):
+                outs[v][k:k + 1] = total[v:v + 1]
+
+    block = pl.BlockSpec((height, targets), lambda i: (lines // height, 0))
+    whole = pl.BlockSpec((rows, targets), lambda i: (0, 0))
+    return pl.pallas_call(
+        body,
+        grid=(1,),
+        out_shape=[jax.ShapeDtypeStruct((rows, targets), jnp.float32)] * vols,
+        in_specs=[block] * (2 * rows),
+        out_specs=[whole] * vols,
+        name="collect",
+    )(*known, *other)
 
 
 def prepare_call(shape, values, known, other):
@@ -127,7 +165,8 @@
         row_ids = lax.broadcasted_iota(jnp.int32, (height, targets), 0)
         lane_ids = lax.broadcasted_iota(jnp.int32, (bz, targets), 0)
         for k in range(rows):
-            spot = known_refs[k][vols * lines:].astype(jnp.float32).astype(jnp.int32)
+            spot = known_refs[k][vols * lines:vols * lines + SPOT_ROWS].astype(jnp.float32)
+            spot = spot.astype(jnp.int32)
             line = spot[0:1] * (blocks * by) + spot[1:2]
             hit_ref[k ^ r0] = (row_ids == line).astype(jnp.bfloat16)
             lane_ref[k ^ r0] = (lane_ids == spot[2:3]).astype(jnp.bfloat16)
@@ -137,10 +176,14 @@
 
                 def plane(kv, carry, source=refs_of[k], start=start, k=k):
                     kind = source[pl.ds(pl.multiple_of(kv * lines, lines), lines)].astype(jnp.float32)
-                    conduct = jnp.zeros((lines, bz), jnp.float32)
-                    for i in range(count):
-                        conduct = jnp.where(kind == float(i), values_ref[i], conduct)
-                    inverse = 1.0 / (MASS_TERM + 6.0 * conduct)
+                    kind = kind.astype(jnp.int32)
+                    choices, bit = [values_ref[i] for i in range(count)], 1
+                    while len(choices) > 1:
+                        odd = (kind & bit) != 0
+                        merged = [jnp.where(odd, two, one)
+                                  for one, two in zip(choices[0::2], choices[1::2])]
+                        choices, bit = merged + choices[len(merged) * 2:], bit * 2
+                    inverse = jnp.broadcast_to(choices[0], (lines, bz))
                     place = (pl.ds((k ^ r0) * bx, bx), kv ^ v0, pl.ds(start, by))
                     inverse_ref[place] = inverse.reshape(bx, by, bz)
                     return carry
@@ -162,19 +205,31 @@
 
 
 def landed_call(volume):
-    excitations = volume.shape[0]
-    few = math.gcd(excitations, 8)
-    block = pl.BlockSpec((few,) + volume.shape[1:], lambda i: (i, 0, 0, 0))
-
-    def body(in_ref, out_ref):
-        out_ref[...] = in_ref[...]
-
+    pieces = 4
+    few = volume.shape[0] // pieces
+
+    def body(in_ref, out_ref, held_ref, sems):
+        loads, stores = [], []
+        for i in range(pieces):
+            span = pl.ds(i * few, few)
+            loads.append(pltpu.make_async_copy(in_ref.at[span], held_ref.at[span], sems.at[i]))
+            stores.append(pltpu.make_async_copy(held_ref.at[span], out_ref.at[span], sems.at[pieces + i]))
+            loads[i].start()
+        for load, store in zip(loads, stores):
+            load.wait()
+            store.start()
+        for store in stores:
+            store.wait()
+
+    hbm = pl.BlockSpec(memory_space=pltpu.HBM)
     return pl.pallas_call(
         body,
-        grid=(excitations // few,),
         out_shape=jax.ShapeDtypeStruct(volume.shape, volume.dtype),
-        in_specs=[block],
-        out_specs=block,
+        in_specs=[hbm],
+        out_specs=hbm,
+        scratch_shapes=[
+            pltpu.VMEM(volume.shape, volume.dtype), pltpu.SemaphoreType.DMA((2 * pieces,))
+        ],
         name="landed",
     )(volume)
 
@@ -346,7 +401,7 @@
 
         def met(value, panel):
             return lax.dot_general(
-                value, panel[:, span], (((1,), (1,)), ((), ())), preferred_element_type=jnp.float32
+                panel[:, span], value, (((1,), (1,)), ((), ())), preferred_element_type=jnp.float32
             )
 
         sums = (
@@ -355,6 +410,7 @@
             met(rounded[1], b_mate),
         )
         for k, value in enumerate(sums):
+            value = value.T
             out_ref[:, k, :] = value + rest[0][:, k, :] if before is not None else value
 
     vmem = pl.BlockSpec(memory_space=pltpu.VMEM)
@@ -403,28 +459,27 @@
     def around_axis(pieces, axis):
         return [pieces[0]] + [mated(piece, axis, k) for k, piece in enumerate(pieces) if k > 0]
 
-    made = start_call(density, panel, shape)
-    parts, quarters = made[:cols], made[cols:]
-
     kinds = class_index.reshape(bx * by, bz).astype(jnp.bfloat16)
     kinds = around_axis([kinds] * vols, "vol")
-    parts = parts[0] + mated(parts[1], "col", 1)
     slab = lax.all_to_all(source, ALL, 0, 0, tiled=True)
     slab = slab.reshape(rows, blocks, bx, by, bz)
-    parts = jnp.stack(around_axis([parts[k] for k in range(rows)], "row"))
     spots = trace_spots(trace_count, trace_cell, targets, shape).astype(jnp.bfloat16)
     spots = jnp.pad(spots, ((0, SPOT_ROWS - spots.shape[0]), (0, 0)))
     known = jnp.concatenate(kinds + [spots])
-    known = around_axis([known] * rows, "row")
-    parts = around_axis([parts[:, k] for k in range(vols)], "vol")
+    made = start_call(density, panel, known, shape)
+    lines, quarters = known.shape[0], made[rows:]
+    known = around_axis(made[:rows], "row")
     other = [mated(piece, "col", 1) for piece in known]
+    parts = collect_call(shape, lines, known, other)
+    parts = around_axis(parts, "vol")
 
     panels = [quarters[0], None, quarters[2], None]
     panels[1] = mated(quarters[1], "row", 1)
     panels[3] = mated(quarters[3], "row", 2)
     densities = [columns(density, low), columns(density, 2 + high)]
 
-    inverse, hit, lane = prepare_call(shape, class_values, known, other)
+    inverses = 1.0 / (MASS_TERM + 6.0 * class_values)
+    inverse, hit, lane = prepare_call(shape, inverses, known, other)
     volume, flux = slab_call(shape, True, slab, inverse, hit, lane, parts)
     flux = flux.reshape(excitations, len(MATES), targets)
     flux = lax.all_to_all(flux, ALL, 0, 0, tiled=True)
@@ -545,7 +600,7 @@
 
 
 def whole_slabs(sizes, targets, block):
-    fits = math.prod(sizes) == block[0] and sizes[0] == 4 and targets == block[3]
+    fits = math.prod(sizes) == block[0] and sizes[:2] == [4, 2] and targets == block[3]
     return fits and all(size & (size - 1) == 0 for size in sizes)
 
 

time: 166 us -> 166 us (level)
  starting transfers between devices: 42.1 us -> 39.4 us
    ppermute x27 -> x23, waiting for transfers between devices: 53.4 us -> 54.6 us  [mated(): lax.ppermute(value, axis, [(i, i ^ mate) for i in range(lax.axis_size(axi...]
    pallas_call x2 -> x3, Pallas kernels: 8.61 us -> 9.72 us  [the longest x1 6.31 us: start_call(): pl.pallas_call(body, out_shape=[jax.ShapeDtypeStruct((lines + 4 * owners,...]
    ppermute x27 -> x23, starting transfers between devices: 27.1 us -> 26.2 us  [mated(): lax.ppermute(value, axis, [(i, i ^ mate) for i in range(lax.axis_size(axi...]
  transfers between devices with their start and end apart: 30 -> 26, of which waited for: 14 -> 10; matrix products, arithmetic and copies ran while one was open for 3% -> 3% of each run, Pallas kernels for 11% -> 12%
where the time goes in v8:
time: 166 us; the launch traced here: 165 us
  waiting for transfers between devices  62 us (37%)
  starting transfers between devices  39.4 us (24%)
  Pallas kernels  34.4 us (21%)
  blocking collectives  19.9 us (12%)
  other arithmetic  5.27 us (3%)
  local copies, waits for them, and re-layouts  2.73 us (2%)
    ppermute x23, waiting for transfers between devices, mated(): lax.ppermute(value, axis, [(i, i ^ mate) for i in range(lax.axis_size(axi...  54.6 us
    ppermute x23, starting transfers between devices, mated(): lax.ppermute(value, axis, [(i, i ^ mate) for i in range(lax.axis_size(axi...  26.2 us
    pallas_call x2, Pallas kernels, slab_call(): pl.pallas_call(body, out_shape=[field, fluxes], in_specs=[vmem] * len(ope...  11.3 us
    all_to_all x1, blocking collectives, split_by_excitation(): flux = lax.all_to_all(flux, ALL, 0, 0, tiled=True)  10.1 us
    all_to_all x1, blocking collectives, split_by_excitation(): parts = lax.all_to_all(parts, ALL, 0, 0, tiled=True)  9.88 us
    all_to_all x1, waiting for transfers between devices, split_by_excitation(): flux = lax.all_to_all(flux, ALL, 0, 0, tiled=True)  7.47 us
    pallas_call x1, Pallas kernels, start_call(): pl.pallas_call(body, out_shape=[jax.ShapeDtypeStruct((lines + 4 * owners,...  6.31 us
    all_to_all x1, starting transfers between devices, split_by_excitation(): slab = lax.all_to_all(source, ALL, 0, 0, tiled=True)  6.13 us
  transfers between devices with their start and end apart: 26, of which 10 were waited for; matrix products, arithmetic and copies ran while one was open for 3% of the time, Pallas kernels for 12%

profile of v8, /device:TPU:0, one launch (start us, length us, event | category | flops | bytes accessed | tf_op | source)
XLA Modules:
  0.0 165.1 jit_solution(15499767038388037892)
XLA Ops:
  1.4 5.1 %collective-permute-start.2 = (bf16[64,128]{1,0:T(8,128)(2,1)S(1)}, bf16[64,128]{1,0:T(8,128)(2,1)S(1)}, u32[]{:S(2)}, u32[]{:S(2)}) collective-permute-start(bf16[64,128]{1,0:T(8,128)(2,1)S(1)} %get-tuple-element.53), channel_id=1, source_target_pairs={{0,3},{1,2},{2,1},{3,0},{4,7},{5,6},{6,5},{7,4},{8,11},{9,10},{10,... | collective-permute-start | bytes 49160 | tf_op jit(solution)/shard_map/ppermute | solution.py:51
  7.1 6.1 %all-to-all-start = ((f32[32,8,8,128]{3,2,1,0:T(8,128)}), f32[32,8,8,128]{3,2,1,0:T(8,128)}, u32[]{:S(2)}, u32[]{:S(2)}) async-start(f32[32,8,8,128]{3,2,1,0:T(8,128)} %param.9), calls=%async_computation | async-start | bytes 2097152 | tf_op jit(solution)/shard_map/all_to_all | solution.py:464
  14.5 6.3 %start.1 = (bf16[320,128]{1,0:T(8,128)(2,1)}, bf16[320,128]{1,0:T(8,128)(2,1)}, bf16[320,128]{1,0:T(8,128)(2,1)}, bf16[320,128]{1,0:T(8,128)(2,1)}, bf16[128,409...) custom-call(f32[32,16384]{1,0:T(8,128)} %density_ref.1, ...), custom_call_target="tpu_custom_call" | custom-call | tf_op jit(solution)/shard_map/start/pallas_call | solution.py:108
  25.0 2.6 %collective-permute-start.5 = (bf16[320,128]{1,0:T(8,128)(2,1)}, bf16[320,128]{1,0:T(8,128)(2,1)S(1)}, u32[]{:S(2)}, u32[]{:S(2)}) collective-permute-start(bf16[320,128]{1,0:T(8,128)(2,1)} %get-tuple-element.30), channel_id=1, source_target_pairs={{0,24},{8,16},{16,8},{24,0},{1,25},{9,17},{17,9},{25,1},{2,26},{10... | collective-permute-start | bytes 245768 | tf_op jit(solution)/shard_map/ppermute | solution.py:51
  27.6 26.0 %collective-permute-done.3.refs_1_ = bf16[320,128]{1,0:T(8,128)(2,1)S(1)} collective-permute-done((bf16[320,128]{1,0:T(8,128)(2,1)}, bf16[320,128]{1,0:T(8,128)(2,1)S(1)}, u32[]{:S(2)}, u32[]{:S(2)}) %collective-permute-start.3) | collective-permute-done | bytes 81952 | tf_op jit(solution)/shard_map/ppermute | solution.py:51
  54.1 2.0 %collective-permute-done.5.refs_3_ = bf16[320,128]{1,0:T(8,128)(2,1)S(1)} collective-permute-done((bf16[320,128]{1,0:T(8,128)(2,1)}, bf16[320,128]{1,0:T(8,128)(2,1)S(1)}, u32[]{:S(2)}, u32[]{:S(2)}) %collective-permute-start.5) | collective-permute-done | bytes 81952 | tf_op jit(solution)/shard_map/ppermute | solution.py:51
  61.1 1.8 %collective-permute-start.11 = (f32[4,128]{1,0:T(4,128)}, f32[4,128]{1,0:T(4,128)S(1)}, u32[]{:S(2)}, u32[]{:S(2)}) collective-permute-start(f32[4,128]{1,0:T(4,128)} %get-tuple-element.36), channel_id=1, source_target_pairs={{0,2},{1,3},{2,0},{3,1},{4,6},{5,7},{6,4},{7,5},{8,10},{9,11},{10,... | collective-permute-start | bytes 6152 | tf_op jit(solution)/shard_map/ppermute | solution.py:51
  65.4 3.6 %prepare.1 = (f32[32,4,16,128]{3,2,1,0:T(8,128)}, bf16[4,512,128]{2,1,0:T(8,128)(2,1)}, bf16[4,128,128]{2,1,0:T(8,128)(2,1)}) custom-call(f32[16]{0:T(128)} %add_divide_fusion.values_ref, bf16[320,128]{1,0:T(8,128)(2,1)} %get-tuple-element.27.refs_0_, bf16[320,128]{1,0:T(8,128)(2,1)} %copy-done.18, bf16[320,128]{1,0:T(8,128)(2,1)} %copy-done.19, ...), custom_call_target="tpu_custom_call" | custom-call | tf_op jit(solution)/shard_map/prepare/pallas_call | solution.py:194
  69.6 5.3 %slab_first.1 = (f32[34,4,16,128]{3,2,1,0:T(8,128)}, f32[4,8,3,128]{3,2,1,0:T(4,128)}) custom-call(f32[4,8,8,8,128]{4,3,2,1,0:T(8,128)} %bitcast.source_ref, f32[32,4,16,128]{3,2,1,0:T(8,128)} %get-tuple-element.31.inverse_ref, bf16[4,512,128]{2,1,0:T(8,128)(2,1)} %get-tuple-element.32.hit_ref, bf16[4,128,128]{2,1,0:T(8,128)(2,1)} %get-tuple-element.33.lane_ref, ...), custom_call_target="tpu_custom_call" | custom-call | tf_op jit(solution)/shard_map/slab_first/pallas_call | solution.py:355
  74.9 3.7 %all-to-all-start.1 = ((f32[32,3,128]{2,1,0:T(4,128)}), f32[32,3,128]{2,1,0:T(4,128)S(1)}, u32[]{:S(2)}, u32[]{:S(2)}) async-start(f32[32,3,128]{2,1,0:T(4,128)} %bitcast.56), calls=%async_computation.1 | async-start | bytes 131072 | tf_op jit(solution)/shard_map/all_to_all | solution.py:485
  78.6 7.5 %all-to-all-done.1.flux_ref = f32[32,3,128]{2,1,0:T(4,128)S(1)} async-done(((f32[32,3,128]{2,1,0:T(4,128)}), f32[32,3,128]{2,1,0:T(4,128)S(1)}, u32[]{:S(2)}, u32[]{:S(2)}) %all-to-all-start.1) | async-done | bytes 49184 | tf_op jit(solution)/shard_map/all_to_all | solution.py:485
  93.6 2.1 %collective-permute-done.15.a_other = bf16[32,2048]{1,0:T(8,128)(2,1)S(1)} collective-permute-done((bf16[32,2048]{1,0:T(8,128)(2,1)S(1)}, bf16[32,2048]{1,0:T(8,128)(2,1)S(1)}, u32[]{:S(2)}, u32[]{:S(2)}) %collective-permute-start.15) | collective-permute-done | bytes 131104 | tf_op jit(solution)/shard_map/ppermute | solution.py:51
  97.1 2.0 %potential.2.rest_0_ = f32[32,3,128]{2,1,0:T(4,128)S(1)} custom-call(f32[32,4096]{1,0:T(8,128)S(1)} %get-tuple-element.55.a_density, f32[32,4096]{1,0:T(8,128)S(1)} %get-tuple-element.54.b_density, bf16[32,2048]{1,0:T(8,128)(2,1)S(1)} %get-tuple-element.43.a_half, bf16[32,2048]{1,0:T(8,128)(2,1)S(1)} %get-tuple-element.46.b_half, ...), custom_call_target="tpu_custom_call" | custom-call | tf_op jit(solution)/shard_map/potential/pallas_call | solution.py:418
  99.3 2.0 %potential.3 = f32[32,3,128]{2,1,0:T(4,128)S(1)} custom-call(f32[32,4096]{1,0:T(8,128)S(1)} %get-tuple-element.55.a_density, f32[32,4096]{1,0:T(8,128)S(1)} %get-tuple-element.54.b_density, bf16[32,2048]{1,0:T(8,128)(2,1)S(1)} %get-tuple-element.44.a_half, bf16[32,2048]{1,0:T(8,128)(2,1)S(1)} %get-tuple-element.45.b_half, ...), custom_call_target="tpu_custom_call" | custom-call | tf_op jit(solution)/shard_map/potential/pallas_call | solution.py:418
  101.3 9.9 %all_to_all.25 = f32[32,3,128]{2,1,0:T(4,128)} all-to-all(f32[32,3,128]{2,1,0:T(4,128)S(1)} %potential.3), channel_id=1, replica_groups=mesh['row'=4,'col'=2,'vol'=4] {'row','col','vol'}, dimensions={0} | all-to-all | bytes 98304 | tf_op jit(solution)/shard_map/all_to_all | solution.py:492
  111.2 6.0 %slab_last.1 = (f32[4,8,8,8,128]{4,3,2,1,0:T(8,128)}, f32[4,8,3,128]{3,2,1,0:T(4,128)}) custom-call(f32[4,8,8,8,128]{4,3,2,1,0:T(8,128)} %bitcast.source_ref, f32[32,4,16,128]{3,2,1,0:T(8,128)} %get-tuple-element.31.inverse_ref, bf16[4,512,128]{2,1,0:T(8,128)(2,1)} %get-tuple-element.32.hit_ref, bf16[4,128,128]{2,1,0:T(8,128)(2,1)} %get-tuple-element.33.lane_ref, ...), custom_call_target="tpu_custom_call" | custom-call | tf_op jit(solution)/shard_map/slab_last/pallas_call | solution.py:355
  117.3 10.1 %all_to_all.26.flux_ref = f32[32,3,128]{2,1,0:T(4,128)S(1)} all-to-all(f32[32,3,128]{2,1,0:T(4,128)} %bitcast.57), channel_id=1, replica_groups=mesh['row'=4,'col'=2,'vol'=4] {'row','col','vol'}, dimensions={0} | all-to-all | bytes 98304 | tf_op jit(solution)/shard_map/all_to_all | solution.py:496
  127.3 2.3 %update.5 = (bf16[32,4096]{1,0:T(8,128)(2,1)}, bf16[32,4096]{1,0:T(8,128)(2,1)S(1)}) custom-call(f32[32,3,128]{2,1,0:T(4,128)S(1)} %all_to_all.26.flux_ref, bf16[128,4096]{1,0:T(8,128)(2,1)S(1)} %copy-done, bf16[128,4096]{1,0:T(8,128)(2,1)S(1)} %collective-permute-done.13.a_mate, bf16[128,4096]{1,0:T(8,128)(2,1)S(1)} %copy-done.1, ...), custom_call_target="tpu_custom_call" | custom-call | tf_op jit(solution)/shard_map/update/pallas_call | solution.py:377
  131.2 3.4 %all-to-all-start.4 = ((f32[32,8,8,128]{3,2,1,0:T(8,128)}), f32[32,8,8,128]{3,2,1,0:T(8,128)}, u32[]{:S(2)}, u32[]{:S(2)}) async-start(f32[32,8,8,128]{3,2,1,0:T(8,128)} %bitcast.54), calls=%async_computation.4 | async-start | bytes 2097152 | tf_op jit(solution)/shard_map/all_to_all | solution.py:498
  136.2 7.3 %collective-permute-done.19 = bf16[32,4096]{1,0:T(8,128)(2,1)S(1)} collective-permute-done((bf16[32,4096]{1,0:T(8,128)(2,1)}, bf16[32,4096]{1,0:T(8,128)(2,1)S(1)}, u32[]{:S(2)}, u32[]{:S(2)}) %collective-permute-start.19) | collective-permute-done | bytes 262176 | tf_op jit(solution)/shard_map/ppermute | solution.py:51
  144.7 7.3 %collective-permute-done.21 = bf16[32,4096]{1,0:T(8,128)(2,1)S(1)} collective-permute-done((bf16[32,4096]{1,0:T(8,128)(2,1)S(1)}, bf16[32,4096]{1,0:T(8,128)(2,1)S(1)}, u32[]{:S(2)}, u32[]{:S(2)}) %collective-permute-start.21) | collective-permute-done | bytes 262176 | tf_op jit(solution)/shard_map/ppermute | solution.py:51
  153.8 5.5 %collective-permute-done.20 = bf16[32,4096]{1,0:T(8,128)(2,1)S(1)} collective-permute-done((bf16[32,4096]{1,0:T(8,128)(2,1)S(1)}, bf16[32,4096]{1,0:T(8,128)(2,1)S(1)}, u32[]{:S(2)}, u32[]{:S(2)}) %collective-permute-start.20) | collective-permute-done | bytes 262176 | tf_op jit(solution)/shard_map/ppermute | solution.py:51
  159.3 2.1 %collective-permute-done.22 = bf16[32,4096]{1,0:T(8,128)(2,1)S(1)} collective-permute-done((bf16[32,4096]{1,0:T(8,128)(2,1)S(1)}, bf16[32,4096]{1,0:T(8,128)(2,1)S(1)}, u32[]{:S(2)}, u32[]{:S(2)}) %collective-permute-start.22) | collective-permute-done | bytes 262176 | tf_op jit(solution)/shard_map/ppermute | solution.py:51
  162.9 2.0 %landed.1 = f32[32,8,8,128]{3,2,1,0:T(8,128)} custom-call(f32[32,8,8,128]{3,2,1,0:T(8,128)} %all-to-all-done.4.in_ref), custom_call_target="tpu_custom_call" | custom-call | tf_op jit(solution)/shard_map/landed/pallas_call | solution.py:225
  (119 shorter events, 31.7 us)
Async XLA Ops:
  1.4 12.4 %collective-permute-start.2 = (bf16[64,128]{1,0:T(8,128)(2,1)S(1)}, bf16[64,128]{1,0:T(8,128)(2,1)S(1)}, u32[]{:S(2)}, u32[]{:S(2)}) collective-permute-start(bf16[64,128]{1,0:T(8,128)(2,1)S(1)} %get-tuple-element.53), channel_id=1, source_target_pairs={{0,3},{1,2},{2,1},{3,0},{4,7},{5,6},{6,5},{7,4},{8,11},{9,10},{10,... | collective-permute-start | bytes 49160 | tf_op jit(solution)/shard_map/ppermute | solution.py:51
  6.5 7.3 %collective-permute-start.1 = (bf16[64,128]{1,0:T(8,128)(2,1)S(1)}, bf16[64,128]{1,0:T(8,128)(2,1)S(1)}, u32[]{:S(2)}, u32[]{:S(2)}) collective-permute-start(bf16[64,128]{1,0:T(8,128)(2,1)S(1)} %get-tuple-element.53), channel_id=1, source_target_pairs={{0,2},{1,3},{2,0},{3,1},{4,6},{5,7},{6,4},{7,5},{8,10},{9,11},{10,... | collective-permute-start | bytes 49160 | tf_op jit(solution)/shard_map/ppermute | solution.py:51
  6.5 7.3 %collective-permute-start = (bf16[64,128]{1,0:T(8,128)(2,1)S(1)}, bf16[64,128]{1,0:T(8,128)(2,1)S(1)}, u32[]{:S(2)}, u32[]{:S(2)}) collective-permute-start(bf16[64,128]{1,0:T(8,128)(2,1)S(1)} %get-tuple-element.53), channel_id=1, source_target_pairs={{0,1},{1,0},{2,3},{3,2},{4,5},{5,4},{6,7},{7,6},{8,9},{9,8},{10,11... | collective-permute-start | bytes 49160 | tf_op jit(solution)/shard_map/ppermute | solution.py:51
  7.1 61.9 %all-to-all-start = ((f32[32,8,8,128]{3,2,1,0:T(8,128)}), f32[32,8,8,128]{3,2,1,0:T(8,128)}, u32[]{:S(2)}, u32[]{:S(2)}) async-start(f32[32,8,8,128]{3,2,1,0:T(8,128)} %param.9), calls=%async_computation | async-start | bytes 2097152 | tf_op jit(solution)/shard_map/all_to_all | solution.py:464
  20.8 57.7 %collective-permute-start.13 = (bf16[128,4096]{1,0:T(8,128)(2,1)}, bf16[128,4096]{1,0:T(8,128)(2,1)S(1)}, u32[]{:S(2)}, u32[]{:S(2)}) collective-permute-start(bf16[128,4096]{1,0:T(8,128)(2,1)} %get-tuple-element.40), channel_id=1, source_target_pairs={{0,8},{8,0},{16,24},{24,16},{1,9},{9,1},{17,25},{25,17},{2,10},{10... | collective-permute-start | bytes 3145736 | tf_op jit(solution)/shard_map/ppermute | solution.py:51
  22.6 56.0 %collective-permute-start.14 = (bf16[128,4096]{1,0:T(8,128)(2,1)}, bf16[128,4096]{1,0:T(8,128)(2,1)}, u32[]{:S(2)}, u32[]{:S(2)}) collective-permute-start(bf16[128,4096]{1,0:T(8,128)(2,1)} %get-tuple-element.42), channel_id=1, source_target_pairs={{0,16},{8,24},{16,0},{24,8},{1,17},{9,25},{17,1},{25,9},{2,18},{10... | collective-permute-start | bytes 3145736 | tf_op jit(solution)/shard_map/ppermute | solution.py:51
  24.1 29.5 %collective-permute-start.3 = (bf16[320,128]{1,0:T(8,128)(2,1)}, bf16[320,128]{1,0:T(8,128)(2,1)S(1)}, u32[]{:S(2)}, u32[]{:S(2)}) collective-permute-start(bf16[320,128]{1,0:T(8,128)(2,1)} %get-tuple-element.28), channel_id=1, source_target_pairs={{0,8},{8,0},{16,24},{24,16},{1,9},{9,1},{17,25},{25,17},{2,10},{10... | collective-permute-start | bytes 245768 | tf_op jit(solution)/shard_map/ppermute | solution.py:51
  24.6 29.0 %collective-permute-start.4 = (bf16[320,128]{1,0:T(8,128)(2,1)}, bf16[320,128]{1,0:T(8,128)(2,1)S(1)}, u32[]{:S(2)}, u32[]{:S(2)}) collective-permute-start(bf16[320,128]{1,0:T(8,128)(2,1)} %get-tuple-element.29), channel_id=1, source_target_pairs={{0,16},{8,24},{16,0},{24,8},{1,17},{9,25},{17,1},{25,9},{2,18},{10... | collective-permute-start | bytes 245768 | tf_op jit(solution)/shard_map/ppermute | solution.py:51
  25.0 31.2 %collective-permute-start.5 = (bf16[320,128]{1,0:T(8,128)(2,1)}, bf16[320,128]{1,0:T(8,128)(2,1)S(1)}, u32[]{:S(2)}, u32[]{:S(2)}) collective-permute-start(bf16[320,128]{1,0:T(8,128)(2,1)} %get-tuple-element.30), channel_id=1, source_target_pairs={{0,24},{8,16},{16,8},{24,0},{1,25},{9,17},{17,9},{25,1},{2,26},{10... | collective-permute-start | bytes 245768 | tf_op jit(solution)/shard_map/ppermute | solution.py:51
  53.6 2.5 %collective-permute-start.6 = (bf16[320,128]{1,0:T(8,128)(2,1)}, bf16[320,128]{1,0:T(8,128)(2,1)S(1)}, u32[]{:S(2)}, u32[]{:S(2)}) collective-permute-start(bf16[320,128]{1,0:T(8,128)(2,1)} %get-tuple-element.27.refs_0_), channel_id=1, source_target_pairs={{0,4},{4,0},{1,5},{5,1},{2,6},{6,2},{3,7},{7,3},{8,12},{12,8},{9,1... | collective-permute-start | bytes 245768 | tf_op jit(solution)/shard_map/ppermute | solution.py:51
  53.6 3.0 %collective-permute-start.7 = (bf16[320,128]{1,0:T(8,128)(2,1)S(1)}, bf16[320,128]{1,0:T(8,128)(2,1)S(1)}, u32[]{:S(2)}, u32[]{:S(2)}) collective-permute-start(bf16[320,128]{1,0:T(8,128)(2,1)S(1)} %collective-permute-done.3.refs_1_), channel_id=1, source_target_pairs={{0,4},{4,0},{1,5},{5,1},{2,6},{6,2},{3,7},{7,3},{8,12},{12,8},{9,1... | collective-permute-start | bytes 245768 | tf_op jit(solution)/shard_map/ppermute | solution.py:51
  59.5 9.5 %collective-permute-start.10 = (f32[4,128]{1,0:T(4,128)}, f32[4,128]{1,0:T(4,128)S(1)}, u32[]{:S(2)}, u32[]{:S(2)}) collective-permute-start(f32[4,128]{1,0:T(4,128)} %get-tuple-element.35), channel_id=1, source_target_pairs={{0,1},{1,0},{2,3},{3,2},{4,5},{5,4},{6,7},{7,6},{8,9},{9,8},{10,11... | collective-permute-start | bytes 6152 | tf_op jit(solution)/shard_map/ppermute | solution.py:51
  61.1 7.9 %collective-permute-start.11 = (f32[4,128]{1,0:T(4,128)}, f32[4,128]{1,0:T(4,128)S(1)}, u32[]{:S(2)}, u32[]{:S(2)}) collective-permute-start(f32[4,128]{1,0:T(4,128)} %get-tuple-element.36), channel_id=1, source_target_pairs={{0,2},{1,3},{2,0},{3,1},{4,6},{5,7},{6,4},{7,5},{8,10},{9,11},{10,... | collective-permute-start | bytes 6152 | tf_op jit(solution)/shard_map/ppermute | solution.py:51
  62.8 6.2 %collective-permute-start.12 = (f32[4,128]{1,0:T(4,128)}, f32[4,128]{1,0:T(4,128)S(1)}, u32[]{:S(2)}, u32[]{:S(2)}) collective-permute-start(f32[4,128]{1,0:T(4,128)} %get-tuple-element.37), channel_id=1, source_target_pairs={{0,3},{1,2},{2,1},{3,0},{4,7},{5,6},{6,5},{7,4},{8,11},{9,10},{10,... | collective-permute-start | bytes 6152 | tf_op jit(solution)/shard_map/ppermute | solution.py:51
  74.9 11.2 %all-to-all-start.1 = ((f32[32,3,128]{2,1,0:T(4,128)}), f32[32,3,128]{2,1,0:T(4,128)S(1)}, u32[]{:S(2)}, u32[]{:S(2)}) async-start(f32[32,3,128]{2,1,0:T(4,128)} %bitcast.56), calls=%async_computation.1 | async-start | bytes 131072 | tf_op jit(solution)/shard_map/all_to_all | solution.py:485
  87.7 11.5 %collective-permute-start.16 = (bf16[32,2048]{1,0:T(8,128)(2,1)S(1)}, bf16[32,2048]{1,0:T(8,128)(2,1)S(1)}, u32[]{:S(2)}, u32[]{:S(2)}) collective-permute-start(bf16[32,2048]{1,0:T(8,128)(2,1)S(1)} %get-tuple-element.44.a_half), channel_id=1, source_target_pairs={{0,16},{8,24},{16,0},{24,8},{1,17},{9,25},{17,1},{25,9},{2,18},{10... | collective-permute-start | bytes 393224 | tf_op jit(solution)/shard_map/ppermute | solution.py:51
  88.5 10.8 %collective-permute-start.17 = (bf16[32,2048]{1,0:T(8,128)(2,1)S(1)}, bf16[32,2048]{1,0:T(8,128)(2,1)S(1)}, u32[]{:S(2)}, u32[]{:S(2)}) collective-permute-start(bf16[32,2048]{1,0:T(8,128)(2,1)S(1)} %get-tuple-element.45.b_half), channel_id=1, source_target_pairs={{0,8},{8,0},{16,24},{24,16},{1,9},{9,1},{17,25},{25,17},{2,10},{10... | collective-permute-start | bytes 393224 | tf_op jit(solution)/shard_map/ppermute | solution.py:51
  90.7 5.0 %collective-permute-start.15 = (bf16[32,2048]{1,0:T(8,128)(2,1)S(1)}, bf16[32,2048]{1,0:T(8,128)(2,1)S(1)}, u32[]{:S(2)}, u32[]{:S(2)}) collective-permute-start(bf16[32,2048]{1,0:T(8,128)(2,1)S(1)} %get-tuple-element.43.a_half), channel_id=1, source_target_pairs={{0,16},{8,24},{16,0},{24,8},{1,17},{9,25},{17,1},{25,9},{2,18},{10... | collective-permute-start | bytes 393224 | tf_op jit(solution)/shard_map/ppermute | solution.py:51
  92.2 5.0 %collective-permute-start.18 = (bf16[32,2048]{1,0:T(8,128)(2,1)S(1)}, bf16[32,2048]{1,0:T(8,128)(2,1)S(1)}, u32[]{:S(2)}, u32[]{:S(2)}) collective-permute-start(bf16[32,2048]{1,0:T(8,128)(2,1)S(1)} %get-tuple-element.46.b_half), channel_id=1, source_target_pairs={{0,8},{8,0},{16,24},{24,16},{1,9},{9,1},{17,25},{25,17},{2,10},{10... | collective-permute-start | bytes 393224 | tf_op jit(solution)/shard_map/ppermute | solution.py:51
  130.4 13.1 %collective-permute-start.19 = (bf16[32,4096]{1,0:T(8,128)(2,1)}, bf16[32,4096]{1,0:T(8,128)(2,1)S(1)}, u32[]{:S(2)}, u32[]{:S(2)}) collective-permute-start(bf16[32,4096]{1,0:T(8,128)(2,1)} %get-tuple-element.49), channel_id=1, source_target_pairs={{0,16},{8,24},{16,0},{24,8},{1,17},{9,25},{17,1},{25,9},{2,18},{10... | collective-permute-start | bytes 786440 | tf_op jit(solution)/shard_map/ppermute | solution.py:51
  131.2 31.8 %all-to-all-start.4 = ((f32[32,8,8,128]{3,2,1,0:T(8,128)}), f32[32,8,8,128]{3,2,1,0:T(8,128)}, u32[]{:S(2)}, u32[]{:S(2)}) async-start(f32[32,8,8,128]{3,2,1,0:T(8,128)} %bitcast.54), calls=%async_computation.4 | async-start | bytes 2097152 | tf_op jit(solution)/shard_map/all_to_all | solution.py:498
  134.6 17.5 %collective-permute-start.21 = (bf16[32,4096]{1,0:T(8,128)(2,1)S(1)}, bf16[32,4096]{1,0:T(8,128)(2,1)S(1)}, u32[]{:S(2)}, u32[]{:S(2)}) collective-permute-start(bf16[32,4096]{1,0:T(8,128)(2,1)S(1)} %copy-done.15), channel_id=1, source_target_pairs={{0,8},{8,0},{16,24},{24,16},{1,9},{9,1},{17,25},{25,17},{2,10},{10... | collective-permute-start | bytes 786440 | tf_op jit(solution)/shard_map/ppermute | solution.py:51
  144.7 14.6 %collective-permute-start.20 = (bf16[32,4096]{1,0:T(8,128)(2,1)S(1)}, bf16[32,4096]{1,0:T(8,128)(2,1)S(1)}, u32[]{:S(2)}, u32[]{:S(2)}) collective-permute-start(bf16[32,4096]{1,0:T(8,128)(2,1)S(1)} %multiply_convert_fusion.1), channel_id=1, source_target_pairs={{0,8},{8,0},{16,24},{24,16},{1,9},{9,1},{17,25},{25,17},{2,10},{10... | collective-permute-start | bytes 786440 | tf_op jit(solution)/shard_map/ppermute | solution.py:51
  152.2 9.1 %collective-permute-start.22 = (bf16[32,4096]{1,0:T(8,128)(2,1)S(1)}, bf16[32,4096]{1,0:T(8,128)(2,1)S(1)}, u32[]{:S(2)}, u32[]{:S(2)}) collective-permute-start(bf16[32,4096]{1,0:T(8,128)(2,1)S(1)} %multiply_convert_fusion), channel_id=1, source_target_pairs={{0,16},{8,24},{16,0},{24,8},{1,17},{9,25},{17,1},{25,9},{2,18},{10... | collective-permute-start | bytes 786440 | tf_op jit(solution)/shard_map/ppermute | solution.py:51
  (32 other events, 279.8 us)

commit v9 on v8

--- a/solution.py
+++ b/solution.py
@@ -21,6 +21,7 @@
 SPOT_ROWS = 32
 PARTS = 2
 VMEM_BYTES = 16 * 2 ** 20
+SLAB_BYTES = 40 * 2 ** 20
 
 
 def relax_factors(count):
@@ -161,7 +162,10 @@
         known_refs, other_refs = refs[:rows], refs[rows:2 * rows]
         inverse_ref, hit_ref, lane_ref = refs[2 * rows:]
         r0, c0, v0 = (lax.axis_index(a) for a in ALL)
-        count = values_ref.shape[0]
+        inverses = [
+            1.0 / (MASS_TERM + 6.0 * jnp.full((by, bz), values_ref[i], jnp.float32))
+            for i in range(values_ref.shape[0])
+        ]
         row_ids = lax.broadcasted_iota(jnp.int32, (height, targets), 0)
         lane_ids = lax.broadcasted_iota(jnp.int32, (bz, targets), 0)
         for k in range(rows):
@@ -176,16 +180,16 @@
 
                 def plane(kv, carry, source=refs_of[k], start=start, k=k):
                     kind = source[pl.ds(pl.multiple_of(kv * lines, lines), lines)].astype(jnp.float32)
-                    kind = kind.astype(jnp.int32)
-                    choices, bit = [values_ref[i] for i in range(count)], 1
+                    kind = kind.astype(jnp.int32).reshape(bx, by, bz)
+                    choices, bit = [value[None] for value in inverses], 1
                     while len(choices) > 1:
                         odd = (kind & bit) != 0
                         merged = [jnp.where(odd, two, one)
                                   for one, two in zip(choices[0::2], choices[1::2])]
                         choices, bit = merged + choices[len(merged) * 2:], bit * 2
-                    inverse = jnp.broadcast_to(choices[0], (lines, bz))
+                    inverse = jnp.broadcast_to(choices[0], (bx, by, bz))
                     place = (pl.ds((k ^ r0) * bx, bx), kv ^ v0, pl.ds(start, by))
-                    inverse_ref[place] = inverse.reshape(bx, by, bz)
+                    inverse_ref[place] = inverse
                     return carry
 
                 lax.fori_loop(0, vols, plane, 0)
@@ -255,10 +259,25 @@
 
     def body(source_ref, inverse_ref, hit_ref, lane_ref, *rest):
         if first:
-            *part_refs, out_ref, flux_ref, other_ref, scaled_ref, ratio_ref = rest
-            volume_ref = None
+            *part_refs, far_ref, flux_ref, other_ref, scaled_ref, ratio_ref, sem = rest[:-6]
+            out_ref, *held, load_sems = rest[-6:]
+            fars = (lane_ref, hit_ref, source_ref, inverse_ref)
+            lane_ref, hit_ref, source_ref, inverse_ref = held
+            whole = [pltpu.make_async_copy(fars[i], held[i], load_sems.at[i]) for i in range(2)]
+            chunks = []
+            for r in range(rows):
+                deep = pl.ds(r * bx, bx)
+                chunks.append((
+                    pltpu.make_async_copy(fars[2].at[r], held[2].at[r], load_sems.at[2 + 2 * r]),
+                    pltpu.make_async_copy(fars[3].at[deep], held[3].at[deep], load_sems.at[3 + 2 * r]),
+                ))
+            for copy in whole + [copy for pair in chunks for copy in pair]:
+                copy.start()
+            result_ref = out_ref
         else:
-            parts_ref, start_ref, volume_ref, flux_ref, out_ref, other_ref, scaled_ref, ratio_ref = rest
+            parts_ref, start_ref, far_ref, flux_ref, out_ref, *rest = rest
+            other_ref, scaled_ref, ratio_ref, volume_ref, sem = rest
+            result_ref = volume_ref
         sub = lax.broadcasted_iota(jnp.int32, (by, bz), 0)
         lan = lax.broadcasted_iota(jnp.int32, (by, bz), 1)
         for ref in (out_ref, other_ref):
@@ -276,6 +295,9 @@
                     for k, mate in enumerate(MATES)
                 )
             potentials.append(potential)
+            if first and r == 0:
+                for copy in whole:
+                    copy.wait()
             weights = [
                 lane_ref[r] * piece.astype(jnp.bfloat16) for piece in parts_of(potential, 3)
             ]
@@ -285,6 +307,9 @@
             )
             added = added[:, :bz] + added[:, bz:2 * bz] + added[:, 2 * bz:]
             added = added.reshape(bx, vols, cols, by, bz)
+            if first:
+                for copy in chunks[r]:
+                    copy.wait()
             for j in range(blocks):
                 c, v = j // vols, j % vols
                 span = (slice(r * bx, (r + 1) * bx), v, slice(c * by, (c + 1) * by))
@@ -335,6 +360,8 @@
                 step(index, 0)
             here = there
 
+        store = pltpu.make_async_copy(result_ref, far_ref, sem)
+        store.start()
         for r in range(rows):
             part = here[1 + r * bx:1 + (r + 1) * bx].reshape(height, bz)
             met = sum(
@@ -345,19 +372,29 @@
             value = value - potentials[r]
             for k, mate in enumerate(MATES):
                 flux_ref[r ^ mate, :, k, :] = jnp.broadcast_to(value, (blocks, targets))
+        store.wait()
 
     vmem = pl.BlockSpec(memory_space=pltpu.VMEM)
     operands = [source, inverse, hit, lane] + (list(parts) if first else [parts, start])
     fluxes = jax.ShapeDtypeStruct((rows, blocks, len(MATES), targets), jnp.float32)
     field = padded if first else (rows, blocks, bx, by, bz)
     field = jax.ShapeDtypeStruct(field, jnp.float32)
-    scratch = [pltpu.VMEM(padded, jnp.float32)] * (1 if first else 2)
+    hbm = pl.BlockSpec(memory_space=pltpu.HBM)
+    work = [pltpu.VMEM(padded, jnp.float32)] + [pltpu.VMEM(planes, jnp.float32)] * 2
+    done = pltpu.SemaphoreType.DMA(())
+    if first:
+        scratch = work + [done, pltpu.VMEM(padded, jnp.float32)]
+        scratch += [pltpu.VMEM(value.shape, value.dtype) for value in (lane, hit, source, inverse)]
+        scratch.append(pltpu.SemaphoreType.DMA((2 + 2 * rows,)))
+    else:
+        scratch = [pltpu.VMEM(padded, jnp.float32)] + work + [pltpu.VMEM(field.shape, jnp.float32), done]
     return pl.pallas_call(
         body,
         out_shape=[field, fluxes],
-        in_specs=[vmem] * len(operands),
-        out_specs=[vmem, vmem],
-        scratch_shapes=scratch + [pltpu.VMEM(planes, jnp.float32)] * 2,
+        in_specs=([hbm] * 4 if first else [vmem] * 4) + [vmem] * (len(operands) - 4),
+        out_specs=[hbm, vmem],
+        scratch_shapes=scratch,
+        compiler_params=None if first else pltpu.CompilerParams(vmem_limit_bytes=SLAB_BYTES),
         name="slab_first" if first else "slab_last",
     )(*operands)
 
@@ -366,19 +403,27 @@
     excitations, width = flux.shape[0], panels[0].shape[1] // parts
     span = slice(part * width, (part + 1) * width)
 
-    def body(flux_ref, a_own, a_mate, b_own, b_mate, a_ref, b_ref):
+    def body(flux_ref, a_own, a_mate, b_own, b_far, a_ref, b_ref, b_mate, sem):
+        load = pltpu.make_async_copy(b_far.at[:, span], b_mate, sem)
+        load.start()
         fluxes = [flux_ref[:, k, :].astype(jnp.bfloat16) for k in range(len(MATES))]
-        for out, own, mate, k in ((a_ref, a_own, a_mate, 1), (b_ref, b_own, b_mate, 2)):
-            value = jnp.dot(fluxes[0], own[:, span], preferred_element_type=jnp.float32)
-            value += jnp.dot(fluxes[k], mate[:, span], preferred_element_type=jnp.float32)
-            out[...] = value.astype(jnp.bfloat16)
+        value = jnp.dot(fluxes[0], a_own[:, span], preferred_element_type=jnp.float32)
+        value += jnp.dot(fluxes[1], a_mate[:, span], preferred_element_type=jnp.float32)
+        a_ref[...] = value.astype(jnp.bfloat16)
+        value = jnp.dot(fluxes[0], b_own[:, span], preferred_element_type=jnp.float32)
+        load.wait()
+        value += jnp.dot(fluxes[2], b_mate[...], preferred_element_type=jnp.float32)
+        b_ref[...] = value.astype(jnp.bfloat16)
 
     vmem = pl.BlockSpec(memory_space=pltpu.VMEM)
     return pl.pallas_call(
         body,
         out_shape=[jax.ShapeDtypeStruct((excitations, width), jnp.bfloat16)] * 2,
-        in_specs=[vmem] * 5,
+        in_specs=[vmem] * 4 + [pl.BlockSpec(memory_space=pltpu.HBM)],
         out_specs=[vmem] * 2,
+        scratch_shapes=[
+            pltpu.VMEM((panels[0].shape[0], width), panels[0].dtype), pltpu.SemaphoreType.DMA(())
+        ],
         compiler_params=pltpu.CompilerParams(vmem_limit_bytes=VMEM_BYTES),
         name="update",
     )(flux, *panels)
@@ -390,8 +435,10 @@
     span = slice(part * width, (part + 1) * width)
 
     def body(a_density, b_density, a_half, b_half, a_other, b_other,
-             a_own, a_mate, b_own, b_mate, *rest):
-        out_ref = rest[-1]
+             a_own, a_mate, b_own, b_far, *rest):
+        out_ref, b_mate, sem = rest[-3:]
+        load = pltpu.make_async_copy(b_far.at[:, span], b_mate, sem)
+        load.start()
         rounded = [
             (density[:, span] + RELAXATION * (half[...].astype(jnp.float32)
                                               + other[...].astype(jnp.float32))).astype(jnp.bfloat16)
@@ -401,25 +448,26 @@
 
         def met(value, panel):
             return lax.dot_general(
-                panel[:, span], value, (((1,), (1,)), ((), ())), preferred_element_type=jnp.float32
+                panel, value, (((1,), (1,)), ((), ())), preferred_element_type=jnp.float32
             )
 
-        sums = (
-            met(rounded[0], a_own) + met(rounded[1], b_own),
-            met(rounded[0], a_mate),
-            met(rounded[1], b_mate),
-        )
-        for k, value in enumerate(sums):
+        def put(k, value):
             value = value.T
             out_ref[:, k, :] = value + rest[0][:, k, :] if before is not None else value
+
+        put(0, met(rounded[0], a_own[:, span]) + met(rounded[1], b_own[:, span]))
+        put(1, met(rounded[0], a_mate[:, span]))
+        load.wait()
+        put(2, met(rounded[1], b_mate[...]))
 
     vmem = pl.BlockSpec(memory_space=pltpu.VMEM)
     operands = [*densities, *halves, *mates, *panels] + ([] if before is None else [before])
     return pl.pallas_call(
         body,
         out_shape=jax.ShapeDtypeStruct((excitations, len(MATES), targets), jnp.float32),
-        in_specs=[vmem] * len(operands),
+        in_specs=[vmem] * 9 + [pl.BlockSpec(memory_space=pltpu.HBM)] + [vmem] * (len(operands) - 10),
         out_specs=vmem,
+        scratch_shapes=[pltpu.VMEM((targets, width), panels[0].dtype), pltpu.SemaphoreType.DMA(())],
         compiler_params=pltpu.CompilerParams(vmem_limit_bytes=VMEM_BYTES),
         name="potential",
     )(*operands)
@@ -470,16 +518,16 @@
     lines, quarters = known.shape[0], made[rows:]
     known = around_axis(made[:rows], "row")
     other = [mated(piece, "col", 1) for piece in known]
-    parts = collect_call(shape, lines, known, other)
-    parts = around_axis(parts, "vol")
+    parts = list(collect_call(shape, lines, known, other))
+    for k in range(1, vols):
+        parts[k] = mated(parts[k], "vol", k)
 
     panels = [quarters[0], None, quarters[2], None]
     panels[1] = mated(quarters[1], "row", 1)
     panels[3] = mated(quarters[3], "row", 2)
     densities = [columns(density, low), columns(density, 2 + high)]
 
-    inverses = 1.0 / (MASS_TERM + 6.0 * class_values)
-    inverse, hit, lane = prepare_call(shape, inverses, known, other)
+    inverse, hit, lane = prepare_call(shape, class_values, known, other)
     volume, flux = slab_call(shape, True, slab, inverse, hit, lane, parts)
     flux = flux.reshape(excitations, len(MATES), targets)
     flux = lax.all_to_all(flux, ALL, 0, 0, tiled=True)
@@ -600,8 +648,7 @@
 
 
 def whole_slabs(sizes, targets, block):
-    fits = math.prod(sizes) == block[0] and sizes[:2] == [4, 2] and targets == block[3]
-    return fits and all(size & (size - 1) == 0 for size in sizes)
+    return math.prod(sizes) == block[0] and sizes == [4, 2, 4] and targets == block[3]
 
 
 def solution(mesh):

time: 166 us -> 163 us (0.982)
    unnamed x63 -> x75, local copies, waits for them, and re-layouts: 2.66 us -> 3.7 us
  transfers between devices with their start and end apart: 26 -> 26, of which waited for: 10 -> 11; matrix products, arithmetic and copies ran while one was open for 3% -> 2% of each run, Pallas kernels for 12% -> 13%
where the time goes in v9:
time: 163 us
  waiting for transfers between devices  62.5 us (38%)
  starting transfers between devices  38.4 us (24%)
  Pallas kernels  33.9 us (21%)
  blocking collectives  18.5 us (11%)
  other arithmetic  4.13 us (3%)
  local copies, waits for them, and re-layouts  3.77 us (2%)
    ppermute x23, waiting for transfers between devices, mated(): lax.ppermute(value, axis, [(i, i ^ mate) for i in range(lax.axis_size(axi...  55 us
    ppermute x23, starting transfers between devices, mated(): lax.ppermute(value, axis, [(i, i ^ mate) for i in range(lax.axis_size(axi...  26.4 us
    pallas_call x2, Pallas kernels, slab_call(): pl.pallas_call(body, out_shape=[field, fluxes], in_specs=([hbm] * 4 if fi...  11.4 us
    all_to_all x1, blocking collectives, split_by_excitation(): parts = lax.all_to_all(parts, ALL, 0, 0, tiled=True)  9.36 us
    all_to_all x1, blocking collectives, split_by_excitation(): flux = lax.all_to_all(flux, ALL, 0, 0, tiled=True)  9.19 us
    all_to_all x1, waiting for transfers between devices, split_by_excitation(): flux = lax.all_to_all(flux, ALL, 0, 0, tiled=True)  7.47 us
    pallas_call x1, Pallas kernels, start_call(): pl.pallas_call(body, out_shape=[jax.ShapeDtypeStruct((lines + 4 * owners,...  6.31 us
    all_to_all x1, starting transfers between devices, split_by_excitation(): slab = lax.all_to_all(source, ALL, 0, 0, tiled=True)  6.13 us
  transfers between devices with their start and end apart: 26, of which 11 were waited for; matrix products, arithmetic and copies ran while one was open for 2% of the time, Pallas kernels for 13%

profile of v9, /device:TPU:0, one launch (start us, length us, event | category | flops | bytes accessed | tf_op | source)
XLA Modules:
  0.0 162.5 jit_solution(6691053455386257786)
XLA Ops:
  1.4 5.1 %collective-permute-start.2 = (bf16[64,128]{1,0:T(8,128)(2,1)S(1)}, bf16[64,128]{1,0:T(8,128)(2,1)S(1)}, u32[]{:S(2)}, u32[]{:S(2)}) collective-permute-start(bf16[64,128]{1,0:T(8,128)(2,1)S(1)} %get-tuple-element.53), channel_id=1, source_target_pairs={{0,3},{1,2},{2,1},{3,0},{4,7},{5,6},{6,5},{7,4},{8,11},{9,10},{10,... | collective-permute-start | bytes 49160 | tf_op jit(solution)/shard_map/ppermute | solution.py:52
  7.1 6.1 %all-to-all-start = ((f32[32,8,8,128]{3,2,1,0:T(8,128)}), f32[32,8,8,128]{3,2,1,0:T(8,128)}, u32[]{:S(2)}, u32[]{:S(2)}) async-start(f32[32,8,8,128]{3,2,1,0:T(8,128)} %param.9), calls=%async_computation | async-start | bytes 2097152 | tf_op jit(solution)/shard_map/all_to_all | solution.py:512
  14.5 6.3 %start.1 = (bf16[320,128]{1,0:T(8,128)(2,1)}, bf16[320,128]{1,0:T(8,128)(2,1)}, bf16[320,128]{1,0:T(8,128)(2,1)}, bf16[320,128]{1,0:T(8,128)(2,1)}, bf16[128,409...) custom-call(f32[32,16384]{1,0:T(8,128)} %density_ref.1, ...), custom_call_target="tpu_custom_call" | custom-call | tf_op jit(solution)/shard_map/start/pallas_call | solution.py:109
  25.0 2.6 %collective-permute-start.5 = (bf16[320,128]{1,0:T(8,128)(2,1)}, bf16[320,128]{1,0:T(8,128)(2,1)S(1)}, u32[]{:S(2)}, u32[]{:S(2)}) collective-permute-start(bf16[320,128]{1,0:T(8,128)(2,1)} %get-tuple-element.30), channel_id=1, source_target_pairs={{0,24},{8,16},{16,8},{24,0},{1,25},{9,17},{17,9},{25,1},{2,26},{10... | collective-permute-start | bytes 245768 | tf_op jit(solution)/shard_map/ppermute | solution.py:52
  27.6 26.0 %collective-permute-done.3.refs_1_ = bf16[320,128]{1,0:T(8,128)(2,1)S(1)} collective-permute-done((bf16[320,128]{1,0:T(8,128)(2,1)}, bf16[320,128]{1,0:T(8,128)(2,1)S(1)}, u32[]{:S(2)}, u32[]{:S(2)}) %collective-permute-start.3) | collective-permute-done | bytes 81952 | tf_op jit(solution)/shard_map/ppermute | solution.py:52
  54.1 2.0 %collective-permute-done.5.refs_3_ = bf16[320,128]{1,0:T(8,128)(2,1)S(1)} collective-permute-done((bf16[320,128]{1,0:T(8,128)(2,1)}, bf16[320,128]{1,0:T(8,128)(2,1)S(1)}, u32[]{:S(2)}, u32[]{:S(2)}) %collective-permute-start.5) | collective-permute-done | bytes 81952 | tf_op jit(solution)/shard_map/ppermute | solution.py:52
  61.1 1.8 %collective-permute-start.11 = (f32[4,128]{1,0:T(4,128)}, f32[4,128]{1,0:T(4,128)S(1)}, u32[]{:S(2)}, u32[]{:S(2)}) collective-permute-start(f32[4,128]{1,0:T(4,128)} %get-tuple-element.36), channel_id=1, source_target_pairs={{0,2},{1,3},{2,0},{3,1},{4,6},{5,7},{6,4},{7,5},{8,10},{9,11},{10,... | collective-permute-start | bytes 6152 | tf_op jit(solution)/shard_map/ppermute | solution.py:52
  64.2 3.5 %prepare.1 = (f32[32,4,16,128]{3,2,1,0:T(8,128)}, bf16[4,512,128]{2,1,0:T(8,128)(2,1)}, bf16[4,128,128]{2,1,0:T(8,128)(2,1)}) custom-call(f32[16]{0:T(128)} %values_ref.1, bf16[320,128]{1,0:T(8,128)(2,1)} %get-tuple-element.27.refs_0_, bf16[320,128]{1,0:T(8,128)(2,1)} %copy-done.24, bf16[320,128]{1,0:T(8,128)(2,1)} %copy-done.25, ...), custom_call_target="tpu_custom_call" | custom-call | tf_op jit(solution)/shard_map/prepare/pallas_call | solution.py:198
  68.9 7.0 %slab_first.1 = (f32[34,4,16,128]{3,2,1,0:T(8,128)}, f32[4,8,3,128]{3,2,1,0:T(4,128)}) custom-call(f32[4,8,8,8,128]{4,3,2,1,0:T(8,128)} %bitcast.source_ref, f32[32,4,16,128]{3,2,1,0:T(8,128)} %get-tuple-element.31.inverse_ref, bf16[4,512,128]{2,1,0:T(8,128)(2,1)} %get-tuple-element.32.hit_ref, bf16[4,128,128]{2,1,0:T(8,128)(2,1)} %get-tuple-element.33.lane_ref, ...), custom_call_target="tpu_custom_call" | custom-call | tf_op jit(solution)/shard_map/slab_first/pallas_call | solution.py:391
  75.8 3.2 %all-to-all-start.1 = ((f32[32,3,128]{2,1,0:T(4,128)}), f32[32,3,128]{2,1,0:T(4,128)S(1)}, u32[]{:S(2)}, u32[]{:S(2)}) async-start(f32[32,3,128]{2,1,0:T(4,128)} %bitcast.57), calls=%async_computation.1 | async-start | bytes 131072 | tf_op jit(solution)/shard_map/all_to_all | solution.py:533
  79.1 7.5 %all-to-all-done.1.flux_ref = f32[32,3,128]{2,1,0:T(4,128)S(1)} async-done(((f32[32,3,128]{2,1,0:T(4,128)}), f32[32,3,128]{2,1,0:T(4,128)S(1)}, u32[]{:S(2)}, u32[]{:S(2)}) %all-to-all-start.1) | async-done | bytes 49184 | tf_op jit(solution)/shard_map/all_to_all | solution.py:533
  93.8 2.1 %collective-permute-done.15.a_other = bf16[32,2048]{1,0:T(8,128)(2,1)S(1)} collective-permute-done((bf16[32,2048]{1,0:T(8,128)(2,1)S(1)}, bf16[32,2048]{1,0:T(8,128)(2,1)S(1)}, u32[]{:S(2)}, u32[]{:S(2)}) %collective-permute-start.15) | collective-permute-done | bytes 131104 | tf_op jit(solution)/shard_map/ppermute | solution.py:52
  97.3 2.0 %potential.2.rest_0_ = f32[32,3,128]{2,1,0:T(4,128)S(1)} custom-call(f32[32,4096]{1,0:T(8,128)S(1)} %get-tuple-element.55.a_density, f32[32,4096]{1,0:T(8,128)S(1)} %get-tuple-element.54.b_density, bf16[32,2048]{1,0:T(8,128)(2,1)S(1)} %get-tuple-element.43.a_half, bf16[32,2048]{1,0:T(8,128)(2,1)S(1)} %get-tuple-element.46.b_half, ...), custom_call_target="tpu_custom_call" | custom-call | tf_op jit(solution)/shard_map/potential/pallas_call | solution.py:465
  99.4 2.0 %potential.3 = f32[32,3,128]{2,1,0:T(4,128)S(1)} custom-call(f32[32,4096]{1,0:T(8,128)S(1)} %get-tuple-element.55.a_density, f32[32,4096]{1,0:T(8,128)S(1)} %get-tuple-element.54.b_density, bf16[32,2048]{1,0:T(8,128)(2,1)S(1)} %get-tuple-element.44.a_half, bf16[32,2048]{1,0:T(8,128)(2,1)S(1)} %get-tuple-element.45.b_half, ...), custom_call_target="tpu_custom_call" | custom-call | tf_op jit(solution)/shard_map/potential/pallas_call | solution.py:465
  101.5 9.4 %all_to_all.25 = f32[32,3,128]{2,1,0:T(4,128)S(1)} all-to-all(f32[32,3,128]{2,1,0:T(4,128)S(1)} %potential.3), channel_id=1, replica_groups=mesh['row'=4,'col'=2,'vol'=4] {'row','col','vol'}, dimensions={0} | all-to-all | bytes 98304 | tf_op jit(solution)/shard_map/all_to_all | solution.py:540
  110.9 4.5 %slab_last.1 = (f32[4,8,8,8,128]{4,3,2,1,0:T(8,128)S(1)}, f32[4,8,3,128]{3,2,1,0:T(4,128)S(1)}) custom-call(f32[4,8,8,8,128]{4,3,2,1,0:T(8,128)} %bitcast.source_ref, f32[32,4,16,128]{3,2,1,0:T(8,128)S(1)} %copy-done.2, bf16[4,512,128]{2,1,0:T(8,128)(2,1)S(1)} %copy-done.3, bf16[4,128,128]{2,1,0:T(8,128)(2,1)S(1)} %copy-done.18, ...), custom_call_target="tpu_custom_call" | custom-call | tf_op jit(solution)/shard_map/slab_last/pallas_call | solution.py:391
  115.4 9.2 %all_to_all.26.flux_ref = f32[32,3,128]{2,1,0:T(4,128)S(1)} all-to-all(f32[32,3,128]{2,1,0:T(4,128)S(1)} %bitcast.56), channel_id=1, replica_groups=mesh['row'=4,'col'=2,'vol'=4] {'row','col','vol'}, dimensions={0} | all-to-all | bytes 98304 | tf_op jit(solution)/shard_map/all_to_all | solution.py:544
  124.6 2.2 %update.5 = (bf16[32,4096]{1,0:T(8,128)(2,1)}, bf16[32,4096]{1,0:T(8,128)(2,1)S(1)}) custom-call(f32[32,3,128]{2,1,0:T(4,128)S(1)} %all_to_all.26.flux_ref, bf16[128,4096]{1,0:T(8,128)(2,1)S(1)} %copy-done, bf16[128,4096]{1,0:T(8,128)(2,1)S(1)} %collective-permute-done.13.a_mate, bf16[128,4096]{1,0:T(8,128)(2,1)S(1)} %copy-done.1, ...), custom_call_target="tpu_custom_call" | custom-call | tf_op jit(solution)/shard_map/update/pallas_call | solution.py:419
  128.3 2.6 %all-to-all-start.4 = ((f32[32,8,8,128]{3,2,1,0:T(8,128)}), f32[32,8,8,128]{3,2,1,0:T(8,128)S(1)}, u32[]{:S(2)}, u32[]{:S(2)}) async-start(f32[32,8,8,128]{3,2,1,0:T(8,128)} %bitcast.54), calls=%async_computation.4 | async-start | bytes 2097152 | tf_op jit(solution)/shard_map/all_to_all | solution.py:546
  132.7 9.5 %collective-permute-done.19 = bf16[32,4096]{1,0:T(8,128)(2,1)S(1)} collective-permute-done((bf16[32,4096]{1,0:T(8,128)(2,1)}, bf16[32,4096]{1,0:T(8,128)(2,1)S(1)}, u32[]{:S(2)}, u32[]{:S(2)}) %collective-permute-start.19) | collective-permute-done | bytes 262176 | tf_op jit(solution)/shard_map/ppermute | solution.py:52
  143.4 5.2 %collective-permute-done.21 = bf16[32,4096]{1,0:T(8,128)(2,1)S(1)} collective-permute-done((bf16[32,4096]{1,0:T(8,128)(2,1)S(1)}, bf16[32,4096]{1,0:T(8,128)(2,1)S(1)}, u32[]{:S(2)}, u32[]{:S(2)}) %collective-permute-start.21) | collective-permute-done | bytes 262176 | tf_op jit(solution)/shard_map/ppermute | solution.py:52
  150.3 5.5 %collective-permute-done.20 = bf16[32,4096]{1,0:T(8,128)(2,1)S(1)} collective-permute-done((bf16[32,4096]{1,0:T(8,128)(2,1)S(1)}, bf16[32,4096]{1,0:T(8,128)(2,1)S(1)}, u32[]{:S(2)}, u32[]{:S(2)}) %collective-permute-start.20) | collective-permute-done | bytes 262176 | tf_op jit(solution)/shard_map/ppermute | solution.py:52
  155.8 2.0 %collective-permute-done.22 = bf16[32,4096]{1,0:T(8,128)(2,1)S(1)} collective-permute-done((bf16[32,4096]{1,0:T(8,128)(2,1)S(1)}, bf16[32,4096]{1,0:T(8,128)(2,1)S(1)}, u32[]{:S(2)}, u32[]{:S(2)}) %collective-permute-start.22) | collective-permute-done | bytes 262176 | tf_op jit(solution)/shard_map/ppermute | solution.py:52
  160.4 2.0 %landed.1 = f32[32,8,8,128]{3,2,1,0:T(8,128)} custom-call(f32[32,8,8,128]{3,2,1,0:T(8,128)} %copy-done.23), custom_call_target="tpu_custom_call" | custom-call | tf_op jit(solution)/shard_map/landed/pallas_call | solution.py:229
  (130 shorter events, 31.8 us)
Async XLA Ops:
  1.4 12.4 %collective-permute-start.2 = (bf16[64,128]{1,0:T(8,128)(2,1)S(1)}, bf16[64,128]{1,0:T(8,128)(2,1)S(1)}, u32[]{:S(2)}, u32[]{:S(2)}) collective-permute-start(bf16[64,128]{1,0:T(8,128)(2,1)S(1)} %get-tuple-element.53), channel_id=1, source_target_pairs={{0,3},{1,2},{2,1},{3,0},{4,7},{5,6},{6,5},{7,4},{8,11},{9,10},{10,... | collective-permute-start | bytes 49160 | tf_op jit(solution)/shard_map/ppermute | solution.py:52
  6.5 7.3 %collective-permute-start.1 = (bf16[64,128]{1,0:T(8,128)(2,1)S(1)}, bf16[64,128]{1,0:T(8,128)(2,1)S(1)}, u32[]{:S(2)}, u32[]{:S(2)}) collective-permute-start(bf16[64,128]{1,0:T(8,128)(2,1)S(1)} %get-tuple-element.53), channel_id=1, source_target_pairs={{0,2},{1,3},{2,0},{3,1},{4,6},{5,7},{6,4},{7,5},{8,10},{9,11},{10,... | collective-permute-start | bytes 49160 | tf_op jit(solution)/shard_map/ppermute | solution.py:52
  6.5 7.3 %collective-permute-start = (bf16[64,128]{1,0:T(8,128)(2,1)S(1)}, bf16[64,128]{1,0:T(8,128)(2,1)S(1)}, u32[]{:S(2)}, u32[]{:S(2)}) collective-permute-start(bf16[64,128]{1,0:T(8,128)(2,1)S(1)} %get-tuple-element.53), channel_id=1, source_target_pairs={{0,1},{1,0},{2,3},{3,2},{4,5},{5,4},{6,7},{7,6},{8,9},{9,8},{10,11... | collective-permute-start | bytes 49160 | tf_op jit(solution)/shard_map/ppermute | solution.py:52
  7.1 61.1 %all-to-all-start = ((f32[32,8,8,128]{3,2,1,0:T(8,128)}), f32[32,8,8,128]{3,2,1,0:T(8,128)}, u32[]{:S(2)}, u32[]{:S(2)}) async-start(f32[32,8,8,128]{3,2,1,0:T(8,128)} %param.9), calls=%async_computation | async-start | bytes 2097152 | tf_op jit(solution)/shard_map/all_to_all | solution.py:512
  20.8 58.2 %collective-permute-start.13 = (bf16[128,4096]{1,0:T(8,128)(2,1)}, bf16[128,4096]{1,0:T(8,128)(2,1)S(1)}, u32[]{:S(2)}, u32[]{:S(2)}) collective-permute-start(bf16[128,4096]{1,0:T(8,128)(2,1)} %get-tuple-element.40), channel_id=1, source_target_pairs={{0,8},{8,0},{16,24},{24,16},{1,9},{9,1},{17,25},{25,17},{2,10},{10... | collective-permute-start | bytes 3145736 | tf_op jit(solution)/shard_map/ppermute | solution.py:52
  22.6 56.5 %collective-permute-start.14 = (bf16[128,4096]{1,0:T(8,128)(2,1)}, bf16[128,4096]{1,0:T(8,128)(2,1)}, u32[]{:S(2)}, u32[]{:S(2)}) collective-permute-start(bf16[128,4096]{1,0:T(8,128)(2,1)} %get-tuple-element.42), channel_id=1, source_target_pairs={{0,16},{8,24},{16,0},{24,8},{1,17},{9,25},{17,1},{25,9},{2,18},{10... | collective-permute-start | bytes 3145736 | tf_op jit(solution)/shard_map/ppermute | solution.py:52
  24.1 29.5 %collective-permute-start.3 = (bf16[320,128]{1,0:T(8,128)(2,1)}, bf16[320,128]{1,0:T(8,128)(2,1)S(1)}, u32[]{:S(2)}, u32[]{:S(2)}) collective-permute-start(bf16[320,128]{1,0:T(8,128)(2,1)} %get-tuple-element.28), channel_id=1, source_target_pairs={{0,8},{8,0},{16,24},{24,16},{1,9},{9,1},{17,25},{25,17},{2,10},{10... | collective-permute-start | bytes 245768 | tf_op jit(solution)/shard_map/ppermute | solution.py:52
  24.6 29.0 %collective-permute-start.4 = (bf16[320,128]{1,0:T(8,128)(2,1)}, bf16[320,128]{1,0:T(8,128)(2,1)S(1)}, u32[]{:S(2)}, u32[]{:S(2)}) collective-permute-start(bf16[320,128]{1,0:T(8,128)(2,1)} %get-tuple-element.29), channel_id=1, source_target_pairs={{0,16},{8,24},{16,0},{24,8},{1,17},{9,25},{17,1},{25,9},{2,18},{10... | collective-permute-start | bytes 245768 | tf_op jit(solution)/shard_map/ppermute | solution.py:52
  25.0 31.2 %collective-permute-start.5 = (bf16[320,128]{1,0:T(8,128)(2,1)}, bf16[320,128]{1,0:T(8,128)(2,1)S(1)}, u32[]{:S(2)}, u32[]{:S(2)}) collective-permute-start(bf16[320,128]{1,0:T(8,128)(2,1)} %get-tuple-element.30), channel_id=1, source_target_pairs={{0,24},{8,16},{16,8},{24,0},{1,25},{9,17},{17,9},{25,1},{2,26},{10... | collective-permute-start | bytes 245768 | tf_op jit(solution)/shard_map/ppermute | solution.py:52
  53.6 2.5 %collective-permute-start.6 = (bf16[320,128]{1,0:T(8,128)(2,1)}, bf16[320,128]{1,0:T(8,128)(2,1)S(1)}, u32[]{:S(2)}, u32[]{:S(2)}) collective-permute-start(bf16[320,128]{1,0:T(8,128)(2,1)} %get-tuple-element.27.refs_0_), channel_id=1, source_target_pairs={{0,4},{4,0},{1,5},{5,1},{2,6},{6,2},{3,7},{7,3},{8,12},{12,8},{9,1... | collective-permute-start | bytes 245768 | tf_op jit(solution)/shard_map/ppermute | solution.py:52
  53.6 3.0 %collective-permute-start.7 = (bf16[320,128]{1,0:T(8,128)(2,1)S(1)}, bf16[320,128]{1,0:T(8,128)(2,1)S(1)}, u32[]{:S(2)}, u32[]{:S(2)}) collective-permute-start(bf16[320,128]{1,0:T(8,128)(2,1)S(1)} %collective-permute-done.3.refs_1_), channel_id=1, source_target_pairs={{0,4},{4,0},{1,5},{5,1},{2,6},{6,2},{3,7},{7,3},{8,12},{12,8},{9,1... | collective-permute-start | bytes 245768 | tf_op jit(solution)/shard_map/ppermute | solution.py:52
  59.5 8.3 %collective-permute-start.10 = (f32[4,128]{1,0:T(4,128)}, f32[4,128]{1,0:T(4,128)S(1)}, u32[]{:S(2)}, u32[]{:S(2)}) collective-permute-start(f32[4,128]{1,0:T(4,128)} %get-tuple-element.35), channel_id=1, source_target_pairs={{0,1},{1,0},{2,3},{3,2},{4,5},{5,4},{6,7},{7,6},{8,9},{9,8},{10,11... | collective-permute-start | bytes 6152 | tf_op jit(solution)/shard_map/ppermute | solution.py:52
  61.1 6.7 %collective-permute-start.11 = (f32[4,128]{1,0:T(4,128)}, f32[4,128]{1,0:T(4,128)S(1)}, u32[]{:S(2)}, u32[]{:S(2)}) collective-permute-start(f32[4,128]{1,0:T(4,128)} %get-tuple-element.36), channel_id=1, source_target_pairs={{0,2},{1,3},{2,0},{3,1},{4,6},{5,7},{6,4},{7,5},{8,10},{9,11},{10,... | collective-permute-start | bytes 6152 | tf_op jit(solution)/shard_map/ppermute | solution.py:52
  62.8 5.4 %collective-permute-start.12 = (f32[4,128]{1,0:T(4,128)}, f32[4,128]{1,0:T(4,128)S(1)}, u32[]{:S(2)}, u32[]{:S(2)}) collective-permute-start(f32[4,128]{1,0:T(4,128)} %get-tuple-element.37), channel_id=1, source_target_pairs={{0,3},{1,2},{2,1},{3,0},{4,7},{5,6},{6,5},{7,4},{8,11},{9,10},{10,... | collective-permute-start | bytes 6152 | tf_op jit(solution)/shard_map/ppermute | solution.py:52
  75.8 10.7 %all-to-all-start.1 = ((f32[32,3,128]{2,1,0:T(4,128)}), f32[32,3,128]{2,1,0:T(4,128)S(1)}, u32[]{:S(2)}, u32[]{:S(2)}) async-start(f32[32,3,128]{2,1,0:T(4,128)} %bitcast.57), calls=%async_computation.1 | async-start | bytes 131072 | tf_op jit(solution)/shard_map/all_to_all | solution.py:533
  88.0 11.4 %collective-permute-start.16 = (bf16[32,2048]{1,0:T(8,128)(2,1)S(1)}, bf16[32,2048]{1,0:T(8,128)(2,1)S(1)}, u32[]{:S(2)}, u32[]{:S(2)}) collective-permute-start(bf16[32,2048]{1,0:T(8,128)(2,1)S(1)} %get-tuple-element.44.a_half), channel_id=1, source_target_pairs={{0,16},{8,24},{16,0},{24,8},{1,17},{9,25},{17,1},{25,9},{2,18},{10... | collective-permute-start | bytes 393224 | tf_op jit(solution)/shard_map/ppermute | solution.py:52
  88.8 10.6 %collective-permute-start.17 = (bf16[32,2048]{1,0:T(8,128)(2,1)S(1)}, bf16[32,2048]{1,0:T(8,128)(2,1)S(1)}, u32[]{:S(2)}, u32[]{:S(2)}) collective-permute-start(bf16[32,2048]{1,0:T(8,128)(2,1)S(1)} %get-tuple-element.45.b_half), channel_id=1, source_target_pairs={{0,8},{8,0},{16,24},{24,16},{1,9},{9,1},{17,25},{25,17},{2,10},{10... | collective-permute-start | bytes 393224 | tf_op jit(solution)/shard_map/ppermute | solution.py:52
  90.8 5.1 %collective-permute-start.15 = (bf16[32,2048]{1,0:T(8,128)(2,1)S(1)}, bf16[32,2048]{1,0:T(8,128)(2,1)S(1)}, u32[]{:S(2)}, u32[]{:S(2)}) collective-permute-start(bf16[32,2048]{1,0:T(8,128)(2,1)S(1)} %get-tuple-element.43.a_half), channel_id=1, source_target_pairs={{0,16},{8,24},{16,0},{24,8},{1,17},{9,25},{17,1},{25,9},{2,18},{10... | collective-permute-start | bytes 393224 | tf_op jit(solution)/shard_map/ppermute | solution.py:52
  92.3 5.0 %collective-permute-start.18 = (bf16[32,2048]{1,0:T(8,128)(2,1)S(1)}, bf16[32,2048]{1,0:T(8,128)(2,1)S(1)}, u32[]{:S(2)}, u32[]{:S(2)}) collective-permute-start(bf16[32,2048]{1,0:T(8,128)(2,1)S(1)} %get-tuple-element.46.b_half), channel_id=1, source_target_pairs={{0,8},{8,0},{16,24},{24,16},{1,9},{9,1},{17,25},{25,17},{2,10},{10... | collective-permute-start | bytes 393224 | tf_op jit(solution)/shard_map/ppermute | solution.py:52
  127.5 14.6 %collective-permute-start.19 = (bf16[32,4096]{1,0:T(8,128)(2,1)}, bf16[32,4096]{1,0:T(8,128)(2,1)S(1)}, u32[]{:S(2)}, u32[]{:S(2)}) collective-permute-start(bf16[32,4096]{1,0:T(8,128)(2,1)} %get-tuple-element.49), channel_id=1, source_target_pairs={{0,16},{8,24},{16,0},{24,8},{1,17},{9,25},{17,1},{25,9},{2,18},{10... | collective-permute-start | bytes 786440 | tf_op jit(solution)/shard_map/ppermute | solution.py:52
  128.3 31.1 %all-to-all-start.4 = ((f32[32,8,8,128]{3,2,1,0:T(8,128)}), f32[32,8,8,128]{3,2,1,0:T(8,128)S(1)}, u32[]{:S(2)}, u32[]{:S(2)}) async-start(f32[32,8,8,128]{3,2,1,0:T(8,128)} %bitcast.54), calls=%async_computation.4 | async-start | bytes 2097152 | tf_op jit(solution)/shard_map/all_to_all | solution.py:546
  131.0 17.6 %collective-permute-start.21 = (bf16[32,4096]{1,0:T(8,128)(2,1)S(1)}, bf16[32,4096]{1,0:T(8,128)(2,1)S(1)}, u32[]{:S(2)}, u32[]{:S(2)}) collective-permute-start(bf16[32,4096]{1,0:T(8,128)(2,1)S(1)} %copy-done.20), channel_id=1, source_target_pairs={{0,8},{8,0},{16,24},{24,16},{1,9},{9,1},{17,25},{25,17},{2,10},{10... | collective-permute-start | bytes 786440 | tf_op jit(solution)/shard_map/ppermute | solution.py:52
  143.3 12.5 %collective-permute-start.20 = (bf16[32,4096]{1,0:T(8,128)(2,1)S(1)}, bf16[32,4096]{1,0:T(8,128)(2,1)S(1)}, u32[]{:S(2)}, u32[]{:S(2)}) collective-permute-start(bf16[32,4096]{1,0:T(8,128)(2,1)S(1)} %multiply_convert_fusion.1), channel_id=1, source_target_pairs={{0,8},{8,0},{16,24},{24,16},{1,9},{9,1},{17,25},{25,17},{2,10},{10... | collective-permute-start | bytes 786440 | tf_op jit(solution)/shard_map/ppermute | solution.py:52
  148.7 9.1 %collective-permute-start.22 = (bf16[32,4096]{1,0:T(8,128)(2,1)S(1)}, bf16[32,4096]{1,0:T(8,128)(2,1)S(1)}, u32[]{:S(2)}, u32[]{:S(2)}) collective-permute-start(bf16[32,4096]{1,0:T(8,128)(2,1)S(1)} %multiply_convert_fusion), channel_id=1, source_target_pairs={{0,16},{8,24},{16,0},{24,8},{1,17},{9,25},{17,1},{25,9},{2,18},{10... | collective-permute-start | bytes 786440 | tf_op jit(solution)/shard_map/ppermute | solution.py:52
  (38 other events, 342.9 us)

commit v10 on v9

--- a/solution.py
+++ b/solution.py
@@ -259,25 +259,10 @@
 
     def body(source_ref, inverse_ref, hit_ref, lane_ref, *rest):
         if first:
-            *part_refs, far_ref, flux_ref, other_ref, scaled_ref, ratio_ref, sem = rest[:-6]
-            out_ref, *held, load_sems = rest[-6:]
-            fars = (lane_ref, hit_ref, source_ref, inverse_ref)
-            lane_ref, hit_ref, source_ref, inverse_ref = held
-            whole = [pltpu.make_async_copy(fars[i], held[i], load_sems.at[i]) for i in range(2)]
-            chunks = []
-            for r in range(rows):
-                deep = pl.ds(r * bx, bx)
-                chunks.append((
-                    pltpu.make_async_copy(fars[2].at[r], held[2].at[r], load_sems.at[2 + 2 * r]),
-                    pltpu.make_async_copy(fars[3].at[deep], held[3].at[deep], load_sems.at[3 + 2 * r]),
-                ))
-            for copy in whole + [copy for pair in chunks for copy in pair]:
-                copy.start()
-            result_ref = out_ref
+            *part_refs, out_ref, flux_ref, other_ref, scaled_ref, ratio_ref = rest
         else:
             parts_ref, start_ref, far_ref, flux_ref, out_ref, *rest = rest
             other_ref, scaled_ref, ratio_ref, volume_ref, sem = rest
-            result_ref = volume_ref
         sub = lax.broadcasted_iota(jnp.int32, (by, bz), 0)
         lan = lax.broadcasted_iota(jnp.int32, (by, bz), 1)
         for ref in (out_ref, other_ref):
@@ -295,9 +280,6 @@
                     for k, mate in enumerate(MATES)
                 )
             potentials.append(potential)
-            if first and r == 0:
-                for copy in whole:
-                    copy.wait()
             weights = [
                 lane_ref[r] * piece.astype(jnp.bfloat16) for piece in parts_of(potential, 3)
             ]
@@ -307,9 +289,6 @@
             )
             added = added[:, :bz] + added[:, bz:2 * bz] + added[:, 2 * bz:]
             added = added.reshape(bx, vols, cols, by, bz)
-            if first:
-                for copy in chunks[r]:
-                    copy.wait()
             for j in range(blocks):
                 c, v = j // vols, j % vols
                 span = (slice(r * bx, (r + 1) * bx), v, slice(c * by, (c + 1) * by))
@@ -360,8 +339,9 @@
                 step(index, 0)
             here = there
 
-        store = pltpu.make_async_copy(result_ref, far_ref, sem)
-        store.start()
+        if not first:
+            store = pltpu.make_async_copy(volume_ref, far_ref, sem)
+            store.start()
         for r in range(rows):
             part = here[1 + r * bx:1 + (r + 1) * bx].reshape(height, bz)
             met = sum(
@@ -372,36 +352,33 @@
             value = value - potentials[r]
             for k, mate in enumerate(MATES):
                 flux_ref[r ^ mate, :, k, :] = jnp.broadcast_to(value, (blocks, targets))
-        store.wait()
+        if not first:
+            store.wait()
 
     vmem = pl.BlockSpec(memory_space=pltpu.VMEM)
     operands = [source, inverse, hit, lane] + (list(parts) if first else [parts, start])
     fluxes = jax.ShapeDtypeStruct((rows, blocks, len(MATES), targets), jnp.float32)
     field = padded if first else (rows, blocks, bx, by, bz)
     field = jax.ShapeDtypeStruct(field, jnp.float32)
-    hbm = pl.BlockSpec(memory_space=pltpu.HBM)
-    work = [pltpu.VMEM(padded, jnp.float32)] + [pltpu.VMEM(planes, jnp.float32)] * 2
-    done = pltpu.SemaphoreType.DMA(())
-    if first:
-        scratch = work + [done, pltpu.VMEM(padded, jnp.float32)]
-        scratch += [pltpu.VMEM(value.shape, value.dtype) for value in (lane, hit, source, inverse)]
-        scratch.append(pltpu.SemaphoreType.DMA((2 + 2 * rows,)))
-    else:
-        scratch = [pltpu.VMEM(padded, jnp.float32)] + work + [pltpu.VMEM(field.shape, jnp.float32), done]
+    scratch = [pltpu.VMEM(padded, jnp.float32)] + [pltpu.VMEM(planes, jnp.float32)] * 2
+    if not first:
+        scratch = [pltpu.VMEM(padded, jnp.float32)] + scratch
+        scratch += [pltpu.VMEM(field.shape, jnp.float32), pltpu.SemaphoreType.DMA(())]
     return pl.pallas_call(
         body,
         out_shape=[field, fluxes],
-        in_specs=([hbm] * 4 if first else [vmem] * 4) + [vmem] * (len(operands) - 4),
-        out_specs=[hbm, vmem],
+        in_specs=[vmem] * len(operands),
+        out_specs=[vmem if first else pl.BlockSpec(memory_space=pltpu.HBM), vmem],
         scratch_shapes=scratch,
         compiler_params=None if first else pltpu.CompilerParams(vmem_limit_bytes=SLAB_BYTES),
         name="slab_first" if first else "slab_last",
     )(*operands)
 
 
-def update_call(flux, panels, part, parts):
+def update_call(flux, panels, part, parts, keep):
     excitations, width = flux.shape[0], panels[0].shape[1] // parts
     span = slice(part * width, (part + 1) * width)
+    far = jax.ShapeDtypeStruct((panels[3].shape[0], width), panels[3].dtype)
 
     def body(flux_ref, a_own, a_mate, b_own, b_far, a_ref, b_ref, b_mate, sem):
         load = pltpu.make_async_copy(b_far.at[:, span], b_mate, sem)
@@ -418,12 +395,10 @@
     vmem = pl.BlockSpec(memory_space=pltpu.VMEM)
     return pl.pallas_call(
         body,
-        out_shape=[jax.ShapeDtypeStruct((excitations, width), jnp.bfloat16)] * 2,
+        out_shape=[jax.ShapeDtypeStruct((excitations, width), jnp.bfloat16)] * 2 + ([far] if keep else []),
         in_specs=[vmem] * 4 + [pl.BlockSpec(memory_space=pltpu.HBM)],
-        out_specs=[vmem] * 2,
-        scratch_shapes=[
-            pltpu.VMEM((panels[0].shape[0], width), panels[0].dtype), pltpu.SemaphoreType.DMA(())
-        ],
+        out_specs=[vmem] * (3 if keep else 2),
+        scratch_shapes=([] if keep else [pltpu.VMEM(far.shape, far.dtype)]) + [pltpu.SemaphoreType.DMA(())],
         compiler_params=pltpu.CompilerParams(vmem_limit_bytes=VMEM_BYTES),
         name="update",
     )(flux, *panels)
@@ -435,10 +410,8 @@
     span = slice(part * width, (part + 1) * width)
 
     def body(a_density, b_density, a_half, b_half, a_other, b_other,
-             a_own, a_mate, b_own, b_far, *rest):
-        out_ref, b_mate, sem = rest[-3:]
-        load = pltpu.make_async_copy(b_far.at[:, span], b_mate, sem)
-        load.start()
+             a_own, a_mate, b_own, b_mate, *rest):
+        out_ref = rest[-1]
         rounded = [
             (density[:, span] + RELAXATION * (half[...].astype(jnp.float32)
                                               + other[...].astype(jnp.float32))).astype(jnp.bfloat16)
@@ -457,7 +430,6 @@
 
         put(0, met(rounded[0], a_own[:, span]) + met(rounded[1], b_own[:, span]))
         put(1, met(rounded[0], a_mate[:, span]))
-        load.wait()
         put(2, met(rounded[1], b_mate[...]))
 
     vmem = pl.BlockSpec(memory_space=pltpu.VMEM)
@@ -465,11 +437,38 @@
     return pl.pallas_call(
         body,
         out_shape=jax.ShapeDtypeStruct((excitations, len(MATES), targets), jnp.float32),
-        in_specs=[vmem] * 9 + [pl.BlockSpec(memory_space=pltpu.HBM)] + [vmem] * (len(operands) - 10),
+        in_specs=[vmem] * len(operands),
         out_specs=vmem,
-        scratch_shapes=[pltpu.VMEM((targets, width), panels[0].dtype), pltpu.SemaphoreType.DMA(())],
         compiler_params=pltpu.CompilerParams(vmem_limit_bytes=VMEM_BYTES),
         name="potential",
+    )(*operands)
+
+
+def totals_call(firsts, ends):
+    groups = len(ends)
+    width = firsts[0][0][0].shape[1]
+
+    def body(*refs):
+        outs, rest = refs[-groups:], list(refs[:-groups])
+        first_refs = [[[rest.pop(0) for _ in pair] for pair in parts] for parts in firsts]
+        end_refs = [[rest.pop(0) for _ in pair] for pair in ends]
+        for group in range(groups):
+            for part, (a, b) in enumerate(first_refs[group]):
+                span = slice(part * width, (part + 1) * width)
+                pieces = [a[...], b[...]] + [ref[:, span] for ref in end_refs[group]]
+                a, b, c, d = (piece.astype(jnp.float32) for piece in pieces)
+                outs[group][:, span] = (RELAXATION * ((a + b) + (c + d))).astype(jnp.bfloat16)
+
+    vmem = pl.BlockSpec(memory_space=pltpu.VMEM)
+    operands = [value for parts in firsts for pair in parts for value in pair]
+    operands += [value for pair in ends for value in pair]
+    return pl.pallas_call(
+        body,
+        out_shape=[jax.ShapeDtypeStruct(pair[0].shape, jnp.bfloat16) for pair in ends],
+        in_specs=[vmem] * len(operands),
+        out_specs=[vmem] * groups,
+        compiler_params=pltpu.CompilerParams(vmem_limit_bytes=VMEM_BYTES),
+        name="totals",
     )(*operands)
 
 
@@ -531,12 +530,16 @@
     volume, flux = slab_call(shape, True, slab, inverse, hit, lane, parts)
     flux = flux.reshape(excitations, len(MATES), targets)
     flux = lax.all_to_all(flux, ALL, 0, 0, tiled=True)
-    halves, mates, parts = [], [], None
+    halves, mates, fars, parts = [], [], [], None
     for part in range(PARTS):
-        halves.append(update_call(flux, panels, part, PARTS))
+        *pair, far = update_call(flux, panels, part, PARTS, True)
+        halves.append(pair)
+        fars.append(far)
         mates.append([mated(halves[part][0], "row", 2), mated(halves[part][1], "row", 1)])
     for part in range(PARTS):
-        parts = potential_call(densities, halves[part], mates[part], panels, part, parts)
+        parts = potential_call(
+            densities, halves[part], mates[part], [*panels[:3], fars[part]], part, parts
+        )
     parts = lax.all_to_all(parts, ALL, 0, 0, tiled=True)
     parts = parts.reshape(rows, blocks, len(MATES), targets)
     volume, flux = slab_call(shape, False, slab, inverse, hit, lane, parts, volume)
@@ -545,17 +548,12 @@
     volume = volume.reshape(excitations, bx, by, bz)
     volume = lax.all_to_all(volume, ALL, 0, 0, tiled=True)
     volume = landed_call(volume)
-    ends = update_call(flux, panels, 0, 1)
+    ends = update_call(flux, panels, 0, 1, False)
     end_mates = [mated(ends[0], "row", 2), mated(ends[1], "row", 1)]
-    totals = []
-    for group in range(2):
-        firsts = [
-            jnp.concatenate([pair[group] for pair in pairs], axis=1) for pairs in (halves, mates)
-        ]
-        a, b, c, d = (
-            value.astype(jnp.float32) for value in (*firsts, ends[group], end_mates[group])
-        )
-        totals.append((RELAXATION * ((a + b) + (c + d))).astype(jnp.bfloat16))
+    totals = totals_call(
+        [[(halves[part][g], mates[part][g]) for part in range(PARTS)] for g in range(2)],
+        list(zip(ends, end_mates)),
+    )
     moved = [mated(totals[0], "row", 1), mated(totals[1], "row", 2)]
     change = [
         jnp.where(low == 0, totals[0], moved[0]), jnp.where(low == 0, moved[0], totals[0]),

time: 163 us -> 164 us (level); the launches traced: 163 us -> 162 us
  waiting for transfers between devices: 62.5 us -> 68.5 us
  Pallas kernels: 33.9 us -> 30.1 us
  local copies, waits for them, and re-layouts: 3.77 us -> 2.01 us
    all_to_all x1, waiting for transfers between devices: 0.01 us -> 6.62 us  [split_by_excitation(): volume = lax.all_to_all(volume, ALL, 0, 0, tiled=True)]
    pallas_call x2, Pallas kernels: 4.04 us -> 1.57 us  [potential_call(): pl.pallas_call(body, out_shape=jax.ShapeDtypeStruct((excitations, len(MAT...]
    unnamed x75 -> x43, local copies, waits for them, and re-layouts: 3.7 us -> 1.94 us
    pallas_call x2 -> x3, Pallas kernels: 11.4 us -> 10.8 us  [the longest x2 10.5 us: slab_call(): pl.pallas_call(body, out_shape=[field, fluxes], in_specs=[vmem] * len(ope...]
  transfers between devices with their start and end apart: 26 -> 26, of which waited for: 11 -> 13; matrix products, arithmetic and copies ran while one was open for 2% -> 1% of each run, Pallas kernels for 13% -> 12%
where the time goes in v10:
time: 164 us; the launch traced here: 162 us
  waiting for transfers between devices  68.5 us (42%)
  starting transfers between devices  38.4 us (23%)
  Pallas kernels  30.1 us (18%)
  blocking collectives  18.5 us (11%)
  other arithmetic  2.97 us (2%)
  local copies, waits for them, and re-layouts  2.01 us (1%)
    ppermute x23, waiting for transfers between devices, mated(): lax.ppermute(value, axis, [(i, i ^ mate) for i in range(lax.axis_size(axi...  54.4 us
    ppermute x23, starting transfers between devices, mated(): lax.ppermute(value, axis, [(i, i ^ mate) for i in range(lax.axis_size(axi...  25.6 us
    pallas_call x2, Pallas kernels, slab_call(): pl.pallas_call(body, out_shape=[field, fluxes], in_specs=[vmem] * len(ope...  10.5 us
    all_to_all x1, blocking collectives, split_by_excitation(): parts = lax.all_to_all(parts, ALL, 0, 0, tiled=True)  9.35 us
    all_to_all x1, blocking collectives, split_by_excitation(): flux = lax.all_to_all(flux, ALL, 0, 0, tiled=True)  9.19 us
    all_to_all x1, waiting for transfers between devices, split_by_excitation(): flux = lax.all_to_all(flux, ALL, 0, 0, tiled=True)  7.47 us
    all_to_all x1, waiting for transfers between devices, split_by_excitation(): volume = lax.all_to_all(volume, ALL, 0, 0, tiled=True)  6.62 us
    pallas_call x1, Pallas kernels, start_call(): pl.pallas_call(body, out_shape=[jax.ShapeDtypeStruct((lines + 4 * owners,...  6.29 us
  transfers between devices with their start and end apart: 26, of which 13 were waited for; matrix products, arithmetic and copies ran while one was open for 1% of the time, Pallas kernels for 12%

profile of v10, /device:TPU:0, one launch (start us, length us, event | category | flops | bytes accessed | tf_op | source)
XLA Modules:
  0.0 161.6 jit_solution(5831892507282241540)
XLA Ops:
  1.4 3.1 %collective-permute-start = (bf16[64,128]{1,0:T(8,128)(2,1)S(1)}, bf16[64,128]{1,0:T(8,128)(2,1)S(1)}, u32[]{:S(2)}, u32[]{:S(2)}) collective-permute-start(bf16[64,128]{1,0:T(8,128)(2,1)S(1)} %get-tuple-element.61), channel_id=1, source_target_pairs={{0,1},{1,0},{2,3},{3,2},{4,5},{5,4},{6,7},{7,6},{8,9},{9,8},{10,11... | collective-permute-start | bytes 49160 | tf_op jit(solution)/shard_map/ppermute | solution.py:52
  4.5 2.6 %collective-permute-start.1 = (bf16[64,128]{1,0:T(8,128)(2,1)S(1)}, bf16[64,128]{1,0:T(8,128)(2,1)S(1)}, u32[]{:S(2)}, u32[]{:S(2)}) collective-permute-start(bf16[64,128]{1,0:T(8,128)(2,1)S(1)} %get-tuple-element.61), channel_id=1, source_target_pairs={{0,2},{1,3},{2,0},{3,1},{4,6},{5,7},{6,4},{7,5},{8,10},{9,11},{10,... | collective-permute-start | bytes 49160 | tf_op jit(solution)/shard_map/ppermute | solution.py:52
  7.1 6.2 %all-to-all-start = ((f32[32,8,8,128]{3,2,1,0:T(8,128)}), f32[32,8,8,128]{3,2,1,0:T(8,128)}, u32[]{:S(2)}, u32[]{:S(2)}) async-start(f32[32,8,8,128]{3,2,1,0:T(8,128)} %param.9), calls=%async_computation | async-start | bytes 2097152 | tf_op jit(solution)/shard_map/all_to_all | solution.py:511
  14.5 6.3 %start.1 = (bf16[320,128]{1,0:T(8,128)(2,1)}, bf16[320,128]{1,0:T(8,128)(2,1)}, bf16[320,128]{1,0:T(8,128)(2,1)}, bf16[320,128]{1,0:T(8,128)(2,1)}, bf16[128,409...) custom-call(f32[32,16384]{1,0:T(8,128)} %density_ref.1, ...), custom_call_target="tpu_custom_call" | custom-call | tf_op jit(solution)/shard_map/start/pallas_call | solution.py:109
  20.8 1.8 %collective-permute-start.13 = (bf16[128,4096]{1,0:T(8,128)(2,1)}, bf16[128,4096]{1,0:T(8,128)(2,1)S(1)}, u32[]{:S(2)}, u32[]{:S(2)}) collective-permute-start(bf16[128,4096]{1,0:T(8,128)(2,1)} %get-tuple-element.44), channel_id=1, source_target_pairs={{0,8},{8,0},{16,24},{24,16},{1,9},{9,1},{17,25},{25,17},{2,10},{10... | collective-permute-start | bytes 3145736 | tf_op jit(solution)/shard_map/ppermute | solution.py:52
  25.0 2.6 %collective-permute-start.5 = (bf16[320,128]{1,0:T(8,128)(2,1)}, bf16[320,128]{1,0:T(8,128)(2,1)S(1)}, u32[]{:S(2)}, u32[]{:S(2)}) collective-permute-start(bf16[320,128]{1,0:T(8,128)(2,1)} %get-tuple-element.34), channel_id=1, source_target_pairs={{0,24},{8,16},{16,8},{24,0},{1,25},{9,17},{17,9},{25,1},{2,26},{10... | collective-permute-start | bytes 245768 | tf_op jit(solution)/shard_map/ppermute | solution.py:52
  27.5 26.0 %collective-permute-done.3.refs_1_ = bf16[320,128]{1,0:T(8,128)(2,1)S(1)} collective-permute-done((bf16[320,128]{1,0:T(8,128)(2,1)}, bf16[320,128]{1,0:T(8,128)(2,1)S(1)}, u32[]{:S(2)}, u32[]{:S(2)}) %collective-permute-start.3) | collective-permute-done | bytes 81952 | tf_op jit(solution)/shard_map/ppermute | solution.py:52
  54.1 2.0 %collective-permute-done.5.refs_3_ = bf16[320,128]{1,0:T(8,128)(2,1)S(1)} collective-permute-done((bf16[320,128]{1,0:T(8,128)(2,1)}, bf16[320,128]{1,0:T(8,128)(2,1)S(1)}, u32[]{:S(2)}, u32[]{:S(2)}) %collective-permute-start.5) | collective-permute-done | bytes 81952 | tf_op jit(solution)/shard_map/ppermute | solution.py:52
  61.1 1.8 %collective-permute-start.11 = (f32[4,128]{1,0:T(4,128)}, f32[4,128]{1,0:T(4,128)S(1)}, u32[]{:S(2)}, u32[]{:S(2)}) collective-permute-start(f32[4,128]{1,0:T(4,128)} %get-tuple-element.40), channel_id=1, source_target_pairs={{0,2},{1,3},{2,0},{3,1},{4,6},{5,7},{6,4},{7,5},{8,10},{9,11},{10,... | collective-permute-start | bytes 6152 | tf_op jit(solution)/shard_map/ppermute | solution.py:52
  64.2 3.6 %prepare.1 = (f32[32,4,16,128]{3,2,1,0:T(8,128)}, bf16[4,512,128]{2,1,0:T(8,128)(2,1)}, bf16[4,128,128]{2,1,0:T(8,128)(2,1)}) custom-call(f32[16]{0:T(128)} %values_ref.1, bf16[320,128]{1,0:T(8,128)(2,1)} %get-tuple-element.31.refs_0_, bf16[320,128]{1,0:T(8,128)(2,1)} %copy-done.8, bf16[320,128]{1,0:T(8,128)(2,1)} %copy-done.9, bf16[320,128]{1,0:T(8,128)(2,1)} %copy-done.10, ...), custom_call_target="tpu_custom_call" | custom-call | tf_op jit(solution)/shard_map/prepare/pallas_call | solution.py:198
  69.0 5.3 %slab_first.1 = (f32[34,4,16,128]{3,2,1,0:T(8,128)}, f32[4,8,3,128]{3,2,1,0:T(4,128)}) custom-call(f32[4,8,8,8,128]{4,3,2,1,0:T(8,128)} %bitcast.source_ref, f32[32,4,16,128]{3,2,1,0:T(8,128)} %get-tuple-element.35.inverse_ref, bf16[4,512,128]{2,1,0:T(8,128)(2,1)} %get-tuple-element.36.hit_ref, bf16[4,128,128]{2,1,0:T(8,128)(2,1)} %get-tuple-element.37.lane_ref, ...), custom_call_target="tpu_custom_call" | custom-call | tf_op jit(solution)/shard_map/slab_first/pallas_call | solution.py:367
  74.3 3.1 %all-to-all-start.1 = ((f32[32,3,128]{2,1,0:T(4,128)}), f32[32,3,128]{2,1,0:T(4,128)S(1)}, u32[]{:S(2)}, u32[]{:S(2)}) async-start(f32[32,3,128]{2,1,0:T(4,128)} %bitcast.56), calls=%async_computation.1 | async-start | bytes 131072 | tf_op jit(solution)/shard_map/all_to_all | solution.py:532
  77.4 7.5 %all-to-all-done.1.flux_ref = f32[32,3,128]{2,1,0:T(4,128)S(1)} async-done(((f32[32,3,128]{2,1,0:T(4,128)}), f32[32,3,128]{2,1,0:T(4,128)S(1)}, u32[]{:S(2)}, u32[]{:S(2)}) %all-to-all-start.1) | async-done | bytes 49184 | tf_op jit(solution)/shard_map/all_to_all | solution.py:532
  96.3 9.3 %all_to_all.25 = f32[32,3,128]{2,1,0:T(4,128)S(1)} all-to-all(f32[32,3,128]{2,1,0:T(4,128)S(1)} %potential.3), channel_id=1, replica_groups=mesh['row'=4,'col'=2,'vol'=4] {'row','col','vol'}, dimensions={0} | all-to-all | bytes 98304 | tf_op jit(solution)/shard_map/all_to_all | solution.py:543
  105.6 5.2 %slab_last.1 = (f32[4,8,8,8,128]{4,3,2,1,0:T(8,128)}, f32[4,8,3,128]{3,2,1,0:T(4,128)S(1)}) custom-call(f32[4,8,8,8,128]{4,3,2,1,0:T(8,128)} %bitcast.source_ref, f32[32,4,16,128]{3,2,1,0:T(8,128)S(1)} %copy-done.2, bf16[4,512,128]{2,1,0:T(8,128)(2,1)S(1)} %copy-done.3, bf16[4,128,128]{2,1,0:T(8,128)(2,1)S(1)} %copy-done.5, f32[4,8,3,128]{3,2,1,0:T(4,128)S(1)} %bitcast.54, ...), custom_call_target="tpu_custom_call" | custom-call | tf_op jit(solution)/shard_map/slab_last/pallas_call | solution.py:367
  110.8 9.2 %all_to_all.26.flux_ref = f32[32,3,128]{2,1,0:T(4,128)S(1)} all-to-all(f32[32,3,128]{2,1,0:T(4,128)S(1)} %bitcast.55), channel_id=1, replica_groups=mesh['row'=4,'col'=2,'vol'=4] {'row','col','vol'}, dimensions={0} | all-to-all | bytes 98304 | tf_op jit(solution)/shard_map/all_to_all | solution.py:547
  120.0 1.6 %update.5 = (bf16[32,4096]{1,0:T(8,128)(2,1)S(1)}, bf16[32,4096]{1,0:T(8,128)(2,1)S(1)}) custom-call(f32[32,3,128]{2,1,0:T(4,128)S(1)} %all_to_all.26.flux_ref, bf16[128,4096]{1,0:T(8,128)(2,1)S(1)} %copy-done, bf16[128,4096]{1,0:T(8,128)(2,1)S(1)} %collective-permute-done.13.a_mate, bf16[128,4096]{1,0:T(8,128)(2,1)S(1)} %copy-done.1, ...), custom_call_target="tpu_custom_call" | custom-call | tf_op jit(solution)/shard_map/update/pallas_call | solution.py:396
  122.9 6.6 %collective-permute-done.19.refs_9_ = bf16[32,4096]{1,0:T(8,128)(2,1)S(1)} collective-permute-done((bf16[32,4096]{1,0:T(8,128)(2,1)S(1)}, bf16[32,4096]{1,0:T(8,128)(2,1)S(1)}, u32[]{:S(2)}, u32[]{:S(2)}) %collective-permute-start.19) | collective-permute-done | bytes 262176 | tf_op jit(solution)/shard_map/ppermute | solution.py:52
  131.1 3.5 %all-to-all-start.4 = ((f32[32,8,8,128]{3,2,1,0:T(8,128)}), f32[32,8,8,128]{3,2,1,0:T(8,128)}, u32[]{:S(2)}, u32[]{:S(2)}) async-start(f32[32,8,8,128]{3,2,1,0:T(8,128)} %bitcast.10), calls=%async_computation.4 | async-start | bytes 2097152 | tf_op jit(solution)/shard_map/all_to_all | solution.py:549
  134.6 1.6 %collective-permute-start.22 = (bf16[32,4096]{1,0:T(8,128)(2,1)S(1)}, bf16[32,4096]{1,0:T(8,128)(2,1)S(1)}, u32[]{:S(2)}, u32[]{:S(2)}) collective-permute-start(bf16[32,4096]{1,0:T(8,128)(2,1)S(1)} %get-tuple-element.58), channel_id=1, source_target_pairs={{0,16},{8,24},{16,0},{24,8},{1,17},{9,25},{17,1},{25,9},{2,18},{10... | collective-permute-start | bytes 786440 | tf_op jit(solution)/shard_map/ppermute | solution.py:52
  136.2 1.6 %collective-permute-done.21 = bf16[32,4096]{1,0:T(8,128)(2,1)S(1)} collective-permute-done((bf16[32,4096]{1,0:T(8,128)(2,1)S(1)}, bf16[32,4096]{1,0:T(8,128)(2,1)S(1)}, u32[]{:S(2)}, u32[]{:S(2)}) %collective-permute-start.21) | collective-permute-done | bytes 262176 | tf_op jit(solution)/shard_map/ppermute | solution.py:52
  137.9 13.3 %collective-permute-done.22 = bf16[32,4096]{1,0:T(8,128)(2,1)S(1)} collective-permute-done((bf16[32,4096]{1,0:T(8,128)(2,1)S(1)}, bf16[32,4096]{1,0:T(8,128)(2,1)S(1)}, u32[]{:S(2)}, u32[]{:S(2)}) %collective-permute-start.22) | collective-permute-done | bytes 262176 | tf_op jit(solution)/shard_map/ppermute | solution.py:52
  152.9 6.6 %all-to-all-done.4.in_ref = f32[32,8,8,128]{3,2,1,0:T(8,128)} async-done(((f32[32,8,8,128]{3,2,1,0:T(8,128)}), f32[32,8,8,128]{3,2,1,0:T(8,128)}, u32[]{:S(2)}, u32[]{:S(2)}) %all-to-all-start.4) | async-done | bytes 1048608 | tf_op jit(solution)/shard_map/all_to_all | solution.py:549
  159.5 2.0 %landed.1 = f32[32,8,8,128]{3,2,1,0:T(8,128)} custom-call(f32[32,8,8,128]{3,2,1,0:T(8,128)} %all-to-all-done.4.in_ref), custom_call_target="tpu_custom_call" | custom-call | tf_op jit(solution)/shard_map/landed/pallas_call | solution.py:229
  (97 shorter events, 28.1 us)
Async XLA Ops:
  1.4 12.4 %collective-permute-start = (bf16[64,128]{1,0:T(8,128)(2,1)S(1)}, bf16[64,128]{1,0:T(8,128)(2,1)S(1)}, u32[]{:S(2)}, u32[]{:S(2)}) collective-permute-start(bf16[64,128]{1,0:T(8,128)(2,1)S(1)} %get-tuple-element.61), channel_id=1, source_target_pairs={{0,1},{1,0},{2,3},{3,2},{4,5},{5,4},{6,7},{7,6},{8,9},{9,8},{10,11... | collective-permute-start | bytes 49160 | tf_op jit(solution)/shard_map/ppermute | solution.py:52
  4.5 9.4 %collective-permute-start.1 = (bf16[64,128]{1,0:T(8,128)(2,1)S(1)}, bf16[64,128]{1,0:T(8,128)(2,1)S(1)}, u32[]{:S(2)}, u32[]{:S(2)}) collective-permute-start(bf16[64,128]{1,0:T(8,128)(2,1)S(1)} %get-tuple-element.61), channel_id=1, source_target_pairs={{0,2},{1,3},{2,0},{3,1},{4,6},{5,7},{6,4},{7,5},{8,10},{9,11},{10,... | collective-permute-start | bytes 49160 | tf_op jit(solution)/shard_map/ppermute | solution.py:52
  7.1 6.8 %collective-permute-start.2 = (bf16[64,128]{1,0:T(8,128)(2,1)S(1)}, bf16[64,128]{1,0:T(8,128)(2,1)S(1)}, u32[]{:S(2)}, u32[]{:S(2)}) collective-permute-start(bf16[64,128]{1,0:T(8,128)(2,1)S(1)} %get-tuple-element.61), channel_id=1, source_target_pairs={{0,3},{1,2},{2,1},{3,0},{4,7},{5,6},{6,5},{7,4},{8,11},{9,10},{10,... | collective-permute-start | bytes 49160 | tf_op jit(solution)/shard_map/ppermute | solution.py:52
  7.1 61.4 %all-to-all-start = ((f32[32,8,8,128]{3,2,1,0:T(8,128)}), f32[32,8,8,128]{3,2,1,0:T(8,128)}, u32[]{:S(2)}, u32[]{:S(2)}) async-start(f32[32,8,8,128]{3,2,1,0:T(8,128)} %param.9), calls=%async_computation | async-start | bytes 2097152 | tf_op jit(solution)/shard_map/all_to_all | solution.py:511
  20.8 56.6 %collective-permute-start.13 = (bf16[128,4096]{1,0:T(8,128)(2,1)}, bf16[128,4096]{1,0:T(8,128)(2,1)S(1)}, u32[]{:S(2)}, u32[]{:S(2)}) collective-permute-start(bf16[128,4096]{1,0:T(8,128)(2,1)} %get-tuple-element.44), channel_id=1, source_target_pairs={{0,8},{8,0},{16,24},{24,16},{1,9},{9,1},{17,25},{25,17},{2,10},{10... | collective-permute-start | bytes 3145736 | tf_op jit(solution)/shard_map/ppermute | solution.py:52
  22.6 54.8 %collective-permute-start.14 = (bf16[128,4096]{1,0:T(8,128)(2,1)}, bf16[128,4096]{1,0:T(8,128)(2,1)}, u32[]{:S(2)}, u32[]{:S(2)}) collective-permute-start(bf16[128,4096]{1,0:T(8,128)(2,1)} %get-tuple-element.46), channel_id=1, source_target_pairs={{0,16},{8,24},{16,0},{24,8},{1,17},{9,25},{17,1},{25,9},{2,18},{10... | collective-permute-start | bytes 3145736 | tf_op jit(solution)/shard_map/ppermute | solution.py:52
  24.1 29.5 %collective-permute-start.3 = (bf16[320,128]{1,0:T(8,128)(2,1)}, bf16[320,128]{1,0:T(8,128)(2,1)S(1)}, u32[]{:S(2)}, u32[]{:S(2)}) collective-permute-start(bf16[320,128]{1,0:T(8,128)(2,1)} %get-tuple-element.32), channel_id=1, source_target_pairs={{0,8},{8,0},{16,24},{24,16},{1,9},{9,1},{17,25},{25,17},{2,10},{10... | collective-permute-start | bytes 245768 | tf_op jit(solution)/shard_map/ppermute | solution.py:52
  24.6 29.0 %collective-permute-start.4 = (bf16[320,128]{1,0:T(8,128)(2,1)}, bf16[320,128]{1,0:T(8,128)(2,1)S(1)}, u32[]{:S(2)}, u32[]{:S(2)}) collective-permute-start(bf16[320,128]{1,0:T(8,128)(2,1)} %get-tuple-element.33), channel_id=1, source_target_pairs={{0,16},{8,24},{16,0},{24,8},{1,17},{9,25},{17,1},{25,9},{2,18},{10... | collective-permute-start | bytes 245768 | tf_op jit(solution)/shard_map/ppermute | solution.py:52
  25.0 31.2 %collective-permute-start.5 = (bf16[320,128]{1,0:T(8,128)(2,1)}, bf16[320,128]{1,0:T(8,128)(2,1)S(1)}, u32[]{:S(2)}, u32[]{:S(2)}) collective-permute-start(bf16[320,128]{1,0:T(8,128)(2,1)} %get-tuple-element.34), channel_id=1, source_target_pairs={{0,24},{8,16},{16,8},{24,0},{1,25},{9,17},{17,9},{25,1},{2,26},{10... | collective-permute-start | bytes 245768 | tf_op jit(solution)/shard_map/ppermute | solution.py:52
  53.6 2.5 %collective-permute-start.6 = (bf16[320,128]{1,0:T(8,128)(2,1)}, bf16[320,128]{1,0:T(8,128)(2,1)S(1)}, u32[]{:S(2)}, u32[]{:S(2)}) collective-permute-start(bf16[320,128]{1,0:T(8,128)(2,1)} %get-tuple-element.31.refs_0_), channel_id=1, source_target_pairs={{0,4},{4,0},{1,5},{5,1},{2,6},{6,2},{3,7},{7,3},{8,12},{12,8},{9,1... | collective-permute-start | bytes 245768 | tf_op jit(solution)/shard_map/ppermute | solution.py:52
  53.6 3.0 %collective-permute-start.7 = (bf16[320,128]{1,0:T(8,128)(2,1)S(1)}, bf16[320,128]{1,0:T(8,128)(2,1)S(1)}, u32[]{:S(2)}, u32[]{:S(2)}) collective-permute-start(bf16[320,128]{1,0:T(8,128)(2,1)S(1)} %collective-permute-done.3.refs_1_), channel_id=1, source_target_pairs={{0,4},{4,0},{1,5},{5,1},{2,6},{6,2},{3,7},{7,3},{8,12},{12,8},{9,1... | collective-permute-start | bytes 245768 | tf_op jit(solution)/shard_map/ppermute | solution.py:52
  59.5 8.3 %collective-permute-start.10 = (f32[4,128]{1,0:T(4,128)}, f32[4,128]{1,0:T(4,128)S(1)}, u32[]{:S(2)}, u32[]{:S(2)}) collective-permute-start(f32[4,128]{1,0:T(4,128)} %get-tuple-element.39), channel_id=1, source_target_pairs={{0,1},{1,0},{2,3},{3,2},{4,5},{5,4},{6,7},{7,6},{8,9},{9,8},{10,11... | collective-permute-start | bytes 6152 | tf_op jit(solution)/shard_map/ppermute | solution.py:52
  61.1 6.7 %collective-permute-start.11 = (f32[4,128]{1,0:T(4,128)}, f32[4,128]{1,0:T(4,128)S(1)}, u32[]{:S(2)}, u32[]{:S(2)}) collective-permute-start(f32[4,128]{1,0:T(4,128)} %get-tuple-element.40), channel_id=1, source_target_pairs={{0,2},{1,3},{2,0},{3,1},{4,6},{5,7},{6,4},{7,5},{8,10},{9,11},{10,... | collective-permute-start | bytes 6152 | tf_op jit(solution)/shard_map/ppermute | solution.py:52
  62.8 5.6 %collective-permute-start.12 = (f32[4,128]{1,0:T(4,128)}, f32[4,128]{1,0:T(4,128)S(1)}, u32[]{:S(2)}, u32[]{:S(2)}) collective-permute-start(f32[4,128]{1,0:T(4,128)} %get-tuple-element.41), channel_id=1, source_target_pairs={{0,3},{1,2},{2,1},{3,0},{4,7},{5,6},{6,5},{7,4},{8,11},{9,10},{10,... | collective-permute-start | bytes 6152 | tf_op jit(solution)/shard_map/ppermute | solution.py:52
  74.3 10.6 %all-to-all-start.1 = ((f32[32,3,128]{2,1,0:T(4,128)}), f32[32,3,128]{2,1,0:T(4,128)S(1)}, u32[]{:S(2)}, u32[]{:S(2)}) async-start(f32[32,3,128]{2,1,0:T(4,128)} %bitcast.56), calls=%async_computation.1 | async-start | bytes 131072 | tf_op jit(solution)/shard_map/all_to_all | solution.py:532
  86.3 5.6 %collective-permute-start.15 = (bf16[32,2048]{1,0:T(8,128)(2,1)S(1)}, bf16[32,2048]{1,0:T(8,128)(2,1)S(1)}, u32[]{:S(2)}, u32[]{:S(2)}) collective-permute-start(bf16[32,2048]{1,0:T(8,128)(2,1)S(1)} %get-tuple-element.47.a_half.refs_0_), channel_id=1, source_target_pairs={{0,16},{8,24},{16,0},{24,8},{1,17},{9,25},{17,1},{25,9},{2,18},{10... | collective-permute-start | bytes 393224 | tf_op jit(solution)/shard_map/ppermute | solution.py:52
  87.1 5.0 %collective-permute-start.17 = (bf16[32,2048]{1,0:T(8,128)(2,1)S(1)}, bf16[32,2048]{1,0:T(8,128)(2,1)S(1)}, u32[]{:S(2)}, u32[]{:S(2)}) collective-permute-start(bf16[32,2048]{1,0:T(8,128)(2,1)S(1)} %get-tuple-element.49.b_half.refs_4_), channel_id=1, source_target_pairs={{0,8},{8,0},{16,24},{24,16},{1,9},{9,1},{17,25},{25,17},{2,10},{10... | collective-permute-start | bytes 393224 | tf_op jit(solution)/shard_map/ppermute | solution.py:52
  89.0 5.2 %collective-permute-start.16 = (bf16[32,2048]{1,0:T(8,128)(2,1)S(1)}, bf16[32,2048]{1,0:T(8,128)(2,1)S(1)}, u32[]{:S(2)}, u32[]{:S(2)}) collective-permute-start(bf16[32,2048]{1,0:T(8,128)(2,1)S(1)} %get-tuple-element.48.a_half.refs_2_), channel_id=1, source_target_pairs={{0,16},{8,24},{16,0},{24,8},{1,17},{9,25},{17,1},{25,9},{2,18},{10... | collective-permute-start | bytes 393224 | tf_op jit(solution)/shard_map/ppermute | solution.py:52
  90.5 5.0 %collective-permute-start.18 = (bf16[32,2048]{1,0:T(8,128)(2,1)S(1)}, bf16[32,2048]{1,0:T(8,128)(2,1)S(1)}, u32[]{:S(2)}, u32[]{:S(2)}) collective-permute-start(bf16[32,2048]{1,0:T(8,128)(2,1)S(1)} %get-tuple-element.50.b_half.refs_6_), channel_id=1, source_target_pairs={{0,8},{8,0},{16,24},{24,16},{1,9},{9,1},{17,25},{25,17},{2,10},{10... | collective-permute-start | bytes 393224 | tf_op jit(solution)/shard_map/ppermute | solution.py:52
  121.7 7.9 %collective-permute-start.19 = (bf16[32,4096]{1,0:T(8,128)(2,1)S(1)}, bf16[32,4096]{1,0:T(8,128)(2,1)S(1)}, u32[]{:S(2)}, u32[]{:S(2)}) collective-permute-start(bf16[32,4096]{1,0:T(8,128)(2,1)S(1)} %get-tuple-element.55.refs_8_), channel_id=1, source_target_pairs={{0,16},{8,24},{16,0},{24,8},{1,17},{9,25},{17,1},{25,9},{2,18},{10... | collective-permute-start | bytes 786440 | tf_op jit(solution)/shard_map/ppermute | solution.py:52
  122.4 7.8 %collective-permute-start.20 = (bf16[32,4096]{1,0:T(8,128)(2,1)S(1)}, bf16[32,4096]{1,0:T(8,128)(2,1)S(1)}, u32[]{:S(2)}, u32[]{:S(2)}) collective-permute-start(bf16[32,4096]{1,0:T(8,128)(2,1)S(1)} %get-tuple-element.56.refs_10_), channel_id=1, source_target_pairs={{0,8},{8,0},{16,24},{24,16},{1,9},{9,1},{17,25},{25,17},{2,10},{10... | collective-permute-start | bytes 786440 | tf_op jit(solution)/shard_map/ppermute | solution.py:52
  130.5 7.4 %collective-permute-start.21 = (bf16[32,4096]{1,0:T(8,128)(2,1)S(1)}, bf16[32,4096]{1,0:T(8,128)(2,1)S(1)}, u32[]{:S(2)}, u32[]{:S(2)}) collective-permute-start(bf16[32,4096]{1,0:T(8,128)(2,1)S(1)} %get-tuple-element.57), channel_id=1, source_target_pairs={{0,8},{8,0},{16,24},{24,16},{1,9},{9,1},{17,25},{25,17},{2,10},{10... | collective-permute-start | bytes 786440 | tf_op jit(solution)/shard_map/ppermute | solution.py:52
  131.1 28.4 %all-to-all-start.4 = ((f32[32,8,8,128]{3,2,1,0:T(8,128)}), f32[32,8,8,128]{3,2,1,0:T(8,128)}, u32[]{:S(2)}, u32[]{:S(2)}) async-start(f32[32,8,8,128]{3,2,1,0:T(8,128)} %bitcast.10), calls=%async_computation.4 | async-start | bytes 2097152 | tf_op jit(solution)/shard_map/all_to_all | solution.py:549
  134.6 16.6 %collective-permute-start.22 = (bf16[32,4096]{1,0:T(8,128)(2,1)S(1)}, bf16[32,4096]{1,0:T(8,128)(2,1)S(1)}, u32[]{:S(2)}, u32[]{:S(2)}) collective-permute-start(bf16[32,4096]{1,0:T(8,128)(2,1)S(1)} %get-tuple-element.58), channel_id=1, source_target_pairs={{0,16},{8,24},{16,0},{24,8},{1,17},{9,25},{17,1},{25,9},{2,18},{10... | collective-permute-start | bytes 786440 | tf_op jit(solution)/shard_map/ppermute | solution.py:52
  (22 other events, 174.4 us)

commit v11 on v10

--- a/solution.py
+++ b/solution.py
@@ -147,6 +147,7 @@
         out_shape=[jax.ShapeDtypeStruct((rows, targets), jnp.float32)] * vols,
         in_specs=[block] * (2 * rows),
         out_specs=[whole] * vols,
+        compiler_params=pltpu.CompilerParams(vmem_limit_bytes=SLAB_BYTES),
         name="collect",
     )(*known, *other)
 
@@ -198,12 +199,13 @@
     return pl.pallas_call(
         body,
         out_shape=[
-            jax.ShapeDtypeStruct((rows * bx, vols, cols * by, bz), jnp.float32),
-            jax.ShapeDtypeStruct((rows, height, targets), jnp.bfloat16),
-            jax.ShapeDtypeStruct((rows, bz, targets), jnp.bfloat16),
+            pltpu.HBM((rows * bx, vols, cols * by, bz), jnp.float32),
+            pltpu.HBM((rows, height, targets), jnp.bfloat16),
+            pltpu.HBM((rows, bz, targets), jnp.bfloat16),
         ],
         in_specs=[pl.BlockSpec(memory_space=pltpu.SMEM)] + [vmem] * (2 * rows),
         out_specs=[vmem] * 3,
+        compiler_params=pltpu.CompilerParams(vmem_limit_bytes=SLAB_BYTES),
         name="prepare",
     )(values, *known, *other)
 
@@ -366,7 +368,7 @@
         scratch += [pltpu.VMEM(field.shape, jnp.float32), pltpu.SemaphoreType.DMA(())]
     return pl.pallas_call(
         body,
-        out_shape=[field, fluxes],
+        out_shape=[field if first else pltpu.HBM(field.shape, field.dtype), fluxes],
         in_specs=[vmem] * len(operands),
         out_specs=[vmem if first else pl.BlockSpec(memory_space=pltpu.HBM), vmem],
         scratch_shapes=scratch,

time: 164 us -> 163 us (level)
  Pallas kernels: 30.1 us -> 28 us
  transfers between devices with their start and end apart: 26 -> 26, of which waited for: 13 -> 14; matrix products, arithmetic and copies ran while one was open for 1% -> 1% of each run, Pallas kernels for 12% -> 10%
where the time goes in v11:
time: 163 us; the launch traced here: 161 us
  waiting for transfers between devices  69 us (42%)
  starting transfers between devices  38.2 us (23%)
  Pallas kernels  28 us (17%)
  blocking collectives  18.5 us (11%)
  other arithmetic  2.97 us (2%)
  local copies, waits for them, and re-layouts  2.82 us (2%)
    ppermute x23, waiting for transfers between devices, mated(): lax.ppermute(value, axis, [(i, i ^ mate) for i in range(lax.axis_size(axi...  55 us
    ppermute x23, starting transfers between devices, mated(): lax.ppermute(value, axis, [(i, i ^ mate) for i in range(lax.axis_size(axi...  25.8 us
    pallas_call x2, Pallas kernels, slab_call(): pl.pallas_call(body, out_shape=[field if first else pltpu.HBM(field.shape...  10.5 us
    all_to_all x1, blocking collectives, split_by_excitation(): parts = lax.all_to_all(parts, ALL, 0, 0, tiled=True)  9.35 us
    all_to_all x1, blocking collectives, split_by_excitation(): flux = lax.all_to_all(flux, ALL, 0, 0, tiled=True)  9.19 us
    all_to_all x1, waiting for transfers between devices, split_by_excitation(): flux = lax.all_to_all(flux, ALL, 0, 0, tiled=True)  7.47 us
    all_to_all x1, waiting for transfers between devices, split_by_excitation(): volume = lax.all_to_all(volume, ALL, 0, 0, tiled=True)  6.62 us
    pallas_call x1, Pallas kernels, start_call(): pl.pallas_call(body, out_shape=[jax.ShapeDtypeStruct((lines + 4 * owners,...  6.29 us
  transfers between devices with their start and end apart: 26, of which 14 were waited for; matrix products, arithmetic and copies ran while one was open for 1% of the time, Pallas kernels for 10%

profile of v11, /device:TPU:0, one launch (start us, length us, event | category | flops | bytes accessed | tf_op | source)
XLA Modules:
  0.0 160.7 jit_solution(17212486504332358956)
XLA Ops:
  1.4 3.1 %collective-permute-start = (bf16[64,128]{1,0:T(8,128)(2,1)S(1)}, bf16[64,128]{1,0:T(8,128)(2,1)S(1)}, u32[]{:S(2)}, u32[]{:S(2)}) collective-permute-start(bf16[64,128]{1,0:T(8,128)(2,1)S(1)} %get-tuple-element.61), channel_id=1, source_target_pairs={{0,1},{1,0},{2,3},{3,2},{4,5},{5,4},{6,7},{7,6},{8,9},{9,8},{10,11... | collective-permute-start | bytes 49160 | tf_op jit(solution)/shard_map/ppermute | solution.py:52
  4.5 2.6 %collective-permute-start.1 = (bf16[64,128]{1,0:T(8,128)(2,1)S(1)}, bf16[64,128]{1,0:T(8,128)(2,1)S(1)}, u32[]{:S(2)}, u32[]{:S(2)}) collective-permute-start(bf16[64,128]{1,0:T(8,128)(2,1)S(1)} %get-tuple-element.61), channel_id=1, source_target_pairs={{0,2},{1,3},{2,0},{3,1},{4,6},{5,7},{6,4},{7,5},{8,10},{9,11},{10,... | collective-permute-start | bytes 49160 | tf_op jit(solution)/shard_map/ppermute | solution.py:52
  7.1 6.2 %all-to-all-start = ((f32[32,8,8,128]{3,2,1,0:T(8,128)}), f32[32,8,8,128]{3,2,1,0:T(8,128)}, u32[]{:S(2)}, u32[]{:S(2)}) async-start(f32[32,8,8,128]{3,2,1,0:T(8,128)} %param.9), calls=%async_computation | async-start | bytes 2097152 | tf_op jit(solution)/shard_map/all_to_all | solution.py:513
  14.5 6.3 %start.1 = (bf16[320,128]{1,0:T(8,128)(2,1)}, bf16[320,128]{1,0:T(8,128)(2,1)}, bf16[320,128]{1,0:T(8,128)(2,1)}, bf16[320,128]{1,0:T(8,128)(2,1)}, bf16[128,409...) custom-call(f32[32,16384]{1,0:T(8,128)} %density_ref.1, ...), custom_call_target="tpu_custom_call" | custom-call | tf_op jit(solution)/shard_map/start/pallas_call | solution.py:109
  20.8 1.8 %collective-permute-start.13 = (bf16[128,4096]{1,0:T(8,128)(2,1)}, bf16[128,4096]{1,0:T(8,128)(2,1)S(1)}, u32[]{:S(2)}, u32[]{:S(2)}) collective-permute-start(bf16[128,4096]{1,0:T(8,128)(2,1)} %get-tuple-element.44), channel_id=1, source_target_pairs={{0,8},{8,0},{16,24},{24,16},{1,9},{9,1},{17,25},{25,17},{2,10},{10... | collective-permute-start | bytes 3145736 | tf_op jit(solution)/shard_map/ppermute | solution.py:52
  24.9 2.6 %collective-permute-start.5 = (bf16[320,128]{1,0:T(8,128)(2,1)}, bf16[320,128]{1,0:T(8,128)(2,1)S(1)}, u32[]{:S(2)}, u32[]{:S(2)}) collective-permute-start(bf16[320,128]{1,0:T(8,128)(2,1)} %get-tuple-element.34), channel_id=1, source_target_pairs={{0,24},{8,16},{16,8},{24,0},{1,25},{9,17},{17,9},{25,1},{2,26},{10... | collective-permute-start | bytes 245768 | tf_op jit(solution)/shard_map/ppermute | solution.py:52
  27.5 26.0 %collective-permute-done.3.refs_1_ = bf16[320,128]{1,0:T(8,128)(2,1)S(1)} collective-permute-done((bf16[320,128]{1,0:T(8,128)(2,1)}, bf16[320,128]{1,0:T(8,128)(2,1)S(1)}, u32[]{:S(2)}, u32[]{:S(2)}) %collective-permute-start.3) | collective-permute-done | bytes 81952 | tf_op jit(solution)/shard_map/ppermute | solution.py:52
  54.1 2.0 %collective-permute-done.5.refs_3_ = bf16[320,128]{1,0:T(8,128)(2,1)S(1)} collective-permute-done((bf16[320,128]{1,0:T(8,128)(2,1)}, bf16[320,128]{1,0:T(8,128)(2,1)S(1)}, u32[]{:S(2)}, u32[]{:S(2)}) %collective-permute-start.5) | collective-permute-done | bytes 81952 | tf_op jit(solution)/shard_map/ppermute | solution.py:52
  60.6 1.9 %collective-permute-start.11 = (f32[4,128]{1,0:T(4,128)S(1)}, f32[4,128]{1,0:T(4,128)S(1)}, u32[]{:S(2)}, u32[]{:S(2)}) collective-permute-start(f32[4,128]{1,0:T(4,128)S(1)} %get-tuple-element.40), channel_id=1, source_target_pairs={{0,2},{1,3},{2,0},{3,1},{4,6},{5,7},{6,4},{7,5},{8,10},{9,11},{10,... | collective-permute-start | bytes 6152 | tf_op jit(solution)/shard_map/ppermute | solution.py:52
  64.0 2.9 %prepare.1 = (f32[32,4,16,128]{3,2,1,0:T(8,128)}, bf16[4,512,128]{2,1,0:T(8,128)(2,1)}, bf16[4,128,128]{2,1,0:T(8,128)(2,1)}) custom-call(f32[16]{0:T(128)S(1)} %copy-done.8, bf16[320,128]{1,0:T(8,128)(2,1)S(1)} %copy-done.6, bf16[320,128]{1,0:T(8,128)(2,1)S(1)} %collective-permute-done.3.refs_1_, bf16[320,128]{1,0:T(8,128)(2,1)S(1)} %collective-permute-done.4.refs_2_, ...), custom_call_target="tpu_custom_call" | custom-call | tf_op jit(solution)/shard_map/prepare/pallas_call | solution.py:199
  68.5 5.3 %slab_first.1 = (f32[34,4,16,128]{3,2,1,0:T(8,128)}, f32[4,8,3,128]{3,2,1,0:T(4,128)}) custom-call(f32[4,8,8,8,128]{4,3,2,1,0:T(8,128)} %bitcast.source_ref, f32[32,4,16,128]{3,2,1,0:T(8,128)} %get-tuple-element.35.inverse_ref, bf16[4,512,128]{2,1,0:T(8,128)(2,1)} %get-tuple-element.36.hit_ref, bf16[4,128,128]{2,1,0:T(8,128)(2,1)} %get-tuple-element.37.lane_ref, ...), custom_call_target="tpu_custom_call" | custom-call | tf_op jit(solution)/shard_map/slab_first/pallas_call | solution.py:369
  73.8 2.7 %all-to-all-start.1 = ((f32[32,3,128]{2,1,0:T(4,128)}), f32[32,3,128]{2,1,0:T(4,128)S(1)}, u32[]{:S(2)}, u32[]{:S(2)}) async-start(f32[32,3,128]{2,1,0:T(4,128)} %bitcast.57), calls=%async_computation.1 | async-start | bytes 131072 | tf_op jit(solution)/shard_map/all_to_all | solution.py:534
  76.5 7.5 %all-to-all-done.1.flux_ref = f32[32,3,128]{2,1,0:T(4,128)S(1)} async-done(((f32[32,3,128]{2,1,0:T(4,128)}), f32[32,3,128]{2,1,0:T(4,128)S(1)}, u32[]{:S(2)}, u32[]{:S(2)}) %all-to-all-start.1) | async-done | bytes 49184 | tf_op jit(solution)/shard_map/all_to_all | solution.py:534
  95.3 9.3 %all_to_all.25 = f32[32,3,128]{2,1,0:T(4,128)S(1)} all-to-all(f32[32,3,128]{2,1,0:T(4,128)S(1)} %potential.3), channel_id=1, replica_groups=mesh['row'=4,'col'=2,'vol'=4] {'row','col','vol'}, dimensions={0} | all-to-all | bytes 98304 | tf_op jit(solution)/shard_map/all_to_all | solution.py:545
  104.7 5.2 %slab_last.1 = (f32[4,8,8,8,128]{4,3,2,1,0:T(8,128)}, f32[4,8,3,128]{3,2,1,0:T(4,128)S(1)}) custom-call(f32[4,8,8,8,128]{4,3,2,1,0:T(8,128)} %bitcast.source_ref, f32[32,4,16,128]{3,2,1,0:T(8,128)S(1)} %copy-done.2, bf16[4,512,128]{2,1,0:T(8,128)(2,1)S(1)} %copy-done.3, bf16[4,128,128]{2,1,0:T(8,128)(2,1)S(1)} %copy-done.5, f32[4,8,3,128]{3,2,1,0:T(4,128)S(1)} %bitcast.54, ...), custom_call_target="tpu_custom_call" | custom-call | tf_op jit(solution)/shard_map/slab_last/pallas_call | solution.py:369
  109.9 9.2 %all_to_all.26.flux_ref = f32[32,3,128]{2,1,0:T(4,128)S(1)} all-to-all(f32[32,3,128]{2,1,0:T(4,128)S(1)} %bitcast.55), channel_id=1, replica_groups=mesh['row'=4,'col'=2,'vol'=4] {'row','col','vol'}, dimensions={0} | all-to-all | bytes 98304 | tf_op jit(solution)/shard_map/all_to_all | solution.py:549
  119.1 1.6 %update.5 = (bf16[32,4096]{1,0:T(8,128)(2,1)S(1)}, bf16[32,4096]{1,0:T(8,128)(2,1)S(1)}) custom-call(f32[32,3,128]{2,1,0:T(4,128)S(1)} %all_to_all.26.flux_ref, bf16[128,4096]{1,0:T(8,128)(2,1)S(1)} %copy-done, bf16[128,4096]{1,0:T(8,128)(2,1)S(1)} %collective-permute-done.13.a_mate, bf16[128,4096]{1,0:T(8,128)(2,1)S(1)} %copy-done.1, ...), custom_call_target="tpu_custom_call" | custom-call | tf_op jit(solution)/shard_map/update/pallas_call | solution.py:398
  122.0 6.6 %collective-permute-done.19.refs_9_ = bf16[32,4096]{1,0:T(8,128)(2,1)S(1)} collective-permute-done((bf16[32,4096]{1,0:T(8,128)(2,1)S(1)}, bf16[32,4096]{1,0:T(8,128)(2,1)S(1)}, u32[]{:S(2)}, u32[]{:S(2)}) %collective-permute-start.19) | collective-permute-done | bytes 262176 | tf_op jit(solution)/shard_map/ppermute | solution.py:52
  130.2 3.5 %all-to-all-start.4 = ((f32[32,8,8,128]{3,2,1,0:T(8,128)}), f32[32,8,8,128]{3,2,1,0:T(8,128)}, u32[]{:S(2)}, u32[]{:S(2)}) async-start(f32[32,8,8,128]{3,2,1,0:T(8,128)} %bitcast.56), calls=%async_computation.4 | async-start | bytes 2097152 | tf_op jit(solution)/shard_map/all_to_all | solution.py:551
  133.7 1.6 %collective-permute-start.22 = (bf16[32,4096]{1,0:T(8,128)(2,1)S(1)}, bf16[32,4096]{1,0:T(8,128)(2,1)S(1)}, u32[]{:S(2)}, u32[]{:S(2)}) collective-permute-start(bf16[32,4096]{1,0:T(8,128)(2,1)S(1)} %get-tuple-element.58), channel_id=1, source_target_pairs={{0,16},{8,24},{16,0},{24,8},{1,17},{9,25},{17,1},{25,9},{2,18},{10... | collective-permute-start | bytes 786440 | tf_op jit(solution)/shard_map/ppermute | solution.py:52
  135.3 1.7 %collective-permute-done.21 = bf16[32,4096]{1,0:T(8,128)(2,1)S(1)} collective-permute-done((bf16[32,4096]{1,0:T(8,128)(2,1)S(1)}, bf16[32,4096]{1,0:T(8,128)(2,1)S(1)}, u32[]{:S(2)}, u32[]{:S(2)}) %collective-permute-start.21) | collective-permute-done | bytes 262176 | tf_op jit(solution)/shard_map/ppermute | solution.py:52
  137.0 13.3 %collective-permute-done.22 = bf16[32,4096]{1,0:T(8,128)(2,1)S(1)} collective-permute-done((bf16[32,4096]{1,0:T(8,128)(2,1)S(1)}, bf16[32,4096]{1,0:T(8,128)(2,1)S(1)}, u32[]{:S(2)}, u32[]{:S(2)}) %collective-permute-start.22) | collective-permute-done | bytes 262176 | tf_op jit(solution)/shard_map/ppermute | solution.py:52
  151.9 6.6 %all-to-all-done.4.in_ref = f32[32,8,8,128]{3,2,1,0:T(8,128)} async-done(((f32[32,8,8,128]{3,2,1,0:T(8,128)}), f32[32,8,8,128]{3,2,1,0:T(8,128)}, u32[]{:S(2)}, u32[]{:S(2)}) %all-to-all-start.4) | async-done | bytes 1048608 | tf_op jit(solution)/shard_map/all_to_all | solution.py:551
  158.6 2.0 %landed.1 = f32[32,8,8,128]{3,2,1,0:T(8,128)} custom-call(f32[32,8,8,128]{3,2,1,0:T(8,128)} %all-to-all-done.4.in_ref), custom_call_target="tpu_custom_call" | custom-call | tf_op jit(solution)/shard_map/landed/pallas_call | solution.py:231
  (91 shorter events, 28.1 us)
Async XLA Ops:
  1.4 12.4 %collective-permute-start = (bf16[64,128]{1,0:T(8,128)(2,1)S(1)}, bf16[64,128]{1,0:T(8,128)(2,1)S(1)}, u32[]{:S(2)}, u32[]{:S(2)}) collective-permute-start(bf16[64,128]{1,0:T(8,128)(2,1)S(1)} %get-tuple-element.61), channel_id=1, source_target_pairs={{0,1},{1,0},{2,3},{3,2},{4,5},{5,4},{6,7},{7,6},{8,9},{9,8},{10,11... | collective-permute-start | bytes 49160 | tf_op jit(solution)/shard_map/ppermute | solution.py:52
  4.5 9.4 %collective-permute-start.1 = (bf16[64,128]{1,0:T(8,128)(2,1)S(1)}, bf16[64,128]{1,0:T(8,128)(2,1)S(1)}, u32[]{:S(2)}, u32[]{:S(2)}) collective-permute-start(bf16[64,128]{1,0:T(8,128)(2,1)S(1)} %get-tuple-element.61), channel_id=1, source_target_pairs={{0,2},{1,3},{2,0},{3,1},{4,6},{5,7},{6,4},{7,5},{8,10},{9,11},{10,... | collective-permute-start | bytes 49160 | tf_op jit(solution)/shard_map/ppermute | solution.py:52
  7.1 6.8 %collective-permute-start.2 = (bf16[64,128]{1,0:T(8,128)(2,1)S(1)}, bf16[64,128]{1,0:T(8,128)(2,1)S(1)}, u32[]{:S(2)}, u32[]{:S(2)}) collective-permute-start(bf16[64,128]{1,0:T(8,128)(2,1)S(1)} %get-tuple-element.61), channel_id=1, source_target_pairs={{0,3},{1,2},{2,1},{3,0},{4,7},{5,6},{6,5},{7,4},{8,11},{9,10},{10,... | collective-permute-start | bytes 49160 | tf_op jit(solution)/shard_map/ppermute | solution.py:52
  7.1 60.8 %all-to-all-start = ((f32[32,8,8,128]{3,2,1,0:T(8,128)}), f32[32,8,8,128]{3,2,1,0:T(8,128)}, u32[]{:S(2)}, u32[]{:S(2)}) async-start(f32[32,8,8,128]{3,2,1,0:T(8,128)} %param.9), calls=%async_computation | async-start | bytes 2097152 | tf_op jit(solution)/shard_map/all_to_all | solution.py:513
  20.8 55.7 %collective-permute-start.13 = (bf16[128,4096]{1,0:T(8,128)(2,1)}, bf16[128,4096]{1,0:T(8,128)(2,1)S(1)}, u32[]{:S(2)}, u32[]{:S(2)}) collective-permute-start(bf16[128,4096]{1,0:T(8,128)(2,1)} %get-tuple-element.44), channel_id=1, source_target_pairs={{0,8},{8,0},{16,24},{24,16},{1,9},{9,1},{17,25},{25,17},{2,10},{10... | collective-permute-start | bytes 3145736 | tf_op jit(solution)/shard_map/ppermute | solution.py:52
  22.6 53.9 %collective-permute-start.14 = (bf16[128,4096]{1,0:T(8,128)(2,1)}, bf16[128,4096]{1,0:T(8,128)(2,1)}, u32[]{:S(2)}, u32[]{:S(2)}) collective-permute-start(bf16[128,4096]{1,0:T(8,128)(2,1)} %get-tuple-element.46), channel_id=1, source_target_pairs={{0,16},{8,24},{16,0},{24,8},{1,17},{9,25},{17,1},{25,9},{2,18},{10... | collective-permute-start | bytes 3145736 | tf_op jit(solution)/shard_map/ppermute | solution.py:52
  24.1 29.5 %collective-permute-start.3 = (bf16[320,128]{1,0:T(8,128)(2,1)}, bf16[320,128]{1,0:T(8,128)(2,1)S(1)}, u32[]{:S(2)}, u32[]{:S(2)}) collective-permute-start(bf16[320,128]{1,0:T(8,128)(2,1)} %get-tuple-element.32), channel_id=1, source_target_pairs={{0,8},{8,0},{16,24},{24,16},{1,9},{9,1},{17,25},{25,17},{2,10},{10... | collective-permute-start | bytes 245768 | tf_op jit(solution)/shard_map/ppermute | solution.py:52
  24.6 29.0 %collective-permute-start.4 = (bf16[320,128]{1,0:T(8,128)(2,1)}, bf16[320,128]{1,0:T(8,128)(2,1)S(1)}, u32[]{:S(2)}, u32[]{:S(2)}) collective-permute-start(bf16[320,128]{1,0:T(8,128)(2,1)} %get-tuple-element.33), channel_id=1, source_target_pairs={{0,16},{8,24},{16,0},{24,8},{1,17},{9,25},{17,1},{25,9},{2,18},{10... | collective-permute-start | bytes 245768 | tf_op jit(solution)/shard_map/ppermute | solution.py:52
  24.9 31.2 %collective-permute-start.5 = (bf16[320,128]{1,0:T(8,128)(2,1)}, bf16[320,128]{1,0:T(8,128)(2,1)S(1)}, u32[]{:S(2)}, u32[]{:S(2)}) collective-permute-start(bf16[320,128]{1,0:T(8,128)(2,1)} %get-tuple-element.34), channel_id=1, source_target_pairs={{0,24},{8,16},{16,8},{24,0},{1,25},{9,17},{17,9},{25,1},{2,26},{10... | collective-permute-start | bytes 245768 | tf_op jit(solution)/shard_map/ppermute | solution.py:52
  53.6 2.5 %collective-permute-start.6 = (bf16[320,128]{1,0:T(8,128)(2,1)}, bf16[320,128]{1,0:T(8,128)(2,1)S(1)}, u32[]{:S(2)}, u32[]{:S(2)}) collective-permute-start(bf16[320,128]{1,0:T(8,128)(2,1)} %get-tuple-element.31.refs_0_), channel_id=1, source_target_pairs={{0,4},{4,0},{1,5},{5,1},{2,6},{6,2},{3,7},{7,3},{8,12},{12,8},{9,1... | collective-permute-start | bytes 245768 | tf_op jit(solution)/shard_map/ppermute | solution.py:52
  53.6 3.0 %collective-permute-start.7 = (bf16[320,128]{1,0:T(8,128)(2,1)S(1)}, bf16[320,128]{1,0:T(8,128)(2,1)S(1)}, u32[]{:S(2)}, u32[]{:S(2)}) collective-permute-start(bf16[320,128]{1,0:T(8,128)(2,1)S(1)} %collective-permute-done.3.refs_1_), channel_id=1, source_target_pairs={{0,4},{4,0},{1,5},{5,1},{2,6},{6,2},{3,7},{7,3},{8,12},{12,8},{9,1... | collective-permute-start | bytes 245768 | tf_op jit(solution)/shard_map/ppermute | solution.py:52
  59.1 7.8 %collective-permute-start.10 = (f32[4,128]{1,0:T(4,128)S(1)}, f32[4,128]{1,0:T(4,128)S(1)}, u32[]{:S(2)}, u32[]{:S(2)}) collective-permute-start(f32[4,128]{1,0:T(4,128)S(1)} %get-tuple-element.39), channel_id=1, source_target_pairs={{0,1},{1,0},{2,3},{3,2},{4,5},{5,4},{6,7},{7,6},{8,9},{9,8},{10,11... | collective-permute-start | bytes 6152 | tf_op jit(solution)/shard_map/ppermute | solution.py:52
  60.6 6.3 %collective-permute-start.11 = (f32[4,128]{1,0:T(4,128)S(1)}, f32[4,128]{1,0:T(4,128)S(1)}, u32[]{:S(2)}, u32[]{:S(2)}) collective-permute-start(f32[4,128]{1,0:T(4,128)S(1)} %get-tuple-element.40), channel_id=1, source_target_pairs={{0,2},{1,3},{2,0},{3,1},{4,6},{5,7},{6,4},{7,5},{8,10},{9,11},{10,... | collective-permute-start | bytes 6152 | tf_op jit(solution)/shard_map/ppermute | solution.py:52
  62.5 5.4 %collective-permute-start.12 = (f32[4,128]{1,0:T(4,128)S(1)}, f32[4,128]{1,0:T(4,128)S(1)}, u32[]{:S(2)}, u32[]{:S(2)}) collective-permute-start(f32[4,128]{1,0:T(4,128)S(1)} %get-tuple-element.41), channel_id=1, source_target_pairs={{0,3},{1,2},{2,1},{3,0},{4,7},{5,6},{6,5},{7,4},{8,11},{9,10},{10,... | collective-permute-start | bytes 6152 | tf_op jit(solution)/shard_map/ppermute | solution.py:52
  73.8 10.2 %all-to-all-start.1 = ((f32[32,3,128]{2,1,0:T(4,128)}), f32[32,3,128]{2,1,0:T(4,128)S(1)}, u32[]{:S(2)}, u32[]{:S(2)}) async-start(f32[32,3,128]{2,1,0:T(4,128)} %bitcast.57), calls=%async_computation.1 | async-start | bytes 131072 | tf_op jit(solution)/shard_map/all_to_all | solution.py:534
  85.4 5.6 %collective-permute-start.15 = (bf16[32,2048]{1,0:T(8,128)(2,1)S(1)}, bf16[32,2048]{1,0:T(8,128)(2,1)S(1)}, u32[]{:S(2)}, u32[]{:S(2)}) collective-permute-start(bf16[32,2048]{1,0:T(8,128)(2,1)S(1)} %get-tuple-element.47.a_half.refs_0_), channel_id=1, source_target_pairs={{0,16},{8,24},{16,0},{24,8},{1,17},{9,25},{17,1},{25,9},{2,18},{10... | collective-permute-start | bytes 393224 | tf_op jit(solution)/shard_map/ppermute | solution.py:52
  86.1 5.0 %collective-permute-start.17 = (bf16[32,2048]{1,0:T(8,128)(2,1)S(1)}, bf16[32,2048]{1,0:T(8,128)(2,1)S(1)}, u32[]{:S(2)}, u32[]{:S(2)}) collective-permute-start(bf16[32,2048]{1,0:T(8,128)(2,1)S(1)} %get-tuple-element.49.b_half.refs_4_), channel_id=1, source_target_pairs={{0,8},{8,0},{16,24},{24,16},{1,9},{9,1},{17,25},{25,17},{2,10},{10... | collective-permute-start | bytes 393224 | tf_op jit(solution)/shard_map/ppermute | solution.py:52
  88.1 5.2 %collective-permute-start.16 = (bf16[32,2048]{1,0:T(8,128)(2,1)S(1)}, bf16[32,2048]{1,0:T(8,128)(2,1)S(1)}, u32[]{:S(2)}, u32[]{:S(2)}) collective-permute-start(bf16[32,2048]{1,0:T(8,128)(2,1)S(1)} %get-tuple-element.48.a_half.refs_2_), channel_id=1, source_target_pairs={{0,16},{8,24},{16,0},{24,8},{1,17},{9,25},{17,1},{25,9},{2,18},{10... | collective-permute-start | bytes 393224 | tf_op jit(solution)/shard_map/ppermute | solution.py:52
  89.6 5.0 %collective-permute-start.18 = (bf16[32,2048]{1,0:T(8,128)(2,1)S(1)}, bf16[32,2048]{1,0:T(8,128)(2,1)S(1)}, u32[]{:S(2)}, u32[]{:S(2)}) collective-permute-start(bf16[32,2048]{1,0:T(8,128)(2,1)S(1)} %get-tuple-element.50.b_half.refs_6_), channel_id=1, source_target_pairs={{0,8},{8,0},{16,24},{24,16},{1,9},{9,1},{17,25},{25,17},{2,10},{10... | collective-permute-start | bytes 393224 | tf_op jit(solution)/shard_map/ppermute | solution.py:52
  120.8 7.9 %collective-permute-start.19 = (bf16[32,4096]{1,0:T(8,128)(2,1)S(1)}, bf16[32,4096]{1,0:T(8,128)(2,1)S(1)}, u32[]{:S(2)}, u32[]{:S(2)}) collective-permute-start(bf16[32,4096]{1,0:T(8,128)(2,1)S(1)} %get-tuple-element.55.refs_8_), channel_id=1, source_target_pairs={{0,16},{8,24},{16,0},{24,8},{1,17},{9,25},{17,1},{25,9},{2,18},{10... | collective-permute-start | bytes 786440 | tf_op jit(solution)/shard_map/ppermute | solution.py:52
  121.5 7.8 %collective-permute-start.20 = (bf16[32,4096]{1,0:T(8,128)(2,1)S(1)}, bf16[32,4096]{1,0:T(8,128)(2,1)S(1)}, u32[]{:S(2)}, u32[]{:S(2)}) collective-permute-start(bf16[32,4096]{1,0:T(8,128)(2,1)S(1)} %get-tuple-element.56.refs_10_), channel_id=1, source_target_pairs={{0,8},{8,0},{16,24},{24,16},{1,9},{9,1},{17,25},{25,17},{2,10},{10... | collective-permute-start | bytes 786440 | tf_op jit(solution)/shard_map/ppermute | solution.py:52
  129.6 7.4 %collective-permute-start.21 = (bf16[32,4096]{1,0:T(8,128)(2,1)S(1)}, bf16[32,4096]{1,0:T(8,128)(2,1)S(1)}, u32[]{:S(2)}, u32[]{:S(2)}) collective-permute-start(bf16[32,4096]{1,0:T(8,128)(2,1)S(1)} %get-tuple-element.57), channel_id=1, source_target_pairs={{0,8},{8,0},{16,24},{24,16},{1,9},{9,1},{17,25},{25,17},{2,10},{10... | collective-permute-start | bytes 786440 | tf_op jit(solution)/shard_map/ppermute | solution.py:52
  130.2 28.4 %all-to-all-start.4 = ((f32[32,8,8,128]{3,2,1,0:T(8,128)}), f32[32,8,8,128]{3,2,1,0:T(8,128)}, u32[]{:S(2)}, u32[]{:S(2)}) async-start(f32[32,8,8,128]{3,2,1,0:T(8,128)} %bitcast.56), calls=%async_computation.4 | async-start | bytes 2097152 | tf_op jit(solution)/shard_map/all_to_all | solution.py:551
  133.7 16.6 %collective-permute-start.22 = (bf16[32,4096]{1,0:T(8,128)(2,1)S(1)}, bf16[32,4096]{1,0:T(8,128)(2,1)S(1)}, u32[]{:S(2)}, u32[]{:S(2)}) collective-permute-start(bf16[32,4096]{1,0:T(8,128)(2,1)S(1)} %get-tuple-element.58), channel_id=1, source_target_pairs={{0,16},{8,24},{16,0},{24,8},{1,17},{9,25},{17,1},{25,9},{2,18},{10... | collective-permute-start | bytes 786440 | tf_op jit(solution)/shard_map/ppermute | solution.py:52
  (19 other events, 208.8 us)

commit v12 on v11

--- a/solution.py
+++ b/solution.py
@@ -108,7 +108,8 @@
     vmem = pl.BlockSpec(memory_space=pltpu.VMEM)
     return pl.pallas_call(
         body,
-        out_shape=[jax.ShapeDtypeStruct((lines + 4 * owners, targets), known.dtype)] * rows
+        out_shape=[pltpu.VMEM((lines + 4 * owners, targets), known.dtype)]
+        + [jax.ShapeDtypeStruct((lines + 4 * owners, targets), known.dtype)] * (rows - 1)
         + [jax.ShapeDtypeStruct((targets, width), panel.dtype)] * rows,
         in_specs=[hbm, hbm, vmem],
         out_specs=[vmem] * rows + [hbm] * rows,
@@ -265,6 +266,7 @@
         else:
             parts_ref, start_ref, far_ref, flux_ref, out_ref, *rest = rest
             other_ref, scaled_ref, ratio_ref, volume_ref, sem = rest
+        stores = []
         sub = lax.broadcasted_iota(jnp.int32, (by, bz), 0)
         lan = lax.broadcasted_iota(jnp.int32, (by, bz), 1)
         for ref in (out_ref, other_ref):
@@ -335,15 +337,18 @@
                         there[x + 1, v, own] = value
                         if last and not first:
                             volume_ref[x // bx, j, x % bx] = value
+                    if last and not first and x % bx == bx - 1:
+                        tile_at = x // bx
+                        stores.append(pltpu.make_async_copy(
+                            volume_ref.at[tile_at], far_ref.at[tile_at], sem.at[tile_at]
+                        ))
+                        stores[-1].start()
                 return carry
 
             for index in range(depth):
                 step(index, 0)
             here = there
 
-        if not first:
-            store = pltpu.make_async_copy(volume_ref, far_ref, sem)
-            store.start()
         for r in range(rows):
             part = here[1 + r * bx:1 + (r + 1) * bx].reshape(height, bz)
             met = sum(
@@ -354,7 +359,7 @@
             value = value - potentials[r]
             for k, mate in enumerate(MATES):
                 flux_ref[r ^ mate, :, k, :] = jnp.broadcast_to(value, (blocks, targets))
-        if not first:
+        for store in stores:
             store.wait()
 
     vmem = pl.BlockSpec(memory_space=pltpu.VMEM)
@@ -365,7 +370,7 @@
     scratch = [pltpu.VMEM(padded, jnp.float32)] + [pltpu.VMEM(planes, jnp.float32)] * 2
     if not first:
         scratch = [pltpu.VMEM(padded, jnp.float32)] + scratch
-        scratch += [pltpu.VMEM(field.shape, jnp.float32), pltpu.SemaphoreType.DMA(())]
+        scratch += [pltpu.VMEM(field.shape, jnp.float32), pltpu.SemaphoreType.DMA((rows,))]
     return pl.pallas_call(
         body,
         out_shape=[field if first else pltpu.HBM(field.shape, field.dtype), fluxes],

time: 163 us -> 161 us (0.988)
  no operation moved by 1% of the time
where the time goes in v12:
time: 161 us; the launch traced here: 160 us
  waiting for transfers between devices  69 us (43%)
  starting transfers between devices  38.3 us (24%)
  Pallas kernels  27.9 us (17%)
  blocking collectives  18.5 us (11%)
  other arithmetic  2.97 us (2%)
  local copies, waits for them, and re-layouts  1.92 us (1%)
    ppermute x23, waiting for transfers between devices, mated(): lax.ppermute(value, axis, [(i, i ^ mate) for i in range(lax.axis_size(axi...  55 us
    ppermute x23, starting transfers between devices, mated(): lax.ppermute(value, axis, [(i, i ^ mate) for i in range(lax.axis_size(axi...  25.8 us
    pallas_call x2, Pallas kernels, slab_call(): pl.pallas_call(body, out_shape=[field if first else pltpu.HBM(field.shape...  10.3 us
    all_to_all x1, blocking collectives, split_by_excitation(): parts = lax.all_to_all(parts, ALL, 0, 0, tiled=True)  9.35 us
    all_to_all x1, blocking collectives, split_by_excitation(): flux = lax.all_to_all(flux, ALL, 0, 0, tiled=True)  9.19 us
    all_to_all x1, waiting for transfers between devices, split_by_excitation(): flux = lax.all_to_all(flux, ALL, 0, 0, tiled=True)  7.47 us
    all_to_all x1, waiting for transfers between devices, split_by_excitation(): volume = lax.all_to_all(volume, ALL, 0, 0, tiled=True)  6.62 us
    pallas_call x1, Pallas kernels, start_call(): pl.pallas_call(body, out_shape=[pltpu.VMEM((lines + 4 * owners, targets),...  6.26 us
  transfers between devices with their start and end apart: 26, of which 14 were waited for; matrix products, arithmetic and copies ran while one was open for 1% of the time, Pallas kernels for 10%

profile of v12, /device:TPU:0, one launch (start us, length us, event | category | flops | bytes accessed | tf_op | source)
XLA Modules:
  0.0 159.7 jit_solution(17650297045997345959)
XLA Ops:
  1.4 3.1 %collective-permute-start = (bf16[64,128]{1,0:T(8,128)(2,1)S(1)}, bf16[64,128]{1,0:T(8,128)(2,1)S(1)}, u32[]{:S(2)}, u32[]{:S(2)}) collective-permute-start(bf16[64,128]{1,0:T(8,128)(2,1)S(1)} %get-tuple-element.61), channel_id=1, source_target_pairs={{0,1},{1,0},{2,3},{3,2},{4,5},{5,4},{6,7},{7,6},{8,9},{9,8},{10,11... | collective-permute-start | bytes 49160 | tf_op jit(solution)/shard_map/ppermute | solution.py:52
  4.5 2.6 %collective-permute-start.1 = (bf16[64,128]{1,0:T(8,128)(2,1)S(1)}, bf16[64,128]{1,0:T(8,128)(2,1)S(1)}, u32[]{:S(2)}, u32[]{:S(2)}) collective-permute-start(bf16[64,128]{1,0:T(8,128)(2,1)S(1)} %get-tuple-element.61), channel_id=1, source_target_pairs={{0,2},{1,3},{2,0},{3,1},{4,6},{5,7},{6,4},{7,5},{8,10},{9,11},{10,... | collective-permute-start | bytes 49160 | tf_op jit(solution)/shard_map/ppermute | solution.py:52
  7.1 6.2 %all-to-all-start = ((f32[32,8,8,128]{3,2,1,0:T(8,128)}), f32[32,8,8,128]{3,2,1,0:T(8,128)}, u32[]{:S(2)}, u32[]{:S(2)}) async-start(f32[32,8,8,128]{3,2,1,0:T(8,128)} %param.9), calls=%async_computation | async-start | bytes 2097152 | tf_op jit(solution)/shard_map/all_to_all | solution.py:518
  14.5 6.3 %start.1 = (bf16[320,128]{1,0:T(8,128)(2,1)S(1)}, bf16[320,128]{1,0:T(8,128)(2,1)}, bf16[320,128]{1,0:T(8,128)(2,1)}, bf16[320,128]{1,0:T(8,128)(2,1)}, bf16[128...) custom-call(f32[32,16384]{1,0:T(8,128)} %density_ref.1, ...), custom_call_target="tpu_custom_call" | custom-call | tf_op jit(solution)/shard_map/start/pallas_call | solution.py:109
  20.8 1.8 %collective-permute-start.13 = (bf16[128,4096]{1,0:T(8,128)(2,1)}, bf16[128,4096]{1,0:T(8,128)(2,1)S(1)}, u32[]{:S(2)}, u32[]{:S(2)}) collective-permute-start(bf16[128,4096]{1,0:T(8,128)(2,1)} %get-tuple-element.44), channel_id=1, source_target_pairs={{0,8},{8,0},{16,24},{24,16},{1,9},{9,1},{17,25},{25,17},{2,10},{10... | collective-permute-start | bytes 3145736 | tf_op jit(solution)/shard_map/ppermute | solution.py:52
  24.9 2.6 %collective-permute-start.5 = (bf16[320,128]{1,0:T(8,128)(2,1)}, bf16[320,128]{1,0:T(8,128)(2,1)S(1)}, u32[]{:S(2)}, u32[]{:S(2)}) collective-permute-start(bf16[320,128]{1,0:T(8,128)(2,1)} %get-tuple-element.34), channel_id=1, source_target_pairs={{0,24},{8,16},{16,8},{24,0},{1,25},{9,17},{17,9},{25,1},{2,26},{10... | collective-permute-start | bytes 245768 | tf_op jit(solution)/shard_map/ppermute | solution.py:52
  27.5 26.1 %collective-permute-done.3.refs_1_ = bf16[320,128]{1,0:T(8,128)(2,1)S(1)} collective-permute-done((bf16[320,128]{1,0:T(8,128)(2,1)}, bf16[320,128]{1,0:T(8,128)(2,1)S(1)}, u32[]{:S(2)}, u32[]{:S(2)}) %collective-permute-start.3) | collective-permute-done | bytes 81952 | tf_op jit(solution)/shard_map/ppermute | solution.py:52
  54.1 2.0 %collective-permute-done.5.refs_3_ = bf16[320,128]{1,0:T(8,128)(2,1)S(1)} collective-permute-done((bf16[320,128]{1,0:T(8,128)(2,1)}, bf16[320,128]{1,0:T(8,128)(2,1)S(1)}, u32[]{:S(2)}, u32[]{:S(2)}) %collective-permute-start.5) | collective-permute-done | bytes 81952 | tf_op jit(solution)/shard_map/ppermute | solution.py:52
  59.7 1.9 %collective-permute-start.11 = (f32[4,128]{1,0:T(4,128)S(1)}, f32[4,128]{1,0:T(4,128)S(1)}, u32[]{:S(2)}, u32[]{:S(2)}) collective-permute-start(f32[4,128]{1,0:T(4,128)S(1)} %get-tuple-element.40), channel_id=1, source_target_pairs={{0,2},{1,3},{2,0},{3,1},{4,6},{5,7},{6,4},{7,5},{8,10},{9,11},{10,... | collective-permute-start | bytes 6152 | tf_op jit(solution)/shard_map/ppermute | solution.py:52
  63.0 2.9 %prepare.1 = (f32[32,4,16,128]{3,2,1,0:T(8,128)}, bf16[4,512,128]{2,1,0:T(8,128)(2,1)}, bf16[4,128,128]{2,1,0:T(8,128)(2,1)}) custom-call(f32[16]{0:T(128)S(1)} %copy-done.7, bf16[320,128]{1,0:T(8,128)(2,1)S(1)} %get-tuple-element.31.refs_0_, bf16[320,128]{1,0:T(8,128)(2,1)S(1)} %collective-permute-done.3.refs_1_, ...), custom_call_target="tpu_custom_call" | custom-call | tf_op jit(solution)/shard_map/prepare/pallas_call | solution.py:200
  67.5 5.3 %slab_first.1 = (f32[34,4,16,128]{3,2,1,0:T(8,128)}, f32[4,8,3,128]{3,2,1,0:T(4,128)}) custom-call(f32[4,8,8,8,128]{4,3,2,1,0:T(8,128)} %bitcast.source_ref, f32[32,4,16,128]{3,2,1,0:T(8,128)} %get-tuple-element.35.inverse_ref, bf16[4,512,128]{2,1,0:T(8,128)(2,1)} %get-tuple-element.36.hit_ref, bf16[4,128,128]{2,1,0:T(8,128)(2,1)} %get-tuple-element.37.lane_ref, ...), custom_call_target="tpu_custom_call" | custom-call | tf_op jit(solution)/shard_map/slab_first/pallas_call | solution.py:374
  72.8 2.8 %all-to-all-start.1 = ((f32[32,3,128]{2,1,0:T(4,128)}), f32[32,3,128]{2,1,0:T(4,128)S(1)}, u32[]{:S(2)}, u32[]{:S(2)}) async-start(f32[32,3,128]{2,1,0:T(4,128)} %bitcast.57), calls=%async_computation.1 | async-start | bytes 131072 | tf_op jit(solution)/shard_map/all_to_all | solution.py:539
  75.6 7.5 %all-to-all-done.1.flux_ref = f32[32,3,128]{2,1,0:T(4,128)S(1)} async-done(((f32[32,3,128]{2,1,0:T(4,128)}), f32[32,3,128]{2,1,0:T(4,128)S(1)}, u32[]{:S(2)}, u32[]{:S(2)}) %all-to-all-start.1) | async-done | bytes 49184 | tf_op jit(solution)/shard_map/all_to_all | solution.py:539
  94.5 9.3 %all_to_all.25 = f32[32,3,128]{2,1,0:T(4,128)S(1)} all-to-all(f32[32,3,128]{2,1,0:T(4,128)S(1)} %potential.3), channel_id=1, replica_groups=mesh['row'=4,'col'=2,'vol'=4] {'row','col','vol'}, dimensions={0} | all-to-all | bytes 98304 | tf_op jit(solution)/shard_map/all_to_all | solution.py:550
  103.8 5.0 %slab_last.1 = (f32[4,8,8,8,128]{4,3,2,1,0:T(8,128)}, f32[4,8,3,128]{3,2,1,0:T(4,128)S(1)}) custom-call(f32[4,8,8,8,128]{4,3,2,1,0:T(8,128)} %bitcast.source_ref, f32[32,4,16,128]{3,2,1,0:T(8,128)S(1)} %copy-done.2, bf16[4,512,128]{2,1,0:T(8,128)(2,1)S(1)} %copy-done.3, bf16[4,128,128]{2,1,0:T(8,128)(2,1)S(1)} %copy-done.5, f32[4,8,3,128]{3,2,1,0:T(4,128)S(1)} %bitcast.54, ...), custom_call_target="tpu_custom_call" | custom-call | tf_op jit(solution)/shard_map/slab_last/pallas_call | solution.py:374
  108.9 9.2 %all_to_all.26.flux_ref = f32[32,3,128]{2,1,0:T(4,128)S(1)} all-to-all(f32[32,3,128]{2,1,0:T(4,128)S(1)} %bitcast.55), channel_id=1, replica_groups=mesh['row'=4,'col'=2,'vol'=4] {'row','col','vol'}, dimensions={0} | all-to-all | bytes 98304 | tf_op jit(solution)/shard_map/all_to_all | solution.py:554
  118.1 1.6 %update.5 = (bf16[32,4096]{1,0:T(8,128)(2,1)S(1)}, bf16[32,4096]{1,0:T(8,128)(2,1)S(1)}) custom-call(f32[32,3,128]{2,1,0:T(4,128)S(1)} %all_to_all.26.flux_ref, bf16[128,4096]{1,0:T(8,128)(2,1)S(1)} %copy-done, bf16[128,4096]{1,0:T(8,128)(2,1)S(1)} %collective-permute-done.13.a_mate, bf16[128,4096]{1,0:T(8,128)(2,1)S(1)} %copy-done.1, ...), custom_call_target="tpu_custom_call" | custom-call | tf_op jit(solution)/shard_map/update/pallas_call | solution.py:403
  121.0 6.6 %collective-permute-done.19.refs_9_ = bf16[32,4096]{1,0:T(8,128)(2,1)S(1)} collective-permute-done((bf16[32,4096]{1,0:T(8,128)(2,1)S(1)}, bf16[32,4096]{1,0:T(8,128)(2,1)S(1)}, u32[]{:S(2)}, u32[]{:S(2)}) %collective-permute-start.19) | collective-permute-done | bytes 262176 | tf_op jit(solution)/shard_map/ppermute | solution.py:52
  129.1 3.5 %all-to-all-start.4 = ((f32[32,8,8,128]{3,2,1,0:T(8,128)}), f32[32,8,8,128]{3,2,1,0:T(8,128)}, u32[]{:S(2)}, u32[]{:S(2)}) async-start(f32[32,8,8,128]{3,2,1,0:T(8,128)} %bitcast.56), calls=%async_computation.4 | async-start | bytes 2097152 | tf_op jit(solution)/shard_map/all_to_all | solution.py:556
  132.7 1.6 %collective-permute-start.22 = (bf16[32,4096]{1,0:T(8,128)(2,1)S(1)}, bf16[32,4096]{1,0:T(8,128)(2,1)S(1)}, u32[]{:S(2)}, u32[]{:S(2)}) collective-permute-start(bf16[32,4096]{1,0:T(8,128)(2,1)S(1)} %get-tuple-element.58), channel_id=1, source_target_pairs={{0,16},{8,24},{16,0},{24,8},{1,17},{9,25},{17,1},{25,9},{2,18},{10... | collective-permute-start | bytes 786440 | tf_op jit(solution)/shard_map/ppermute | solution.py:52
  134.3 1.6 %collective-permute-done.21 = bf16[32,4096]{1,0:T(8,128)(2,1)S(1)} collective-permute-done((bf16[32,4096]{1,0:T(8,128)(2,1)S(1)}, bf16[32,4096]{1,0:T(8,128)(2,1)S(1)}, u32[]{:S(2)}, u32[]{:S(2)}) %collective-permute-start.21) | collective-permute-done | bytes 262176 | tf_op jit(solution)/shard_map/ppermute | solution.py:52
  136.0 13.3 %collective-permute-done.22 = bf16[32,4096]{1,0:T(8,128)(2,1)S(1)} collective-permute-done((bf16[32,4096]{1,0:T(8,128)(2,1)S(1)}, bf16[32,4096]{1,0:T(8,128)(2,1)S(1)}, u32[]{:S(2)}, u32[]{:S(2)}) %collective-permute-start.22) | collective-permute-done | bytes 262176 | tf_op jit(solution)/shard_map/ppermute | solution.py:52
  150.9 6.6 %all-to-all-done.4.in_ref = f32[32,8,8,128]{3,2,1,0:T(8,128)} async-done(((f32[32,8,8,128]{3,2,1,0:T(8,128)}), f32[32,8,8,128]{3,2,1,0:T(8,128)}, u32[]{:S(2)}, u32[]{:S(2)}) %all-to-all-start.4) | async-done | bytes 1048608 | tf_op jit(solution)/shard_map/all_to_all | solution.py:556
  157.5 2.0 %landed.1 = f32[32,8,8,128]{3,2,1,0:T(8,128)} custom-call(f32[32,8,8,128]{3,2,1,0:T(8,128)} %all-to-all-done.4.in_ref), custom_call_target="tpu_custom_call" | custom-call | tf_op jit(solution)/shard_map/landed/pallas_call | solution.py:232
  (89 shorter events, 27.2 us)
Async XLA Ops:
  1.4 12.4 %collective-permute-start = (bf16[64,128]{1,0:T(8,128)(2,1)S(1)}, bf16[64,128]{1,0:T(8,128)(2,1)S(1)}, u32[]{:S(2)}, u32[]{:S(2)}) collective-permute-start(bf16[64,128]{1,0:T(8,128)(2,1)S(1)} %get-tuple-element.61), channel_id=1, source_target_pairs={{0,1},{1,0},{2,3},{3,2},{4,5},{5,4},{6,7},{7,6},{8,9},{9,8},{10,11... | collective-permute-start | bytes 49160 | tf_op jit(solution)/shard_map/ppermute | solution.py:52
  4.5 9.4 %collective-permute-start.1 = (bf16[64,128]{1,0:T(8,128)(2,1)S(1)}, bf16[64,128]{1,0:T(8,128)(2,1)S(1)}, u32[]{:S(2)}, u32[]{:S(2)}) collective-permute-start(bf16[64,128]{1,0:T(8,128)(2,1)S(1)} %get-tuple-element.61), channel_id=1, source_target_pairs={{0,2},{1,3},{2,0},{3,1},{4,6},{5,7},{6,4},{7,5},{8,10},{9,11},{10,... | collective-permute-start | bytes 49160 | tf_op jit(solution)/shard_map/ppermute | solution.py:52
  7.1 6.8 %collective-permute-start.2 = (bf16[64,128]{1,0:T(8,128)(2,1)S(1)}, bf16[64,128]{1,0:T(8,128)(2,1)S(1)}, u32[]{:S(2)}, u32[]{:S(2)}) collective-permute-start(bf16[64,128]{1,0:T(8,128)(2,1)S(1)} %get-tuple-element.61), channel_id=1, source_target_pairs={{0,3},{1,2},{2,1},{3,0},{4,7},{5,6},{6,5},{7,4},{8,11},{9,10},{10,... | collective-permute-start | bytes 49160 | tf_op jit(solution)/shard_map/ppermute | solution.py:52
  7.1 59.9 %all-to-all-start = ((f32[32,8,8,128]{3,2,1,0:T(8,128)}), f32[32,8,8,128]{3,2,1,0:T(8,128)}, u32[]{:S(2)}, u32[]{:S(2)}) async-start(f32[32,8,8,128]{3,2,1,0:T(8,128)} %param.9), calls=%async_computation | async-start | bytes 2097152 | tf_op jit(solution)/shard_map/all_to_all | solution.py:518
  20.8 54.8 %collective-permute-start.13 = (bf16[128,4096]{1,0:T(8,128)(2,1)}, bf16[128,4096]{1,0:T(8,128)(2,1)S(1)}, u32[]{:S(2)}, u32[]{:S(2)}) collective-permute-start(bf16[128,4096]{1,0:T(8,128)(2,1)} %get-tuple-element.44), channel_id=1, source_target_pairs={{0,8},{8,0},{16,24},{24,16},{1,9},{9,1},{17,25},{25,17},{2,10},{10... | collective-permute-start | bytes 3145736 | tf_op jit(solution)/shard_map/ppermute | solution.py:52
  22.6 53.1 %collective-permute-start.14 = (bf16[128,4096]{1,0:T(8,128)(2,1)}, bf16[128,4096]{1,0:T(8,128)(2,1)}, u32[]{:S(2)}, u32[]{:S(2)}) collective-permute-start(bf16[128,4096]{1,0:T(8,128)(2,1)} %get-tuple-element.46), channel_id=1, source_target_pairs={{0,16},{8,24},{16,0},{24,8},{1,17},{9,25},{17,1},{25,9},{2,18},{10... | collective-permute-start | bytes 3145736 | tf_op jit(solution)/shard_map/ppermute | solution.py:52
  24.0 29.6 %collective-permute-start.3 = (bf16[320,128]{1,0:T(8,128)(2,1)}, bf16[320,128]{1,0:T(8,128)(2,1)S(1)}, u32[]{:S(2)}, u32[]{:S(2)}) collective-permute-start(bf16[320,128]{1,0:T(8,128)(2,1)} %get-tuple-element.32), channel_id=1, source_target_pairs={{0,8},{8,0},{16,24},{24,16},{1,9},{9,1},{17,25},{25,17},{2,10},{10... | collective-permute-start | bytes 245768 | tf_op jit(solution)/shard_map/ppermute | solution.py:52
  24.6 29.0 %collective-permute-start.4 = (bf16[320,128]{1,0:T(8,128)(2,1)}, bf16[320,128]{1,0:T(8,128)(2,1)S(1)}, u32[]{:S(2)}, u32[]{:S(2)}) collective-permute-start(bf16[320,128]{1,0:T(8,128)(2,1)} %get-tuple-element.33), channel_id=1, source_target_pairs={{0,16},{8,24},{16,0},{24,8},{1,17},{9,25},{17,1},{25,9},{2,18},{10... | collective-permute-start | bytes 245768 | tf_op jit(solution)/shard_map/ppermute | solution.py:52
  24.9 31.2 %collective-permute-start.5 = (bf16[320,128]{1,0:T(8,128)(2,1)}, bf16[320,128]{1,0:T(8,128)(2,1)S(1)}, u32[]{:S(2)}, u32[]{:S(2)}) collective-permute-start(bf16[320,128]{1,0:T(8,128)(2,1)} %get-tuple-element.34), channel_id=1, source_target_pairs={{0,24},{8,16},{16,8},{24,0},{1,25},{9,17},{17,9},{25,1},{2,26},{10... | collective-permute-start | bytes 245768 | tf_op jit(solution)/shard_map/ppermute | solution.py:52
  53.6 2.5 %collective-permute-start.6 = (bf16[320,128]{1,0:T(8,128)(2,1)S(1)}, bf16[320,128]{1,0:T(8,128)(2,1)S(1)}, u32[]{:S(2)}, u32[]{:S(2)}) collective-permute-start(bf16[320,128]{1,0:T(8,128)(2,1)S(1)} %get-tuple-element.31.refs_0_), channel_id=1, source_target_pairs={{0,4},{4,0},{1,5},{5,1},{2,6},{6,2},{3,7},{7,3},{8,12},{12,8},{9,1... | collective-permute-start | bytes 245768 | tf_op jit(solution)/shard_map/ppermute | solution.py:52
  53.6 3.0 %collective-permute-start.7 = (bf16[320,128]{1,0:T(8,128)(2,1)S(1)}, bf16[320,128]{1,0:T(8,128)(2,1)S(1)}, u32[]{:S(2)}, u32[]{:S(2)}) collective-permute-start(bf16[320,128]{1,0:T(8,128)(2,1)S(1)} %collective-permute-done.3.refs_1_), channel_id=1, source_target_pairs={{0,4},{4,0},{1,5},{5,1},{2,6},{6,2},{3,7},{7,3},{8,12},{12,8},{9,1... | collective-permute-start | bytes 245768 | tf_op jit(solution)/shard_map/ppermute | solution.py:52
  58.1 7.8 %collective-permute-start.10 = (f32[4,128]{1,0:T(4,128)S(1)}, f32[4,128]{1,0:T(4,128)S(1)}, u32[]{:S(2)}, u32[]{:S(2)}) collective-permute-start(f32[4,128]{1,0:T(4,128)S(1)} %get-tuple-element.39), channel_id=1, source_target_pairs={{0,1},{1,0},{2,3},{3,2},{4,5},{5,4},{6,7},{7,6},{8,9},{9,8},{10,11... | collective-permute-start | bytes 6152 | tf_op jit(solution)/shard_map/ppermute | solution.py:52
  59.7 6.3 %collective-permute-start.11 = (f32[4,128]{1,0:T(4,128)S(1)}, f32[4,128]{1,0:T(4,128)S(1)}, u32[]{:S(2)}, u32[]{:S(2)}) collective-permute-start(f32[4,128]{1,0:T(4,128)S(1)} %get-tuple-element.40), channel_id=1, source_target_pairs={{0,2},{1,3},{2,0},{3,1},{4,6},{5,7},{6,4},{7,5},{8,10},{9,11},{10,... | collective-permute-start | bytes 6152 | tf_op jit(solution)/shard_map/ppermute | solution.py:52
  61.6 5.4 %collective-permute-start.12 = (f32[4,128]{1,0:T(4,128)S(1)}, f32[4,128]{1,0:T(4,128)S(1)}, u32[]{:S(2)}, u32[]{:S(2)}) collective-permute-start(f32[4,128]{1,0:T(4,128)S(1)} %get-tuple-element.41), channel_id=1, source_target_pairs={{0,3},{1,2},{2,1},{3,0},{4,7},{5,6},{6,5},{7,4},{8,11},{9,10},{10,... | collective-permute-start | bytes 6152 | tf_op jit(solution)/shard_map/ppermute | solution.py:52
  72.8 10.3 %all-to-all-start.1 = ((f32[32,3,128]{2,1,0:T(4,128)}), f32[32,3,128]{2,1,0:T(4,128)S(1)}, u32[]{:S(2)}, u32[]{:S(2)}) async-start(f32[32,3,128]{2,1,0:T(4,128)} %bitcast.57), calls=%async_computation.1 | async-start | bytes 131072 | tf_op jit(solution)/shard_map/all_to_all | solution.py:539
  84.5 5.6 %collective-permute-start.15 = (bf16[32,2048]{1,0:T(8,128)(2,1)S(1)}, bf16[32,2048]{1,0:T(8,128)(2,1)S(1)}, u32[]{:S(2)}, u32[]{:S(2)}) collective-permute-start(bf16[32,2048]{1,0:T(8,128)(2,1)S(1)} %get-tuple-element.47.a_half.refs_0_), channel_id=1, source_target_pairs={{0,16},{8,24},{16,0},{24,8},{1,17},{9,25},{17,1},{25,9},{2,18},{10... | collective-permute-start | bytes 393224 | tf_op jit(solution)/shard_map/ppermute | solution.py:52
  85.3 5.0 %collective-permute-start.17 = (bf16[32,2048]{1,0:T(8,128)(2,1)S(1)}, bf16[32,2048]{1,0:T(8,128)(2,1)S(1)}, u32[]{:S(2)}, u32[]{:S(2)}) collective-permute-start(bf16[32,2048]{1,0:T(8,128)(2,1)S(1)} %get-tuple-element.49.b_half.refs_4_), channel_id=1, source_target_pairs={{0,8},{8,0},{16,24},{24,16},{1,9},{9,1},{17,25},{25,17},{2,10},{10... | collective-permute-start | bytes 393224 | tf_op jit(solution)/shard_map/ppermute | solution.py:52
  87.2 5.2 %collective-permute-start.16 = (bf16[32,2048]{1,0:T(8,128)(2,1)S(1)}, bf16[32,2048]{1,0:T(8,128)(2,1)S(1)}, u32[]{:S(2)}, u32[]{:S(2)}) collective-permute-start(bf16[32,2048]{1,0:T(8,128)(2,1)S(1)} %get-tuple-element.48.a_half.refs_2_), channel_id=1, source_target_pairs={{0,16},{8,24},{16,0},{24,8},{1,17},{9,25},{17,1},{25,9},{2,18},{10... | collective-permute-start | bytes 393224 | tf_op jit(solution)/shard_map/ppermute | solution.py:52
  88.7 5.0 %collective-permute-start.18 = (bf16[32,2048]{1,0:T(8,128)(2,1)S(1)}, bf16[32,2048]{1,0:T(8,128)(2,1)S(1)}, u32[]{:S(2)}, u32[]{:S(2)}) collective-permute-start(bf16[32,2048]{1,0:T(8,128)(2,1)S(1)} %get-tuple-element.50.b_half.refs_6_), channel_id=1, source_target_pairs={{0,8},{8,0},{16,24},{24,16},{1,9},{9,1},{17,25},{25,17},{2,10},{10... | collective-permute-start | bytes 393224 | tf_op jit(solution)/shard_map/ppermute | solution.py:52
  119.7 7.9 %collective-permute-start.19 = (bf16[32,4096]{1,0:T(8,128)(2,1)S(1)}, bf16[32,4096]{1,0:T(8,128)(2,1)S(1)}, u32[]{:S(2)}, u32[]{:S(2)}) collective-permute-start(bf16[32,4096]{1,0:T(8,128)(2,1)S(1)} %get-tuple-element.55.refs_8_), channel_id=1, source_target_pairs={{0,16},{8,24},{16,0},{24,8},{1,17},{9,25},{17,1},{25,9},{2,18},{10... | collective-permute-start | bytes 786440 | tf_op jit(solution)/shard_map/ppermute | solution.py:52
  120.5 7.8 %collective-permute-start.20 = (bf16[32,4096]{1,0:T(8,128)(2,1)S(1)}, bf16[32,4096]{1,0:T(8,128)(2,1)S(1)}, u32[]{:S(2)}, u32[]{:S(2)}) collective-permute-start(bf16[32,4096]{1,0:T(8,128)(2,1)S(1)} %get-tuple-element.56.refs_10_), channel_id=1, source_target_pairs={{0,8},{8,0},{16,24},{24,16},{1,9},{9,1},{17,25},{25,17},{2,10},{10... | collective-permute-start | bytes 786440 | tf_op jit(solution)/shard_map/ppermute | solution.py:52
  128.6 7.4 %collective-permute-start.21 = (bf16[32,4096]{1,0:T(8,128)(2,1)S(1)}, bf16[32,4096]{1,0:T(8,128)(2,1)S(1)}, u32[]{:S(2)}, u32[]{:S(2)}) collective-permute-start(bf16[32,4096]{1,0:T(8,128)(2,1)S(1)} %get-tuple-element.57), channel_id=1, source_target_pairs={{0,8},{8,0},{16,24},{24,16},{1,9},{9,1},{17,25},{25,17},{2,10},{10... | collective-permute-start | bytes 786440 | tf_op jit(solution)/shard_map/ppermute | solution.py:52
  129.1 28.4 %all-to-all-start.4 = ((f32[32,8,8,128]{3,2,1,0:T(8,128)}), f32[32,8,8,128]{3,2,1,0:T(8,128)}, u32[]{:S(2)}, u32[]{:S(2)}) async-start(f32[32,8,8,128]{3,2,1,0:T(8,128)} %bitcast.56), calls=%async_computation.4 | async-start | bytes 2097152 | tf_op jit(solution)/shard_map/all_to_all | solution.py:556
  132.7 16.6 %collective-permute-start.22 = (bf16[32,4096]{1,0:T(8,128)(2,1)S(1)}, bf16[32,4096]{1,0:T(8,128)(2,1)S(1)}, u32[]{:S(2)}, u32[]{:S(2)}) collective-permute-start(bf16[32,4096]{1,0:T(8,128)(2,1)S(1)} %get-tuple-element.58), channel_id=1, source_target_pairs={{0,16},{8,24},{16,0},{24,8},{1,17},{9,25},{17,1},{25,9},{2,18},{10... | collective-permute-start | bytes 786440 | tf_op jit(solution)/shard_map/ppermute | solution.py:52
  (18 other events, 205.2 us)
